TPU v7x, 32 devices: a whole 2x2x4 slice. The times are simulated.
32 devices in a mesh: ctx: 16 (over z, x, core), wa: 2 (over y).
Axes of the slice: x: 2, y: 2, z: 4, core: 2. Of those that a mesh axis runs over, the one named last changes fastest.
Arguments:
- tokens: bfloat16 [8192, 1472], P(('ctx', 'wa')), may hold values from -6 to 6
- doc_lengths: int32 [8], replicated, may hold values from 1 to 4096, 8192 in all
- key_mask: bfloat16 [8192], P('ctx'), may hold values from -3 to 0
- gain_attn: float32 [1472], replicated, may hold values from 0.1 to 1.9
- w_query: bfloat16 [1472, 384], P(None, 'wa'), may hold values from -0.0625 to 0.0625
- w_key: bfloat16 [1472, 384], P(None, 'wa'), may hold values from -0.0625 to 0.0625
- w_value: bfloat16 [1472, 384], P(None, 'wa'), may hold values from -0.15625 to 0.15625
- w_out: bfloat16 [384, 1472], P('wa'), may hold values from -1.5 to 1.5
- bias_table: float32 [32, 6], P(None, 'wa'), may hold values from -4 to 4
- gain_ffn: float32 [1472], replicated, may hold values from 0.1 to 1.9
- w_gate: bfloat16 [1472, 3584], P(None, 'wa'), may hold values from -0.15625 to 0.15625
- w_up: bfloat16 [1472, 3584], P(None, 'wa'), may hold values from -0.15625 to 0.15625
- w_down: bfloat16 [3584, 1472], P('wa'), may hold values from -0.09375 to 0.09375
- cotangent: bfloat16 [8192, 1472], P(('ctx', 'wa')), may hold values from -6 to 6
Outputs:
- layer_out: bfloat16 [8192, 1472], P(('ctx', 'wa'))
- grad_tokens: float32 [8192, 1472], P(('ctx', 'wa'))
- grad_mask: float32 [8192], P(('ctx', 'wa'))
- grad_gain_attn: float32 [1472], replicated
- grad_w_query: float32 [1472, 384], P(None, 'wa')
- grad_w_key: float32 [1472, 384], P(None, 'wa')
- grad_w_value: float32 [1472, 384], P(None, 'wa')
- grad_w_out: float32 [384, 1472], P('wa')
- grad_table: float32 [32, 6], P(None, 'wa')
- grad_gain_ffn: float32 [1472], replicated
- grad_w_gate: float32 [1472, 3584], P(None, ('wa', 'ctx'))
- grad_w_up: float32 [1472, 3584], P(None, ('wa', 'ctx'))
- grad_w_down: float32 [3584, 1472], P(('wa', 'ctx'))
Inputs may be any that keep to these rules, and one draw needn't show every extreme that they name: `doc_lengths`: document lengths in stream order; they add up to 8192, and the longest is exactly 4096.
All inputs are finite; a program needn't handle non-finite values.
Results may differ from a plain program's by a relative error of at most 0.018.
Values may be sent and summed in bfloat16 or wider, within the bound.
A program may use at most 192 MiB of HBM per device.

v0:
```python
import jax
import jax.numpy as jnp
from jax import lax
from jax.sharding import PartitionSpec as P

MAXLEN = 8192


bucket_edges = (12, 16, 23, 32, 46, 64, 91)
neg_big = -1e30
eps = 1e-06
highest = lax.Precision.HIGHEST
far_reach = 91


def shortened(shard):

    def short(part):
        return part.astype(jnp.bfloat16) if part.dtype == jnp.float32 else part

    return jax.tree.map(short, shard)


def from_behind(block, axis, distance):
    devices = range(lax.axis_size(axis))
    route = [(i - distance, i) for i in devices if i - distance in devices]
    return lax.ppermute(block, axis, route)


def bucket_of(relative):
    relative = jnp.asarray(relative, jnp.int32)
    distance = jnp.abs(relative)
    bucket = jnp.minimum(distance, 8) + 16 * (relative > 0).astype(jnp.int32)
    for edge in bucket_edges:
        bucket = bucket + (distance >= edge).astype(jnp.int32)
    return bucket


def norm_forward(inputs, gain):
    inv_root = lax.rsqrt(jnp.mean(inputs * inputs, axis=-1, keepdims=True) + eps)
    return (inputs * inv_root * gain, inv_root)


def norm_backward(inputs, inv_root, gain, grad_normed):
    scaled = gain * grad_normed
    cubed = inv_root * inv_root * inv_root
    grad_inputs = inv_root * scaled - inputs * cubed * jnp.mean(
        inputs * scaled, axis=-1, keepdims=True
    )
    grad_gain = jnp.sum(grad_normed * inputs * inv_root, axis=0)
    return (grad_inputs, grad_gain)


def gated(gate, upward):
    return jax.nn.gelu(gate, approximate=True) * upward


def doc_index(positions, starts, total_rows):
    found = jnp.sum((positions[:, None] >= starts[None, :]).astype(jnp.int32), axis=1) - 1
    inside = (positions >= 0) & (positions < total_rows)
    return jnp.where(inside, found, -1)


def one_hot_block(delta, rows, buckets):
    spots = jnp.arange(rows, dtype=jnp.int32)
    relative = delta + spots[None, :] - spots[:, None]
    return (bucket_of(relative)[:, :, None] == jnp.arange(buckets, dtype=jnp.int32)).astype(
        jnp.float32
    )


def far_row(delta, buckets):
    return (bucket_of(delta) == jnp.arange(buckets, dtype=jnp.int32)).astype(jnp.float32)


def is_far(delta, rows):
    return jnp.abs(delta) - rows + 1 >= far_reach


def block_bias(table, delta, rows):

    def block_near(unused):
        return jnp.einsum(
            "qkb,bh->hqk", one_hot_block(delta, rows, table.shape[0]), table, precision=highest
        )

    def block_far(unused):
        row_vals = jnp.sum(far_row(delta, table.shape[0])[:, None] * table, axis=0)
        return jnp.broadcast_to(row_vals[:, None, None], (table.shape[1], rows, rows))

    return lax.cond(is_far(delta, rows), block_far, block_near, 0)


def table_grad(delta, grad_scores, rows, buckets):

    def table_near(unused):
        return jnp.einsum(
            "qkb,hqk->bh", one_hot_block(delta, rows, buckets), grad_scores, precision=highest
        )

    def table_far(unused):
        return far_row(delta, buckets)[:, None] * jnp.sum(grad_scores, axis=(1, 2))[None, :]

    return lax.cond(is_far(delta, rows), table_far, table_near, 0)


def shards(
    tokens,
    doc_lengths,
    key_mask,
    gain_attn,
    w_query,
    w_key,
    w_value,
    w_out,
    bias_table,
    gain_ffn,
    w_gate,
    w_up,
    w_down,
    cotangent,
):
    own_rows = tokens.shape[0]
    group = lax.axis_size("wa")
    cycle_size = lax.axis_size("ctx")
    pair = own_rows * group
    heads_here = bias_table.shape[1]
    buckets = bias_table.shape[0]
    head_width = w_query.shape[1] // heads_here
    total_rows = pair * cycle_size
    doc_most = min(MAXLEN, total_rows // 2)
    reach = min(cycle_size - 1, (doc_most - 1) // pair + 1)
    base = lax.axis_index("ctx") * pair
    spots = jnp.arange(pair, dtype=jnp.int32)
    starts = jnp.cumsum(doc_lengths) - doc_lengths
    query_docs = doc_index(base + spots, starts, total_rows)
    tokens_wide = tokens.astype(jnp.float32)
    normed_attn, inv_attn = norm_forward(tokens_wide, gain_attn)
    normed_low = normed_attn.astype(jnp.bfloat16)
    pair_normed, pair_cot = (
        lax.all_gather(normed_low, "wa", axis=0, tiled=True),
        lax.all_gather(cotangent, "wa", axis=0, tiled=True),
    )
    queries = jnp.dot(pair_normed, w_query, preferred_element_type=jnp.float32).astype(jnp.bfloat16)
    keys = jnp.dot(pair_normed, w_key, preferred_element_type=jnp.float32).astype(jnp.bfloat16)
    values = jnp.dot(pair_normed, w_value, preferred_element_type=jnp.float32).astype(jnp.bfloat16)
    queries_h = queries.reshape(pair, heads_here, head_width)
    own_block = (keys, values, key_mask)

    def block_scores(block, delta):
        key_docs = doc_index(base + delta + spots, starts, total_rows)
        same = query_docs[:, None] == key_docs[None, :]
        product = jnp.einsum(
            "qhd,khd->hqk",
            queries_h,
            block[0].reshape(pair, heads_here, head_width),
            preferred_element_type=jnp.float32,
        )
        scores = (
            product
            + block_bias(bias_table, delta, pair)
            + block[2].astype(jnp.float32)[None, None, :]
        )
        return jnp.where(same[None], scores, neg_big)

    def add_stats(block, delta, state):

        def compute(current):
            row_max, row_sum = current
            scores = block_scores(block, delta)
            new_max = jnp.maximum(row_max, jnp.max(scores, axis=-1))
            new_sum = row_sum * jnp.exp(row_max - new_max) + jnp.sum(
                jnp.exp(scores - new_max[..., None]), axis=-1
            )
            return (new_max, new_sum)

        return compute(state)

    first_scores = block_scores(own_block, 0)
    first_max = jnp.max(first_scores, axis=-1)
    first_sum = jnp.sum(jnp.exp(first_scores - first_max[..., None]), axis=-1)

    def collect(carry, unused):
        lower, upper, row_max, row_sum, hop_count = carry
        lower = jax.tree.map(
            lambda part, own: part.astype(own.dtype), from_behind(shortened(lower), "ctx", 1), lower
        )
        upper = jax.tree.map(
            lambda part, own: part.astype(own.dtype),
            from_behind(shortened(upper), "ctx", -1),
            upper,
        )
        hop_count = hop_count + 1
        row_max, row_sum = add_stats(lower, -hop_count * pair, (row_max, row_sum))
        row_max, row_sum = add_stats(upper, hop_count * pair, (row_max, row_sum))
        return ((lower, upper, row_max, row_sum, hop_count), (lower, upper))

    start_carry = (own_block, own_block, first_max, first_sum, jnp.int32(0))
    final_carry, stacks = lax.scan(collect, start_carry, None, length=reach)
    lower_stack, upper_stack = stacks
    log_total = final_carry[2] + jnp.log(final_carry[3])
    hop_list = jnp.arange(1, reach + 1, dtype=jnp.int32)

    def add_output(block, delta, mixed):

        def compute(current):
            scores = block_scores(block, delta)
            weights = jnp.exp(scores - log_total[..., None]).astype(jnp.bfloat16)
            return current + jnp.einsum(
                "hqk,khd->qhd",
                weights,
                block[1].reshape(pair, heads_here, head_width),
                preferred_element_type=jnp.float32,
            )

        return compute(mixed)

    def output_step(mixed, slot):
        lower, upper, hop_count = slot
        mixed = add_output(lower, -hop_count * pair, mixed)
        return (add_output(upper, hop_count * pair, mixed), None)

    mixed_start = add_output(own_block, 0, jnp.zeros((pair, heads_here, head_width), jnp.float32))
    mixed, unused_out = lax.scan(output_step, mixed_start, (lower_stack, upper_stack, hop_list))
    attended = mixed.reshape(pair, -1).astype(jnp.bfloat16)
    branch = lax.psum_scatter(
        jnp.dot(attended, w_out, preferred_element_type=jnp.float32).astype(jnp.bfloat16),
        "wa",
        scatter_dimension=0,
        tiled=True,
    ).astype(jnp.float32)
    hidden = tokens_wide + branch
    normed_ffn, inv_ffn = norm_forward(hidden, gain_ffn)
    ffn_low = normed_ffn.astype(jnp.bfloat16)
    pair_ffn = lax.all_gather(ffn_low, "wa", axis=0, tiled=True)
    gate = jnp.dot(pair_ffn, w_gate, preferred_element_type=jnp.float32)
    upward = jnp.dot(pair_ffn, w_up, preferred_element_type=jnp.float32)
    inner = gated(gate, upward).astype(jnp.bfloat16)
    ffn_part = jnp.dot(inner, w_down, preferred_element_type=jnp.float32)
    layer_out = (
        hidden
        + lax.psum_scatter(
            ffn_part.astype(jnp.bfloat16), "wa", scatter_dimension=0, tiled=True
        ).astype(jnp.float32)
    ).astype(jnp.bfloat16)
    grad_inner = jnp.dot(pair_cot, w_down.T, preferred_element_type=jnp.float32)
    down_half = jnp.dot(inner.T, pair_cot, preferred_element_type=jnp.float32)
    unused_value, pullback = jax.vjp(gated, gate, upward)
    grad_gate, grad_upward = pullback(grad_inner)
    grad_gate = grad_gate.astype(jnp.bfloat16)
    grad_upward = grad_upward.astype(jnp.bfloat16)
    gate_half = jnp.dot(pair_ffn.T, grad_gate, preferred_element_type=jnp.float32)
    up_half = jnp.dot(pair_ffn.T, grad_upward, preferred_element_type=jnp.float32)
    grad_pair_ffn = jnp.dot(grad_gate, w_gate.T, preferred_element_type=jnp.float32) + jnp.dot(
        grad_upward, w_up.T, preferred_element_type=jnp.float32
    )
    grad_normed_ffn = lax.psum_scatter(
        grad_pair_ffn.astype(jnp.bfloat16), "wa", scatter_dimension=0, tiled=True
    ).astype(jnp.float32)
    grad_w_gate, grad_w_up, grad_w_down = (
        lax.psum_scatter(gate_half, "ctx", scatter_dimension=1, tiled=True),
        lax.psum_scatter(up_half, "ctx", scatter_dimension=1, tiled=True),
        lax.psum_scatter(down_half, "ctx", scatter_dimension=0, tiled=True),
    )
    hidden_step, gain_ffn_part = norm_backward(hidden, inv_ffn, gain_ffn, grad_normed_ffn)
    grad_hidden = cotangent.astype(jnp.float32) + hidden_step
    pair_branch = lax.all_gather(grad_hidden.astype(jnp.bfloat16), "wa", axis=0, tiled=True)
    out_part = jnp.dot(attended.T, pair_branch, preferred_element_type=jnp.float32)
    grad_attended = (
        jnp.dot(pair_branch, w_out.T, preferred_element_type=jnp.float32)
        .astype(jnp.bfloat16)
        .reshape(pair, heads_here, head_width)
    )
    row_terms = jnp.einsum("qhd,qhd->hq", grad_attended.astype(jnp.float32), mixed)

    def block_grads(block, delta, state):

        def compute(current):
            grad_q, grad_tab, grad_k, grad_v, grad_m = current
            keys_h = block[0].reshape(pair, heads_here, head_width)
            values_h = block[1].reshape(pair, heads_here, head_width)
            scores = block_scores(block, delta)
            probs = jnp.exp(scores - log_total[..., None])
            grad_weights = jnp.einsum(
                "qhd,khd->hqk", grad_attended, values_h, preferred_element_type=jnp.float32
            )
            grad_scores = probs * (grad_weights - row_terms[..., None])
            scores_low = grad_scores.astype(jnp.bfloat16)
            weights = probs.astype(jnp.bfloat16)
            grad_q = grad_q + jnp.einsum(
                "hqk,khd->qhd", scores_low, keys_h, preferred_element_type=jnp.float32
            )
            grad_k = grad_k + jnp.einsum(
                "hqk,qhd->khd", scores_low, queries_h, preferred_element_type=jnp.float32
            ).reshape(pair, -1)
            grad_v = grad_v + jnp.einsum(
                "hqk,qhd->khd", weights, grad_attended, preferred_element_type=jnp.float32
            ).reshape(pair, -1)
            grad_m = grad_m + jnp.sum(grad_scores, axis=(0, 1))
            grad_tab = grad_tab + table_grad(delta, grad_scores, pair, buckets)
            return (grad_q, grad_tab, grad_k, grad_v, grad_m)

        return compute(state)

    def pass_down(accum):
        return jax.tree.map(
            lambda part, own: part.astype(own.dtype),
            from_behind(shortened(accum), "ctx", -1),
            accum,
        )

    def pass_up(accum):
        return jax.tree.map(
            lambda part, own: part.astype(own.dtype), from_behind(shortened(accum), "ctx", 1), accum
        )

    key_zeros = jnp.zeros((pair, heads_here * head_width), jnp.float32)
    empty_acc = (key_zeros, key_zeros, jnp.zeros((pair,), jnp.float32))
    local_state = block_grads(
        own_block,
        0,
        (
            jnp.zeros((pair, heads_here, head_width), jnp.float32),
            jnp.zeros((buckets, heads_here), jnp.float32),
        )
        + empty_acc,
    )

    def return_step(carry, slot):
        grad_q, grad_tab, lower_acc, upper_acc = carry
        lower, upper, hop_count = slot
        state = block_grads(lower, -hop_count * pair, (grad_q, grad_tab) + lower_acc)
        grad_q, grad_tab, lower_acc = (state[0], state[1], pass_down(state[2:]))
        state = block_grads(upper, hop_count * pair, (grad_q, grad_tab) + upper_acc)
        grad_q, grad_tab, upper_acc = (state[0], state[1], pass_up(state[2:]))
        return ((grad_q, grad_tab, lower_acc, upper_acc), None)

    back_start = (local_state[0], local_state[1], empty_acc, empty_acc)
    back_final, unused_back = lax.scan(
        return_step, back_start, (lower_stack, upper_stack, hop_list), reverse=True
    )
    grad_q, grad_tab, lower_acc, upper_acc = back_final
    grad_keys = (local_state[2] + lower_acc[0] + upper_acc[0]).astype(jnp.bfloat16)
    grad_values = (local_state[3] + lower_acc[1] + upper_acc[1]).astype(jnp.bfloat16)
    mask_total = local_state[4] + lower_acc[2] + upper_acc[2]
    grad_queries = grad_q.reshape(pair, -1).astype(jnp.bfloat16)
    query_part = jnp.dot(pair_normed.T, grad_queries, preferred_element_type=jnp.float32)
    key_part = jnp.dot(pair_normed.T, grad_keys, preferred_element_type=jnp.float32)
    value_part = jnp.dot(pair_normed.T, grad_values, preferred_element_type=jnp.float32)
    grad_pair = jnp.dot(grad_queries, w_query.T, preferred_element_type=jnp.float32)
    grad_pair = grad_pair + jnp.dot(grad_keys, w_key.T, preferred_element_type=jnp.float32)
    grad_pair = grad_pair + jnp.dot(grad_values, w_value.T, preferred_element_type=jnp.float32)
    grad_normed_attn, grad_mask = (
        lax.psum_scatter(
            grad_pair.astype(jnp.bfloat16), "wa", scatter_dimension=0, tiled=True
        ).astype(jnp.float32),
        lax.psum_scatter(
            mask_total.astype(jnp.bfloat16), "wa", scatter_dimension=0, tiled=True
        ).astype(jnp.float32),
    )
    token_step, gain_attn_part = norm_backward(tokens_wide, inv_attn, gain_attn, grad_normed_attn)
    grad_tokens = grad_hidden + token_step
    grad_gain_attn, grad_gain_ffn = lax.psum((gain_attn_part, gain_ffn_part), ("ctx", "wa"))
    grad_w_query, grad_w_key, grad_w_value, grad_w_out, grad_table = lax.psum(
        (query_part, key_part, value_part, out_part, grad_tab), "ctx"
    )
    return (
        layer_out,
        grad_tokens,
        grad_mask,
        grad_gain_attn,
        grad_w_query,
        grad_w_key,
        grad_w_value,
        grad_w_out,
        grad_table,
        grad_gain_ffn,
        grad_w_gate,
        grad_w_up,
        grad_w_down,
    )


def solution(mesh):
    placed = (
        P(("ctx", "wa"), None),
        P(),
        P("ctx"),
        P(),
        P(None, "wa"),
        P(None, "wa"),
        P(None, "wa"),
        P("wa", None),
        P(None, "wa"),
        P(),
        P(None, "wa"),
        P(None, "wa"),
        P("wa", None),
        P(("ctx", "wa"), None),
    )
    return jax.shard_map(
        shards,
        mesh=mesh,
        in_specs=placed,
        out_specs=(
            P(("ctx", "wa"), None),
            P(("ctx", "wa"), None),
            P(("ctx", "wa")),
            P(),
            P(None, "wa"),
            P(None, "wa"),
            P(None, "wa"),
            P("wa", None),
            P(None, "wa"),
            P(),
            P(None, ("wa", "ctx")),
            P(None, ("wa", "ctx")),
            P(("wa", "ctx"), None),
        ),
        check_vma=False,
    )
```

profile of v0, /device:TPU:0, one launch (start us, length us, event | category | flops | bytes accessed | tf_op | source)
XLA Modules:
  0.0 1975.2 jit_solution(9850412752235423931)
XLA Ops:
  16.5 11.5 fusion.155
  28.0 13.5 all-gather.5.cloned.1.call-done
  53.9 386.4 %while.94 = (s32[]{:T(128)}, bf16[512,192]{0,1:T(8,128)(2,1)}, bf16[512,192]{1,0:T(8,128)(2,1)S(1)}, bf16[512]{0:T(512)(128)(2,1)S(1)}, bf16[512,192]{0,1:T(8,12...) while((s32[]{:T(128)}, bf16[512,192]{0,1:T(8,128)(2,1)}, ...), condition=%wide.region_18.19_spmd.clone.clone, body=%wide.region_5.18_spmd.clone.clone.sunk | while | flops 850958336 | bytes 96400944 | solution.py:199
  65.3 17.5 conditional.33
  66.3 11.6 fusion.8
  82.8 17.5 conditional.32
  83.8 11.6 fusion.21
  443.6 168.3 %while.95 = (s32[]{:T(128)}, f32[512,3,64]{0,2,1:T(8,128)}, bf16[8,512,192]{1,2,0:T(8,128)(2,1)}, s32[512]{0:T(512)S(1)}, s32[8]{0:T(128)S(1)}, /*index=5*/s32[]...) while((s32[]{:T(128)}, f32[512,3,64]{0,2,1:T(8,128)}, ...), condition=%wide.region_28.29_spmd.clone.clone, body=%wide.region_19.28_spmd.clone.clone.sunk | while | flops 1046183936 | bytes 34792624 | solution.py:224
  448.8 17.5 conditional.35
  449.9 11.6 fusion.47
  466.3 17.5 conditional.34
  467.4 11.6 fusion.34
  614.9 30.5 %reduce-scatter.8.cloned.1.call-done = bf16[256,1472]{0,1:T(8,128)(2,1)} async-done(((bf16[512,1472]{0,1:T(8,128)(2,1)}), bf16[256,1472]{0,1:T(8,128)(2,1)}) %reduce-scatter.8.cloned.1.call-update) | async-done | bytes 753680 | tf_op jit(solution)/shard_map/reduce_scatter | solution.py:226
  649.8 26.0 %all-gather.7.cloned.1.call-done = bf16[512,1472]{0,1:T(8,128)(2,1)} async-done(((bf16[256,1472]{0,1:T(8,128)(2,1)}), bf16[512,1472]{0,1:T(8,128)(2,1)}) %all-gather.7.cloned.1.call-update) | async-done | bytes 1507344 | tf_op jit(solution)/shard_map/all_gather | solution.py:235
  691.3 12.4 all-gather.9.cloned.1.call-done
  703.7 10.9 multiply_convert_fusion
  727.6 25.5 %reduce-scatter.12.cloned.1.call-done = bf16[256,1472]{0,1:T(8,128)(2,1)} async-done(((bf16[512,1472]{0,1:T(8,128)(2,1)}), bf16[256,1472]{0,1:T(8,128)(2,1)}) %reduce-scatter.12.cloned.1.call-update) | async-done | bytes 753680 | tf_op jit(solution)/shard_map/reduce_scatter | solution.py:257
  758.4 26.3 %all-gather.11.cloned.1.call-done = bf16[512,1472]{0,1:T(8,128)(2,1)} async-done(((bf16[256,1472]{0,1:T(8,128)(2,1)}), bf16[512,1472]{0,1:T(8,128)(2,1)}) %all-gather.11.cloned.1.call-update) | async-done | bytes 1507344 | tf_op jit(solution)/shard_map/all_gather | solution.py:267
  791.6 18.3 fusion.188
  813.3 582.4 %while.96 = (s32[]{:T(128)}, f32[512,3,64]{0,2,1:T(8,128)}, f32[32,3]{0,1:T(4,128)}, f32[512,192]{0,1:T(8,128)}, f32[512,192]{0,1:T(8,128)}, /*index=5*/f32[512]...) while((s32[]{:T(128)}, f32[512,3,64]{0,2,1:T(8,128)}, ...), condition=%wide.region_51.52_spmd.clone.clone, body=%wide.region_34.51_spmd.clone.clone.sunk | while | flops 2294518016 | bytes 134267744 | solution.py:339
  1269.9 12.3 conditional.37
  1298.0 12.5 conditional.36
  1328.9 23.5 %conditional.39 = (f32[32,3]{0,1:T(4,128)S(1)}) conditional(s32[]{:T(128)} %convert_element_type.1670, (s32[]{:T(128)}, f32[3,512,512]{2,1,0:T(8,128)S(1)}) %tuple.306, (s32[]{:T(128)}, f32[3,512,512]{2,1,0:T(8,128)S(1)}) %tuple.306), branch_computations={%region_43.43_spmd, %region_44.45_spmd} | conditional | flops 317456896 | bytes 11538828 | solution.py:104
  1334.8 17.5 fusion.86
  1352.9 23.9 %conditional.38 = (f32[32,3]{0,1:T(4,128)S(1)}) conditional(s32[]{:T(128)} %convert_element_type.1669, (s32[]{:T(128)}, f32[3,512,512]{2,1,0:T(8,128)}) %tuple.358, (s32[]{:T(128)}, f32[3,512,512]{2,1,0:T(8,128)}) %tuple.359), branch_computations={%region_46.46_spmd, %region_47.48_spmd} | conditional | flops 317456896 | bytes 11538828 | solution.py:104
  1359.3 17.6 fusion.98
  1441.2 32.6 %psum.54 = f32[32,3]{0,1:T(4,128)} all-reduce(f32[32,3]{0,1:T(4,128)S(1)} %copy-done.68), channel_id=1, replica_groups=mesh['ctx'=16,'wa'=2] {'ctx'}, use_global_device_ids=true, to_apply=%region_62.63 | all-reduce | flops 96 | bytes 768 | tf_op jit(solution)/shard_map/psum | solution.py:364
  1481.6 38.5 %all-reduce.1 = (f32[1472]{0:T(1024)}, f32[1472]{0:T(1024)}) all-reduce(f32[1472]{0:T(1024)S(1)} %get-tuple-element.2394, f32[1472]{0:T(1024)S(1)} %copy-done.71), channel_id=1, replica_groups=mesh['ctx'=16,'wa'=2] {'ctx','wa'}, use_global_device_ids=true, to_apply=%region_57.58 | all-reduce | flops 2944 | bytes 23552 | tf_op jit(solution)/shard_map/psum | solution.py:363
  1523.6 56.6 %all-reduce.5.cloned.1.call-done = (f32[1472,192]{0,1:T(8,128)}, f32[1472,192]{0,1:T(8,128)}, f32[1472,192]{0,1:T(8,128)}, f32[192,1472]{1,0:T(8,128)}) async-done(((f32[1472,192]{0,1:T(8,128)}, f32[1472,192]{0,1:T(8,128)}, f32[1472,192]{0,1:T(8,128)}, f32[192,1472]{1,0:T(8,128)}), (f32[1472,192]{0,1:T(8,128)}, f32[1472,192]{0,1:T(8,128)}, f32[1472,192]{0,1:T(8,128)}, ...) | async-done | bytes 4522000 | tf_op jit(solution)/shard_map/psum | solution.py:364
  1580.2 127.3 %reduce-scatter.20.cloned.1.call-done = f32[112,1472]{1,0:T(8,128)} async-done(((f32[1792,1472]{1,0:T(8,128)}), f32[112,1472]{1,0:T(8,128)}) %reduce-scatter.20.cloned.1.call-update) | async-done | bytes 659472 | tf_op jit(solution)/shard_map/reduce_scatter | solution.py:263
  1707.5 127.7 %reduce-scatter.18.cloned.1.call-done = f32[1472,112]{0,1:T(8,128)} async-done(((f32[1472,1792]{0,1:T(8,128)}), f32[1472,112]{0,1:T(8,128)}) %reduce-scatter.18.cloned.1.call-update) | async-done | bytes 659472 | tf_op jit(solution)/shard_map/reduce_scatter | solution.py:262
  1835.3 127.1 %reduce-scatter.16.cloned.1.call-done = f32[1472,112]{0,1:T(8,128)} async-done(((f32[1472,1792]{0,1:T(8,128)}), f32[1472,112]{0,1:T(8,128)}) %reduce-scatter.16.cloned.1.call-update) | async-done | bytes 659472 | tf_op jit(solution)/shard_map/reduce_scatter | solution.py:261
  (1659 shorter events, 1245.7 us)
Async XLA Ops:
  12.2 633.2 %reduce-scatter.8.cloned.1.call-start = ((), (), s32[]{:S(2)}) async-start(), calls=%async_computation.8 | async-start | bytes 2260992 | tf_op jit(solution)/shard_map/reduce_scatter | solution.py:226
  54.2 46.1 %collective-permute-start.5 = (bf16[512]{0:T(512)(128)(2,1)}, bf16[512]{0:T(512)(128)(2,1)S(1)}, u32[]{:S(2)}, u32[]{:S(2)}) collective-permute-start(bf16[512]{0:T(512)(128)(2,1)} %get-tuple-element.3043), channel_id=1, source_target_pairs={{2,0},{4,2},{6,4},{8,6},{10,8},{12,10},{14,12},{16,14},{18,16},{20... | collective-permute-start | bytes 3080 | tf_op jit(solution)/shard_map/while/body/eval_jaxpr/ppermute | solution.py:27
  55.5 50.4 %collective-permute-start.2 = (bf16[512]{0:T(512)(128)(2,1)S(1)}, bf16[512]{0:T(512)(128)(2,1)S(1)}, u32[]{:S(2)}, u32[]{:S(2)}) collective-permute-start(bf16[512]{0:T(512)(128)(2,1)S(1)} %get-tuple-element.3040), channel_id=1, source_target_pairs={{0,2},{2,4},{4,6},{6,8},{8,10},{10,12},{12,14},{14,16},{16,18},{18... | collective-permute-start | bytes 3080 | tf_op jit(solution)/shard_map/while/body/eval_jaxpr/ppermute | solution.py:27
  58.5 53.9 %collective-permute-start.3 = (bf16[512,192]{0,1:T(8,128)(2,1)}, bf16[512,192]{0,1:T(8,128)(2,1)S(1)}, u32[]{:S(2)}, u32[]{:S(2)}) collective-permute-start(bf16[512,192]{0,1:T(8,128)(2,1)} %get-tuple-element.3041), channel_id=1, source_target_pairs={{2,0},{4,2},{6,4},{8,6},{10,8},{12,10},{14,12},{16,14},{18,16},{20... | collective-permute-start | bytes 589832 | tf_op jit(solution)/shard_map/while/body/eval_jaxpr/ppermute | solution.py:27
  59.8 47.9 %collective-permute-start = (bf16[512,192]{0,1:T(8,128)(2,1)}, bf16[512,192]{0,1:T(8,128)(2,1)S(1)}, u32[]{:S(2)}, u32[]{:S(2)}) collective-permute-start(bf16[512,192]{0,1:T(8,128)(2,1)} %get-tuple-element.3038), channel_id=1, source_target_pairs={{0,2},{2,4},{4,6},{6,8},{8,10},{10,12},{12,14},{14,16},{16,18},{18... | collective-permute-start | bytes 589832 | tf_op jit(solution)/shard_map/while/body/eval_jaxpr/ppermute | solution.py:27
  63.4 48.7 %collective-permute-start.4 = (bf16[512,192]{1,0:T(8,128)(2,1)}, bf16[512,192]{1,0:T(8,128)(2,1)S(1)}, u32[]{:S(2)}, u32[]{:S(2)}) collective-permute-start(bf16[512,192]{1,0:T(8,128)(2,1)} %get-tuple-element.3042), channel_id=1, source_target_pairs={{2,0},{4,2},{6,4},{8,6},{10,8},{12,10},{14,12},{16,14},{18,16},{20... | collective-permute-start | bytes 589832 | tf_op jit(solution)/shard_map/while/body/eval_jaxpr/ppermute | solution.py:27
  614.8 60.9 %all-gather.7.cloned.1.call-start = ((), (), s32[]{:S(2)}) async-start(), calls=%async_computation.9 | async-start | bytes 2260992 | tf_op jit(solution)/shard_map/all_gather | solution.py:235
  649.2 54.5 %all-gather.9.cloned.1.call-start = ((), (), s32[]{:S(2)}) async-start(), calls=%async_computation.11 | async-start | bytes 2260992 | tf_op jit(solution)/shard_map/all_gather | solution.py:142
  649.7 103.3 %reduce-scatter.12.cloned.1.call-start = ((), (), s32[]{:S(2)}) async-start(), calls=%async_computation.12 | async-start | bytes 2260992 | tf_op jit(solution)/shard_map/reduce_scatter | solution.py:257
  727.5 57.2 %all-gather.11.cloned.1.call-start = ((), (), s32[]{:S(2)}) async-start(), calls=%async_computation.13 | async-start | bytes 2260992 | tf_op jit(solution)/shard_map/all_gather | solution.py:267
  758.1 721.6 %reduce-scatter.14.cloned.1.call-start = ((), (), s32[]{:S(2)}) async-start(), calls=%async_computation.14 | async-start | bytes 2260992 | tf_op jit(solution)/shard_map/reduce_scatter | solution.py:354
  892.4 41.0 %collective-permute-start.7 = (bf16[512,192]{0,1:T(8,128)(2,1)}, bf16[512,192]{0,1:T(8,128)(2,1)}, u32[]{:S(2)}, u32[]{:S(2)}) collective-permute-start(bf16[512,192]{0,1:T(8,128)(2,1)} %fusion.398), channel_id=1, source_target_pairs={{2,0},{4,2},{6,4},{8,6},{10,8},{12,10},{14,12},{16,14},{18,16},{20... | collective-permute-start | bytes 589832 | tf_op jit(solution)/shard_map/while/body/eval_jaxpr/ppermute | solution.py:27
  956.1 41.7 %collective-permute-start.7 = (bf16[512,192]{0,1:T(8,128)(2,1)}, bf16[512,192]{0,1:T(8,128)(2,1)}, u32[]{:S(2)}, u32[]{:S(2)}) collective-permute-start(bf16[512,192]{0,1:T(8,128)(2,1)} %fusion.398), channel_id=1, source_target_pairs={{2,0},{4,2},{6,4},{8,6},{10,8},{12,10},{14,12},{16,14},{18,16},{20... | collective-permute-start | bytes 589832 | tf_op jit(solution)/shard_map/while/body/eval_jaxpr/ppermute | solution.py:27
  958.5 41.0 %collective-permute-start.6 = (bf16[512,192]{0,1:T(8,128)(2,1)}, bf16[512,192]{0,1:T(8,128)(2,1)}, u32[]{:S(2)}, u32[]{:S(2)}) collective-permute-start(bf16[512,192]{0,1:T(8,128)(2,1)} %fusion.396), channel_id=1, source_target_pairs={{2,0},{4,2},{6,4},{8,6},{10,8},{12,10},{14,12},{16,14},{18,16},{20... | collective-permute-start | bytes 589832 | tf_op jit(solution)/shard_map/while/body/eval_jaxpr/ppermute | solution.py:27
  1020.6 41.7 %collective-permute-start.7 = (bf16[512,192]{0,1:T(8,128)(2,1)}, bf16[512,192]{0,1:T(8,128)(2,1)}, u32[]{:S(2)}, u32[]{:S(2)}) collective-permute-start(bf16[512,192]{0,1:T(8,128)(2,1)} %fusion.398), channel_id=1, source_target_pairs={{2,0},{4,2},{6,4},{8,6},{10,8},{12,10},{14,12},{16,14},{18,16},{20... | collective-permute-start | bytes 589832 | tf_op jit(solution)/shard_map/while/body/eval_jaxpr/ppermute | solution.py:27
  1023.0 41.0 %collective-permute-start.6 = (bf16[512,192]{0,1:T(8,128)(2,1)}, bf16[512,192]{0,1:T(8,128)(2,1)}, u32[]{:S(2)}, u32[]{:S(2)}) collective-permute-start(bf16[512,192]{0,1:T(8,128)(2,1)} %fusion.396), channel_id=1, source_target_pairs={{2,0},{4,2},{6,4},{8,6},{10,8},{12,10},{14,12},{16,14},{18,16},{20... | collective-permute-start | bytes 589832 | tf_op jit(solution)/shard_map/while/body/eval_jaxpr/ppermute | solution.py:27
  1084.9 41.7 %collective-permute-start.7 = (bf16[512,192]{0,1:T(8,128)(2,1)}, bf16[512,192]{0,1:T(8,128)(2,1)}, u32[]{:S(2)}, u32[]{:S(2)}) collective-permute-start(bf16[512,192]{0,1:T(8,128)(2,1)} %fusion.398), channel_id=1, source_target_pairs={{2,0},{4,2},{6,4},{8,6},{10,8},{12,10},{14,12},{16,14},{18,16},{20... | collective-permute-start | bytes 589832 | tf_op jit(solution)/shard_map/while/body/eval_jaxpr/ppermute | solution.py:27
  1087.3 41.0 %collective-permute-start.6 = (bf16[512,192]{0,1:T(8,128)(2,1)}, bf16[512,192]{0,1:T(8,128)(2,1)}, u32[]{:S(2)}, u32[]{:S(2)}) collective-permute-start(bf16[512,192]{0,1:T(8,128)(2,1)} %fusion.396), channel_id=1, source_target_pairs={{2,0},{4,2},{6,4},{8,6},{10,8},{12,10},{14,12},{16,14},{18,16},{20... | collective-permute-start | bytes 589832 | tf_op jit(solution)/shard_map/while/body/eval_jaxpr/ppermute | solution.py:27
  1149.2 41.7 %collective-permute-start.7 = (bf16[512,192]{0,1:T(8,128)(2,1)}, bf16[512,192]{0,1:T(8,128)(2,1)}, u32[]{:S(2)}, u32[]{:S(2)}) collective-permute-start(bf16[512,192]{0,1:T(8,128)(2,1)} %fusion.398), channel_id=1, source_target_pairs={{2,0},{4,2},{6,4},{8,6},{10,8},{12,10},{14,12},{16,14},{18,16},{20... | collective-permute-start | bytes 589832 | tf_op jit(solution)/shard_map/while/body/eval_jaxpr/ppermute | solution.py:27
  1151.6 41.0 %collective-permute-start.6 = (bf16[512,192]{0,1:T(8,128)(2,1)}, bf16[512,192]{0,1:T(8,128)(2,1)}, u32[]{:S(2)}, u32[]{:S(2)}) collective-permute-start(bf16[512,192]{0,1:T(8,128)(2,1)} %fusion.396), channel_id=1, source_target_pairs={{2,0},{4,2},{6,4},{8,6},{10,8},{12,10},{14,12},{16,14},{18,16},{20... | collective-permute-start | bytes 589832 | tf_op jit(solution)/shard_map/while/body/eval_jaxpr/ppermute | solution.py:27
  1213.7 41.7 %collective-permute-start.7 = (bf16[512,192]{0,1:T(8,128)(2,1)}, bf16[512,192]{0,1:T(8,128)(2,1)}, u32[]{:S(2)}, u32[]{:S(2)}) collective-permute-start(bf16[512,192]{0,1:T(8,128)(2,1)} %fusion.398), channel_id=1, source_target_pairs={{2,0},{4,2},{6,4},{8,6},{10,8},{12,10},{14,12},{16,14},{18,16},{20... | collective-permute-start | bytes 589832 | tf_op jit(solution)/shard_map/while/body/eval_jaxpr/ppermute | solution.py:27
  1216.1 41.0 %collective-permute-start.6 = (bf16[512,192]{0,1:T(8,128)(2,1)}, bf16[512,192]{0,1:T(8,128)(2,1)}, u32[]{:S(2)}, u32[]{:S(2)}) collective-permute-start(bf16[512,192]{0,1:T(8,128)(2,1)} %fusion.396), channel_id=1, source_target_pairs={{2,0},{4,2},{6,4},{8,6},{10,8},{12,10},{14,12},{16,14},{18,16},{20... | collective-permute-start | bytes 589832 | tf_op jit(solution)/shard_map/while/body/eval_jaxpr/ppermute | solution.py:27
  1287.3 89.6 %collective-permute-start.8 = (bf16[512]{0:T(512)(128)(2,1)}, bf16[512]{0:T(512)(128)(2,1)}, u32[]{:S(2)}, u32[]{:S(2)}) collective-permute-start(bf16[512]{0:T(512)(128)(2,1)} %fusion.399), channel_id=1, source_target_pairs={{2,0},{4,2},{6,4},{8,6},{10,8},{12,10},{14,12},{16,14},{18,16},{20... | collective-permute-start | bytes 3080 | tf_op jit(solution)/shard_map/while/body/eval_jaxpr/ppermute | solution.py:27
  1289.7 92.0 %collective-permute-start.7 = (bf16[512,192]{0,1:T(8,128)(2,1)}, bf16[512,192]{0,1:T(8,128)(2,1)}, u32[]{:S(2)}, u32[]{:S(2)}) collective-permute-start(bf16[512,192]{0,1:T(8,128)(2,1)} %fusion.398), channel_id=1, source_target_pairs={{2,0},{4,2},{6,4},{8,6},{10,8},{12,10},{14,12},{16,14},{18,16},{20... | collective-permute-start | bytes 589832 | tf_op jit(solution)/shard_map/while/body/eval_jaxpr/ppermute | solution.py:27
  1292.2 91.3 %collective-permute-start.6 = (bf16[512,192]{0,1:T(8,128)(2,1)}, bf16[512,192]{0,1:T(8,128)(2,1)}, u32[]{:S(2)}, u32[]{:S(2)}) collective-permute-start(bf16[512,192]{0,1:T(8,128)(2,1)} %fusion.396), channel_id=1, source_target_pairs={{2,0},{4,2},{6,4},{8,6},{10,8},{12,10},{14,12},{16,14},{18,16},{20... | collective-permute-start | bytes 589832 | tf_op jit(solution)/shard_map/while/body/eval_jaxpr/ppermute | solution.py:27
  1314.0 66.5 %collective-permute-start.11 = (bf16[512]{0:T(512)(128)(2,1)}, bf16[512]{0:T(512)(128)(2,1)}, u32[]{:S(2)}, u32[]{:S(2)}) collective-permute-start(bf16[512]{0:T(512)(128)(2,1)} %fusion.404), channel_id=1, source_target_pairs={{0,2},{2,4},{4,6},{6,8},{8,10},{10,12},{12,14},{14,16},{16,18},{18... | collective-permute-start | bytes 3080 | tf_op jit(solution)/shard_map/while/body/eval_jaxpr/ppermute | solution.py:27
  1322.1 63.0 %collective-permute-start.9 = (bf16[512,192]{0,1:T(8,128)(2,1)}, bf16[512,192]{0,1:T(8,128)(2,1)}, u32[]{:S(2)}, u32[]{:S(2)}) collective-permute-start(bf16[512,192]{0,1:T(8,128)(2,1)} %fusion.401), channel_id=1, source_target_pairs={{0,2},{2,4},{4,6},{6,8},{8,10},{10,12},{12,14},{14,16},{16,18},{18... | collective-permute-start | bytes 589832 | tf_op jit(solution)/shard_map/while/body/eval_jaxpr/ppermute | solution.py:27
  1402.7 117.4 %reduce-scatter.10.cloned.1.call-start = ((), (), s32[]{:S(2)}) async-start(), calls=%async_computation.10 | async-start | bytes 2260992 | tf_op jit(solution)/shard_map/reduce_scatter | solution.py:242
  1410.1 170.2 %all-reduce.5.cloned.1.call-start = ((), (), s32[]{:S(2)}) async-start(), calls=%async_computation.18 | async-start | bytes 9437184 | tf_op jit(solution)/shard_map/psum | solution.py:364
  1416.8 290.7 %reduce-scatter.20.cloned.1.call-start = ((), (), s32[]{:S(2)}) async-start(), calls=%async_computation.17 | async-start | bytes 11698176 | tf_op jit(solution)/shard_map/reduce_scatter | solution.py:263
  1424.3 410.9 %reduce-scatter.18.cloned.1.call-start = ((), (), s32[]{:S(2)}) async-start(), calls=%async_computation.16 | async-start | bytes 11698176 | tf_op jit(solution)/shard_map/reduce_scatter | solution.py:262
  1432.0 530.3 %reduce-scatter.16.cloned.1.call-start = ((), (), s32[]{:S(2)}) async-start(), calls=%async_computation.15 | async-start | bytes 11698176 | tf_op jit(solution)/shard_map/reduce_scatter | solution.py:261
  (328 other events, 5866.3 us)
Sparse Core Ops, SparseCore 0:
  12.3 29.1 all-gather.4
  615.0 30.3 reduce-scatter.7
  649.3 26.4 all-gather.6
  677.2 26.4 all-gather.8
  727.7 25.3 reduce-scatter.11
  758.2 26.4 all-gather.10
  1402.9 26.6 reduce-scatter.13
  1431.9 25.3 reduce-scatter.9
  1461.9 118.2 all-reduce.4
  1584.8 122.7 reduce-scatter.19
  1712.8 122.4 reduce-scatter.17
  1839.8 122.4 reduce-scatter.15
where the time goes:
time: 1990 us; the launch traced here: 1980 us
  waiting for transfers between devices  574 us (29%)
  matrix products  415 us (21%)
  local copies, waits for them, and re-layouts  286 us (14%)
  starting transfers between devices  278 us (14%)
  other arithmetic  246 us (12%)
  loops' own time  83.5 us (4%)
  blocking collectives  76.3 us (4%)
    ppermute x96, starting transfers between devices, from_behind(): return lax.ppermute(block, axis, route)  277 us
    reduce_scatter x1, waiting for transfers between devices, shards(): lax.psum_scatter(up_half, 'ctx', scatter_dimension=1, tiled=True)  128 us
    reduce_scatter x1, waiting for transfers between devices, shards(): lax.psum_scatter(down_half, 'ctx', scatter_dimension=0, tiled=True)  127 us
    reduce_scatter x1, waiting for transfers between devices, shards(): lax.psum_scatter(gate_half, 'ctx', scatter_dimension=1, tiled=True)  127 us
    dot_general x33, matrix products, block_scores(): jnp.einsum('qhd,khd->hqk', queries_h, block[0].reshape(pair, heads_here,...  96.4 us
    dynamic_slice x64, local copies, waits for them, and re-layouts, shards(): lax.scan(output_step, mixed_start, (lower_stack, upper_stack, hop_list))  83.2 us
    dot_general x7, matrix products, block_near(): jnp.einsum('qkb,bh->hqk', one_hot_block(delta, rows, table.shape[0]), tab...  78.3 us
    broadcast_in_dim x42, local copies, waits for them, and re-layouts, block_far(): jnp.broadcast_to(row_vals[:, None, None], (table.shape[1], rows, rows))  66.4 us
  transfers between devices with their start and end apart: 108, of which 10 were waited for; matrix products, arithmetic and copies ran while one was open for 24% of the time, Pallas kernels for 0%

commit v1 on v0

v1 whole, which is shorter than its diff:
```python
import functools

import jax
import jax.numpy as jnp
from jax import lax
from jax.experimental import pallas as pl
from jax.experimental.pallas import tpu as pltpu
from jax.sharding import PartitionSpec as P

MAXLEN = 8192

bucket_edges = (12, 16, 23, 32, 46, 64, 91)
neg_big = -1e30
eps = 1e-06
far_left_bucket = 15
far_right_bucket = 31
WIDE = 256
TQ = 256
TK = 512
EDGE = 128
PAD = TK + EDGE
f32 = jnp.float32
bf16 = jnp.bfloat16


def bucket_of(relative):
    distance = jnp.abs(relative)
    bucket = jnp.minimum(distance, 8) + 16 * (relative > 0).astype(jnp.int32)
    for edge in bucket_edges:
        bucket = bucket + (distance >= edge).astype(jnp.int32)
    return bucket


def norm_forward(inputs, gain):
    inv_root = lax.rsqrt(jnp.mean(inputs * inputs, axis=-1, keepdims=True) + eps)
    return (inputs * inv_root * gain, inv_root)


def norm_backward(inputs, inv_root, gain, grad_normed):
    scaled = gain * grad_normed
    cubed = inv_root * inv_root * inv_root
    grad_inputs = inv_root * scaled - inputs * cubed * jnp.mean(
        inputs * scaled, axis=-1, keepdims=True
    )
    grad_gain = jnp.sum(grad_normed * inputs * inv_root, axis=0)
    return (grad_inputs, grad_gain)


def gated(gate, upward):
    return jax.nn.gelu(gate, approximate=True) * upward


def nt(a, b):
    return lax.dot_general(a, b, (((1,), (1,)), ((), ())), preferred_element_type=f32)


def nn(a, b):
    return lax.dot_general(a, b, (((1,), (0,)), ((), ())), preferred_element_type=f32)


def split3(x):
    hi = x.astype(bf16)
    rest = x - hi.astype(f32)
    mid = rest.astype(bf16)
    return (hi, mid, (rest - mid.astype(f32)).astype(bf16))


class Plan:
    def __init__(self, heads, width, docs):
        self.heads = heads
        self.width = width
        self.bits = max(1, (docs - 1).bit_length())
        self.cols = heads * width
        self.mask_lane = self.cols
        self.doc_lane = self.cols + 1
        self.stat_lane = self.doc_lane + 2 * self.bits
        assert self.stat_lane + 3 * heads <= WIDE and self.cols + 64 == WIDE and width == 64

    def key_lanes(self, lane, h):
        own = (lane >= h * self.width) & (lane < (h + 1) * self.width)
        aug = (lane >= self.mask_lane) & (lane < self.stat_lane)
        stat = (lane >= self.stat_lane + 3 * h) & (lane < self.stat_lane + 3 * h + 3)
        return own | aug | stat

    def value_lanes(self, lane, h):
        own = (lane >= 64 + h * self.width) & (lane < 64 + (h + 1) * self.width)
        return own | ((lane >= 3 * h) & (lane < 3 * h + 3))


def lanes_of(rows, width=WIDE):
    return lax.broadcasted_iota(jnp.int32, (rows, width), 1)


def near_kernel(heads, table_ref, near_ref):
    row = lax.broadcasted_iota(jnp.int32, (EDGE, 3 * EDGE), 0)
    col = lax.broadcasted_iota(jnp.int32, (EDGE, 3 * EDGE), 1)
    relative = col - EDGE - row
    for flip in range(2):
        bucket = bucket_of(-relative if flip else relative)
        left, right = (far_left_bucket, far_right_bucket)
        if flip:
            left, right = (right, left)
        for h in range(heads):
            base = jnp.full((EDGE, 3 * EDGE), table_ref[0, h], f32)
            for b in range(1, 32):
                base = jnp.where(bucket == b, table_ref[b, h], base)
            far_l = jnp.full((EDGE, EDGE), table_ref[left, h], f32)
            far_r = jnp.full((EDGE, EDGE), table_ref[right, h], f32)
            near_ref[flip, h, :EDGE, : 3 * EDGE] = base
            near_ref[flip, h, :EDGE, 3 * EDGE :] = far_r
            near_ref[flip, h, EDGE:, EDGE:] = base
            near_ref[flip, h, EDGE:, :EDGE] = far_l


def build_keys(plan, g_ref, kaug_ref, km, vm, rows):
    km[:PAD, :] = jnp.broadcast_to(
        jnp.where(pad_lanes(plan), neg_big, 0.0).astype(bf16), (PAD, WIDE)
    )
    km[pl.ds(PAD + rows, PAD), :] = km[:PAD, :]
    vm[:PAD, :] = jnp.zeros((PAD, WIDE), bf16)
    vm[pl.ds(PAD + rows, PAD), :] = jnp.zeros((PAD, WIDE), bf16)
    step = 512
    low = lanes_of(step, 128) < 64
    ones = (lanes_of(step, 128) < 3 * plan.heads).astype(bf16)

    def body(n, unused):
        at = pl.multiple_of(n * step, step)
        to = pl.multiple_of(PAD + n * step, 128)
        middle = g_ref[pl.ds(at, step), 128:256]
        km[pl.ds(to, step), 0:128] = g_ref[pl.ds(at, step), 0:128]
        km[pl.ds(to, step), 128:256] = jnp.where(low, middle, kaug_ref[pl.ds(at, step), :])
        vm[pl.ds(to, step), 0:128] = jnp.where(low, ones, middle)
        vm[pl.ds(to, step), 128:256] = g_ref[pl.ds(at, step), 256:384]
        return unused

    lax.fori_loop(0, rows // step, body, 0)


def pad_lanes(plan):
    lane = lanes_of(1)
    return (lane >= plan.doc_lane) & (lane < plan.stat_lane)


def fwd_kernel(
    plan, rows, pair, bounds, table_ref, g_ref, kaug_ref, q_ref, near_ref,
    low_ref, wide_ref, qb_ref, km, vm, acc, row_max, qh_ref,
):
    build_keys(plan, g_ref, kaug_ref, km, vm, rows)
    lane = lanes_of(TQ)

    def tile(t, unused):
        start = pl.multiple_of(bounds[0] + t * TQ, 128)
        n_left, n_right = (bounds[1 + 2 * t], bounds[2 + 2 * t])
        out = pl.ds(pl.multiple_of(t * TQ, TQ), TQ)
        q = q_ref[out, :]
        near = pl.ds(pl.multiple_of(start + PAD - EDGE, 128), TK)
        for h in range(plan.heads):
            qh = jnp.where(plan.key_lanes(lane, h), q, jnp.zeros_like(q))
            qh_ref[h] = qh
            s = nt(qh, km[near, :]) + near_ref[0, h]
            top = jnp.max(s, axis=1, keepdims=True)
            p = jnp.exp(s - top).astype(bf16)
            acc[h] = nn(p, vm[near, :])
            row_max[h] = jnp.broadcast_to(top, (TQ, 128))

        def far(bucket):
            def step(first, n):
                span = pl.ds(pl.multiple_of(first + n, 128), TK)
                for h in range(plan.heads):
                    s = nt(qh_ref[h], km[span, :])
                    offset = table_ref[bucket, h]
                    old = row_max[h][:, :1]
                    top = jnp.maximum(old, jnp.max(s, axis=1, keepdims=True) + offset)
                    p = jnp.exp(s - (top - offset)).astype(bf16)
                    acc[h] = acc[h] * jnp.exp(old - top) + nn(p, vm[span, :])
                    row_max[h] = jnp.broadcast_to(top, (TQ, 128))
            return step

        left, right = (far(far_left_bucket), far(far_right_bucket))

        @pl.loop(0, n_left)
        def _(n):
            left(start + PAD - EDGE - TK, -n * TK)

        @pl.loop(0, n_right)
        def _(n):
            right(start + PAD - EDGE + TK, n * TK)

        wide = jnp.zeros((TQ, WIDE), f32)
        qb = jnp.where(lane < plan.stat_lane, q, jnp.zeros_like(q))
        for h in range(plan.heads):
            total = acc[h][:, 3 * h : 3 * h + 1]
            log_total = row_max[h][:, :1] + jnp.log(total)
            wide = jnp.where(lane // 64 == h + 1, acc[h] / total, wide)
            for i, part in enumerate(split3(-log_total)):
                qb = jnp.where(lane == plan.stat_lane + 3 * h + i, part, qb)
        wide_ref[out, :] = wide
        low_ref[out, :] = wide.astype(bf16)
        qb_ref[out, :] = qb
        return unused

    lax.fori_loop(0, pair // TQ, tile, 0)


def dq_kernel(
    plan, rows, pair, bounds, table_ref, g_ref, kaug_ref, qb_ref, do_ref, near_ref,
    dq_ref, tab_ref, km, vm, acc, qh_ref, doh_ref, near_acc, far_acc,
):
    build_keys(plan, g_ref, kaug_ref, km, vm, rows)
    lane = lanes_of(TQ)
    near_acc[...] = jnp.zeros_like(near_acc)
    far_acc[...] = jnp.zeros_like(far_acc)

    def tile(t, unused):
        start = pl.multiple_of(bounds[0] + t * TQ, 128)
        n_left, n_right = (bounds[1 + 2 * t], bounds[2 + 2 * t])
        out = pl.ds(pl.multiple_of(t * TQ, TQ), TQ)
        q = qb_ref[out, :]
        do = do_ref[out, :]
        near = pl.ds(pl.multiple_of(start + PAD - EDGE, 128), TK)

        def grads(h, s, span):
            p = jnp.exp(s)
            return p * nt(doh_ref[h], vm[span, :])

        for h in range(plan.heads):
            qh_ref[h] = jnp.where(plan.key_lanes(lane, h), q, jnp.zeros_like(q))
            doh_ref[h] = jnp.where(plan.value_lanes(lane, h), do, jnp.zeros_like(do))
            ds = grads(h, nt(qh_ref[h], km[near, :]) + near_ref[0, h], near)
            near_acc[h] += ds
            acc[h] = nn(ds.astype(bf16), km[near, :])

        def far(bucket, slot):
            def step(first, n):
                span = pl.ds(pl.multiple_of(first + n, 128), TK)
                for h in range(plan.heads):
                    ds = grads(h, nt(qh_ref[h], km[span, :]) + table_ref[bucket, h], span)
                    acc[h] += nn(ds.astype(bf16), km[span, :])
                    far_acc[slot, h] += (
                        ds[:, 0:128] + ds[:, 128:256] + ds[:, 256:384] + ds[:, 384:512]
                    )
            return step

        left, right = (far(far_left_bucket, 0), far(far_right_bucket, 1))

        @pl.loop(0, n_left)
        def _(n):
            left(start + PAD - EDGE - TK, -n * TK)

        @pl.loop(0, n_right)
        def _(n):
            right(start + PAD - EDGE + TK, n * TK)

        total = jnp.zeros((TQ, WIDE), f32)
        for h in range(plan.heads):
            total = jnp.where(lane // 64 == h, acc[h], total)
        dq_ref[out, :] = total.astype(bf16)
        return unused

    lax.fori_loop(0, pair // TQ, tile, 0)
    row = lax.broadcasted_iota(jnp.int32, (EDGE, 3 * EDGE), 0)
    col = lax.broadcasted_iota(jnp.int32, (EDGE, 3 * EDGE), 1)
    bucket = bucket_of(col - EDGE - row)
    for h in range(plan.heads):
        band = near_acc[h, :EDGE, : 3 * EDGE] + near_acc[h, EDGE:, EDGE:]
        extra_right = near_acc[h, :EDGE, 3 * EDGE :]
        extra_left = near_acc[h, EDGE:, :EDGE]
        for b in range(32):
            part = jnp.sum(jnp.where(bucket == b, band, 0.0), axis=0, keepdims=True)
            part = part[:, :128] + part[:, 128:256] + part[:, 256:]
            if b == far_left_bucket:
                part = part + jnp.sum(far_acc[0, h], axis=0, keepdims=True)
                part = part + jnp.sum(extra_left, axis=0, keepdims=True)
            if b == far_right_bucket:
                part = part + jnp.sum(far_acc[1, h], axis=0, keepdims=True)
                part = part + jnp.sum(extra_right, axis=0, keepdims=True)
            tab_ref[h, b : b + 1, :] = part


def dkv_kernel(
    plan, rows, pair, bounds, table_ref, qall_ref, doall_ref, g_ref, kaug_ref, near_ref,
    dk_ref, dv_ref, qp, dop, kh_ref, vh_ref, acc_k, acc_v,
):
    lane = lanes_of(TQ)
    first = lanes_of(1)
    stat = (first >= plan.stat_lane) & (first < plan.stat_lane + 3 * plan.heads)
    qp[:PAD, :] = jnp.broadcast_to(jnp.where(stat, neg_big, 0.0).astype(bf16), (PAD, WIDE))
    qp[pl.ds(PAD + rows, PAD), :] = qp[:PAD, :]
    dop[:PAD, :] = jnp.zeros((PAD, WIDE), bf16)
    dop[pl.ds(PAD + rows, PAD), :] = jnp.zeros((PAD, WIDE), bf16)
    step = 512

    def fill(n, unused):
        at = pl.multiple_of(n * step, step)
        to = pl.multiple_of(PAD + n * step, 128)
        qp[pl.ds(to, step), :] = qall_ref[pl.ds(at, step), :]
        dop[pl.ds(to, step), :] = doall_ref[pl.ds(at, step), :]
        return unused

    lax.fori_loop(0, rows // step, fill, 0)
    low = lanes_of(TQ, 128) < 64
    ones = (lanes_of(TQ, 128) < 3 * plan.heads).astype(bf16)

    def tile(t, unused):
        start = pl.multiple_of(bounds[0] + t * TQ, 128)
        n_left, n_right = (bounds[1 + 2 * t], bounds[2 + 2 * t])
        out = pl.ds(pl.multiple_of(t * TQ, TQ), TQ)
        middle = g_ref[out, 128:256]
        k = jnp.concatenate([g_ref[out, 0:128], jnp.where(low, middle, kaug_ref[out, :])], axis=1)
        v = jnp.concatenate([jnp.where(low, ones, middle), g_ref[out, 256:384]], axis=1)
        near = pl.ds(pl.multiple_of(start + PAD - EDGE, 128), TK)

        def grads(h, s, span):
            p = jnp.exp(s)
            ds = p * nt(vh_ref[h], dop[span, :])
            return nn(p.astype(bf16), dop[span, :]), nn(ds.astype(bf16), qp[span, :])

        for h in range(plan.heads):
            kh_ref[h] = jnp.where(plan.key_lanes(lane, h), k, jnp.zeros_like(k))
            vh_ref[h] = jnp.where(plan.value_lanes(lane, h), v, jnp.zeros_like(v))
            acc_v[h], acc_k[h] = grads(h, nt(kh_ref[h], qp[near, :]) + near_ref[1, h], near)

        def far(bucket):
            def step(first, n):
                span = pl.ds(pl.multiple_of(first + n, 128), TK)
                for h in range(plan.heads):
                    add_v, add_k = grads(
                        h, nt(kh_ref[h], qp[span, :]) + table_ref[bucket, h], span
                    )
                    acc_v[h] += add_v
                    acc_k[h] += add_k
            return step

        left, right = (far(far_right_bucket), far(far_left_bucket))

        @pl.loop(0, n_left)
        def _(n):
            left(start + PAD - EDGE - TK, -n * TK)

        @pl.loop(0, n_right)
        def _(n):
            right(start + PAD - EDGE + TK, n * TK)

        dk = jnp.zeros((TQ, WIDE), f32)
        dv = jnp.zeros((TQ, WIDE), f32)
        mask_grad = jnp.zeros((TQ, 1), f32)
        for h in range(plan.heads):
            dk = jnp.where(lane // 64 == h, acc_k[h], dk)
            dv = jnp.where(lane // 64 == h + 1, acc_v[h], dv)
            mask_grad = mask_grad + acc_k[h][:, plan.mask_lane : plan.mask_lane + 1]
        dk_ref[out, :] = jnp.where(lane == plan.mask_lane, mask_grad, dk)
        dv_ref[out, :] = dv.astype(bf16)
        return unused

    lax.fori_loop(0, pair // TQ, tile, 0)


def grad_attended_kernel(plan, branch_ref, w_ref, wide_ref, do_ref):
    rows = branch_ref.shape[0]
    lane = lanes_of(rows)
    grad = nt(branch_ref[...], w_ref[...]).astype(bf16)
    terms = grad.astype(f32) * wide_ref[...]
    out = grad
    for h in range(plan.heads):
        row_term = jnp.sum(
            jnp.where(lane // 64 == h + 1, terms, 0.0), axis=1, keepdims=True
        )
        for i, part in enumerate(split3(-row_term)):
            out = jnp.where(lane == 3 * h + i, part, out)
    do_ref[...] = out


vmem = pl.BlockSpec(memory_space=pltpu.VMEM)
smem = pl.BlockSpec(memory_space=pltpu.SMEM)


def params():
    return pltpu.CompilerParams(vmem_limit_bytes=56 * 2**20)


def shards(
    tokens,
    doc_lengths,
    key_mask,
    gain_attn,
    w_query,
    w_key,
    w_value,
    w_out,
    bias_table,
    gain_ffn,
    w_gate,
    w_up,
    w_down,
    cotangent,
):
    own_rows, model = tokens.shape
    group = lax.axis_size("wa")
    cycle_size = lax.axis_size("ctx")
    pair = own_rows * group
    heads = bias_table.shape[1]
    docs = doc_lengths.shape[0]
    plan = Plan(heads, w_query.shape[1] // heads, docs)
    total_rows = pair * cycle_size
    doc_most = min(MAXLEN, total_rows // 2)
    reach = min(cycle_size - 1, (doc_most - 1) // pair + 1)
    base = lax.axis_index("ctx") * pair
    rows = min(total_rows, (2 * reach + 1) * pair)
    origin = jnp.clip(base - reach * pair, 0, total_rows - rows).astype(jnp.int32)
    ends = jnp.cumsum(doc_lengths).astype(jnp.int32)
    starts = ends - doc_lengths

    def doc_at(positions):
        return jnp.sum((positions[:, None] >= starts[None, :]).astype(jnp.int32), axis=1) - 1

    tiles = pair // TQ
    tile_start = base + TQ * jnp.arange(tiles, dtype=jnp.int32)
    first_doc = jnp.arange(docs, dtype=jnp.int32)[None, :] == doc_at(tile_start)[:, None]
    last_doc = jnp.arange(docs, dtype=jnp.int32)[None, :] == doc_at(tile_start + TQ - 1)[:, None]
    low_end = jnp.sum(jnp.where(first_doc, starts[None, :], 0), axis=1)
    high_end = jnp.sum(jnp.where(last_doc, ends[None, :], 0), axis=1)
    n_left = jnp.maximum(0, (tile_start - EDGE - low_end + TK - 1) // TK)
    n_right = jnp.maximum(0, (high_end - (tile_start - EDGE + TK) + TK - 1) // TK)
    bounds = jnp.concatenate(
        [(base - origin)[None], jnp.stack([n_left, n_right], axis=1).reshape(-1)]
    ).astype(jnp.int32)

    mask_all = lax.all_gather(key_mask, "ctx", axis=0, tiled=True)
    tokens_wide = tokens.astype(f32)
    normed_attn, inv_attn = norm_forward(tokens_wide, gain_attn)
    normed_low = normed_attn.astype(bf16)
    pair_normed, pair_cot = (
        lax.all_gather(normed_low, "wa", axis=0, tiled=True),
        lax.all_gather(cotangent, "wa", axis=0, tiled=True),
    )
    w_kv = jnp.concatenate([w_key, w_value], axis=1)
    own_kv = jnp.dot(pair_normed, w_kv, preferred_element_type=f32).astype(bf16)
    queries = jnp.dot(pair_normed, w_query, preferred_element_type=f32).astype(bf16)

    def window(gathered):
        if rows == total_rows:
            return gathered
        return lax.dynamic_slice_in_dim(gathered, origin, rows, 0)

    gather = functools.partial(lax.all_gather, axis_name="ctx", axis=0, tiled=True)
    kv_all = window(gather(own_kv))
    positions = origin + jnp.arange(rows, dtype=jnp.int32)
    doc_of = doc_at(positions)
    lane = jnp.arange(128, dtype=jnp.int32)[None, :] + 128
    code = lane - plan.doc_lane
    bit_differs = ((doc_of[:, None] >> (code >> 1)) & 1) != (code & 1)
    k_aug = jnp.where(
        lane == plan.mask_lane,
        window(mask_all).astype(f32)[:, None],
        jnp.where(
            lane < plan.stat_lane,
            jnp.where(bit_differs & (code >= 0), neg_big, 0.0),
            (lane < plan.stat_lane + 3 * heads).astype(f32),
        ),
    ).astype(bf16)
    own_docs = doc_at(base + jnp.arange(pair, dtype=jnp.int32))
    own_differs = ((own_docs[:, None] >> (code >> 1)) & 1) != (code & 1)
    q_aug = jnp.where(
        lane == plan.mask_lane, 1.0, ((lane < plan.stat_lane) & ~own_differs).astype(f32)
    ).astype(bf16)
    q_wide = jnp.concatenate(
        [queries, q_aug[:, plan.cols - 128 :]], axis=1
    )
    near_bias = pl.pallas_call(
        functools.partial(near_kernel, heads),
        out_shape=jax.ShapeDtypeStruct((2, heads, TQ, TK), f32),
        in_specs=[smem],
        out_specs=vmem,
        compiler_params=params(),
        name="near_bias",
    )(bias_table)

    padded = rows + 2 * PAD
    attended, mixed, q_back = pl.pallas_call(
        functools.partial(fwd_kernel, plan, rows, pair),
        out_shape=(
            jax.ShapeDtypeStruct((pair, WIDE), bf16),
            jax.ShapeDtypeStruct((pair, WIDE), f32),
            jax.ShapeDtypeStruct((pair, WIDE), bf16),
        ),
        in_specs=[smem, smem, vmem, vmem, vmem, vmem],
        out_specs=(vmem, vmem, vmem),
        scratch_shapes=[
            pltpu.VMEM((padded, WIDE), bf16),
            pltpu.VMEM((padded, WIDE), bf16),
            pltpu.VMEM((heads, TQ, WIDE), f32),
            pltpu.VMEM((heads, TQ, 128), f32),
            pltpu.VMEM((heads, TQ, WIDE), bf16),
        ],
        compiler_params=params(),
        name="attention_forward",
    )(bounds, bias_table, kv_all, k_aug, q_wide, near_bias)
    q_all = window(gather(q_back))
    w_out_pad = jnp.concatenate([jnp.zeros((64, model), bf16), w_out], axis=0)
    branch = lax.psum_scatter(
        jnp.dot(attended, w_out_pad, preferred_element_type=f32).astype(bf16),
        "wa",
        scatter_dimension=0,
        tiled=True,
    ).astype(f32)
    hidden = tokens_wide + branch
    normed_ffn, inv_ffn = norm_forward(hidden, gain_ffn)
    ffn_low = normed_ffn.astype(bf16)
    pair_ffn = lax.all_gather(ffn_low, "wa", axis=0, tiled=True)
    gate = jnp.dot(pair_ffn, w_gate, preferred_element_type=f32)
    upward = jnp.dot(pair_ffn, w_up, preferred_element_type=f32)
    inner = gated(gate, upward).astype(bf16)
    ffn_part = jnp.dot(inner, w_down, preferred_element_type=f32)
    layer_out = (
        hidden
        + lax.psum_scatter(
            ffn_part.astype(bf16), "wa", scatter_dimension=0, tiled=True
        ).astype(f32)
    ).astype(bf16)
    grad_inner = jnp.dot(pair_cot, w_down.T, preferred_element_type=f32)
    down_half = jnp.dot(inner.T, pair_cot, preferred_element_type=f32).astype(bf16)
    unused_value, pullback = jax.vjp(gated, gate, upward)
    grad_gate, grad_upward = pullback(grad_inner)
    grad_gate = grad_gate.astype(bf16)
    grad_upward = grad_upward.astype(bf16)
    grad_pair_ffn = jnp.dot(grad_gate, w_gate.T, preferred_element_type=f32) + jnp.dot(
        grad_upward, w_up.T, preferred_element_type=f32
    )
    grad_normed_ffn = lax.psum_scatter(
        grad_pair_ffn.astype(bf16), "wa", scatter_dimension=0, tiled=True
    ).astype(f32)
    gate_half = jnp.dot(pair_ffn.T, grad_gate, preferred_element_type=f32).astype(bf16)
    up_half = jnp.dot(pair_ffn.T, grad_upward, preferred_element_type=f32).astype(bf16)
    grad_w_gate, grad_w_up, grad_w_down = (
        lax.psum_scatter(gate_half, "ctx", scatter_dimension=1, tiled=True).astype(f32),
        lax.psum_scatter(up_half, "ctx", scatter_dimension=1, tiled=True).astype(f32),
        lax.psum_scatter(down_half, "ctx", scatter_dimension=0, tiled=True).astype(f32),
    )
    hidden_step, gain_ffn_part = norm_backward(hidden, inv_ffn, gain_ffn, grad_normed_ffn)
    grad_hidden = cotangent.astype(f32) + hidden_step
    pair_branch = lax.all_gather(grad_hidden.astype(bf16), "wa", axis=0, tiled=True)
    out_part = jnp.dot(attended.T, pair_branch, preferred_element_type=f32)[64:]
    do_wide = pl.pallas_call(
        functools.partial(grad_attended_kernel, plan),
        out_shape=jax.ShapeDtypeStruct((pair, WIDE), bf16),
        in_specs=[vmem, vmem, vmem],
        out_specs=vmem,
        compiler_params=params(),
        name="grad_attended",
    )(pair_branch, w_out_pad, mixed)
    do_all = window(gather(do_wide))

    grad_queries, table_part = pl.pallas_call(
        functools.partial(dq_kernel, plan, rows, pair),
        out_shape=(
            jax.ShapeDtypeStruct((pair, WIDE), bf16),
            jax.ShapeDtypeStruct((heads, 32, 128), f32),
        ),
        in_specs=[smem, smem, vmem, vmem, vmem, vmem, vmem],
        out_specs=(vmem, vmem),
        scratch_shapes=[
            pltpu.VMEM((padded, WIDE), bf16),
            pltpu.VMEM((padded, WIDE), bf16),
            pltpu.VMEM((heads, TQ, WIDE), f32),
            pltpu.VMEM((heads, TQ, WIDE), bf16),
            pltpu.VMEM((heads, TQ, WIDE), bf16),
            pltpu.VMEM((heads, TQ, TK), f32),
            pltpu.VMEM((2, heads, TQ, 128), f32),
        ],
        compiler_params=params(),
        name="attention_grad_queries",
    )(bounds, bias_table, kv_all, k_aug, q_back, do_wide, near_bias)
    own_aug = lax.dynamic_slice_in_dim(k_aug, base - origin, pair, 0)
    grad_keys, grad_values = pl.pallas_call(
        functools.partial(dkv_kernel, plan, rows, pair),
        out_shape=(
            jax.ShapeDtypeStruct((pair, WIDE), f32),
            jax.ShapeDtypeStruct((pair, WIDE), bf16),
        ),
        in_specs=[smem, smem, vmem, vmem, vmem, vmem, vmem],
        out_specs=(vmem, vmem),
        scratch_shapes=[
            pltpu.VMEM((padded, WIDE), bf16),
            pltpu.VMEM((padded, WIDE), bf16),
            pltpu.VMEM((heads, TQ, WIDE), bf16),
            pltpu.VMEM((heads, TQ, WIDE), bf16),
            pltpu.VMEM((heads, TQ, WIDE), f32),
            pltpu.VMEM((heads, TQ, WIDE), f32),
        ],
        compiler_params=params(),
        name="attention_grad_keys",
    )(bounds, bias_table, q_all, do_all, own_kv, own_aug, near_bias)
    grad_tab = jnp.sum(table_part, axis=2).T
    mask_total = grad_keys[:, plan.mask_lane]
    cols = plan.cols
    grad_qkv = jnp.concatenate(
        [grad_queries[:, :cols], grad_keys[:, :cols].astype(bf16), grad_values[:, 64:]], axis=1
    )
    w_qkv = jnp.concatenate([w_query, w_key, w_value], axis=1)
    qkv_part = jnp.dot(pair_normed.T, grad_qkv, preferred_element_type=f32)
    grad_pair = jnp.dot(grad_qkv, w_qkv.T, preferred_element_type=f32)
    grad_normed_attn, grad_mask = (
        lax.psum_scatter(
            grad_pair.astype(bf16), "wa", scatter_dimension=0, tiled=True
        ).astype(f32),
        lax.psum_scatter(
            mask_total.astype(bf16), "wa", scatter_dimension=0, tiled=True
        ).astype(f32),
    )
    token_step, gain_attn_part = norm_backward(tokens_wide, inv_attn, gain_attn, grad_normed_attn)
    grad_tokens = grad_hidden + token_step
    grad_gain_attn, grad_gain_ffn = lax.psum((gain_attn_part, gain_ffn_part), ("ctx", "wa"))
    grad_w_qkv, grad_w_out, grad_table = lax.psum((qkv_part, out_part, grad_tab), "ctx")
    return (
        layer_out,
        grad_tokens,
        grad_mask,
        grad_gain_attn,
        grad_w_qkv[:, :cols],
        grad_w_qkv[:, cols : 2 * cols],
        grad_w_qkv[:, 2 * cols :],
        grad_w_out,
        grad_table,
        grad_gain_ffn,
        grad_w_gate,
        grad_w_up,
        grad_w_down,
    )


def solution(mesh):
    placed = (
        P(("ctx", "wa"), None),
        P(),
        P("ctx"),
        P(),
        P(None, "wa"),
        P(None, "wa"),
        P(None, "wa"),
        P("wa", None),
        P(None, "wa"),
        P(),
        P(None, "wa"),
        P(None, "wa"),
        P("wa", None),
        P(("ctx", "wa"), None),
    )
    return jax.shard_map(
        shards,
        mesh=mesh,
        in_specs=placed,
        out_specs=(
            P(("ctx", "wa"), None),
            P(("ctx", "wa"), None),
            P(("ctx", "wa")),
            P(),
            P(None, "wa"),
            P(None, "wa"),
            P(None, "wa"),
            P("wa", None),
            P(None, "wa"),
            P(),
            P(None, ("wa", "ctx")),
            P(None, ("wa", "ctx")),
            P(("wa", "ctx"), None),
        ),
        check_vma=False,
    )
```

time: 1990 us -> 903 us (0.45)
  matrix products: 415 us -> 83.9 us
  starting transfers between devices: 278 us -> 1.72 us
  local copies, waits for them, and re-layouts: 286 us -> 27.7 us
  other arithmetic: 246 us -> 27.7 us
  Pallas kernels: 0 us -> 92.5 us
  loops' own time: 83.5 us -> 0 us
  waiting for transfers between devices: 574 us -> 545 us
  blocking collectives: 76.3 us -> 97.6 us
    dot_general x149 -> x15, matrix products: 415 us -> 83.9 us  [the longest x1 10.8 us: shards(): grad_inner = jnp.dot(pair_cot, w_down.T, preferred_element_type=f32)]
    ppermute x96 -> x0, starting transfers between devices: 277 us -> none  [from_behind(): return lax.ppermute(block, axis, route)]
    reduce_scatter x1, waiting for transfers between devices: 127 us -> 0.2 us  [shards(): lax.psum_scatter(gate_half, 'ctx', scatter_dimension=1, tiled=True)]
    convert_element_type x202 -> x11, other arithmetic: 136 us -> 14.8 us  [the longest x1 4.51 us: shards(): k_aug = jnp.where(lane == plan.mask_lane, window(mask_all).astype(f32)[:,...]
    pallas_call x0 -> x5, Pallas kernels: none -> 92.5 us  [the longest x1 30.1 us: shards(): pl.pallas_call(functools.partial(fwd_kernel, plan, rows, pair), out_shape...]
    another operation x67 -> x0, loops' own time: 83.5 us -> none  [the longest x16 34 us: table_grad(): return lax.cond(is_far(delta, rows), table_far, table_near, 0)]
    dynamic_slice x64 -> x1, local copies, waits for them, and re-layouts: 83.2 us -> 1.6 us  [shards(): own_aug = lax.dynamic_slice_in_dim(k_aug, base - origin, pair, 0)]
    all_gather x1 -> x4, waiting for transfers between devices: 26.3 us -> 97.8 us  [the longest x1 47.4 us: shards(): do_all = window(gather(do_wide))]
  transfers between devices with their start and end apart: 108 -> 15, of which waited for: 10 -> 14; matrix products, arithmetic and copies ran while one was open for 24% -> 10% of each run, Pallas kernels for 0% -> 7%
where the time goes in v1:
time: 903 us; the launch traced here: 892 us
  waiting for transfers between devices  545 us (60%)
  blocking collectives  97.6 us (11%)
  Pallas kernels  92.5 us (10%)
  matrix products  83.9 us (9%)
  local copies, waits for them, and re-layouts  27.7 us (3%)
  other arithmetic  27.7 us (3%)
  between operations  15.4 us (2%)
    psum x1, waiting for transfers between devices, shards(): lax.psum((qkv_part, out_part, grad_tab), 'ctx')  113 us
    reduce_scatter x1, waiting for transfers between devices, shards(): lax.psum_scatter(up_half, 'ctx', scatter_dimension=1, tiled=True)  81.7 us
    reduce_scatter x1, waiting for transfers between devices, shards(): lax.psum_scatter(down_half, 'ctx', scatter_dimension=0, tiled=True)  81 us
    all_gather x1, waiting for transfers between devices, shards(): do_all = window(gather(do_wide))  47.4 us
    psum x1, blocking collectives, shards(): lax.psum((gain_attn_part, gain_ffn_part), ('ctx', 'wa'))  39.4 us
    psum x1, blocking collectives, shards(): lax.psum((qkv_part, out_part, grad_tab), 'ctx')  31.5 us
    pallas_call x1, Pallas kernels, shards(): pl.pallas_call(functools.partial(fwd_kernel, plan, rows, pair), out_shape...  30.1 us
    all_gather x1, waiting for transfers between devices, shards(): lax.all_gather(normed_low, 'wa', axis=0, tiled=True)  30 us
  transfers between devices with their start and end apart: 15, of which 14 were waited for; matrix products, arithmetic and copies ran while one was open for 10% of the time, Pallas kernels for 7%

profile of v1, /device:TPU:0, one launch (start us, length us, event | category | flops | bytes accessed | tf_op | source)
XLA Modules:
  0.0 891.6 jit_solution(4570879063093459781)
XLA Ops:
  10.2 30.0 %all-gather.9.cloned.1.call-done = bf16[512,1472]{1,0:T(8,128)(2,1)} async-done(((bf16[256,1472]{1,0:T(8,128)(2,1)}), bf16[512,1472]{1,0:T(8,128)(2,1)}) %all-gather.9.cloned.1.call-update) | async-done | bytes 1507344 | tf_op jit(solution)/shard_map/all_gather | solution.py:433
  44.7 21.7 %all-gather = bf16[16,1,512]{2,1,0:T(2,128)(2,1)S(1)} all-gather(bf16[1,1,512]{2,1,0:T(2,128)(2,1)S(1)} %reshape.281), channel_id=1, replica_groups=mesh['ctx'=16,'wa'=2] {'ctx'}, dimensions={0}, use_global_device_ids=true | all-gather | bytes 17408 | tf_op jit(solution)/shard_map/all_gather | solution.py:428
  67.1 5.0 near_bias.1.near_ref
  73.3 4.5 select_convert_fusion.kaug_ref
  79.4 25.8 %all-gather.11.cloned.1.call-done.g_ref = bf16[8192,384]{1,0:T(8,128)(2,1)} async-done(((bf16[512,384]{1,0:T(8,128)(2,1)}), bf16[8192,384]{1,0:T(8,128)(2,1)}) %all-gather.11.cloned.1.call-update) | async-done | bytes 6291472 | tf_op jit(solution)/shard_map/all_gather | solution.py:446
  105.3 30.1 %attention_forward.1 = (bf16[512,256]{1,0:T(8,128)(2,1)}, f32[512,256]{1,0:T(8,128)}, bf16[512,256]{1,0:T(8,128)(2,1)}) custom-call(s32[5]{0:T(128)} %pad_add_fusion.1.bounds, f32[32,3]{1,0:T(8,128)} %copy.91.table_ref, bf16[8192,384]{1,0:T(8,128)(2,1)} %all-gather.11.cloned.1.call-done.g_ref, bf16[8192,128]{1,0:T(8,128)(2,1)} %select_convert_fusion.kaug_ref, ...), custom_call_target="tpu_custom_call" | custom-call | tf_op jit(solution)/shard_map/attention_forward/pallas_call | solution.py:479
  138.6 24.3 %reduce-scatter.8.cloned.1.call-done = bf16[256,1472]{1,0:T(8,128)(2,1)} async-done(((bf16[512,1472]{1,0:T(8,128)(2,1)}), bf16[256,1472]{1,0:T(8,128)(2,1)}) %reduce-scatter.8.cloned.1.call-update) | async-done | bytes 753680 | tf_op jit(solution)/shard_map/reduce_scatter | solution.py:500
  166.8 26.3 %all-gather.13.cloned.1.call-done = bf16[512,1472]{1,0:T(8,128)(2,1)} async-done(((bf16[256,1472]{1,0:T(8,128)(2,1)}), bf16[512,1472]{1,0:T(8,128)(2,1)}) %all-gather.13.cloned.1.call-update) | async-done | bytes 1507344 | tf_op jit(solution)/shard_map/all_gather | solution.py:509
  193.1 7.9 fusion.58
  201.0 7.6 fusion.59
  208.7 12.3 %all-gather.15.cloned.1.call-done = bf16[512,1472]{0,1:T(8,128)(2,1)} async-done(((bf16[256,1472]{0,1:T(8,128)(2,1)}), bf16[512,1472]{0,1:T(8,128)(2,1)}) %all-gather.15.cloned.1.call-update) | async-done | bytes 1507344 | tf_op jit(solution)/shard_map/all_gather | solution.py:434
  221.0 10.8 %multiply_convert_fusion = (bf16[512,1792]{1,0:T(8,128)(2,1)S(1)}, bf16[512,1792]{1,0:T(8,128)(2,1)S(1)}, bf16[512,1792]{1,0:T(8,128)(2,1)}) fusion(f32[512,1792]{1,0:T(8,128)} %fusion.58, f32[512,1792]{1,0:T(8,128)} %fusion.59, bf16[512,1472]{0,1:T(8,128)(2,1)} %all-gather.15.cloned.1.call-done, bf16[1792,1472]{0,1:T(8,128)(2,1)} %param.26), kind=kOutput, calls=%fused_computation.15 | convolution fusion | flops 2724986880 | bytes 19628032 | tf_op jit(solution)/shard_map/dot_general | solution.py:520
  231.8 6.2 fusion.60
  238.1 6.6 convolution_add_fusion
  247.7 25.9 %reduce-scatter.12.cloned.1.call-done = bf16[256,1472]{1,0:T(8,128)(2,1)} async-done(((bf16[512,1472]{1,0:T(8,128)(2,1)}), bf16[256,1472]{1,0:T(8,128)(2,1)}) %reduce-scatter.12.cloned.1.call-update) | async-done | bytes 753680 | tf_op jit(solution)/shard_map/reduce_scatter | solution.py:529
  279.7 24.6 %all-gather.17.cloned.1.call-done.branch_ref = bf16[512,1472]{1,0:T(8,128)(2,1)} async-done(((bf16[256,1472]{1,0:T(8,128)(2,1)}), bf16[512,1472]{1,0:T(8,128)(2,1)}) %all-gather.17.cloned.1.call-update) | async-done | bytes 1507344 | tf_op jit(solution)/shard_map/all_gather | solution.py:541
  307.9 7.5 convolution_convert_fusion.2
  315.4 7.4 convolution_convert_fusion.1
  322.9 7.4 convolution_convert_fusion
  332.2 28.4 %attention_grad_queries.1 = (bf16[512,256]{1,0:T(8,128)(2,1)}, f32[3,32,128]{2,1,0:T(8,128)}) custom-call(s32[5]{0:T(128)} %pad_add_fusion.1.bounds, f32[32,3]{1,0:T(8,128)} %copy.91.table_ref, bf16[8192,384]{1,0:T(8,128)(2,1)} %all-gather.11.cloned.1.call-done.g_ref, bf16[8192,128]{1,0:T(8,128)(2,1)} %select_convert_fusion.kaug_ref, ...), custom_call_target="tpu_custom_call" | custom-call | tf_op jit(solution)/shard_map/attention_grad_queries/pallas_call | solution.py:553
  362.3 47.4 %all-gather.21.cloned.1.call-done.doall_ref = bf16[8192,256]{1,0:T(8,128)(2,1)} async-done(((bf16[512,256]{1,0:T(8,128)(2,1)}), bf16[8192,256]{1,0:T(8,128)(2,1)}) %all-gather.21.cloned.1.call-update) | async-done | bytes 4194320 | tf_op jit(solution)/shard_map/all_gather | solution.py:551
  409.6 25.7 %attention_grad_keys.1 = (f32[512,256]{1,0:T(8,128)}, bf16[512,256]{1,0:T(8,128)(2,1)}) custom-call(s32[5]{0:T(128)} %pad_add_fusion.1.bounds, f32[32,3]{1,0:T(8,128)} %copy.91.table_ref, bf16[8192,256]{1,0:T(8,128)(2,1)} %all-gather.19.cloned.1.call-done.qall_ref, bf16[8192,256]{1,0:T(8,128)(2,1)} %all-gather.21.cloned.1.call-done.doall_ref, ...), custom_call_target="tpu_custom_call" | custom-call | tf_op jit(solution)/shard_map/attention_grad_keys/pallas_call | solution.py:574
  442.3 4.2 convolution_convert_fusion.3
  449.4 7.1 convolution_convert_fusion.5
  460.5 31.5 %psum.38 = f32[32,3]{0,1:T(4,128)} all-reduce(f32[32,3]{0,1:T(4,128)S(1)} %bitcast.54), channel_id=1, replica_groups=mesh['ctx'=16,'wa'=2] {'ctx'}, use_global_device_ids=true, to_apply=%region_21.22 | all-reduce | flops 96 | bytes 768 | tf_op jit(solution)/shard_map/psum | solution.py:613
  494.1 81.7 %reduce-scatter.18.cloned.1.call-done = bf16[1472,112]{0,1:T(8,128)(2,1)} async-done(((bf16[1472,1792]{0,1:T(8,128)(2,1)}), bf16[1472,112]{0,1:T(8,128)(2,1)}) %reduce-scatter.18.cloned.1.call-update) | async-done | bytes 329744 | tf_op jit(solution)/shard_map/reduce_scatter | solution.py:536
  577.7 81.0 %reduce-scatter.20.cloned.1.call-done = bf16[112,1472]{1,0:T(8,128)(2,1)} async-done(((bf16[1792,1472]{1,0:T(8,128)(2,1)}), bf16[112,1472]{1,0:T(8,128)(2,1)}) %reduce-scatter.20.cloned.1.call-update) | async-done | bytes 329744 | tf_op jit(solution)/shard_map/reduce_scatter | solution.py:537
  660.8 4.9 all-reduce.1
  666.3 113.3 %all-reduce.6.cloned.1.call-done = (f32[1472,576]{0,1:T(8,128)}, f32[192,1472]{1,0:T(8,128)}) async-done(((f32[1472,576]{0,1:T(8,128)}, f32[192,1472]{1,0:T(8,128)}), (f32[1472,576]{0,1:T(8,128)}, f32[192,1472]{1,0:T(8,128)})) %all-reduce.6.cloned.1.call-update) | async-done | bytes 4522000 | tf_op jit(solution)/shard_map/psum | solution.py:613
  783.5 24.3 %reduce-scatter.14.cloned.1.call-done = bf16[256,1472]{1,0:T(8,128)(2,1)} async-done(((bf16[512,1472]{1,0:T(8,128)(2,1)}), bf16[256,1472]{1,0:T(8,128)(2,1)}) %reduce-scatter.14.cloned.1.call-update) | async-done | bytes 753680 | tf_op jit(solution)/shard_map/reduce_scatter | solution.py:603
  809.4 26.6 %reduce-scatter.10.cloned.1.call-done = bf16[256,1472]{1,0:T(8,128)(2,1)} async-done(((bf16[512,1472]{1,0:T(8,128)(2,1)}), bf16[256,1472]{1,0:T(8,128)(2,1)}) %reduce-scatter.10.cloned.1.call-update) | async-done | bytes 753680 | tf_op jit(solution)/shard_map/reduce_scatter | solution.py:516
  844.2 39.4 %all-reduce.2 = (f32[1472]{0:T(1024)}, f32[1472]{0:T(1024)}) all-reduce(f32[1472]{0:T(1024)S(1)} %get-tuple-element.94, f32[1472]{0:T(1024)S(1)} %get-tuple-element.92), channel_id=1, replica_groups=mesh['ctx'=16,'wa'=2] {'ctx','wa'}, use_global_device_ids=true, to_apply=%region_17.18 | all-reduce | flops 2944 | bytes 23552 | tf_op jit(solution)/shard_map/psum | solution.py:612
  (152 shorter events, 68.7 us)
Async XLA Ops:
  7.2 33.0 %all-gather.9.cloned.1.call-start = ((), (), s32[]{:S(2)}) async-start(), calls=%async_computation.7 | async-start | bytes 2359296 | tf_op jit(solution)/shard_map/all_gather | solution.py:433
  8.6 31.5 %copy-start.17 = (bf16[1472,192]{0,1:T(8,128)(2,1)S(1)}, bf16[1472,192]{0,1:T(8,128)(2,1)}, u32[]{:S(2)}) copy-start(bf16[1472,192]{0,1:T(8,128)(2,1)} %param.20) | copy-start | bytes 1695748
  8.6 31.5 %copy-start.18 = (bf16[1472,192]{0,1:T(8,128)(2,1)S(1)}, bf16[1472,192]{0,1:T(8,128)(2,1)}, u32[]{:S(2)}) copy-start(bf16[1472,192]{0,1:T(8,128)(2,1)} %param.19) | copy-start | bytes 1695748
  10.1 33.3 %copy-start.20 = (s32[8]{0:T(128)S(1)}, s32[8]{0:T(128)}, u32[]{:S(2)}) copy-start(s32[8]{0:T(128)} %param.15) | copy-start | bytes 100
  10.1 34.6 %copy-start.15 = (bf16[512]{0:T(512)(128)(2,1)S(1)}, bf16[512]{0:T(512)(128)(2,1)}, u32[]{:S(2)}) copy-start(bf16[512]{0:T(512)(128)(2,1)} %param.16) | copy-start | bytes 3076
  10.1 56.3 %copy-start.14 = (f32[32,3]{0,1:T(4,128)S(1)}, f32[32,3]{0,1:T(4,128)}, u32[]{:S(2)}) copy-start(f32[32,3]{0,1:T(4,128)} %param.22) | copy-start | bytes 1156
  10.1 95.2 %all-gather.11.cloned.1.call-start = ((), (), s32[]{:S(2)}) async-start(), calls=%async_computation.8 | async-start | bytes 6684672 | tf_op jit(solution)/shard_map/all_gather | solution.py:446
  43.3 119.6 %reduce-scatter.8.cloned.1.call-start = ((), (), s32[]{:S(2)}) async-start(), calls=%async_computation.9 | async-start | bytes 2359296 | tf_op jit(solution)/shard_map/reduce_scatter | solution.py:500
  72.1 5.7 copy-start.6
  72.1 5.7 copy-start.19
  79.4 55.9 %copy-start.5 = (bf16[192,1472]{1,0:T(8,128)(2,1)S(1)}, bf16[192,1472]{1,0:T(8,128)(2,1)}, u32[]{:S(2)}) copy-start(bf16[192,1472]{1,0:T(8,128)(2,1)} %param.21) | copy-start | bytes 1695748
  138.5 26.0 %copy-start.11 = (f32[1472]{0:T(1024)S(1)}, f32[1472]{0:T(1024)}, u32[]{:S(2)}) copy-start(f32[1472]{0:T(1024)} %param.23) | copy-start | bytes 17668
  138.5 54.6 %all-gather.13.cloned.1.call-start = ((), (), s32[]{:S(2)}) async-start(), calls=%async_computation.10 | async-start | bytes 2359296 | tf_op jit(solution)/shard_map/all_gather | solution.py:509
  165.7 55.3 %all-gather.15.cloned.1.call-start = ((), (), s32[]{:S(2)}) async-start(), calls=%async_computation.12 | async-start | bytes 2260992 | tf_op jit(solution)/shard_map/all_gather | solution.py:434
  166.3 107.3 %reduce-scatter.12.cloned.1.call-start = ((), (), s32[]{:S(2)}) async-start(), calls=%async_computation.13 | async-start | bytes 2359296 | tf_op jit(solution)/shard_map/reduce_scatter | solution.py:529
  193.1 7.9 copy-start.16
  231.8 6.2 copy-start.23
  231.8 6.2 copy-start.22
  247.4 56.9 %all-gather.17.cloned.1.call-start = ((), (), s32[]{:S(2)}) async-start(), calls=%async_computation.14 | async-start | bytes 2359296 | tf_op jit(solution)/shard_map/all_gather | solution.py:541
  276.9 85.3 %all-gather.19.cloned.1.call-start = ((), (), s32[]{:S(2)}) async-start(), calls=%async_computation.15 | async-start | bytes 4456448 | tf_op jit(solution)/shard_map/all_gather | solution.py:498
  277.7 131.9 %all-gather.21.cloned.1.call-start = ((), (), s32[]{:S(2)}) async-start(), calls=%async_computation.16 | async-start | bytes 4456448 | tf_op jit(solution)/shard_map/all_gather | solution.py:551
  307.7 184.6 %reduce-scatter.16.cloned.1.call-start = ((), (), s32[]{:S(2)}) async-start(), calls=%async_computation.18 | async-start | bytes 5849088 | tf_op jit(solution)/shard_map/reduce_scatter | solution.py:535
  315.4 260.4 %reduce-scatter.18.cloned.1.call-start = ((), (), s32[]{:S(2)}) async-start(), calls=%async_computation.19 | async-start | bytes 5849088 | tf_op jit(solution)/shard_map/reduce_scatter | solution.py:536
  322.9 335.8 %reduce-scatter.20.cloned.1.call-start = ((), (), s32[]{:S(2)}) async-start(), calls=%async_computation.20 | async-start | bytes 5849088 | tf_op jit(solution)/shard_map/reduce_scatter | solution.py:537
  330.4 449.3 %all-reduce.6.cloned.1.call-start = ((), (), s32[]{:S(2)}) async-start(), calls=%async_computation.21 | async-start | bytes 9437184 | tf_op jit(solution)/shard_map/psum | solution.py:613
  332.2 28.4 %copy-start.2 = (bf16[512,1472]{1,0:T(8,128)(2,1)S(1)}, bf16[512,1472]{1,0:T(8,128)(2,1)}, u32[]{:S(2)}) copy-start(bf16[512,1472]{1,0:T(8,128)(2,1)} %all-gather.17.cloned.1.call-done.branch_ref) | copy-start | bytes 4521988
  332.2 28.4 %copy-start.9 = (bf16[512,256]{1,0:T(8,128)(2,1)S(1)}, bf16[512,256]{1,0:T(8,128)(2,1)}, u32[]{:S(2)}) copy-start(bf16[512,256]{1,0:T(8,128)(2,1)} %get-tuple-element.20) | copy-start | bytes 786436
  409.6 28.5 %copy-start.7 = (bf16[512,1472]{1,0:T(8,128)(2,1)S(1)}, bf16[512,1472]{1,0:T(8,128)(2,1)}, u32[]{:S(2)}) copy-start(bf16[512,1472]{1,0:T(8,128)(2,1)} %all-gather.9.cloned.1.call-done) | copy-start | bytes 4521988
  442.3 365.5 %reduce-scatter.14.cloned.1.call-start = ((), (), s32[]{:S(2)}) async-start(), calls=%async_computation.17 | async-start | bytes 2359296 | tf_op jit(solution)/shard_map/reduce_scatter | solution.py:603
  449.1 386.9 %reduce-scatter.10.cloned.1.call-start = ((), (), s32[]{:S(2)}) async-start(), calls=%async_computation.11 | async-start | bytes 2359296 | tf_op jit(solution)/shard_map/reduce_scatter | solution.py:516
  839.9 3.1 copy-start.3
  839.9 43.7 %copy-start.8 = (f32[192,1472]{1,0:T(8,128)S(1)}, f32[192,1472]{1,0:T(8,128)}, u32[]{:S(2)}) copy-start(f32[192,1472]{1,0:T(8,128)} %get-tuple-element.129) | copy-start | bytes 3391492
  (7 other events, 12.4 us)
Sparse Core Ops, SparseCore 0:
  10.2 29.8 all-gather.8
  43.4 61.7 all-gather.10
  138.6 24.2 reduce-scatter.7
  165.8 27.2 all-gather.12
  194.5 26.4 all-gather.14
  247.5 26.0 reduce-scatter.11
  277.1 27.2 all-gather.16
  307.0 50.7 all-gather.18
  360.5 49.0 all-gather.20
  413.4 78.8 reduce-scatter.15
  496.6 79.1 reduce-scatter.17
  579.5 79.0 reduce-scatter.19
  663.4 116.2 all-reduce.5
  781.8 25.8 reduce-scatter.13
  809.9 26.0 reduce-scatter.9

commit v2 on v1

--- a/solution.py
+++ b/solution.py
@@ -376,6 +376,301 @@
 
 def params():
     return pltpu.CompilerParams(vmem_limit_bytes=56 * 2**20)
+
+
+class Spot:
+    def __init__(self, lines):
+        index = lax.axis_index("ctx")
+        self.wa = lax.axis_index("wa")
+        self.index = index
+        self.lines = lines
+        self.z = index // 4
+        self.x = (index // 2) % 2
+        self.core = index % 2
+
+    def core_mate(self):
+        return (self.index + 1 - 2 * self.core, self.wa)
+
+    def x_mate(self):
+        return (self.index + 2 - 4 * self.x, self.wa)
+
+    def z_mate(self, step):
+        return (jnp.clip(self.index + 4 * step, 0, 4 * self.lines - 1), self.wa)
+
+    def y_mate(self):
+        return (self.index, 1 - self.wa)
+
+
+def send(src, dst, send_sem, recv_sem, device):
+    return pltpu.make_async_remote_copy(
+        src_ref=src,
+        dst_ref=dst,
+        send_sem=send_sem,
+        recv_sem=recv_sem,
+        device_id=device,
+        device_id_type=pl.DeviceIdType.MESH,
+    )
+
+
+def greet(spot, with_y):
+    barrier = pltpu.get_barrier_semaphore()
+    mates = [spot.core_mate(), spot.x_mate()] + ([spot.y_mate()] if with_y else [])
+    for mate in mates:
+        pl.semaphore_signal(barrier, inc=1, device_id=mate, device_id_type=pl.DeviceIdType.MESH)
+
+    @pl.when(spot.z + 1 < spot.lines)
+    def _():
+        pl.semaphore_signal(
+            barrier, inc=1, device_id=spot.z_mate(1), device_id_type=pl.DeviceIdType.MESH
+        )
+
+    @pl.when(spot.z > 0)
+    def _():
+        pl.semaphore_signal(
+            barrier, inc=1, device_id=spot.z_mate(-1), device_id_type=pl.DeviceIdType.MESH
+        )
+
+    above = (spot.z + 1 < spot.lines).astype(jnp.int32)
+    below = (spot.z > 0).astype(jnp.int32)
+    pl.semaphore_wait(barrier, len(mates) + above + below)
+
+
+def added(a, b):
+    return (a.astype(f32) + b.astype(f32)).astype(bf16)
+
+
+def scatter_kernel(lines, units, z_first, *refs):
+    count = 3
+    parts, outs = (refs[:count], refs[count : 2 * count])
+    mine, core_in, x_in, up_in, down_in, load_sem, core_sem, x_sem, up_sem, down_sem = refs[
+        2 * count :
+    ]
+    spot = Spot(lines)
+    z, x, core = (spot.z, spot.x, spot.core)
+    greet(spot, False)
+    loads = []
+    cores = []
+    order = z_first + [u for u in range(len(units)) if u not in z_first]
+
+    def rows_of(u):
+        return pl.ds(units[u][1], units[u][2])
+
+    for u in order:
+        m = units[u][0]
+        load = pltpu.make_async_copy(
+            parts[m].at[:, :, core, rows_of(u)], mine.at[m, :, :, rows_of(u)], load_sem.at[u]
+        )
+        load.start()
+        loads.append(load)
+        copy = send(
+            parts[m].at[:, :, 1 - core, rows_of(u)],
+            core_in.at[m, :, :, rows_of(u)],
+            core_sem.at[0, u],
+            core_sem.at[1, u],
+            spot.core_mate(),
+        )
+        copy.start()
+        cores.append(copy)
+
+    def add_slices(into, source, u, x_slot):
+        m = units[u][0]
+
+        def body(line, unused):
+            at = (m, line, x_slot, rows_of(u))
+            into[at] = added(into[at], source[at])
+            return unused
+
+        lax.fori_loop(0, lines, body, 0)
+
+    def x_copy(u, both):
+        m = units[u][0]
+        if both:
+            src = mine.at[m, :, 1 - x, rows_of(u)]
+            dst = x_in.at[m, :, rows_of(u)]
+        else:
+            src = mine.at[m, z, 1 - x, rows_of(u)]
+            dst = x_in.at[m, z, rows_of(u)]
+        return send(src, dst, x_sem.at[0, u], x_sem.at[1, u], spot.x_mate())
+
+    def line_flow(u, slots):
+        m = units[u][0]
+        n = len(slots)
+
+        def slot_copies(step, d):
+            ring, sem = (up_in, up_sem) if step > 0 else (down_in, down_sem)
+            return [
+                send(
+                    mine.at[m, d, s, rows_of(u)],
+                    ring.at[m, d, s, rows_of(u)],
+                    sem.at[0, u, d, i],
+                    sem.at[1, u, d, i],
+                    spot.z_mate(step),
+                )
+                for i, s in enumerate(slots)
+            ]
+
+        def receive(step, d):
+            ring = up_in if step > 0 else down_in
+            for copy, s in zip(slot_copies(step, d), slots):
+                copy.wait_recv()
+                at = (m, d, s, rows_of(u))
+                mine[at] = added(mine[at], ring[at])
+
+        def ends_first():
+            @pl.when(z == 0)
+            def _():
+                for d in range(lines - 1, 0, -1):
+                    for copy in slot_copies(1, d):
+                        copy.start()
+
+            @pl.when(z == lines - 1)
+            def _():
+                for d in range(lines - 1):
+                    for copy in slot_copies(-1, d):
+                        copy.start()
+
+        def relay():
+            def body(k, unused):
+                high = lines - 1 - k
+
+                @pl.when((z < high) & (z > 0))
+                def _():
+                    receive(1, high)
+                    for copy in slot_copies(1, high):
+                        copy.start()
+
+                @pl.when((z > k) & (z + 1 < lines))
+                def _():
+                    receive(-1, k)
+                    for copy in slot_copies(-1, k):
+                        copy.start()
+
+                return unused
+
+            lax.fori_loop(0, lines - 1, body, 0)
+
+        def arrive():
+            @pl.when(z > 0)
+            def _():
+                receive(1, z)
+
+            @pl.when(z + 1 < lines)
+            def _():
+                receive(-1, z)
+
+        def finish(k, unused):
+            @pl.when(z < lines - 1 - k)
+            def _():
+                for copy in slot_copies(1, lines - 1 - k):
+                    copy.wait_send()
+
+            @pl.when(z > k)
+            def _():
+                for copy in slot_copies(-1, k):
+                    copy.wait_send()
+
+            return unused
+
+        return (
+            ends_first,
+            relay,
+            arrive,
+            lambda: lax.fori_loop(0, lines - 1, finish, 0),
+        )
+
+    def store(u):
+        m = units[u][0]
+        outs[m][rows_of(u), :] = mine[m, z, x, rows_of(u)].astype(f32)
+
+    pending = {}
+    for i, u in enumerate(order):
+        loads[i].wait()
+        cores[i].wait()
+        if u in z_first:
+            add_slices(mine, core_in, u, 0)
+            add_slices(mine, core_in, u, 1)
+        else:
+            add_slices(mine, core_in, u, 1 - x)
+            copy = x_copy(u, True)
+            copy.start()
+            pending[u] = copy
+            add_slices(mine, core_in, u, x)
+    x_first = [u for u in order if u not in z_first]
+    flows = {u: line_flow(u, [0, 1] if u in z_first else [x]) for u in order}
+    last = {}
+
+    def x_stage(u):
+        m = units[u][0]
+        pending[u].wait()
+
+        def body(line, unused):
+            at = (m, line, x, rows_of(u))
+            mine[at] = added(mine[at], x_in[m, line, rows_of(u)])
+            return unused
+
+        lax.fori_loop(0, lines, body, 0)
+
+    def settle(u):
+        flows[u][2]()
+        if u in z_first:
+            last[u] = x_copy(u, False)
+            last[u].start()
+        else:
+            store(u)
+
+    for t in range(len(order) + 2):
+        if t < len(order):
+            u = order[t]
+            if u not in z_first:
+                x_stage(u)
+            flows[u][0]()
+        if 0 <= t - 1 < len(order):
+            flows[order[t - 1]][1]()
+        if 0 <= t - 2 < len(order):
+            settle(order[t - 2])
+    for u, copy in last.items():
+        m = units[u][0]
+        copy.wait()
+        at = (m, z, x, rows_of(u))
+        mine[at] = added(mine[at], x_in[m, z, rows_of(u)])
+        store(u)
+    for u in order:
+        flows[u][3]()
+
+
+def reduce_scatter(parts, cycle_size):
+    lines = cycle_size // 4
+    units_here, model = parts[0].shape
+    rows = units_here // cycle_size
+    cut = (rows // 2 + 15) // 16 * 16
+    pieces = [(0, cut), (cut, rows - cut)] if cut < rows else [(0, rows)]
+    units = [(m, at, size) for m in range(3) for at, size in pieces]
+    z_first = [len(units) - 1]
+    shaped = [part.reshape(lines, 2, 2, rows, model) for part in parts]
+    hbm = pl.BlockSpec(memory_space=pl.ANY)
+    n = len(units)
+    return pl.pallas_call(
+        functools.partial(scatter_kernel, lines, units, z_first),
+        out_shape=[jax.ShapeDtypeStruct((rows, model), f32)] * 3,
+        in_specs=[hbm] * 3,
+        out_specs=[vmem] * 3,
+        scratch_shapes=[
+            pltpu.VMEM((3, lines, 2, rows, model), bf16),
+            pltpu.VMEM((3, lines, 2, rows, model), bf16),
+            pltpu.VMEM((3, lines, rows, model), bf16),
+            pltpu.VMEM((3, lines, 2, rows, model), bf16),
+            pltpu.VMEM((3, lines, 2, rows, model), bf16),
+            pltpu.SemaphoreType.DMA((n,)),
+            pltpu.SemaphoreType.DMA((2, n)),
+            pltpu.SemaphoreType.DMA((2, n)),
+            pltpu.SemaphoreType.DMA((2, n, lines, 2)),
+            pltpu.SemaphoreType.DMA((2, n, lines, 2)),
+        ],
+        compiler_params=pltpu.CompilerParams(
+            vmem_limit_bytes=58 * 2**20, collective_id=1, has_side_effects=True
+        ),
+        name="weight_scatter",
+    )(*shaped)
 
 
 def shards(
@@ -529,13 +824,12 @@
     grad_normed_ffn = lax.psum_scatter(
         grad_pair_ffn.astype(bf16), "wa", scatter_dimension=0, tiled=True
     ).astype(f32)
-    gate_half = jnp.dot(pair_ffn.T, grad_gate, preferred_element_type=f32).astype(bf16)
-    up_half = jnp.dot(pair_ffn.T, grad_upward, preferred_element_type=f32).astype(bf16)
-    grad_w_gate, grad_w_up, grad_w_down = (
-        lax.psum_scatter(gate_half, "ctx", scatter_dimension=1, tiled=True).astype(f32),
-        lax.psum_scatter(up_half, "ctx", scatter_dimension=1, tiled=True).astype(f32),
-        lax.psum_scatter(down_half, "ctx", scatter_dimension=0, tiled=True).astype(f32),
-    )
+    gate_half = jnp.dot(grad_gate.T, pair_ffn, preferred_element_type=f32).astype(bf16)
+    up_half = jnp.dot(grad_upward.T, pair_ffn, preferred_element_type=f32).astype(bf16)
+    grad_w_down, grad_w_gate, grad_w_up = reduce_scatter(
+        [down_half, gate_half, up_half], cycle_size
+    )
+    grad_w_gate, grad_w_up = (grad_w_gate.T, grad_w_up.T)
     hidden_step, gain_ffn_part = norm_backward(hidden, inv_ffn, gain_ffn, grad_normed_ffn)
     grad_hidden = cotangent.astype(f32) + hidden_step
     pair_branch = lax.all_gather(grad_hidden.astype(bf16), "wa", axis=0, tiled=True)

time: 903 us -> 751 us (0.83)
  waiting for transfers between devices: 545 us -> 269 us
  Pallas kernels: 92.5 us -> 199 us
  local copies, waits for them, and re-layouts: 27.7 us -> 55.5 us
    reduce_scatter x3 -> x0, waiting for transfers between devices: 163 us -> none  [the longest x1 81.7 us: shards(): lax.psum_scatter(up_half, 'ctx', scatter_dimension=1, tiled=True)]
    pallas_call x0 -> x1, Pallas kernels: none -> 145 us  [reduce_scatter(): pl.pallas_call(functools.partial(scatter_kernel, lines, units, z_first),...]
    psum x1, waiting for transfers between devices: 113 us -> 0.01 us  [shards(): lax.psum((qkv_part, out_part, grad_tab), 'ctx')]
    all_gather x1, waiting for transfers between devices: 0.01 us -> 30.3 us  [shards(): q_all = window(gather(q_back))]
    reduce_scatter x1, waiting for transfers between devices: 26.6 us -> 0.02 us  [shards(): lax.psum_scatter(ffn_part.astype(bf16), 'wa', scatter_dimension=0, tiled=...]
    convert_element_type x0 -> x3, local copies, waits for them, and re-layouts: none -> 24.8 us  [the longest x1 8.28 us: shards(): jnp.dot(inner.T, pair_cot, preferred_element_type=f32).astype(bf16)]
    reduce_scatter x1, waiting for transfers between devices: 24.3 us -> 0.01 us  [shards(): lax.psum_scatter(grad_pair.astype(bf16), 'wa', scatter_dimension=0, tiled...]
    reduce_scatter x1, waiting for transfers between devices: 24.3 us -> 40.2 us  [shards(): lax.psum_scatter(jnp.dot(attended, w_out_pad, preferred_element_type=f32)...]
  transfers between devices with their start and end apart: 15 -> 12, of which waited for: 14 -> 9; matrix products, arithmetic and copies ran while one was open for 10% -> 14% of each run, Pallas kernels for 7% -> 23%
where the time goes in v2:
time: 751 us; the launch traced here: 740 us
  waiting for transfers between devices  269 us (36%)
  Pallas kernels  199 us (26%)
  blocking collectives  93.7 us (12%)
  matrix products  83.2 us (11%)
  local copies, waits for them, and re-layouts  55.5 us (7%)
  other arithmetic  22.3 us (3%)
  between operations  15.7 us (2%)
    pallas_call x1, Pallas kernels, reduce_scatter(): pl.pallas_call(functools.partial(scatter_kernel, lines, units, z_first),...  145 us
    all_gather x1, waiting for transfers between devices, shards(): do_all = window(gather(do_wide))  51.8 us
    reduce_scatter x1, waiting for transfers between devices, shards(): lax.psum_scatter(jnp.dot(attended, w_out_pad, preferred_element_type=f32)...  40.2 us
    psum x1, blocking collectives, shards(): lax.psum((gain_attn_part, gain_ffn_part), ('ctx', 'wa'))  37 us
    all_gather x1, waiting for transfers between devices, shards(): q_all = window(gather(q_back))  30.3 us
    psum x1, blocking collectives, shards(): lax.psum((qkv_part, out_part, grad_tab), 'ctx')  30.1 us
    all_gather x1, waiting for transfers between devices, shards(): lax.all_gather(normed_low, 'wa', axis=0, tiled=True)  30 us
    all_gather x1, waiting for transfers between devices, shards(): pair_ffn = lax.all_gather(ffn_low, 'wa', axis=0, tiled=True)  26.3 us
  transfers between devices with their start and end apart: 12, of which 9 were waited for; matrix products, arithmetic and copies ran while one was open for 14% of the time, Pallas kernels for 23%

profile of v2, /device:TPU:0, one launch (start us, length us, event | category | flops | bytes accessed | tf_op | source)
XLA Modules:
  0.0 739.7 jit_solution(555310465487703011)
XLA Ops:
  10.2 30.0 %all-gather.9.cloned.1.call-done = bf16[512,1472]{1,0:T(8,128)(2,1)} async-done(((bf16[256,1472]{1,0:T(8,128)(2,1)}), bf16[512,1472]{1,0:T(8,128)(2,1)}) %all-gather.9.cloned.1.call-update) | async-done | bytes 1507344 | tf_op jit(solution)/shard_map/all_gather | solution.py:728
  45.1 21.7 %all-gather = bf16[16,1,512]{2,1,0:T(2,128)(2,1)S(1)} all-gather(bf16[1,1,512]{2,1,0:T(2,128)(2,1)S(1)} %reshape.293), channel_id=1, replica_groups=mesh['ctx'=16,'wa'=2] {'ctx'}, dimensions={0}, use_global_device_ids=true | all-gather | bytes 17408 | tf_op jit(solution)/shard_map/all_gather | solution.py:723
  67.1 5.1 near_bias.1.near_ref
  73.4 4.6 select_convert_fusion.kaug_ref
  79.7 25.8 %all-gather.11.cloned.1.call-done.g_ref = bf16[8192,384]{1,0:T(8,128)(2,1)} async-done(((bf16[512,384]{1,0:T(8,128)(2,1)}), bf16[8192,384]{1,0:T(8,128)(2,1)}) %all-gather.11.cloned.1.call-update) | async-done | bytes 6291472 | tf_op jit(solution)/shard_map/all_gather | solution.py:741
  105.5 16.0 %attention_forward.1 = (bf16[512,256]{1,0:T(8,128)(2,1)}, f32[512,256]{1,0:T(8,128)}, bf16[512,256]{1,0:T(8,128)(2,1)}) custom-call(s32[5]{0:T(128)} %pad_add_fusion.1.bounds, f32[32,3]{1,0:T(8,128)} %copy.103.table_ref, bf16[8192,384]{1,0:T(8,128)(2,1)} %all-gather.11.cloned.1.call-done.g_ref, bf16[8192,128]{1,0:T(8,128)(2,1)} %select_convert_fusion.kaug_ref, ...), custom_call_target="tpu_custom_call" | custom-call | tf_op jit(solution)/shard_map/attention_forward/pallas_call | solution.py:774
  124.7 40.2 %reduce-scatter.5.cloned.1.call-done = bf16[256,1472]{1,0:T(8,128)(2,1)} async-done(((bf16[512,1472]{1,0:T(8,128)(2,1)}), bf16[256,1472]{1,0:T(8,128)(2,1)}) %reduce-scatter.5.cloned.1.call-update) | async-done | bytes 753680 | tf_op jit(solution)/shard_map/reduce_scatter | solution.py:795
  168.7 26.3 %all-gather.13.cloned.1.call-done = bf16[512,1472]{1,0:T(8,128)(2,1)} async-done(((bf16[256,1472]{1,0:T(8,128)(2,1)}), bf16[512,1472]{1,0:T(8,128)(2,1)}) %all-gather.13.cloned.1.call-update) | async-done | bytes 1507344 | tf_op jit(solution)/shard_map/all_gather | solution.py:804
  195.0 8.0 %fusion.58 = f32[512,1792]{1,0:T(8,128)} fusion(bf16[512,1472]{1,0:T(8,128)(2,1)} %all-gather.13.cloned.1.call-done, bf16[1472,1792]{1,0:T(8,128)(2,1)} %param.24), kind=kOutput, calls=%fused_computation.131 | convolution fusion | flops 2701131776 | bytes 10452992 | tf_op jit(solution)/shard_map/dot_general | solution.py:805
  203.0 7.5 %fusion.59 = f32[512,1792]{1,0:T(8,128)} fusion(bf16[512,1472]{1,0:T(8,128)(2,1)S(1)} %copy-done.18, bf16[1472,1792]{1,0:T(8,128)(2,1)} %param.25), kind=kOutput, calls=%fused_computation.132 | convolution fusion | flops 2701131776 | bytes 10452992 | tf_op jit(solution)/shard_map/dot_general | solution.py:806
  210.5 12.4 %all-gather.15.cloned.1.call-done = bf16[512,1472]{0,1:T(8,128)(2,1)} async-done(((bf16[256,1472]{0,1:T(8,128)(2,1)}), bf16[512,1472]{0,1:T(8,128)(2,1)}) %all-gather.15.cloned.1.call-update) | async-done | bytes 1507344 | tf_op jit(solution)/shard_map/all_gather | solution.py:729
  222.9 10.8 %multiply_convert_fusion = (bf16[512,1792]{1,0:T(8,128)(2,1)S(1)}, bf16[512,1792]{1,0:T(8,128)(2,1)S(1)}, bf16[512,1792]{1,0:T(8,128)(2,1)}) fusion(f32[512,1792]{1,0:T(8,128)} %fusion.58, f32[512,1792]{1,0:T(8,128)} %fusion.59, bf16[512,1472]{0,1:T(8,128)(2,1)} %all-gather.15.cloned.1.call-done, bf16[1792,1472]{0,1:T(8,128)(2,1)} %param.26), kind=kOutput, calls=%fused_computation.15 | convolution fusion | flops 2724986880 | bytes 19628032 | tf_op jit(solution)/shard_map/dot_general | solution.py:815
  233.8 6.2 fusion.60
  240.0 6.6 convolution_add_fusion
  249.7 25.9 %reduce-scatter.9.cloned.1.call-done = bf16[256,1472]{1,0:T(8,128)(2,1)} async-done(((bf16[512,1472]{1,0:T(8,128)(2,1)}), bf16[256,1472]{1,0:T(8,128)(2,1)}) %reduce-scatter.9.cloned.1.call-update) | async-done | bytes 753680 | tf_op jit(solution)/shard_map/reduce_scatter | solution.py:824
  281.7 24.6 %all-gather.17.cloned.1.call-done.branch_ref = bf16[512,1472]{1,0:T(8,128)(2,1)} async-done(((bf16[256,1472]{1,0:T(8,128)(2,1)}), bf16[512,1472]{1,0:T(8,128)(2,1)}) %all-gather.17.cloned.1.call-update) | async-done | bytes 1507344 | tf_op jit(solution)/shard_map/all_gather | solution.py:835
  311.5 16.4 %attention_grad_queries.1 = (bf16[512,256]{1,0:T(8,128)(2,1)}, f32[3,32,128]{2,1,0:T(8,128)}) custom-call(s32[5]{0:T(128)} %pad_add_fusion.1.bounds, f32[32,3]{1,0:T(8,128)} %copy.103.table_ref, bf16[8192,384]{1,0:T(8,128)(2,1)} %all-gather.11.cloned.1.call-done.g_ref, bf16[8192,128]{1,0:T(8,128)(2,1)} %select_convert_fusion.kaug_ref, ...), custom_call_target="tpu_custom_call" | custom-call | tf_op jit(solution)/shard_map/attention_grad_queries/pallas_call | solution.py:847
  329.5 30.3 %all-gather.19.cloned.1.call-done.qall_ref = bf16[8192,256]{1,0:T(8,128)(2,1)} async-done(((bf16[512,256]{1,0:T(8,128)(2,1)}), bf16[8192,256]{1,0:T(8,128)(2,1)}) %all-gather.19.cloned.1.call-update) | async-done | bytes 4194320 | tf_op jit(solution)/shard_map/all_gather | solution.py:793
  359.8 51.8 %all-gather.21.cloned.1.call-done.doall_ref = bf16[8192,256]{1,0:T(8,128)(2,1)} async-done(((bf16[512,256]{1,0:T(8,128)(2,1)}), bf16[8192,256]{1,0:T(8,128)(2,1)}) %all-gather.21.cloned.1.call-update) | async-done | bytes 4194320 | tf_op jit(solution)/shard_map/all_gather | solution.py:845
  411.6 13.9 %attention_grad_keys.1 = (f32[512,256]{1,0:T(8,128)}, bf16[512,256]{1,0:T(8,128)(2,1)}) custom-call(s32[5]{0:T(128)} %pad_add_fusion.1.bounds, f32[32,3]{1,0:T(8,128)} %copy.103.table_ref, bf16[8192,256]{1,0:T(8,128)(2,1)} %all-gather.19.cloned.1.call-done.qall_ref, bf16[8192,256]{1,0:T(8,128)(2,1)} %all-gather.21.cloned.1.call-done.doall_ref, ...), custom_call_target="tpu_custom_call" | custom-call | tf_op jit(solution)/shard_map/attention_grad_keys/pallas_call | solution.py:868
  431.8 4.2 convolution_convert_fusion.3
  440.1 7.1 convolution_convert_fusion.5
  449.9 7.2 convolution_convert_fusion
  457.1 8.3 %copy.111 = bf16[1792,1472]{1,0:T(8,128)(2,1)} copy(bf16[1792,1472]{0,1:T(8,128)(2,1)} %convolution_convert_fusion) | data formatting | bytes 10551296 | tf_op jit(solution)/shard_map/convert_element_type | solution.py:816
  465.4 7.3 convolution_convert_fusion.2
  472.6 8.3 %copy.112 = bf16[1792,1472]{1,0:T(8,128)(2,1)} copy(bf16[1792,1472]{0,1:T(8,128)(2,1)} %convolution_convert_fusion.2) | data formatting | bytes 10551296 | tf_op jit(solution)/shard_map/convert_element_type | solution.py:827
  480.9 7.3 convolution_convert_fusion.1
  488.2 8.3 %copy.113 = bf16[1792,1472]{1,0:T(8,128)(2,1)} copy(bf16[1792,1472]{0,1:T(8,128)(2,1)} %convolution_convert_fusion.1) | data formatting | bytes 10551296 | tf_op jit(solution)/shard_map/convert_element_type | solution.py:828
  496.5 144.6 %weight_scatter.1 = (f32[112,1472]{1,0:T(8,128)}, f32[112,1472]{1,0:T(8,128)}, f32[112,1472]{1,0:T(8,128)}) custom-call(bf16[4,2,2,112,1472]{4,3,2,1,0:T(8,128)(2,1)} %bitcast.54, bf16[4,2,2,112,1472]{4,3,2,1,0:T(8,128)(2,1)} %bitcast.55, bf16[4,2,2,112,1472]{4,3,2,1,0:T(8,128)(2,1)} %bitcast.56), custom_call_target="tpu_custom_call" | custom-call | tf_op jit(solution)/shard_map/weight_scatter/pallas_call | solution.py:652
  641.2 30.1 %psum.38 = f32[32,3]{0,1:T(4,128)} all-reduce(f32[32,3]{0,1:T(4,128)S(1)} %bitcast.64), channel_id=1, replica_groups=mesh['ctx'=16,'wa'=2] {'ctx'}, use_global_device_ids=true, to_apply=%region_21.22 | all-reduce | flops 96 | bytes 768 | tf_op jit(solution)/shard_map/psum | solution.py:907
  671.4 4.9 all-reduce.1
  691.9 37.0 %all-reduce.2 = (f32[1472]{0:T(1024)}, f32[1472]{0:T(1024)}) all-reduce(f32[1472]{0:T(1024)S(1)} %get-tuple-element.100, f32[1472]{0:T(1024)S(1)} %get-tuple-element.98), channel_id=1, replica_groups=mesh['ctx'=16,'wa'=2] {'ctx','wa'}, use_global_device_ids=true, to_apply=%region_17.18 | all-reduce | flops 2944 | bytes 23552 | tf_op jit(solution)/shard_map/psum | solution.py:906
  (151 shorter events, 65.4 us)
Async XLA Ops:
  7.2 33.0 %all-gather.9.cloned.1.call-start = ((), (), s32[]{:S(2)}) async-start(), calls=%async_computation.4 | async-start | bytes 2359296 | tf_op jit(solution)/shard_map/all_gather | solution.py:728
  8.6 31.5 %copy-start.19 = (bf16[1472,192]{0,1:T(8,128)(2,1)S(1)}, bf16[1472,192]{0,1:T(8,128)(2,1)}, u32[]{:S(2)}) copy-start(bf16[1472,192]{0,1:T(8,128)(2,1)} %param.20) | copy-start | bytes 1695748
  8.6 31.5 %copy-start.20 = (bf16[1472,192]{0,1:T(8,128)(2,1)S(1)}, bf16[1472,192]{0,1:T(8,128)(2,1)}, u32[]{:S(2)}) copy-start(bf16[1472,192]{0,1:T(8,128)(2,1)} %param.19) | copy-start | bytes 1695748
  10.1 33.3 %copy-start.22 = (s32[8]{0:T(128)S(1)}, s32[8]{0:T(128)}, u32[]{:S(2)}) copy-start(s32[8]{0:T(128)} %param.15) | copy-start | bytes 100
  10.1 34.3 %copy-start.16 = (f32[32,3]{0,1:T(4,128)S(1)}, f32[32,3]{0,1:T(4,128)}, u32[]{:S(2)}) copy-start(f32[32,3]{0,1:T(4,128)} %param.22) | copy-start | bytes 1156
  10.1 35.0 %copy-start.17 = (bf16[512]{0:T(512)(128)(2,1)S(1)}, bf16[512]{0:T(512)(128)(2,1)}, u32[]{:S(2)}) copy-start(bf16[512]{0:T(512)(128)(2,1)} %param.16) | copy-start | bytes 3076
  10.1 95.3 %all-gather.11.cloned.1.call-start = ((), (), s32[]{:S(2)}) async-start(), calls=%async_computation.5 | async-start | bytes 6684672 | tf_op jit(solution)/shard_map/all_gather | solution.py:741
  43.3 121.5 %reduce-scatter.5.cloned.1.call-start = ((), (), s32[]{:S(2)}) async-start(), calls=%async_computation.6 | async-start | bytes 2359296 | tf_op jit(solution)/shard_map/reduce_scatter | solution.py:795
  72.3 5.8 copy-start.5
  72.3 5.8 copy-start.21
  79.7 41.8 %copy-start.4 = (bf16[192,1472]{1,0:T(8,128)(2,1)S(1)}, bf16[192,1472]{1,0:T(8,128)(2,1)}, u32[]{:S(2)}) copy-start(bf16[192,1472]{1,0:T(8,128)(2,1)} %param.21) | copy-start | bytes 1695748
  124.6 41.8 %copy-start.13 = (f32[1472]{0:T(1024)S(1)}, f32[1472]{0:T(1024)}, u32[]{:S(2)}) copy-start(f32[1472]{0:T(1024)} %param.23) | copy-start | bytes 17668
  124.6 70.4 %all-gather.13.cloned.1.call-start = ((), (), s32[]{:S(2)}) async-start(), calls=%async_computation.7 | async-start | bytes 2359296 | tf_op jit(solution)/shard_map/all_gather | solution.py:804
  167.6 55.3 %all-gather.15.cloned.1.call-start = ((), (), s32[]{:S(2)}) async-start(), calls=%async_computation.9 | async-start | bytes 2260992 | tf_op jit(solution)/shard_map/all_gather | solution.py:729
  168.2 107.4 %reduce-scatter.9.cloned.1.call-start = ((), (), s32[]{:S(2)}) async-start(), calls=%async_computation.10 | async-start | bytes 2359296 | tf_op jit(solution)/shard_map/reduce_scatter | solution.py:824
  195.0 8.0 %copy-start.18 = (bf16[512,1472]{1,0:T(8,128)(2,1)S(1)}, bf16[512,1472]{1,0:T(8,128)(2,1)}, u32[]{:S(2)}) copy-start(bf16[512,1472]{1,0:T(8,128)(2,1)} %all-gather.13.cloned.1.call-done) | copy-start | bytes 4521988
  233.8 6.2 copy-start.25
  233.8 6.2 copy-start.24
  246.7 2.7 copy-start.3
  249.3 56.9 %all-gather.17.cloned.1.call-start = ((), (), s32[]{:S(2)}) async-start(), calls=%async_computation.11 | async-start | bytes 2359296 | tf_op jit(solution)/shard_map/all_gather | solution.py:835
  278.9 80.9 %all-gather.19.cloned.1.call-start = ((), (), s32[]{:S(2)}) async-start(), calls=%async_computation.12 | async-start | bytes 4456448 | tf_op jit(solution)/shard_map/all_gather | solution.py:793
  279.6 131.9 %all-gather.21.cloned.1.call-start = ((), (), s32[]{:S(2)}) async-start(), calls=%async_computation.13 | async-start | bytes 4456448 | tf_op jit(solution)/shard_map/all_gather | solution.py:845
  309.6 367.4 %all-reduce.6.cloned.1.call-start = ((), (), s32[]{:S(2)}) async-start(), calls=%async_computation.15 | async-start | bytes 9437184 | tf_op jit(solution)/shard_map/psum | solution.py:907
  311.5 16.4 %copy-start.2 = (bf16[512,1472]{1,0:T(8,128)(2,1)S(1)}, bf16[512,1472]{1,0:T(8,128)(2,1)}, u32[]{:S(2)}) copy-start(bf16[512,1472]{1,0:T(8,128)(2,1)} %all-gather.17.cloned.1.call-done.branch_ref) | copy-start | bytes 4521988
  311.5 16.4 %copy-start.8 = (bf16[512,256]{1,0:T(8,128)(2,1)S(1)}, bf16[512,256]{1,0:T(8,128)(2,1)}, u32[]{:S(2)}) copy-start(bf16[512,256]{1,0:T(8,128)(2,1)} %get-tuple-element.23) | copy-start | bytes 786436
  411.6 16.2 %copy-start.6 = (bf16[512,1472]{1,0:T(8,128)(2,1)S(1)}, bf16[512,1472]{1,0:T(8,128)(2,1)}, u32[]{:S(2)}) copy-start(bf16[512,1472]{1,0:T(8,128)(2,1)} %all-gather.9.cloned.1.call-done) | copy-start | bytes 4521988
  431.8 249.1 %reduce-scatter.11.cloned.1.call-start = ((), (), s32[]{:S(2)}) async-start(), calls=%async_computation.14 | async-start | bytes 2359296 | tf_op jit(solution)/shard_map/reduce_scatter | solution.py:897
  436.0 2.9 copy-start.23
  438.6 243.9 %reduce-scatter.7.cloned.1.call-start = ((), (), s32[]{:S(2)}) async-start(), calls=%async_computation.8 | async-start | bytes 2359296 | tf_op jit(solution)/shard_map/reduce_scatter | solution.py:811
  496.5 144.6 %copy-start.15 = (f32[3,32,128]{2,1,0:T(8,128)S(1)}, f32[3,32,128]{2,1,0:T(8,128)}, u32[]{:S(2)}) copy-start(f32[3,32,128]{2,1,0:T(8,128)} %get-tuple-element.29) | copy-start | bytes 147460
  688.8 40.1 %copy-start.7 = (f32[192,1472]{1,0:T(8,128)S(1)}, f32[192,1472]{1,0:T(8,128)}, u32[]{:S(2)}) copy-start(f32[192,1472]{1,0:T(8,128)} %get-tuple-element.148) | copy-start | bytes 3391492
  691.9 38.0 %copy-start.12 = (f32[112,1472]{1,0:T(8,128)S(1)}, f32[112,1472]{1,0:T(8,128)}, u32[]{:S(2)}) copy-start(f32[112,1472]{1,0:T(8,128)} %get-tuple-element.30) | copy-start | bytes 1978372
  (6 other events, 9.8 us)
Sparse Core Ops, SparseCore 0:
  10.2 29.8 all-gather.8
  43.4 61.9 all-gather.10
  124.7 40.0 reduce-scatter.4
  167.8 27.2 all-gather.12
  196.5 26.4 all-gather.14
  249.5 26.0 reduce-scatter.8
  279.0 27.2 all-gather.16
  309.0 50.7 all-gather.18
  362.5 49.0 all-gather.20
  431.9 156.7 all-reduce.5
  591.0 28.7 reduce-scatter.10
  622.0 26.0 reduce-scatter.6

commit v3 on v2

--- a/solution.py
+++ b/solution.py
@@ -279,7 +279,7 @@
 
 def dkv_kernel(
     plan, rows, pair, bounds, table_ref, qall_ref, doall_ref, g_ref, kaug_ref, near_ref,
-    dk_ref, dv_ref, qp, dop, kh_ref, vh_ref, acc_k, acc_v,
+    dk_ref, dv_ref, mask_ref, qp, dop, kh_ref, vh_ref, acc_k, acc_v,
 ):
     lane = lanes_of(TQ)
     first = lanes_of(1)
@@ -348,7 +348,8 @@
             dk = jnp.where(lane // 64 == h, acc_k[h], dk)
             dv = jnp.where(lane // 64 == h + 1, acc_v[h], dv)
             mask_grad = mask_grad + acc_k[h][:, plan.mask_lane : plan.mask_lane + 1]
-        dk_ref[out, :] = jnp.where(lane == plan.mask_lane, mask_grad, dk)
+        mask_ref[t] = jnp.transpose(jnp.broadcast_to(mask_grad, (TQ, 128)))[:8, :]
+        dk_ref[out, :] = dk.astype(bf16)
         dv_ref[out, :] = dv.astype(bf16)
         return unused
 
@@ -671,6 +672,363 @@
         ),
         name="weight_scatter",
     )(*shaped)
+
+def tn(a, b):
+    return lax.dot_general(a, b, (((0,), (0,)), ((), ())), preferred_element_type=f32)
+
+
+def line_relay(spot, start, receive):
+    def level(k, unused):
+        @pl.when(spot.z - k >= 0)
+        def _():
+            if_first(k, lambda: receive(1, spot.z - k))
+
+            @pl.when(spot.z + 1 < spot.lines)
+            def _():
+                start(1, spot.z - k)
+
+        @pl.when(spot.z + k < spot.lines)
+        def _():
+            if_first(k, lambda: receive(-1, spot.z + k))
+
+            @pl.when(spot.z > 0)
+            def _():
+                start(-1, spot.z + k)
+
+        return unused
+
+    def if_first(k, run):
+        @pl.when(k > 0)
+        def _():
+            run()
+
+    return level
+
+
+def finish_kernel(
+    plan, lines, dq_ref, dk_ref, dv_ref, mask_ref, w3_ref, normed_ref, att_ref, branch_ref,
+    tokens_ref, gain_ref, hidden_ref, gh_ref, ffn_ref, small_ref,
+    out_ref, gt_ref, gm_ref, weights_ref, total_ref,
+    mine, core_in, x_in, up_in, down_in, all_w, y_out, y_in, own_part, ffn_in, mask_in,
+    small_own, small_y, small_core, small_x, small_all,
+    y_sem, core_sem, x_sem, up_sem, down_sem, gz_sem, gx_sem, gc_sem, sz_sem,
+):
+    spot = Spot(lines)
+    z, x, core, wa = (spot.z, spot.x, spot.core, spot.wa)
+    greet(spot, True)
+    half = tokens_ref.shape[0]
+    quarter = half // 2
+    model = tokens_ref.shape[1]
+    rows = mine.shape[3]
+
+    def grad_rows(at):
+        at = pl.ds(pl.multiple_of(at, quarter), quarter)
+        return (
+            nt(dq_ref[at, :], w3_ref[:, 0:256])
+            + nt(dk_ref[at, :], w3_ref[:, 256:512])
+            + nt(dv_ref[at, :], w3_ref[:, 512:768])
+        )
+
+    def y_copy(i):
+        return send(y_out.at[i], y_in.at[i], y_sem.at[0, i], y_sem.at[1, i], spot.y_mate())
+
+    def theirs(i, unused):
+        y_out[i] = grad_rows((1 - wa) * half + i * quarter).astype(bf16)
+        y_copy(i).start()
+        return unused
+
+    lax.fori_loop(0, 2, theirs, 0)
+    mask_copy = send(
+        mask_ref.at[1 - wa], mask_in, y_sem.at[0, 2], y_sem.at[1, 2], spot.y_mate()
+    )
+    mask_copy.start()
+
+    def fill(product, matrix):
+        for j in range(plan.cols // rows):
+            s = matrix * (plan.cols // rows) + j
+            mine[s // 4, (s // 2) % 2, s % 2] = product[j * rows : (j + 1) * rows].astype(bf16)
+
+    fill(tn(dq_ref[...], normed_ref[...])[: plan.cols], 0)
+    fill(tn(dk_ref[...], normed_ref[...])[: plan.cols], 1)
+    fill(tn(dv_ref[...], normed_ref[...])[64:], 2)
+    fill(tn(att_ref[...], branch_ref[...])[64:], 3)
+    core_copy = send(
+        mine.at[:, :, 1 - core], core_in, core_sem.at[0, 0], core_sem.at[1, 0], spot.core_mate()
+    )
+    core_copy.start()
+    their_rows = pl.ds(pl.multiple_of((1 - wa) * half, half), half)
+    ffn_copy = send(
+        ffn_ref.at[their_rows], ffn_in, y_sem.at[0, 3], y_sem.at[1, 3], spot.y_mate()
+    )
+    ffn_copy.start()
+
+    def ours(i, unused):
+        own_part[pl.ds(pl.multiple_of(i * quarter, quarter), quarter), :] = grad_rows(
+            wa * half + i * quarter
+        )
+        return unused
+
+    lax.fori_loop(0, 2, ours, 0)
+    core_copy.wait()
+
+    def x_copy(d):
+        return send(
+            mine.at[d, 1 - x, core], x_in.at[d], x_sem.at[0, d], x_sem.at[1, d], spot.x_mate()
+        )
+
+    def core_add(d, unused):
+        mine[d, 1 - x, core] = added(mine[d, 1 - x, core], core_in[d, 1 - x])
+        x_copy(d).start()
+        return unused
+
+    lax.fori_loop(0, lines, core_add, 0)
+
+    def core_add_own(d, unused):
+        mine[d, x, core] = added(mine[d, x, core], core_in[d, x])
+        return unused
+
+    lax.fori_loop(0, lines, core_add_own, 0)
+
+    gain_sum = jnp.zeros((1, model), f32)
+    step = 32
+    for i in range(2):
+        y_copy(i).wait()
+
+        def normal(j, total, i=i):
+            at = pl.ds(pl.multiple_of(i * quarter + j * step, step), step)
+            there = pl.ds(pl.multiple_of(j * step, step), step)
+            grad = own_part[at, :] + y_in[i, there, :].astype(f32)
+            rows_in = tokens_ref[at, :].astype(f32)
+            inv = lax.rsqrt(jnp.mean(rows_in * rows_in, axis=-1, keepdims=True) + eps)
+            scaled = gain_ref[...] * grad
+            mean = jnp.mean(rows_in * scaled, axis=-1, keepdims=True)
+            gt_ref[at, :] = gh_ref[at, :] + inv * scaled - rows_in * (inv * inv * inv * mean)
+            return total + jnp.sum(grad * rows_in * inv, axis=0, keepdims=True)
+
+        gain_sum = lax.fori_loop(0, quarter // step, normal, gain_sum)
+    small_own[...] = small_ref[...]
+    small_own[0:1, :] = gain_sum
+    small_copy = send(
+        small_own, small_y, y_sem.at[0, 4], y_sem.at[1, 4], spot.y_mate()
+    )
+    small_copy.start()
+    mask_copy.wait()
+    gm_ref[...] = mask_ref[wa] + mask_in[...]
+
+    def flow(step, d):
+        ring, sem = (up_in, up_sem) if step > 0 else (down_in, down_sem)
+        return send(
+            mine.at[d, x, core], ring.at[d], sem.at[0, d], sem.at[1, d], spot.z_mate(step)
+        )
+
+    def merge(step, d):
+        flow(step, d).wait_recv()
+        ring = up_in if step > 0 else down_in
+        mine[d, x, core] = added(mine[d, x, core], ring[d])
+
+    def x_add(d, unused):
+        x_copy(d).wait()
+        mine[d, x, core] = added(mine[d, x, core], x_in[d])
+
+        @pl.when((z == 0) & (d > 0))
+        def _():
+            flow(1, d).start()
+
+        @pl.when((z == lines - 1) & (d < lines - 1))
+        def _():
+            flow(-1, d).start()
+
+        return unused
+
+    lax.fori_loop(0, lines, x_add, 0)
+    small_copy.wait()
+    row = lax.broadcasted_iota(jnp.int32, small_own.shape, 0)
+    small_x[0] = small_own[...] + jnp.where(row < 2, small_y[...], 0.0)
+    small_core_copy = send(
+        small_x.at[0], small_core, core_sem.at[0, 1], core_sem.at[1, 1], spot.core_mate()
+    )
+    small_core_copy.start()
+
+    def relay(k, unused):
+        high = lines - 1 - k
+
+        @pl.when((z < high) & (z > 0))
+        def _():
+            merge(1, high)
+            flow(1, high).start()
+
+        @pl.when((z > k) & (z + 1 < lines))
+        def _():
+            merge(-1, k)
+            flow(-1, k).start()
+
+        return unused
+
+    lax.fori_loop(0, lines - 1, relay, 0)
+    small_core_copy.wait()
+    small_x[1] = small_x[0] + small_core[...]
+    small_x_copy = send(
+        small_x.at[1], small_x.at[2], x_sem.at[0, lines], x_sem.at[1, lines], spot.x_mate()
+    )
+    small_x_copy.start()
+
+    @pl.when(z > 0)
+    def _():
+        merge(1, z)
+
+    @pl.when(z + 1 < lines)
+    def _():
+        merge(-1, z)
+
+    all_w[z, x, core] = mine[z, x, core]
+
+    def pass_w(step, d):
+        i = 0 if step > 0 else 1
+        return send(
+            all_w.at[d, x, core], all_w.at[d, x, core], gz_sem.at[i, d], gz_sem.at[2 + i, d],
+            spot.z_mate(step),
+        )
+
+    def pass_s(step, d):
+        i = 0 if step > 0 else 1
+        return send(
+            small_all.at[d], small_all.at[d], sz_sem.at[i, d], sz_sem.at[2 + i, d],
+            spot.z_mate(step),
+        )
+
+    def across(d):
+        return send(
+            all_w.at[d, x, core], all_w.at[d, x, core], gx_sem.at[0, d], gx_sem.at[1, d],
+            spot.x_mate(),
+        )
+
+    def beside(d):
+        return send(
+            all_w.at[d, :, core], all_w.at[d, :, core], gc_sem.at[0, d], gc_sem.at[1, d],
+            spot.core_mate(),
+        )
+
+    small_x_copy.wait()
+    small_all[z] = small_x[1] + small_x[2]
+
+    def receive(step, d):
+        pass_w(step, d).wait_recv()
+        across(d).start()
+
+    across(z).start()
+    lax.fori_loop(
+        0, lines, line_relay(spot, lambda s, d: pass_w(s, d).start(), receive), 0
+    )
+    lax.fori_loop(
+        0,
+        lines,
+        line_relay(
+            spot, lambda s, d: pass_s(s, d).start(), lambda s, d: pass_s(s, d).wait_recv()
+        ),
+        0,
+    )
+
+    def add_small(d, total):
+        return total + small_all[d]
+
+    total_ref[...] = lax.fori_loop(1, lines, add_small, small_all[0])
+    ffn_copy.wait()
+
+    def last(j, unused):
+        at = pl.ds(pl.multiple_of(j * step, step), step)
+        here = pl.ds(pl.multiple_of(wa * half + j * step, step), step)
+        total = hidden_ref[at, :] + ffn_ref[here, :].astype(f32) + ffn_in[at, :].astype(f32)
+        out_ref[at, :] = total.astype(bf16)
+        return unused
+
+    lax.fori_loop(0, half // step, last, 0)
+
+    def spread(d, unused):
+        across(d).wait()
+        beside(d).start()
+        return unused
+
+    lax.fori_loop(0, lines, spread, 0)
+
+    def copy_out(d, unused):
+        beside(d).wait()
+        weights_ref[d] = all_w[d]
+        return unused
+
+    lax.fori_loop(0, lines, copy_out, 0)
+
+    def drain(d, unused):
+        @pl.when((z < d))
+        def _():
+            flow(1, d).wait_send()
+
+        @pl.when((z > d))
+        def _():
+            flow(-1, d).wait_send()
+
+        @pl.when((d <= z) & (z + 1 < lines))
+        def _():
+            pass_w(1, d).wait_send()
+            pass_s(1, d).wait_send()
+
+        @pl.when((d >= z) & (z > 0))
+        def _():
+            pass_w(-1, d).wait_send()
+            pass_s(-1, d).wait_send()
+
+        return unused
+
+    lax.fori_loop(0, lines, drain, 0)
+
+
+def finish(plan, cycle_size, *operands):
+    lines = cycle_size // 4
+    half, model = operands[8].shape
+    rows = 4 * plan.cols // cycle_size
+    dma = pltpu.SemaphoreType.DMA
+    return pl.pallas_call(
+        functools.partial(finish_kernel, plan, lines),
+        out_shape=[
+            jax.ShapeDtypeStruct((half, model), bf16),
+            jax.ShapeDtypeStruct((half, model), f32),
+            jax.ShapeDtypeStruct((8, half), f32),
+            jax.ShapeDtypeStruct((lines, 2, 2, rows, model), bf16),
+            jax.ShapeDtypeStruct((8, model), f32),
+        ],
+        in_specs=[vmem] * len(operands),
+        out_specs=[vmem] * 5,
+        scratch_shapes=[
+            pltpu.VMEM((lines, 2, 2, rows, model), bf16),
+            pltpu.VMEM((lines, 2, rows, model), bf16),
+            pltpu.VMEM((lines, rows, model), bf16),
+            pltpu.VMEM((lines, rows, model), bf16),
+            pltpu.VMEM((lines, rows, model), bf16),
+            pltpu.VMEM((lines, 2, 2, rows, model), bf16),
+            pltpu.VMEM((2, half // 2, model), bf16),
+            pltpu.VMEM((2, half // 2, model), bf16),
+            pltpu.VMEM((half, model), f32),
+            pltpu.VMEM((half, model), bf16),
+            pltpu.VMEM((8, half), f32),
+            pltpu.VMEM((8, model), f32),
+            pltpu.VMEM((8, model), f32),
+            pltpu.VMEM((8, model), f32),
+            pltpu.VMEM((3, 8, model), f32),
+            pltpu.VMEM((lines, 8, model), f32),
+            dma((2, 5)),
+            dma((2, 2)),
+            dma((2, lines + 1)),
+            dma((2, lines)),
+            dma((2, lines)),
+            dma((4, lines)),
+            dma((2, lines)),
+            dma((2, lines)),
+            dma((4, lines)),
+        ],
+        compiler_params=pltpu.CompilerParams(
+            vmem_limit_bytes=58 * 2**20, collective_id=2, has_side_effects=True
+        ),
+        name="finish",
+    )(*operands)
 
 
 def shards(
@@ -806,12 +1164,6 @@
     upward = jnp.dot(pair_ffn, w_up, preferred_element_type=f32)
     inner = gated(gate, upward).astype(bf16)
     ffn_part = jnp.dot(inner, w_down, preferred_element_type=f32)
-    layer_out = (
-        hidden
-        + lax.psum_scatter(
-            ffn_part.astype(bf16), "wa", scatter_dimension=0, tiled=True
-        ).astype(f32)
-    ).astype(bf16)
     grad_inner = jnp.dot(pair_cot, w_down.T, preferred_element_type=f32)
     down_half = jnp.dot(inner.T, pair_cot, preferred_element_type=f32).astype(bf16)
     unused_value, pullback = jax.vjp(gated, gate, upward)
@@ -833,7 +1185,6 @@
     hidden_step, gain_ffn_part = norm_backward(hidden, inv_ffn, gain_ffn, grad_normed_ffn)
     grad_hidden = cotangent.astype(f32) + hidden_step
     pair_branch = lax.all_gather(grad_hidden.astype(bf16), "wa", axis=0, tiled=True)
-    out_part = jnp.dot(attended.T, pair_branch, preferred_element_type=f32)[64:]
     do_wide = pl.pallas_call(
         functools.partial(grad_attended_kernel, plan),
         out_shape=jax.ShapeDtypeStruct((pair, WIDE), bf16),
@@ -865,14 +1216,15 @@
         name="attention_grad_queries",
     )(bounds, bias_table, kv_all, k_aug, q_back, do_wide, near_bias)
     own_aug = lax.dynamic_slice_in_dim(k_aug, base - origin, pair, 0)
-    grad_keys, grad_values = pl.pallas_call(
+    grad_keys, grad_values, mask_part = pl.pallas_call(
         functools.partial(dkv_kernel, plan, rows, pair),
         out_shape=(
-            jax.ShapeDtypeStruct((pair, WIDE), f32),
             jax.ShapeDtypeStruct((pair, WIDE), bf16),
+            jax.ShapeDtypeStruct((pair, WIDE), bf16),
+            jax.ShapeDtypeStruct((tiles, 8, TQ), f32),
         ),
         in_specs=[smem, smem, vmem, vmem, vmem, vmem, vmem],
-        out_specs=(vmem, vmem),
+        out_specs=(vmem, vmem, vmem),
         scratch_shapes=[
             pltpu.VMEM((padded, WIDE), bf16),
             pltpu.VMEM((padded, WIDE), bf16),
@@ -884,38 +1236,45 @@
         compiler_params=params(),
         name="attention_grad_keys",
     )(bounds, bias_table, q_all, do_all, own_kv, own_aug, near_bias)
-    grad_tab = jnp.sum(table_part, axis=2).T
-    mask_total = grad_keys[:, plan.mask_lane]
     cols = plan.cols
-    grad_qkv = jnp.concatenate(
-        [grad_queries[:, :cols], grad_keys[:, :cols].astype(bf16), grad_values[:, 64:]], axis=1
-    )
-    w_qkv = jnp.concatenate([w_query, w_key, w_value], axis=1)
-    qkv_part = jnp.dot(pair_normed.T, grad_qkv, preferred_element_type=f32)
-    grad_pair = jnp.dot(grad_qkv, w_qkv.T, preferred_element_type=f32)
-    grad_normed_attn, grad_mask = (
-        lax.psum_scatter(
-            grad_pair.astype(bf16), "wa", scatter_dimension=0, tiled=True
-        ).astype(f32),
-        lax.psum_scatter(
-            mask_total.astype(bf16), "wa", scatter_dimension=0, tiled=True
-        ).astype(f32),
-    )
-    token_step, gain_attn_part = norm_backward(tokens_wide, inv_attn, gain_attn, grad_normed_attn)
-    grad_tokens = grad_hidden + token_step
-    grad_gain_attn, grad_gain_ffn = lax.psum((gain_attn_part, gain_ffn_part), ("ctx", "wa"))
-    grad_w_qkv, grad_w_out, grad_table = lax.psum((qkv_part, out_part, grad_tab), "ctx")
+    gap = jnp.zeros((model, WIDE - cols), bf16)
+    w_wide = jnp.concatenate([w_query, gap, w_key, gap, gap, w_value], axis=1)
+    table_row = jnp.sum(table_part, axis=2).reshape(1, -1)
+    table_row = jnp.pad(table_row, ((0, 0), (0, model - table_row.shape[1])))
+    small = jnp.concatenate(
+        [jnp.zeros((1, model), f32), gain_ffn_part[None], table_row, jnp.zeros((5, model), f32)],
+        axis=0,
+    )
+    layer_out, grad_tokens, grad_mask, weights, totals = finish(
+        plan,
+        cycle_size,
+        grad_queries,
+        grad_keys,
+        grad_values,
+        mask_part.reshape(group, 8, own_rows),
+        w_wide,
+        pair_normed,
+        attended,
+        pair_branch,
+        tokens,
+        gain_attn[None],
+        hidden,
+        grad_hidden,
+        ffn_part.astype(bf16),
+        small,
+    )
+    weights = weights.reshape(4, cols, model).astype(f32)
     return (
         layer_out,
         grad_tokens,
-        grad_mask,
-        grad_gain_attn,
-        grad_w_qkv[:, :cols],
-        grad_w_qkv[:, cols : 2 * cols],
-        grad_w_qkv[:, 2 * cols :],
-        grad_w_out,
-        grad_table,
-        grad_gain_ffn,
+        grad_mask[0],
+        totals[0],
+        weights[0].T,
+        weights[1].T,
+        weights[2].T,
+        weights[3],
+        totals[2, : heads * 32].reshape(heads, 32).T,
+        totals[1],
         grad_w_gate,
         grad_w_up,
         grad_w_down,

time: 751 us -> 672 us (0.89)
  Pallas kernels: 199 us -> 282 us
  blocking collectives: 93.7 us -> 21.7 us
  waiting for transfers between devices: 269 us -> 198 us
  matrix products: 83.2 us -> 62.5 us
  local copies, waits for them, and re-layouts: 55.5 us -> 67.1 us
    pallas_call x0 -> x1, Pallas kernels: none -> 107 us  [finish(): pl.pallas_call(functools.partial(finish_kernel, plan, lines), out_shape=[...]
    psum x2 -> x0, blocking collectives: 67 us -> none  [the longest x1 37 us: shards(): lax.psum((gain_attn_part, gain_ffn_part), ('ctx', 'wa'))]
    all_gather x1, waiting for transfers between devices: 51.8 us -> 0.01 us  [shards(): do_all = window(gather(do_wide))]
    all_gather x1, waiting for transfers between devices: 30.3 us -> 0.01 us  [shards(): q_all = window(gather(q_back))]
    pallas_call x1, Pallas kernels: 145 us -> 127 us  [reduce_scatter(): pl.pallas_call(functools.partial(scatter_kernel, lines, units, z_first),...]
    concatenate x0 -> x4, local copies, waits for them, and re-layouts: none -> 13 us  [the longest x2 13 us: shards(): w_wide = jnp.concatenate([w_query, gap, w_key, gap, gap, w_value], axis=1)]
    all_gather x1, waiting for transfers between devices: 12.4 us -> 24.3 us  [shards(): lax.all_gather(cotangent, 'wa', axis=0, tiled=True)]
    dot_general x3 -> x0, matrix products: 9.75 us -> none  [the longest x1 4.16 us: shards(): grad_pair = jnp.dot(grad_qkv, w_qkv.T, preferred_element_type=f32)]
  transfers between devices with their start and end apart: 12 -> 9, of which waited for: 9 -> 7; matrix products, arithmetic and copies ran while one was open for 14% -> 14% of each run, Pallas kernels for 23% -> 23%
where the time goes in v3:
time: 672 us; the launch traced here: 663 us
  Pallas kernels  282 us (42%)
  waiting for transfers between devices  198 us (29%)
  local copies, waits for them, and re-layouts  67.1 us (10%)
  matrix products  62.5 us (9%)
  blocking collectives  21.7 us (3%)
  other arithmetic  17.4 us (3%)
  between operations  14.7 us (2%)
    pallas_call x1, Pallas kernels, reduce_scatter(): pl.pallas_call(functools.partial(scatter_kernel, lines, units, z_first),...  127 us
    pallas_call x1, Pallas kernels, finish(): pl.pallas_call(functools.partial(finish_kernel, plan, lines), out_shape=[...  107 us
    reduce_scatter x1, waiting for transfers between devices, shards(): lax.psum_scatter(jnp.dot(attended, w_out_pad, preferred_element_type=f32)...  43.3 us
    all_gather x1, waiting for transfers between devices, shards(): lax.all_gather(normed_low, 'wa', axis=0, tiled=True)  30 us
    all_gather x1, waiting for transfers between devices, shards(): kv_all = window(gather(own_kv))  26 us
    reduce_scatter x1, waiting for transfers between devices, shards(): lax.psum_scatter(grad_pair_ffn.astype(bf16), 'wa', scatter_dimension=0, t...  25.9 us
    all_gather x1, waiting for transfers between devices, shards(): lax.all_gather(grad_hidden.astype(bf16), 'wa', axis=0, tiled=True)  25.6 us
    all_gather x1, waiting for transfers between devices, shards(): lax.all_gather(cotangent, 'wa', axis=0, tiled=True)  24.3 us
  transfers between devices with their start and end apart: 9, of which 7 were waited for; matrix products, arithmetic and copies ran while one was open for 14% of the time, Pallas kernels for 23%

profile of v3, /device:TPU:0, one launch (start us, length us, event | category | flops | bytes accessed | tf_op | source)
XLA Modules:
  0.0 663.4 jit_solution(7285696767644784872)
XLA Ops:
  10.2 30.0 %all-gather.9.cloned.1.call-done.normed_ref = bf16[512,1472]{1,0:T(8,128)(2,1)} async-done(((bf16[256,1472]{1,0:T(8,128)(2,1)}), bf16[512,1472]{1,0:T(8,128)(2,1)}) %all-gather.9.cloned.1.call-update) | async-done | bytes 1507344 | tf_op jit(solution)/shard_map/all_gather | solution.py:1086
  40.2 3.1 convolution_convert_fusion.5.g_ref
  45.1 21.7 %all-gather = bf16[16,1,512]{2,1,0:T(2,128)(2,1)S(1)} all-gather(bf16[1,1,512]{2,1,0:T(2,128)(2,1)S(1)} %reshape.296), channel_id=1, replica_groups=mesh['ctx'=16,'wa'=2] {'ctx'}, dimensions={0}, use_global_device_ids=true | all-gather | bytes 17408 | tf_op jit(solution)/shard_map/all_gather | solution.py:1081
  67.1 5.0 near_bias.1.near_ref
  73.3 4.6 select_convert_fusion.kaug_ref
  79.5 26.0 %all-gather.11.cloned.1.call-done.g_ref = bf16[8192,384]{1,0:T(8,128)(2,1)} async-done(((bf16[512,384]{1,0:T(8,128)(2,1)}), bf16[8192,384]{1,0:T(8,128)(2,1)}) %all-gather.11.cloned.1.call-update) | async-done | bytes 6291472 | tf_op jit(solution)/shard_map/all_gather | solution.py:1099
  105.5 13.4 %attention_forward.1 = (bf16[512,256]{1,0:T(8,128)(2,1)}, f32[512,256]{1,0:T(8,128)}, bf16[512,256]{1,0:T(8,128)(2,1)}) custom-call(s32[5]{0:T(128)} %pad_add_fusion.1.bounds, f32[32,3]{1,0:T(8,128)} %copy.98.table_ref, bf16[8192,384]{1,0:T(8,128)(2,1)} %all-gather.11.cloned.1.call-done.g_ref, bf16[8192,128]{1,0:T(8,128)(2,1)} %select_convert_fusion.kaug_ref, ...), custom_call_target="tpu_custom_call" | custom-call | tf_op jit(solution)/shard_map/attention_forward/pallas_call | solution.py:1132
  122.7 43.3 %reduce-scatter.3.cloned.1.call-done = bf16[256,1472]{1,0:T(8,128)(2,1)} async-done(((bf16[512,1472]{1,0:T(8,128)(2,1)}), bf16[256,1472]{1,0:T(8,128)(2,1)}) %reduce-scatter.3.cloned.1.call-update) | async-done | bytes 753680 | tf_op jit(solution)/shard_map/reduce_scatter | solution.py:1153
  169.6 24.3 %all-gather.13.cloned.1.call-done = bf16[512,1472]{0,1:T(8,128)(2,1)} async-done(((bf16[256,1472]{0,1:T(8,128)(2,1)}), bf16[512,1472]{0,1:T(8,128)(2,1)}) %all-gather.13.cloned.1.call-update) | async-done | bytes 1507344 | tf_op jit(solution)/shard_map/all_gather | solution.py:1087
  193.9 7.9 %fusion.44 = f32[512,1792]{1,0:T(8,128)} fusion(bf16[512,1472]{0,1:T(8,128)(2,1)} %all-gather.13.cloned.1.call-done, bf16[1792,1472]{0,1:T(8,128)(2,1)} %param.26), kind=kOutput, calls=%fused_computation.111 | convolution fusion | flops 2701131776 | bytes 10452992 | tf_op jit(solution)/shard_map/dot_general | solution.py:1167
  201.8 21.4 %all-gather.15.cloned.1.call-done = bf16[512,1472]{1,0:T(8,128)(2,1)} async-done(((bf16[256,1472]{1,0:T(8,128)(2,1)}), bf16[512,1472]{1,0:T(8,128)(2,1)}) %all-gather.15.cloned.1.call-update) | async-done | bytes 1507344 | tf_op jit(solution)/shard_map/all_gather | solution.py:1162
  223.2 6.1 fusion.45
  229.4 9.0 %multiply_convert_fusion = (bf16[512,1792]{1,0:T(8,128)(2,1)}, bf16[512,1792]{1,0:T(8,128)(2,1)S(1)}, bf16[512,1792]{1,0:T(8,128)(2,1)S(1)}) fusion(f32[512,1792]{1,0:T(8,128)S(1)} %fusion.45, f32[512,1792]{1,0:T(8,128)S(1)} %copy-done.23, bf16[512,1472]{1,0:T(8,128)(2,1)S(1)} %copy-done.20, bf16[1472,1792]{1,0:T(8,128)(2,1)} %param.25), kind=kOutput, calls=%fused_computation.15 | convolution fusion | flops 2724986880 | bytes 19628032 | tf_op jit(solution)/shard_map/dot_general | solution.py:1164
  238.4 3.1 fusion.46
  241.6 4.0 convolution_add_fusion
  245.6 2.7 copy.97
  248.6 25.9 %reduce-scatter.5.cloned.1.call-done = bf16[256,1472]{1,0:T(8,128)(2,1)} async-done(((bf16[512,1472]{1,0:T(8,128)(2,1)}), bf16[256,1472]{1,0:T(8,128)(2,1)}) %reduce-scatter.5.cloned.1.call-update) | async-done | bytes 753680 | tf_op jit(solution)/shard_map/reduce_scatter | solution.py:1176
  280.1 25.6 %all-gather.17.cloned.1.call-done.branch_ref = bf16[512,1472]{1,0:T(8,128)(2,1)} async-done(((bf16[256,1472]{1,0:T(8,128)(2,1)}), bf16[512,1472]{1,0:T(8,128)(2,1)}) %all-gather.17.cloned.1.call-update) | async-done | bytes 1507344 | tf_op jit(solution)/shard_map/all_gather | solution.py:1187
  305.8 3.4 grad_attended.1.do_ref
  311.3 12.9 %concatenate.26.w3_ref = bf16[1472,768]{1,0:T(8,128)(2,1)} concatenate(bf16[1472,192]{1,0:T(8,128)(2,1)S(1)} %copy.100, bf16[1472,64]{1,0:T(8,128)(2,1)S(1)} %broadcast_in_dim.122, bf16[1472,192]{1,0:T(8,128)(2,1)S(1)} %copy.101, bf16[1472,128]{1,0:T(8,128)(2,1)S(1)} %concatenate.25, bf16[1472,192]{1,0:T(8,128)(2,1)S(1)} %copy.102), dimensions={1} | concatenate | bytes 4521984 | tf_op jit(solution)/shard_map/concatenate | solution.py:1241
  325.8 6.0 convolution_convert_fusion.4
  333.4 7.2 %convolution_convert_fusion = bf16[1792,1472]{0,1:T(8,128)(2,1)} fusion(bf16[512,1472]{0,1:T(8,128)(2,1)} %all-gather.13.cloned.1.call-done, bf16[512,1792]{1,0:T(8,128)(2,1)} %get-tuple-element.105), kind=kOutput, calls=%fused_computation | convolution fusion | flops 2703769600 | bytes 8617984 | tf_op jit(solution)/shard_map/dot_general | solution.py:1168
  340.6 8.4 %copy.105 = bf16[1792,1472]{1,0:T(8,128)(2,1)} copy(bf16[1792,1472]{0,1:T(8,128)(2,1)} %convolution_convert_fusion) | data formatting | bytes 10551296 | tf_op jit(solution)/shard_map/convert_element_type | solution.py:1168
  349.0 6.9 %convolution_convert_fusion.2 = bf16[1792,1472]{0,1:T(8,128)(2,1)} fusion(bf16[512,1792]{1,0:T(8,128)(2,1)} %copy-done.25, bf16[512,1472]{1,0:T(8,128)(2,1)S(1)} %copy-done.21), kind=kOutput, calls=%fused_computation.2 | convolution fusion | flops 2703769600 | bytes 8617984 | tf_op jit(solution)/shard_map/dot_general | solution.py:1179
  355.9 8.2 %copy.106 = bf16[1792,1472]{1,0:T(8,128)(2,1)} copy(bf16[1792,1472]{0,1:T(8,128)(2,1)} %convolution_convert_fusion.2) | data formatting | bytes 10551296 | tf_op jit(solution)/shard_map/convert_element_type | solution.py:1179
  364.1 6.8 %convolution_convert_fusion.1 = bf16[1792,1472]{0,1:T(8,128)(2,1)} fusion(bf16[512,1792]{1,0:T(8,128)(2,1)} %copy-done.24, bf16[512,1472]{1,0:T(8,128)(2,1)S(1)} %copy-done.21), kind=kOutput, calls=%fused_computation.1 | convolution fusion | flops 2703769600 | bytes 8617984 | tf_op jit(solution)/shard_map/dot_general | solution.py:1180
  371.0 8.4 %copy.107 = bf16[1792,1472]{1,0:T(8,128)(2,1)} copy(bf16[1792,1472]{0,1:T(8,128)(2,1)} %convolution_convert_fusion.1) | data formatting | bytes 10551296 | tf_op jit(solution)/shard_map/convert_element_type | solution.py:1180
  379.4 126.6 %weight_scatter.1 = (f32[112,1472]{1,0:T(8,128)}, f32[112,1472]{1,0:T(8,128)}, f32[112,1472]{1,0:T(8,128)}) custom-call(bf16[4,2,2,112,1472]{4,3,2,1,0:T(8,128)(2,1)} %bitcast.61, bf16[4,2,2,112,1472]{4,3,2,1,0:T(8,128)(2,1)} %bitcast.62, bf16[4,2,2,112,1472]{4,3,2,1,0:T(8,128)(2,1)} %bitcast.63), custom_call_target="tpu_custom_call" | custom-call | tf_op jit(solution)/shard_map/weight_scatter/pallas_call | solution.py:653
  506.0 14.2 %attention_grad_queries.1 = (bf16[512,256]{1,0:T(8,128)(2,1)}, f32[3,32,128]{2,1,0:T(8,128)}) custom-call(s32[5]{0:T(128)} %pad_add_fusion.1.bounds, f32[32,3]{1,0:T(8,128)} %copy.98.table_ref, bf16[8192,384]{1,0:T(8,128)(2,1)} %all-gather.11.cloned.1.call-done.g_ref, bf16[8192,128]{1,0:T(8,128)(2,1)} %select_convert_fusion.kaug_ref, ...), custom_call_target="tpu_custom_call" | custom-call | tf_op jit(solution)/shard_map/attention_grad_queries/pallas_call | solution.py:1198
  521.9 11.6 %attention_grad_keys.1 = (bf16[512,256]{1,0:T(8,128)(2,1)}, bf16[512,256]{1,0:T(8,128)(2,1)}, f32[2,8,256]{2,1,0:T(8,128)}) custom-call(s32[5]{0:T(128)} %pad_add_fusion.1.bounds, f32[32,3]{1,0:T(8,128)} %copy.98.table_ref, bf16[8192,256]{1,0:T(8,128)(2,1)} %all-gather.19.cloned.1.call-done.qall_ref, ...), custom_call_target="tpu_custom_call" | custom-call | tf_op jit(solution)/shard_map/attention_grad_keys/pallas_call | solution.py:1219
  533.5 107.4 %finish.1 = (bf16[256,1472]{1,0:T(8,128)(2,1)}, f32[256,1472]{1,0:T(8,128)}, f32[8,256]{1,0:T(8,128)}, bf16[4,2,2,48,1472]{4,3,2,1,0:T(8,128)(2,1)}, f32[8,1472]{1,0:T(8,128)}) custom-call(bf16[512,256]{1,0:T(8,128)(2,1)} %get-tuple-element.32.dq_ref, bf16[512,256]{1,0:T(8,128)(2,1)} %get-tuple-element.33.dk_ref, bf16[512,256]{1,0:T(8,128)(2,1)} %get-tuple-element.34.dv_ref, ...), custom_call_target="tpu_custom_call" | custom-call | tf_op jit(solution)/shard_map/finish/pallas_call | solution.py:989
  645.4 3.1 copy.109
  (154 shorter events, 40.3 us)
Async XLA Ops:
  7.2 33.0 %all-gather.9.cloned.1.call-start = ((), (), s32[]{:S(2)}) async-start(), calls=%async_computation.2 | async-start | bytes 2359296 | tf_op jit(solution)/shard_map/all_gather | solution.py:1086
  8.6 267.7 %copy-start = (bf16[256,1472]{1,0:T(8,128)(2,1)}, bf16[256,1472]{1,0:T(8,128)(2,1)S(1)}, u32[]{:S(2)}) copy-start(bf16[256,1472]{1,0:T(8,128)(2,1)S(1)} %copy.91.tokens_ref) | copy-start | bytes 2260996
  8.6 31.5 %copy-start.12 = (bf16[1472,192]{0,1:T(8,128)(2,1)S(1)}, bf16[1472,192]{0,1:T(8,128)(2,1)}, u32[]{:S(2)}) copy-start(bf16[1472,192]{0,1:T(8,128)(2,1)} %param.19) | copy-start | bytes 1695748
  8.7 31.5 %copy-start.14 = (bf16[1472,192]{0,1:T(8,128)(2,1)S(1)}, bf16[1472,192]{0,1:T(8,128)(2,1)}, u32[]{:S(2)}) copy-start(bf16[1472,192]{0,1:T(8,128)(2,1)} %param.20) | copy-start | bytes 1695748
  10.1 33.3 %copy-start.22 = (s32[8]{0:T(128)S(1)}, s32[8]{0:T(128)}, u32[]{:S(2)}) copy-start(s32[8]{0:T(128)} %param.15) | copy-start | bytes 100
  10.1 34.3 %copy-start.18 = (f32[32,3]{0,1:T(4,128)S(1)}, f32[32,3]{0,1:T(4,128)}, u32[]{:S(2)}) copy-start(f32[32,3]{0,1:T(4,128)} %param.22) | copy-start | bytes 1156
  10.1 35.0 %copy-start.19 = (bf16[512]{0:T(512)(128)(2,1)S(1)}, bf16[512]{0:T(512)(128)(2,1)}, u32[]{:S(2)}) copy-start(bf16[512]{0:T(512)(128)(2,1)} %param.16) | copy-start | bytes 3076
  10.1 95.3 %all-gather.11.cloned.1.call-start = ((), (), s32[]{:S(2)}) async-start(), calls=%async_computation.3 | async-start | bytes 6684672 | tf_op jit(solution)/shard_map/all_gather | solution.py:1099
  43.3 122.6 %reduce-scatter.3.cloned.1.call-start = ((), (), s32[]{:S(2)}) async-start(), calls=%async_computation.4 | async-start | bytes 2359296 | tf_op jit(solution)/shard_map/reduce_scatter | solution.py:1153
  72.1 5.7 copy-start.7
  72.1 5.7 copy-start.10
  79.5 39.4 %copy-start.5 = (bf16[192,1472]{1,0:T(8,128)(2,1)S(1)}, bf16[192,1472]{1,0:T(8,128)(2,1)}, u32[]{:S(2)}) copy-start(bf16[192,1472]{1,0:T(8,128)(2,1)} %param.21) | copy-start | bytes 1695748
  122.0 45.5 %copy-start.16 = (f32[1472]{0:T(1024)S(1)}, f32[1472]{0:T(1024)}, u32[]{:S(2)}) copy-start(f32[1472]{0:T(1024)} %param.23) | copy-start | bytes 17668
  122.1 71.8 %all-gather.13.cloned.1.call-start = ((), (), s32[]{:S(2)}) async-start(), calls=%async_computation.5 | async-start | bytes 2260992 | tf_op jit(solution)/shard_map/all_gather | solution.py:1087
  122.6 100.5 %all-gather.15.cloned.1.call-start = ((), (), s32[]{:S(2)}) async-start(), calls=%async_computation.6 | async-start | bytes 2359296 | tf_op jit(solution)/shard_map/all_gather | solution.py:1162
  169.2 105.3 %reduce-scatter.5.cloned.1.call-start = ((), (), s32[]{:S(2)}) async-start(), calls=%async_computation.7 | async-start | bytes 2359296 | tf_op jit(solution)/shard_map/reduce_scatter | solution.py:1176
  223.2 6.1 copy-start.20
  223.2 6.1 copy-start.23
  223.2 15.2 %slice-start = ((s8[5275648]{0:T(1024)(128)(4,1)}), s8[4194304]{0:T(1024)(128)(4,1)S(1)}, s32[]{:S(2)}) async-start(s8[5275648]{0:T(1024)(128)(4,1)} %bitcast.73), calls=%async_computation.11 | async-start | bytes 8388608
  223.2 18.3 %slice-start.2 = ((s8[5275648]{0:T(1024)(128)(4,1)}), s8[4194304]{0:T(1024)(128)(4,1)S(1)}, s32[]{:S(2)}) async-start(s8[5275648]{0:T(1024)(128)(4,1)} %bitcast.75), calls=%async_computation.13 | async-start | bytes 8388608
  229.3 9.0 %slice-start.1 = ((s8[5275648]{0:T(1024)(128)(4,1)}), s8[1081344]{0:T(1024)(128)(4,1)S(1)}, s32[]{:S(2)}) async-start(s8[5275648]{0:T(1024)(128)(4,1)} %bitcast.73), calls=%async_computation.12 | async-start | bytes 2162688
  229.4 12.2 %slice-start.3 = ((s8[5275648]{0:T(1024)(128)(4,1)}), s8[1081344]{0:T(1024)(128)(4,1)S(1)}, s32[]{:S(2)}) async-start(s8[5275648]{0:T(1024)(128)(4,1)} %bitcast.75), calls=%async_computation.14 | async-start | bytes 2162688
  238.4 3.1 copy-start.25
  238.4 3.1 copy-start.24
  248.3 57.5 %all-gather.17.cloned.1.call-start = ((), (), s32[]{:S(2)}) async-start(), calls=%async_computation.8 | async-start | bytes 2359296 | tf_op jit(solution)/shard_map/all_gather | solution.py:1187
  278.4 243.6 %all-gather.19.cloned.1.call-start = ((), (), s32[]{:S(2)}) async-start(), calls=%async_computation.9 | async-start | bytes 4456448 | tf_op jit(solution)/shard_map/all_gather | solution.py:1151
  279.1 242.8 %all-gather.21.cloned.1.call-start = ((), (), s32[]{:S(2)}) async-start(), calls=%async_computation.10 | async-start | bytes 4456448 | tf_op jit(solution)/shard_map/all_gather | solution.py:1196
  280.1 29.1 %copy-start.11 = (bf16[1472,192]{0,1:T(8,128)(2,1)S(1)}, bf16[1472,192]{0,1:T(8,128)(2,1)}, u32[]{:S(2)}) copy-start(bf16[1472,192]{0,1:T(8,128)(2,1)} %param.18) | copy-start | bytes 1695748
  305.8 3.7 copy-start.13
  340.6 8.4 %copy-start.21 = (bf16[512,1472]{1,0:T(8,128)(2,1)S(1)}, bf16[512,1472]{1,0:T(8,128)(2,1)}, u32[]{:S(2)}) copy-start(bf16[512,1472]{1,0:T(8,128)(2,1)} %all-gather.15.cloned.1.call-done) | copy-start | bytes 4521988
  645.4 4.4 copy-start.2
  652.2 3.5 copy-start.8
  (7 other events, 14.4 us)
Sparse Core Ops, SparseCore 0:
  10.2 29.8 all-gather.8
  43.4 61.9 all-gather.10
  122.2 43.7 reduce-scatter.2
  167.4 26.4 all-gather.12
  195.9 27.2 all-gather.14
  248.4 26.0 reduce-scatter.4
  278.5 27.2 all-gather.16
  308.5 50.5 all-gather.18
  361.8 61.9 all-gather.20

commit v4 on v3

--- a/solution.py
+++ b/solution.py
@@ -1031,6 +1031,264 @@
     )(*operands)
 
 
+root = 0.7978845608028654
+cubic = 0.044715
+
+
+def middle_kernel(
+    plan, cycle_size, att_ref, mixed_ref, wout_ref, tokens_ref, cot_ref, gain_ref,
+    wg_hbm, wu_hbm, wd_hbm,
+    hidden_ref, gh_ref, branch_ref, ffn_ref, do_ref, gain_part_ref, stack_hbm,
+    wg, wu, wd, inner, gg, gu, x_ref, a_out, a_in, d_out, d_in, acc_f, acc_g, own_g, rows_buf,
+    load_sem, y_sem, out_sem,
+):
+    spot = Spot(cycle_size // 4)
+    wa = spot.wa
+    half, model = tokens_ref.shape
+    units = wd.shape[0]
+    chunk = half // 4
+    loads = [
+        pltpu.make_async_copy(src, dst, load_sem.at[i])
+        for i, (src, dst) in enumerate(((wg_hbm, wg), (wu_hbm, wu), (wd_hbm, wd)))
+    ]
+    for load in loads:
+        load.start()
+    barrier = pltpu.get_barrier_semaphore()
+    pl.semaphore_signal(
+        barrier, inc=1, device_id=spot.y_mate(), device_id_type=pl.DeviceIdType.MESH
+    )
+    pl.semaphore_wait(barrier, 1)
+    ours = wa * half
+    theirs = (1 - wa) * half
+
+    def rows_at(start, size):
+        return pl.ds(pl.multiple_of(start, size), size)
+
+    def a_copy(i):
+        return send(a_out.at[i], a_in.at[i], y_sem.at[0, i], y_sem.at[1, i], spot.y_mate())
+
+    def d_copy(i):
+        return send(
+            d_out.at[i], d_in.at[i], y_sem.at[0, 4 + i], y_sem.at[1, 4 + i], spot.y_mate()
+        )
+
+    def b_copy(i, base):
+        at = rows_at(base + i * chunk, chunk)
+        return send(
+            x_ref.at[at], x_ref.at[at], y_sem.at[0, 8 + i], y_sem.at[1, 8 + i], spot.y_mate()
+        )
+
+    def e_copy(i, base):
+        at = rows_at(base + i * chunk, chunk)
+        return send(
+            branch_ref.at[at], branch_ref.at[at], y_sem.at[0, 12 + i], y_sem.at[1, 12 + i],
+            spot.y_mate(),
+        )
+
+    def send_branch(i, unused):
+        a_out[i] = nn(att_ref[rows_at(theirs + i * chunk, chunk), :], wout_ref[...]).astype(bf16)
+        a_copy(i).start()
+        return unused
+
+    lax.fori_loop(0, 4, send_branch, 0)
+
+    def own_branch(i, unused):
+        at = rows_at(i * chunk, chunk)
+        hidden_ref[at, :] = tokens_ref[at, :].astype(f32) + nn(
+            att_ref[rows_at(ours + i * chunk, chunk), :], wout_ref[...]
+        )
+        return unused
+
+    lax.fori_loop(0, 4, own_branch, 0)
+
+    def normal(i, unused):
+        a_copy(i).wait()
+        at = rows_at(i * chunk, chunk)
+        hidden = hidden_ref[at, :] + a_in[i].astype(f32)
+        hidden_ref[at, :] = hidden
+        inv = lax.rsqrt(jnp.mean(hidden * hidden, axis=-1, keepdims=True) + eps)
+        x_ref[rows_at(ours + i * chunk, chunk), :] = (hidden * inv * gain_ref[...]).astype(bf16)
+        b_copy(i, ours).start()
+        return unused
+
+    lax.fori_loop(0, 4, normal, 0)
+    for load in loads:
+        load.wait()
+    wide = 256
+
+    def feed(base):
+        rows = rows_at(base, half)
+        acc_f[...] = jnp.zeros_like(acc_f)
+        acc_g[...] = jnp.zeros_like(acc_g)
+
+        def tile(u, unused):
+            cols = rows_at(u * wide, wide)
+            gate = nn(x_ref[rows, :], wg[:, cols])
+            upward = nn(x_ref[rows, :], wu[:, cols])
+            grad_inner = nt(cot_ref[rows, :], wd[cols, :])
+            square = gate * gate
+            bend = jnp.tanh(root * gate * (1.0 + cubic * square))
+            side = 0.5 * (1.0 + bend)
+            gelu = gate * side
+            slope = side + 0.5 * gate * (1.0 - bend * bend) * (
+                root * (1.0 + 3.0 * cubic * square)
+            )
+            inner_low = (gelu * upward).astype(bf16)
+            gate_low = (grad_inner * upward * slope).astype(bf16)
+            up_low = (grad_inner * gelu).astype(bf16)
+            inner[rows, cols] = inner_low
+            gg[rows, cols] = gate_low
+            gu[rows, cols] = up_low
+            acc_g[...] += nt(gate_low, wg[:, cols]) + nt(up_low, wu[:, cols])
+            acc_f[...] += nn(inner_low, wd[cols, :])
+            return unused
+
+        lax.fori_loop(0, units // wide, tile, 0)
+        ffn_ref[rows, :] = acc_f[...].astype(bf16)
+
+    feed(ours)
+    own_g[...] = acc_g[...]
+
+    def b_wait(i, unused):
+        b_copy(i, theirs).wait_recv()
+        return unused
+
+    lax.fori_loop(0, 4, b_wait, 0)
+    feed(theirs)
+
+    def send_grad(i, unused):
+        d_out[i] = acc_g[rows_at(i * chunk, chunk), :].astype(bf16)
+        d_copy(i).start()
+        return unused
+
+    lax.fori_loop(0, 4, send_grad, 0)
+    parts = 2
+    span = units // parts
+    slices = cycle_size // parts
+    size = units // cycle_size
+
+    def out_copy(n):
+        m, p = (n // parts, n % parts)
+        return pltpu.make_async_copy(
+            rows_buf.at[n % 2],
+            stack_hbm.at[pl.ds(p * slices, slices), m],
+            out_sem.at[n],
+        )
+
+    for n in range(3 * parts):
+        m, p = (n // parts, n % parts)
+        left = (inner, gg, gu)[m]
+        right = (cot_ref, x_ref, x_ref)[m]
+        if n >= 2:
+            out_copy(n - 2).wait()
+        turned = jnp.transpose(left[:, p * span : (p + 1) * span])
+        for c in range(0, model, wide):
+            end = min(model, c + wide)
+            product = nn(turned, right[:, c:end]).astype(bf16)
+            for s in range(slices):
+                rows_buf[n % 2, s, :, c:end] = product[s * size : (s + 1) * size]
+        out_copy(n).start()
+
+    def normal_back(i, total):
+        d_copy(i).wait()
+        at = rows_at(i * chunk, chunk)
+        grad = own_g[at, :] + d_in[i].astype(f32)
+        hidden = hidden_ref[at, :]
+        inv = lax.rsqrt(jnp.mean(hidden * hidden, axis=-1, keepdims=True) + eps)
+        scaled = gain_ref[...] * grad
+        mean = jnp.mean(hidden * scaled, axis=-1, keepdims=True)
+        pair_at = rows_at(ours + i * chunk, chunk)
+        grad_hidden = (
+            cot_ref[pair_at, :].astype(f32) + inv * scaled - hidden * (inv * inv * inv * mean)
+        )
+        gh_ref[at, :] = grad_hidden
+        branch_ref[pair_at, :] = grad_hidden.astype(bf16)
+        e_copy(i, ours).start()
+        return total + jnp.sum(grad * hidden * inv, axis=0, keepdims=True)
+
+    gain_part_ref[...] = lax.fori_loop(0, 4, normal_back, jnp.zeros((1, model), f32))
+
+    def attended_grads(base):
+        rows = rows_at(base, half)
+        lane = lanes_of(half)
+        grad = nt(branch_ref[rows, :], wout_ref[...]).astype(bf16)
+        terms = grad.astype(f32) * mixed_ref[rows, :]
+        out = grad
+        for h in range(plan.heads):
+            row_term = jnp.sum(
+                jnp.where(lane // 64 == h + 1, terms, 0.0), axis=1, keepdims=True
+            )
+            for i, part in enumerate(split3(-row_term)):
+                out = jnp.where(lane == 3 * h + i, part, out)
+        do_ref[rows, :] = out
+
+    attended_grads(ours)
+
+    def e_wait(i, unused):
+        e_copy(i, theirs).wait_recv()
+        return unused
+
+    lax.fori_loop(0, 4, e_wait, 0)
+    attended_grads(theirs)
+    for n in (3 * parts - 2, 3 * parts - 1):
+        out_copy(n).wait()
+
+    def drain(i, unused):
+        b_copy(i, ours).wait_send()
+        e_copy(i, ours).wait_send()
+        return unused
+
+    lax.fori_loop(0, 4, drain, 0)
+
+
+def middle(plan, cycle_size, attended, mixed, w_out, tokens, cot, gain, w_gate, w_up, w_down):
+    half, model = tokens.shape
+    pair = attended.shape[0]
+    units = w_down.shape[0]
+    size = units // cycle_size
+    chunk = half // 4
+    hbm = pl.BlockSpec(memory_space=pl.ANY)
+    dma = pltpu.SemaphoreType.DMA
+    return pl.pallas_call(
+        functools.partial(middle_kernel, plan, cycle_size),
+        out_shape=[
+            jax.ShapeDtypeStruct((half, model), f32),
+            jax.ShapeDtypeStruct((half, model), f32),
+            jax.ShapeDtypeStruct((pair, model), bf16),
+            jax.ShapeDtypeStruct((pair, model), bf16),
+            jax.ShapeDtypeStruct((pair, WIDE), bf16),
+            jax.ShapeDtypeStruct((1, model), f32),
+            jax.ShapeDtypeStruct((cycle_size, 3, size, model), bf16),
+        ],
+        in_specs=[vmem] * 6 + [hbm] * 3,
+        out_specs=[vmem] * 6 + [hbm],
+        scratch_shapes=[
+            pltpu.VMEM((model, units), bf16),
+            pltpu.VMEM((model, units), bf16),
+            pltpu.VMEM((units, model), bf16),
+            pltpu.VMEM((pair, units), bf16),
+            pltpu.VMEM((pair, units), bf16),
+            pltpu.VMEM((pair, units), bf16),
+            pltpu.VMEM((pair, model), bf16),
+            pltpu.VMEM((4, chunk, model), bf16),
+            pltpu.VMEM((4, chunk, model), bf16),
+            pltpu.VMEM((4, chunk, model), bf16),
+            pltpu.VMEM((4, chunk, model), bf16),
+            pltpu.VMEM((half, model), f32),
+            pltpu.VMEM((half, model), f32),
+            pltpu.VMEM((half, model), f32),
+            pltpu.VMEM((2, cycle_size // 2, size, model), bf16),
+            dma((3,)),
+            dma((2, 16)),
+            dma((6,)),
+        ],
+        compiler_params=pltpu.CompilerParams(
+            vmem_limit_bytes=60 * 2**20, collective_id=3, has_side_effects=True
+        ),
+        name="feed_forward",
+    )(attended, mixed, w_out, tokens, cot, gain, w_gate, w_up, w_down)
+
+
 def shards(
     tokens,
     doc_lengths,
@@ -1150,49 +1408,25 @@
     )(bounds, bias_table, kv_all, k_aug, q_wide, near_bias)
     q_all = window(gather(q_back))
     w_out_pad = jnp.concatenate([jnp.zeros((64, model), bf16), w_out], axis=0)
-    branch = lax.psum_scatter(
-        jnp.dot(attended, w_out_pad, preferred_element_type=f32).astype(bf16),
-        "wa",
-        scatter_dimension=0,
-        tiled=True,
+    hidden, grad_hidden, pair_branch, ffn_part, do_wide, gain_ffn_part, stacked = middle(
+        plan,
+        cycle_size,
+        attended,
+        mixed,
+        w_out_pad,
+        tokens,
+        pair_cot,
+        gain_ffn[None],
+        w_gate,
+        w_up,
+        w_down,
+    )
+    units = stacked.shape[2]
+    stacked = lax.psum_scatter(
+        stacked.reshape(-1, model), "ctx", scatter_dimension=0, tiled=True
     ).astype(f32)
-    hidden = tokens_wide + branch
-    normed_ffn, inv_ffn = norm_forward(hidden, gain_ffn)
-    ffn_low = normed_ffn.astype(bf16)
-    pair_ffn = lax.all_gather(ffn_low, "wa", axis=0, tiled=True)
-    gate = jnp.dot(pair_ffn, w_gate, preferred_element_type=f32)
-    upward = jnp.dot(pair_ffn, w_up, preferred_element_type=f32)
-    inner = gated(gate, upward).astype(bf16)
-    ffn_part = jnp.dot(inner, w_down, preferred_element_type=f32)
-    grad_inner = jnp.dot(pair_cot, w_down.T, preferred_element_type=f32)
-    down_half = jnp.dot(inner.T, pair_cot, preferred_element_type=f32).astype(bf16)
-    unused_value, pullback = jax.vjp(gated, gate, upward)
-    grad_gate, grad_upward = pullback(grad_inner)
-    grad_gate = grad_gate.astype(bf16)
-    grad_upward = grad_upward.astype(bf16)
-    grad_pair_ffn = jnp.dot(grad_gate, w_gate.T, preferred_element_type=f32) + jnp.dot(
-        grad_upward, w_up.T, preferred_element_type=f32
-    )
-    grad_normed_ffn = lax.psum_scatter(
-        grad_pair_ffn.astype(bf16), "wa", scatter_dimension=0, tiled=True
-    ).astype(f32)
-    gate_half = jnp.dot(grad_gate.T, pair_ffn, preferred_element_type=f32).astype(bf16)
-    up_half = jnp.dot(grad_upward.T, pair_ffn, preferred_element_type=f32).astype(bf16)
-    grad_w_down, grad_w_gate, grad_w_up = reduce_scatter(
-        [down_half, gate_half, up_half], cycle_size
-    )
-    grad_w_gate, grad_w_up = (grad_w_gate.T, grad_w_up.T)
-    hidden_step, gain_ffn_part = norm_backward(hidden, inv_ffn, gain_ffn, grad_normed_ffn)
-    grad_hidden = cotangent.astype(f32) + hidden_step
-    pair_branch = lax.all_gather(grad_hidden.astype(bf16), "wa", axis=0, tiled=True)
-    do_wide = pl.pallas_call(
-        functools.partial(grad_attended_kernel, plan),
-        out_shape=jax.ShapeDtypeStruct((pair, WIDE), bf16),
-        in_specs=[vmem, vmem, vmem],
-        out_specs=vmem,
-        compiler_params=params(),
-        name="grad_attended",
-    )(pair_branch, w_out_pad, mixed)
+    grad_w_down = stacked[:units]
+    grad_w_gate, grad_w_up = (stacked[units : 2 * units].T, stacked[2 * units :].T)
     do_all = window(gather(do_wide))
 
     grad_queries, table_part = pl.pallas_call(
@@ -1242,7 +1476,7 @@
     table_row = jnp.sum(table_part, axis=2).reshape(1, -1)
     table_row = jnp.pad(table_row, ((0, 0), (0, model - table_row.shape[1])))
     small = jnp.concatenate(
-        [jnp.zeros((1, model), f32), gain_ffn_part[None], table_row, jnp.zeros((5, model), f32)],
+        [jnp.zeros((1, model), f32), gain_ffn_part, table_row, jnp.zeros((5, model), f32)],
         axis=0,
     )
     layer_out, grad_tokens, grad_mask, weights, totals = finish(
@@ -1260,7 +1494,7 @@
         gain_attn[None],
         hidden,
         grad_hidden,
-        ffn_part.astype(bf16),
+        ffn_part,
         small,
     )
     weights = weights.reshape(4, cols, model).astype(f32)

time: 672 us -> 504 us (0.75)
  matrix products: 62.5 us -> 3.81 us
  waiting for transfers between devices: 198 us -> 141 us
  local copies, waits for them, and re-layouts: 67.1 us -> 35.9 us
  Pallas kernels: 282 us -> 268 us
    dot_general x10 -> x0, matrix products: 58.6 us -> none  [the longest x1 9 us: shards(): upward = jnp.dot(pair_ffn, w_up, preferred_element_type=f32)]
    all_gather x2 -> x0, waiting for transfers between devices: 47 us -> none  [the longest x1 25.6 us: shards(): lax.all_gather(grad_hidden.astype(bf16), 'wa', axis=0, tiled=True)]
    all_gather x1, waiting for transfers between devices: 0.01 us -> 40.5 us  [shards(): do_all = window(gather(do_wide))]
    pallas_call x2 -> x1, Pallas kernels: 130 us -> 90.3 us  [middle(): pl.pallas_call(functools.partial(middle_kernel, plan, cycle_size), out_sh...]
    pallas_call x1, Pallas kernels: 107 us -> 140 us  [finish(): pl.pallas_call(functools.partial(finish_kernel, plan, lines), out_shape=[...]
    reduce_scatter x2 -> x1, waiting for transfers between devices: 69.2 us -> 38.8 us  [shards(): lax.psum_scatter(stacked.reshape(-1, model), 'ctx', scatter_dimension=0,...]
    convert_element_type x5 -> x0, local copies, waits for them, and re-layouts: 28.2 us -> none  [the longest x1 8.43 us: shards(): jnp.dot(grad_upward.T, pair_ffn, preferred_element_type=f32).astype(bf16)]
    all_gather x1, waiting for transfers between devices: 24.3 us -> 6.99 us  [shards(): lax.all_gather(cotangent, 'wa', axis=0, tiled=True)]
  transfers between devices with their start and end apart: 9 -> 6, of which waited for: 7 -> 5; matrix products, arithmetic and copies ran while one was open for 14% -> 8% of each run, Pallas kernels for 23% -> 54%
where the time goes in v4:
time: 504 us; the launch traced here: 497 us
  Pallas kernels  268 us (53%)
  waiting for transfers between devices  141 us (28%)
  local copies, waits for them, and re-layouts  35.9 us (7%)
  blocking collectives  21.5 us (4%)
  between operations  14.9 us (3%)
  other arithmetic  11.8 us (2%)
    pallas_call x1, Pallas kernels, finish(): pl.pallas_call(functools.partial(finish_kernel, plan, lines), out_shape=[...  140 us
    pallas_call x1, Pallas kernels, middle(): pl.pallas_call(functools.partial(middle_kernel, plan, cycle_size), out_sh...  90.3 us
    all_gather x1, waiting for transfers between devices, shards(): do_all = window(gather(do_wide))  40.5 us
    reduce_scatter x1, waiting for transfers between devices, shards(): lax.psum_scatter(stacked.reshape(-1, model), 'ctx', scatter_dimension=0,...  38.8 us
    all_gather x1, waiting for transfers between devices, shards(): lax.all_gather(normed_low, 'wa', axis=0, tiled=True)  30 us
    all_gather x1, waiting for transfers between devices, shards(): kv_all = window(gather(own_kv))  24.5 us
    all_gather x1, blocking collectives, shards(): mask_all = lax.all_gather(key_mask, 'ctx', axis=0, tiled=True)  21.5 us
    unnamed x40, local copies, waits for them, and re-layouts  18.4 us
  transfers between devices with their start and end apart: 6, of which 5 were waited for; matrix products, arithmetic and copies ran while one was open for 8% of the time, Pallas kernels for 54%

profile of v4, /device:TPU:0, one launch (start us, length us, event | category | flops | bytes accessed | tf_op | source)
XLA Modules:
  0.0 497.3 jit_solution(596402998421579577)
XLA Ops:
  7.2 1.4 copy.76.tokens_ref
  8.9 1.1 fusion.3
  10.2 30.0 %all-gather.7.cloned.1.call-done.normed_ref = bf16[512,1472]{1,0:T(8,128)(2,1)} async-done(((bf16[256,1472]{1,0:T(8,128)(2,1)}), bf16[512,1472]{1,0:T(8,128)(2,1)}) %all-gather.7.cloned.1.call-update) | async-done | bytes 1507344 | tf_op jit(solution)/shard_map/all_gather | solution.py:1344
  40.2 3.2 convolution_convert_fusion.g_ref
  43.4 1.2 copy.80
  46.6 21.5 %all-gather = bf16[16,1,512]{2,1,0:T(2,128)(2,1)S(1)} all-gather(bf16[1,1,512]{2,1,0:T(2,128)(2,1)S(1)} %reshape.269), channel_id=1, replica_groups=mesh['ctx'=16,'wa'=2] {'ctx'}, dimensions={0}, use_global_device_ids=true | all-gather | bytes 17408 | tf_op jit(solution)/shard_map/all_gather | solution.py:1339
  68.5 5.2 %near_bias.1.near_ref = f32[2,3,256,512]{3,2,1,0:T(8,128)} custom-call(f32[32,3]{1,0:T(8,128)} %copy.83.table_ref), custom_call_target="tpu_custom_call" | custom-call | tf_op jit(solution)/shard_map/near_bias/pallas_call | solution.py:1380
  74.6 4.6 select_convert_fusion.kaug_ref
  80.0 0.8 pad_maximum_fusion.q_ref
  80.8 24.5 %all-gather.9.cloned.1.call-done.g_ref = bf16[8192,384]{1,0:T(8,128)(2,1)} async-done(((bf16[512,384]{1,0:T(8,128)(2,1)}), bf16[8192,384]{1,0:T(8,128)(2,1)}) %all-gather.9.cloned.1.call-update) | async-done | bytes 6291472 | tf_op jit(solution)/shard_map/all_gather | solution.py:1357
  105.4 10.9 %attention_forward.1 = (bf16[512,256]{1,0:T(8,128)(2,1)}, f32[512,256]{1,0:T(8,128)}, bf16[512,256]{1,0:T(8,128)(2,1)}) custom-call(s32[5]{0:T(128)} %pad_add_fusion.1.bounds, f32[32,3]{1,0:T(8,128)} %copy.83.table_ref, bf16[8192,384]{1,0:T(8,128)(2,1)} %all-gather.9.cloned.1.call-done.g_ref, bf16[8192,128]{1,0:T(8,128)(2,1)} %select_convert_fusion.kaug_ref, ...), custom_call_target="tpu_custom_call" | custom-call | tf_op jit(solution)/shard_map/attention_forward/pallas_call | solution.py:1390
  117.1 8.3 %copy.82.wd_hbm = bf16[1792,1472]{1,0:T(8,128)(2,1)} copy(bf16[1792,1472]{0,1:T(8,128)(2,1)} %param.26) | data formatting | bytes 10551296 | tf_op args[12]
  125.4 0.9 concatenate.24.wout_ref
  126.3 7.0 %all-gather.11.cloned.1.call-done.cot_ref = bf16[512,1472]{1,0:T(8,128)(2,1)} async-done(((bf16[256,1472]{1,0:T(8,128)(2,1)}), bf16[512,1472]{1,0:T(8,128)(2,1)}) %all-gather.11.cloned.1.call-update) | async-done | bytes 1507344 | tf_op jit(solution)/shard_map/all_gather | solution.py:1345
  133.3 90.3 %feed_forward.1 = (f32[256,1472]{1,0:T(8,128)}, f32[256,1472]{1,0:T(8,128)}, bf16[512,1472]{1,0:T(8,128)(2,1)}, bf16[512,1472]{1,0:T(8,128)(2,1)}, bf16[512,256]...) custom-call(bf16[512,256]{1,0:T(8,128)(2,1)} %get-tuple-element.34.att_ref, ...), custom_call_target="tpu_custom_call" | custom-call | tf_op jit(solution)/shard_map/feed_forward/pallas_call | solution.py:1252
  225.9 4.3 concatenate.26.w3_ref
  230.2 1.6 constant_dynamic-slice_fusion.kaug_ref
  231.8 12.1 %attention_grad_queries.1 = (bf16[512,256]{1,0:T(8,128)(2,1)}, f32[3,32,128]{2,1,0:T(8,128)}) custom-call(s32[5]{0:T(128)} %pad_add_fusion.1.bounds, f32[32,3]{1,0:T(8,128)} %copy.83.table_ref, bf16[8192,384]{1,0:T(8,128)(2,1)} %all-gather.9.cloned.1.call-done.g_ref, bf16[8192,128]{1,0:T(8,128)(2,1)} %select_convert_fusion.kaug_ref, ...), custom_call_target="tpu_custom_call" | custom-call | tf_op jit(solution)/shard_map/attention_grad_queries/pallas_call | solution.py:1432
  244.0 0.9 reduce_sum.85
  245.0 0.7 fusion.9.small_ref
  245.7 40.5 %all-gather.15.cloned.1.call-done.doall_ref = bf16[8192,256]{1,0:T(8,128)(2,1)} async-done(((bf16[512,256]{1,0:T(8,128)(2,1)}), bf16[8192,256]{1,0:T(8,128)(2,1)}) %all-gather.15.cloned.1.call-update) | async-done | bytes 4194320 | tf_op jit(solution)/shard_map/all_gather | solution.py:1430
  286.1 9.4 %attention_grad_keys.1 = (bf16[512,256]{1,0:T(8,128)(2,1)}, bf16[512,256]{1,0:T(8,128)(2,1)}, f32[2,8,256]{2,1,0:T(8,128)}) custom-call(s32[5]{0:T(128)} %pad_add_fusion.1.bounds, f32[32,3]{1,0:T(8,128)} %copy.83.table_ref, bf16[8192,256]{1,0:T(8,128)(2,1)} %all-gather.13.cloned.1.call-done.qall_ref, ...), custom_call_target="tpu_custom_call" | custom-call | tf_op jit(solution)/shard_map/attention_grad_keys/pallas_call | solution.py:1453
  295.6 139.5 %finish.1 = (bf16[256,1472]{1,0:T(8,128)(2,1)}, f32[256,1472]{1,0:T(8,128)}, f32[8,256]{1,0:T(8,128)}, bf16[4,2,2,48,1472]{4,3,2,1,0:T(8,128)(2,1)}, f32[8,1472]{1,0:T(8,128)}) custom-call(bf16[512,256]{1,0:T(8,128)(2,1)} %get-tuple-element.37.dq_ref, bf16[512,256]{1,0:T(8,128)(2,1)} %get-tuple-element.38.dk_ref, bf16[512,256]{1,0:T(8,128)(2,1)} %get-tuple-element.39.dv_ref, ...), custom_call_target="tpu_custom_call" | custom-call | tf_op jit(solution)/shard_map/finish/pallas_call | solution.py:989
  435.1 2.3 copy.89
  437.4 3.1 copy.90
  440.5 1.3 slice.41
  443.1 1.5 slice_reduce_fusion
  444.7 2.4 fusion.25
  447.1 38.8 %reduce-scatter.2.cloned.1.call-done = bf16[336,1472]{1,0:T(8,128)(2,1)} async-done(((bf16[5376,1472]{1,0:T(8,128)(2,1)}), bf16[336,1472]{1,0:T(8,128)(2,1)}) %reduce-scatter.2.cloned.1.call-update) | async-done | bytes 989200 | tf_op jit(solution)/shard_map/reduce_scatter | solution.py:1425
  485.9 1.5 convert_element_type.67
  487.3 1.2 slice_bitcast_fusion
  489.1 0.9 slice.62
  (91 shorter events, 9.4 us)
Async XLA Ops:
  7.2 1.7 copy-start.9
  7.2 33.0 %all-gather.7.cloned.1.call-start = ((), (), s32[]{:S(2)}) async-start(), calls=%async_computation.1 | async-start | bytes 2359296 | tf_op jit(solution)/shard_map/all_gather | solution.py:1344
  8.6 1.4 copy-start
  8.6 31.5 %copy-start.7 = (bf16[1472,192]{0,1:T(8,128)(2,1)S(1)}, bf16[1472,192]{0,1:T(8,128)(2,1)}, u32[]{:S(2)}) copy-start(bf16[1472,192]{0,1:T(8,128)(2,1)} %param.19) | copy-start | bytes 1695748
  8.7 31.5 %copy-start.8 = (bf16[1472,192]{0,1:T(8,128)(2,1)S(1)}, bf16[1472,192]{0,1:T(8,128)(2,1)}, u32[]{:S(2)}) copy-start(bf16[1472,192]{0,1:T(8,128)(2,1)} %param.20) | copy-start | bytes 1695748
  10.1 33.3 %copy-start.4 = (bf16[256,1472]{0,1:T(8,128)(2,1)S(1)}, bf16[256,1472]{0,1:T(8,128)(2,1)}, u32[]{:S(2)}) copy-start(bf16[256,1472]{0,1:T(8,128)(2,1)} %param.27) | copy-start | bytes 2260996
  10.1 95.3 %all-gather.9.cloned.1.call-start = ((), (), s32[]{:S(2)}) async-start(), calls=%async_computation.2 | async-start | bytes 6684672 | tf_op jit(solution)/shard_map/all_gather | solution.py:1357
  43.3 1.4 copy-start.14
  43.3 2.5 copy-start.12
  43.3 3.3 copy-start.13
  43.3 90.0 %all-gather.11.cloned.1.call-start = ((), (), s32[]{:S(2)}) async-start(), calls=%async_computation.3 | async-start | bytes 2359296 | tf_op jit(solution)/shard_map/all_gather | solution.py:1345
  44.6 201.1 %all-gather.13.cloned.1.call-start = ((), (), s32[]{:S(2)}) async-start(), calls=%async_computation.4 | async-start | bytes 4456448 | tf_op jit(solution)/shard_map/all_gather | solution.py:1409
  73.8 5.4 %copy-start.3 = (bf16[512,1472]{1,0:T(8,128)(2,1)S(1)}, bf16[512,1472]{1,0:T(8,128)(2,1)}, u32[]{:S(2)}) copy-start(bf16[512,1472]{1,0:T(8,128)(2,1)} %all-gather.7.cloned.1.call-done.normed_ref) | copy-start | bytes 4521988
  73.8 5.4 %copy-start.6 = (bf16[1472,192]{0,1:T(8,128)(2,1)S(1)}, bf16[1472,192]{0,1:T(8,128)(2,1)}, u32[]{:S(2)}) copy-start(bf16[1472,192]{0,1:T(8,128)(2,1)} %param.18) | copy-start | bytes 1695748
  80.8 35.6 %copy-start.10 = (f32[1472]{0:T(1024)S(1)}, f32[1472]{0:T(1024)}, u32[]{:S(2)}) copy-start(f32[1472]{0:T(1024)} %param.23) | copy-start | bytes 17668
  116.3 169.9 %all-gather.15.cloned.1.call-start = ((), (), s32[]{:S(2)}) async-start(), calls=%async_computation.5 | async-start | bytes 4456448 | tf_op jit(solution)/shard_map/all_gather | solution.py:1430
  117.1 8.3 %copy-start.5 = (bf16[192,1472]{1,0:T(8,128)(2,1)S(1)}, bf16[192,1472]{1,0:T(8,128)(2,1)}, u32[]{:S(2)}) copy-start(bf16[192,1472]{1,0:T(8,128)(2,1)} %param.21) | copy-start | bytes 1695748
  223.7 262.2 %reduce-scatter.2.cloned.1.call-start = ((), (), s32[]{:S(2)}) async-start(), calls=%async_computation.6 | async-start | bytes 17547264 | tf_op jit(solution)/shard_map/reduce_scatter | solution.py:1425
  231.8 13.1 %copy-start.11 = (f32[1,1472]{1,0:T(1,128)S(1)}, f32[1,1472]{1,0:T(1,128)}, u32[]{:S(2)}) copy-start(f32[1,1472]{1,0:T(1,128)} %get-tuple-element.45) | copy-start | bytes 17668
  437.4 7.3 %copy-start.1 = (bf16[4,2,2,48,1472]{4,3,2,1,0:T(8,128)(2,1)S(1)}, bf16[4,2,2,48,1472]{4,3,2,1,0:T(8,128)(2,1)}, u32[]{:S(2)}) copy-start(bf16[4,2,2,48,1472]{4,3,2,1,0:T(8,128)(2,1)} %get-tuple-element.51) | copy-start | bytes 6782980
  487.3 1.7 copy-start.2
Sparse Core Ops, SparseCore 0:
  10.2 29.8 all-gather.6
  43.5 61.8 all-gather.8
  107.5 25.8 all-gather.10
  135.9 51.3 all-gather.12
  223.8 62.2 all-gather.14
  290.2 195.5 reduce-scatter.1

commit v5 on v4

--- a/solution.py
+++ b/solution.py
@@ -672,6 +672,273 @@
         ),
         name="weight_scatter",
     )(*shaped)
+
+def first_kernel(
+    plan, lines, span, tokens_ref, gain_ref, aug_ref, wq_hbm, wk_hbm, wv_hbm,
+    x_ref, q_ref, own_ref, all_hbm,
+    weights, zeros, load_sem, y_sem, own_sem, zero_sem, z_sem, x_sem, c_sem,
+):
+    spot = Spot(lines)
+    z, x, core, wa = (spot.z, spot.x, spot.core, spot.wa)
+    half, model = tokens_ref.shape
+    cols = plan.cols
+    chunk = half // 4
+    loads = [
+        pltpu.make_async_copy(src, weights.at[pl.ds(i * cols, cols)], load_sem.at[i])
+        for i, src in enumerate((wk_hbm, wv_hbm, wq_hbm))
+    ]
+    for load in loads:
+        load.start()
+    greet(spot, True)
+    zeros[...] = jnp.zeros_like(zeros)
+
+    def outside(d):
+        return (d < z - span) | (d > z + span)
+
+    def zero_copies(d):
+        return [
+            pltpu.make_async_copy(zeros, all_hbm.at[d, a, b], zero_sem.at[d, a, b])
+            for a in range(2)
+            for b in range(2)
+        ]
+
+    def zero_start(d, unused):
+        @pl.when(outside(d))
+        def _():
+            for copy in zero_copies(d):
+                copy.start()
+
+        return unused
+
+    def rows_at(start, size):
+        return pl.ds(pl.multiple_of(start, size), size)
+
+    ours = wa * half
+    theirs = (1 - wa) * half
+
+    def y_copy(i, base):
+        at = rows_at(base + i * chunk, chunk)
+        return send(x_ref.at[at], x_ref.at[at], y_sem.at[0, i], y_sem.at[1, i], spot.y_mate())
+
+    def normal(i, unused):
+        rows_in = tokens_ref[rows_at(i * chunk, chunk), :].astype(f32)
+        inv = lax.rsqrt(jnp.mean(rows_in * rows_in, axis=-1, keepdims=True) + eps)
+        x_ref[rows_at(ours + i * chunk, chunk), :] = (rows_in * inv * gain_ref[...]).astype(bf16)
+        y_copy(i, ours).start()
+        return unused
+
+    lax.fori_loop(0, 4, normal, 0)
+    for load in loads:
+        load.wait()
+
+    def project(base):
+        rows = rows_at(base, half)
+        qkv = nt(x_ref[rows, :], weights[...]).astype(bf16)
+        own_ref[rows, :] = qkv[:, : 2 * cols]
+        q_ref[rows, :] = aug_ref[rows, :]
+        q_ref[rows, :cols] = qkv[:, 2 * cols :]
+
+    pieces = [
+        (ours, half, True),
+        (theirs, half // 2, True),
+        (theirs + half // 2, half // 2, False),
+    ]
+
+    def piece_rows(p):
+        return rows_at(pieces[p][0], pieces[p][1])
+
+    def source(p, d, a):
+        return all_hbm.at[d, a, core, piece_rows(p)]
+
+    def pass_copy(p, step, d, own):
+        i = 0 if step > 0 else 1
+        if pieces[p][2]:
+            dst = source(p, d, x)
+            src = own_ref.at[piece_rows(p)] if own else dst
+        else:
+            dst = all_hbm.at[d, :, core, piece_rows(p)]
+            src = dst
+        return send(src, dst, z_sem.at[p, i, d], z_sem.at[p, 2 + i, d], spot.z_mate(step))
+
+    def across(p, d, own):
+        dst = source(p, d, x)
+        src = own_ref.at[piece_rows(p)] if own else dst
+        return send(src, dst, x_sem.at[p, 0, d], x_sem.at[p, 1, d], spot.x_mate())
+
+    def beside(p, d):
+        part = all_hbm.at[d, :, core, piece_rows(p)]
+        return send(part, part, c_sem.at[p, 0, d], c_sem.at[p, 1, d], spot.core_mate())
+
+    def own_copy(p):
+        return pltpu.make_async_copy(
+            own_ref.at[piece_rows(p)], source(p, z, x), own_sem.at[p]
+        )
+
+    def both_ways(p, own):
+        @pl.when(z + 1 < lines)
+        def _():
+            pass_copy(p, 1, z, own).start()
+
+        @pl.when(z > 0)
+        def _():
+            pass_copy(p, -1, z, own).start()
+
+    def begin(p):
+        own_copy(p).start()
+        across(p, z, True).start()
+        if pieces[p][2]:
+            both_ways(p, True)
+
+    def level(p, k):
+        @pl.when(z - k >= 0)
+        def _():
+            d = jnp.maximum(z - k, 0)
+            pass_copy(p, 1, d, False).wait_recv()
+            if k < span:
+
+                @pl.when(z + 1 < lines)
+                def _():
+                    pass_copy(p, 1, d, False).start()
+
+            if pieces[p][2]:
+                across(p, d, False).start()
+            else:
+                beside(p, d).start()
+
+        @pl.when(z + k < lines)
+        def _():
+            d = jnp.minimum(z + k, lines - 1)
+            pass_copy(p, -1, d, False).wait_recv()
+            if k < span:
+
+                @pl.when(z > 0)
+                def _():
+                    pass_copy(p, -1, d, False).start()
+
+            if pieces[p][2]:
+                across(p, d, False).start()
+            else:
+                beside(p, d).start()
+
+    def turn(p):
+        across(p, z, True).wait()
+        own_copy(p).wait()
+        both_ways(p, False)
+        beside(p, z).start()
+
+    def settle(p, k):
+        for sign in (1, -1) if k else (1,):
+            d = z - sign * k
+
+            @pl.when((d >= 0) & (d < lines))
+            def _(d=d):
+                d = jnp.clip(d, 0, lines - 1)
+                across(p, d, k == 0).wait()
+                if k == 0:
+                    own_copy(p).wait()
+                beside(p, d).start()
+
+    project(ours)
+    begin(0)
+    lax.fori_loop(0, lines, zero_start, 0)
+
+    def y_wait(i, unused):
+        y_copy(i, theirs).wait_recv()
+        return unused
+
+    lax.fori_loop(0, 2, y_wait, 0)
+    level(0, 1)
+    lax.fori_loop(2, 4, y_wait, 0)
+    project(theirs)
+    begin(2)
+    begin(1)
+    if span > 1:
+        level(0, 2)
+    settle(0, 0)
+    turn(2)
+    level(1, 1)
+    settle(0, 1)
+    level(2, 1)
+    if span > 1:
+        level(1, 2)
+        settle(0, 2)
+    settle(1, 0)
+    settle(1, 1)
+    if span > 1:
+        level(2, 2)
+        settle(1, 2)
+    for k in range(3, span + 1):
+        for p in range(3):
+            level(p, k)
+        for p in range(2):
+            settle(p, k)
+
+    def finish_line(d, unused):
+        @pl.when(~outside(d))
+        def _():
+            for p in range(3):
+                beside(p, d).wait()
+
+        @pl.when(outside(d))
+        def _():
+            for copy in zero_copies(d):
+                copy.wait()
+
+        for p in range(3):
+
+            @pl.when((z + 1 < lines) & (d <= z) & (d > z - span))
+            def _(p=p):
+                pass_copy(p, 1, d, False).wait_send()
+
+            @pl.when((z > 0) & (d >= z) & (d < z + span))
+            def _(p=p):
+                pass_copy(p, -1, d, False).wait_send()
+
+        return unused
+
+    lax.fori_loop(0, lines, finish_line, 0)
+
+    def y_drain(i, unused):
+        y_copy(i, ours).wait_send()
+        return unused
+
+    lax.fori_loop(0, 4, y_drain, 0)
+
+
+def first(plan, cycle_size, reach, tokens, gain, aug, w_query, w_key, w_value):
+    lines = cycle_size // 4
+    span = min(lines - 1, (reach + 3) // 4)
+    half, model = tokens.shape
+    pair = 2 * half
+    hbm = pl.BlockSpec(memory_space=pl.ANY)
+    dma = pltpu.SemaphoreType.DMA
+    return pl.pallas_call(
+        functools.partial(first_kernel, plan, lines, span),
+        out_shape=[
+            jax.ShapeDtypeStruct((pair, model), bf16),
+            jax.ShapeDtypeStruct((pair, WIDE), bf16),
+            jax.ShapeDtypeStruct((pair, 2 * plan.cols), bf16),
+            jax.ShapeDtypeStruct((lines, 2, 2, pair, 2 * plan.cols), bf16),
+        ],
+        in_specs=[vmem] * 3 + [hbm] * 3,
+        out_specs=[vmem] * 3 + [hbm],
+        scratch_shapes=[
+            pltpu.VMEM((3 * plan.cols, model), bf16),
+            pltpu.VMEM((pair, 2 * plan.cols), bf16),
+            dma((3,)),
+            dma((2, 4)),
+            dma((3,)),
+            dma((lines, 2, 2)),
+            dma((3, 4, lines)),
+            dma((3, 2, lines)),
+            dma((3, 2, lines)),
+        ],
+        compiler_params=pltpu.CompilerParams(
+            vmem_limit_bytes=56 * 2**20, collective_id=4, has_side_effects=True
+        ),
+        name="project_gather",
+    )(tokens, gain, aug, w_query.T, w_key.T, w_value.T)
+
 
 def tn(a, b):
     return lax.dot_general(a, b, (((0,), (0,)), ((), ())), preferred_element_type=f32)
@@ -1045,7 +1312,7 @@
     spot = Spot(cycle_size // 4)
     wa = spot.wa
     half, model = tokens_ref.shape
-    units = wd.shape[0]
+    units = wd.shape[1]
     chunk = half // 4
     loads = [
         pltpu.make_async_copy(src, dst, load_sem.at[i])
@@ -1125,7 +1392,7 @@
             cols = rows_at(u * wide, wide)
             gate = nn(x_ref[rows, :], wg[:, cols])
             upward = nn(x_ref[rows, :], wu[:, cols])
-            grad_inner = nt(cot_ref[rows, :], wd[cols, :])
+            grad_inner = nn(cot_ref[rows, :], wd[:, cols])
             square = gate * gate
             bend = jnp.tanh(root * gate * (1.0 + cubic * square))
             side = 0.5 * (1.0 + bend)
@@ -1140,7 +1407,7 @@
             gg[rows, cols] = gate_low
             gu[rows, cols] = up_low
             acc_g[...] += nt(gate_low, wg[:, cols]) + nt(up_low, wu[:, cols])
-            acc_f[...] += nn(inner_low, wd[cols, :])
+            acc_f[...] += nt(inner_low, wd[:, cols])
             return unused
 
         lax.fori_loop(0, units // wide, tile, 0)
@@ -1265,7 +1532,7 @@
         scratch_shapes=[
             pltpu.VMEM((model, units), bf16),
             pltpu.VMEM((model, units), bf16),
-            pltpu.VMEM((units, model), bf16),
+            pltpu.VMEM((model, units), bf16),
             pltpu.VMEM((pair, units), bf16),
             pltpu.VMEM((pair, units), bf16),
             pltpu.VMEM((pair, units), bf16),
@@ -1286,7 +1553,7 @@
             vmem_limit_bytes=60 * 2**20, collective_id=3, has_side_effects=True
         ),
         name="feed_forward",
-    )(attended, mixed, w_out, tokens, cot, gain, w_gate, w_up, w_down)
+    )(attended, mixed, w_out, tokens, cot, gain, w_gate, w_up, w_down.T)
 
 
 def shards(
@@ -1337,16 +1604,7 @@
     ).astype(jnp.int32)
 
     mask_all = lax.all_gather(key_mask, "ctx", axis=0, tiled=True)
-    tokens_wide = tokens.astype(f32)
-    normed_attn, inv_attn = norm_forward(tokens_wide, gain_attn)
-    normed_low = normed_attn.astype(bf16)
-    pair_normed, pair_cot = (
-        lax.all_gather(normed_low, "wa", axis=0, tiled=True),
-        lax.all_gather(cotangent, "wa", axis=0, tiled=True),
-    )
-    w_kv = jnp.concatenate([w_key, w_value], axis=1)
-    own_kv = jnp.dot(pair_normed, w_kv, preferred_element_type=f32).astype(bf16)
-    queries = jnp.dot(pair_normed, w_query, preferred_element_type=f32).astype(bf16)
+    pair_cot = lax.all_gather(cotangent, "wa", axis=0, tiled=True)
 
     def window(gathered):
         if rows == total_rows:
@@ -1354,7 +1612,6 @@
         return lax.dynamic_slice_in_dim(gathered, origin, rows, 0)
 
     gather = functools.partial(lax.all_gather, axis_name="ctx", axis=0, tiled=True)
-    kv_all = window(gather(own_kv))
     positions = origin + jnp.arange(rows, dtype=jnp.int32)
     doc_of = doc_at(positions)
     lane = jnp.arange(128, dtype=jnp.int32)[None, :] + 128
@@ -1374,9 +1631,11 @@
     q_aug = jnp.where(
         lane == plan.mask_lane, 1.0, ((lane < plan.stat_lane) & ~own_differs).astype(f32)
     ).astype(bf16)
-    q_wide = jnp.concatenate(
-        [queries, q_aug[:, plan.cols - 128 :]], axis=1
+    q_aug = jnp.concatenate([jnp.zeros((pair, 128), bf16), q_aug], axis=1)
+    pair_normed, q_wide, own_kv, kv_all = first(
+        plan, cycle_size, reach, tokens, gain_attn[None], q_aug, w_query, w_key, w_value
     )
+    kv_all = window(kv_all.reshape(total_rows, 2 * plan.cols))
     near_bias = pl.pallas_call(
         functools.partial(near_kernel, heads),
         out_shape=jax.ShapeDtypeStruct((2, heads, TQ, TK), f32),

time: 504 us -> 480 us (0.952)
  waiting for transfers between devices: 141 us -> 77.8 us
  Pallas kernels: 268 us -> 317 us
  local copies, waits for them, and re-layouts: 35.9 us -> 29.6 us
    all_gather x3 -> x1, waiting for transfers between devices: 61.5 us -> 0.01 us  [shards(): pair_cot = lax.all_gather(cotangent, 'wa', axis=0, tiled=True)]
    pallas_call x0 -> x1, Pallas kernels: none -> 43.6 us  [first(): pl.pallas_call(functools.partial(first_kernel, plan, lines, span), out_sh...]
    unnamed x40 -> x35, local copies, waits for them, and re-layouts: 18.4 us -> 11.8 us
    pallas_call x1, Pallas kernels: 140 us -> 134 us  [finish(): pl.pallas_call(functools.partial(finish_kernel, plan, lines), out_shape=[...]
  transfers between devices with their start and end apart: 6 -> 4, of which waited for: 5 -> 2; matrix products, arithmetic and copies ran while one was open for 8% -> 7% of each run, Pallas kernels for 54% -> 67%
where the time goes in v5:
time: 480 us; the launch traced here: 472 us
  Pallas kernels  317 us (66%)
  waiting for transfers between devices  77.8 us (16%)
  local copies, waits for them, and re-layouts  29.6 us (6%)
  blocking collectives  23.1 us (5%)
  between operations  14.5 us (3%)
  other arithmetic  9.48 us (2%)
    pallas_call x1, Pallas kernels, finish(): pl.pallas_call(functools.partial(finish_kernel, plan, lines), out_shape=[...  134 us
    pallas_call x1, Pallas kernels, middle(): pl.pallas_call(functools.partial(middle_kernel, plan, cycle_size), out_sh...  91.5 us
    pallas_call x1, Pallas kernels, first(): pl.pallas_call(functools.partial(first_kernel, plan, lines, span), out_sh...  43.6 us
    all_gather x1, waiting for transfers between devices, shards(): do_all = window(gather(do_wide))  38.9 us
    reduce_scatter x1, waiting for transfers between devices, shards(): lax.psum_scatter(stacked.reshape(-1, model), 'ctx', scatter_dimension=0,...  38.5 us
    all_gather x1, blocking collectives, shards(): mask_all = lax.all_gather(key_mask, 'ctx', axis=0, tiled=True)  23.1 us
    pallas_call x1, Pallas kernels, shards(): pl.pallas_call(functools.partial(dq_kernel, plan, rows, pair), out_shape=...  15.3 us
    pallas_call x1, Pallas kernels, shards(): pl.pallas_call(functools.partial(fwd_kernel, plan, rows, pair), out_shape...  14.8 us
  transfers between devices with their start and end apart: 4, of which 2 were waited for; matrix products, arithmetic and copies ran while one was open for 7% of the time, Pallas kernels for 67%

profile of v5, /device:TPU:0, one launch (start us, length us, event | category | flops | bytes accessed | tf_op | source)
XLA Modules:
  0.0 472.0 jit_solution(18056657861646275654)
XLA Ops:
  7.3 2.3 copy.59
  10.8 0.7 copy.61.table_ref
  11.5 1.2 copy.56.tokens_ref
  12.7 0.6 broadcast_in_dim.110.gain_ref
  13.5 23.1 %all-gather = bf16[16,1,512]{2,1,0:T(2,128)(2,1)S(1)} all-gather(bf16[1,1,512]{2,1,0:T(2,128)(2,1)S(1)} %reshape.264), channel_id=1, replica_groups=mesh['ctx'=16,'wa'=2] {'ctx'}, dimensions={0}, use_global_device_ids=true | all-gather | bytes 17408 | tf_op jit(solution)/shard_map/all_gather | solution.py:1606
  36.7 5.0 %near_bias.1.near_ref = f32[2,3,256,512]{3,2,1,0:T(8,128)} custom-call(f32[32,3]{1,0:T(8,128)} %copy.61.table_ref), custom_call_target="tpu_custom_call" | custom-call | tf_op jit(solution)/shard_map/near_bias/pallas_call | solution.py:1639
  42.5 0.7 concatenate.19.aug_ref
  43.2 43.6 %project_gather.1 = (bf16[512,1472]{1,0:T(8,128)(2,1)}, bf16[512,256]{1,0:T(8,128)(2,1)}, bf16[512,384]{1,0:T(8,128)(2,1)}, bf16[4,2,2,512,384]{4,3,2,1,0:T(8,128)(2,1)}) custom-call(bf16[256,1472]{1,0:T(8,128)(2,1)} %copy.56.tokens_ref, f32[1,1472]{1,0:T(1,128)} %broadcast_in_dim.110.gain_ref, bf16[512,256]{1,0:T(8,128)(2,1)} %concatenate.19.aug_ref, ...), custom_call_target="tpu_custom_call" | custom-call | tf_op jit(solution)/shard_map/project_gather/pallas_call | solution.py:915
  86.9 4.6 select_convert_fusion.kaug_ref
  91.4 14.8 %attention_forward.1 = (bf16[512,256]{1,0:T(8,128)(2,1)}, f32[512,256]{1,0:T(8,128)}, bf16[512,256]{1,0:T(8,128)(2,1)}) custom-call(s32[5]{0:T(128)} %pad_add_fusion.1.bounds, f32[32,3]{1,0:T(8,128)} %copy.61.table_ref, bf16[8192,384]{1,0:T(8,128)(2,1)} %bitcast.44, bf16[8192,128]{1,0:T(8,128)(2,1)} %select_convert_fusion.kaug_ref, ...), custom_call_target="tpu_custom_call" | custom-call | tf_op jit(solution)/shard_map/attention_forward/pallas_call | solution.py:1649
  106.3 0.9 concatenate.20.wout_ref
  107.8 91.5 %feed_forward.1 = (f32[256,1472]{1,0:T(8,128)}, f32[256,1472]{1,0:T(8,128)}, bf16[512,1472]{1,0:T(8,128)(2,1)}, bf16[512,1472]{1,0:T(8,128)(2,1)}, bf16[512,256]...) custom-call(bf16[512,256]{1,0:T(8,128)(2,1)} %get-tuple-element.40.att_ref, ...), custom_call_target="tpu_custom_call" | custom-call | tf_op jit(solution)/shard_map/feed_forward/pallas_call | solution.py:1519
  200.0 0.7 copy-done.2
  201.7 4.3 concatenate.22.w3_ref
  206.1 1.6 constant_dynamic-slice_fusion.kaug_ref
  207.7 15.3 %attention_grad_queries.1 = (bf16[512,256]{1,0:T(8,128)(2,1)}, f32[3,32,128]{2,1,0:T(8,128)}) custom-call(s32[5]{0:T(128)} %pad_add_fusion.1.bounds, f32[32,3]{1,0:T(8,128)} %copy.61.table_ref, bf16[8192,384]{1,0:T(8,128)(2,1)} %bitcast.45, bf16[8192,128]{1,0:T(8,128)(2,1)} %select_convert_fusion.kaug_ref, bf16[512,256]{1,0:T(8,128)(2,1)} %get-tuple-element.39.qb_ref, ...), custom_call_target="tpu_custom_call" | custom-call | tf_op jit(solution)/shard_map/attention_grad_queries/pallas_call | solution.py:1691
  222.9 0.9 reduce_sum.75
  223.9 0.7 fusion.3.small_ref
  224.6 38.9 %all-gather.9.cloned.1.call-done.doall_ref = bf16[8192,256]{1,0:T(8,128)(2,1)} async-done(((bf16[512,256]{1,0:T(8,128)(2,1)}), bf16[8192,256]{1,0:T(8,128)(2,1)}) %all-gather.9.cloned.1.call-update) | async-done | bytes 4194320 | tf_op jit(solution)/shard_map/all_gather | solution.py:1689
  263.5 12.7 %attention_grad_keys.1 = (bf16[512,256]{1,0:T(8,128)(2,1)}, bf16[512,256]{1,0:T(8,128)(2,1)}, f32[2,8,256]{2,1,0:T(8,128)}) custom-call(s32[5]{0:T(128)} %pad_add_fusion.1.bounds, f32[32,3]{1,0:T(8,128)} %copy.61.table_ref, bf16[8192,256]{1,0:T(8,128)(2,1)} %all-gather.7.cloned.1.call-done.qall_ref, ...), custom_call_target="tpu_custom_call" | custom-call | tf_op jit(solution)/shard_map/attention_grad_keys/pallas_call | solution.py:1712
  276.1 134.2 %finish.1 = (bf16[256,1472]{1,0:T(8,128)(2,1)}, f32[256,1472]{1,0:T(8,128)}, f32[8,256]{1,0:T(8,128)}, bf16[4,2,2,48,1472]{4,3,2,1,0:T(8,128)(2,1)}, f32[8,1472]{1,0:T(8,128)}) custom-call(bf16[512,256]{1,0:T(8,128)(2,1)} %get-tuple-element.43.dq_ref, bf16[512,256]{1,0:T(8,128)(2,1)} %get-tuple-element.45.dk_ref, bf16[512,256]{1,0:T(8,128)(2,1)} %get-tuple-element.46.dv_ref, ...), custom_call_target="tpu_custom_call" | custom-call | tf_op jit(solution)/shard_map/finish/pallas_call | solution.py:1256
  410.4 2.4 copy.67
  412.8 3.0 copy.68
  415.8 1.3 slice.37
  417.1 0.7 slice_reduce_fusion.2
  417.8 0.7 reshape_squeeze.3
  418.4 1.5 slice_reduce_fusion
  419.9 2.4 fusion.18
  422.3 38.5 %reduce-scatter.2.cloned.1.call-done = bf16[336,1472]{1,0:T(8,128)(2,1)} async-done(((bf16[5376,1472]{1,0:T(8,128)(2,1)}), bf16[336,1472]{1,0:T(8,128)(2,1)}) %reduce-scatter.2.cloned.1.call-update) | async-done | bytes 989200 | tf_op jit(solution)/shard_map/reduce_scatter | solution.py:1684
  460.9 1.5 convert_element_type.51
  462.4 1.2 slice_bitcast_fusion
  464.1 0.9 slice.54
  (71 shorter events, 5.0 us)
Async XLA Ops:
  7.2 2.6 copy-start.12
  7.2 3.6 copy-start.10
  7.2 4.3 copy-start.5
  7.2 5.5 %copy-start.7 = (f32[1472]{0:T(1024)S(1)}, f32[1472]{0:T(1024)}, u32[]{:S(2)}) copy-start(f32[1472]{0:T(1024)} %param.17) | copy-start | bytes 17668
  7.2 6.3 %copy-start.11 = (bf16[512]{0:T(512)(128)(2,1)S(1)}, bf16[512]{0:T(512)(128)(2,1)}, u32[]{:S(2)}) copy-start(bf16[512]{0:T(512)(128)(2,1)} %param.16) | copy-start | bytes 3076
  7.2 100.6 %all-gather.5.cloned.1.call-start = ((), (), s32[]{:S(2)}) async-start(), calls=%async_computation.1 | async-start | bytes 2359296 | tf_op jit(solution)/shard_map/all_gather | solution.py:1607
  9.6 215.0 %all-gather.7.cloned.1.call-start = ((), (), s32[]{:S(2)}) async-start(), calls=%async_computation.2 | async-start | bytes 4456448 | tf_op jit(solution)/shard_map/all_gather | solution.py:1668
  91.4 14.8 %copy-start.6 = (bf16[192,1472]{1,0:T(8,128)(2,1)S(1)}, bf16[192,1472]{1,0:T(8,128)(2,1)}, u32[]{:S(2)}) copy-start(bf16[192,1472]{1,0:T(8,128)(2,1)} %param.21) | copy-start | bytes 1695748
  91.4 15.8 %copy-start.8 = (f32[1472]{0:T(1024)S(1)}, f32[1472]{0:T(1024)}, u32[]{:S(2)}) copy-start(f32[1472]{0:T(1024)} %param.23) | copy-start | bytes 17668
  106.2 157.2 %all-gather.9.cloned.1.call-start = ((), (), s32[]{:S(2)}) async-start(), calls=%async_computation.3 | async-start | bytes 4456448 | tf_op jit(solution)/shard_map/all_gather | solution.py:1689
  199.4 261.5 %reduce-scatter.2.cloned.1.call-start = ((), (), s32[]{:S(2)}) async-start(), calls=%async_computation.4 | async-start | bytes 17547264 | tf_op jit(solution)/shard_map/reduce_scatter | solution.py:1684
  199.6 1.1 copy-start.2
  199.6 1.3 copy-start.3
  200.0 1.3 copy-start.4
  207.7 16.2 %copy-start.9 = (f32[1,1472]{1,0:T(1,128)S(1)}, f32[1,1472]{1,0:T(1,128)}, u32[]{:S(2)}) copy-start(f32[1,1472]{1,0:T(1,128)} %get-tuple-element.53) | copy-start | bytes 17668
  410.4 9.6 %copy-start = (bf16[4,2,2,48,1472]{4,3,2,1,0:T(8,128)(2,1)S(1)}, bf16[4,2,2,48,1472]{4,3,2,1,0:T(8,128)(2,1)}, u32[]{:S(2)}) copy-start(bf16[4,2,2,48,1472]{4,3,2,1,0:T(8,128)(2,1)} %get-tuple-element.59) | copy-start | bytes 6782980
  462.4 1.7 copy-start.1
Sparse Core Ops, SparseCore 0:
  10.2 29.9 all-gather.4
  106.4 63.3 all-gather.6
  199.5 63.9 all-gather.8
  267.6 193.2 reduce-scatter.1

commit v6 on v5

--- a/solution.py
+++ b/solution.py
@@ -440,8 +440,7 @@
     return (a.astype(f32) + b.astype(f32)).astype(bf16)
 
 
-def scatter_kernel(lines, units, z_first, *refs):
-    count = 3
+def scatter_kernel(lines, units, z_first, count, *refs):
     parts, outs = (refs[:count], refs[count : 2 * count])
     mine, core_in, x_in, up_in, down_in, load_sem, core_sem, x_sem, up_sem, down_sem = refs[
         2 * count :
@@ -641,26 +640,26 @@
 
 def reduce_scatter(parts, cycle_size):
     lines = cycle_size // 4
-    units_here, model = parts[0].shape
-    rows = units_here // cycle_size
+    count = len(parts)
+    rows, model = parts[0].shape[1:]
     cut = (rows // 2 + 15) // 16 * 16
     pieces = [(0, cut), (cut, rows - cut)] if cut < rows else [(0, rows)]
-    units = [(m, at, size) for m in range(3) for at, size in pieces]
+    units = [(m, at, size) for m in range(count) for at, size in pieces]
     z_first = [len(units) - 1]
     shaped = [part.reshape(lines, 2, 2, rows, model) for part in parts]
     hbm = pl.BlockSpec(memory_space=pl.ANY)
     n = len(units)
     return pl.pallas_call(
-        functools.partial(scatter_kernel, lines, units, z_first),
-        out_shape=[jax.ShapeDtypeStruct((rows, model), f32)] * 3,
-        in_specs=[hbm] * 3,
-        out_specs=[vmem] * 3,
+        functools.partial(scatter_kernel, lines, units, z_first, count),
+        out_shape=[jax.ShapeDtypeStruct((rows, model), f32)] * count,
+        in_specs=[hbm] * count,
+        out_specs=[vmem] * count,
         scratch_shapes=[
-            pltpu.VMEM((3, lines, 2, rows, model), bf16),
-            pltpu.VMEM((3, lines, 2, rows, model), bf16),
-            pltpu.VMEM((3, lines, rows, model), bf16),
-            pltpu.VMEM((3, lines, 2, rows, model), bf16),
-            pltpu.VMEM((3, lines, 2, rows, model), bf16),
+            pltpu.VMEM((count, lines, 2, rows, model), bf16),
+            pltpu.VMEM((count, lines, 2, rows, model), bf16),
+            pltpu.VMEM((count, lines, rows, model), bf16),
+            pltpu.VMEM((count, lines, 2, rows, model), bf16),
+            pltpu.VMEM((count, lines, 2, rows, model), bf16),
             pltpu.SemaphoreType.DMA((n,)),
             pltpu.SemaphoreType.DMA((2, n)),
             pltpu.SemaphoreType.DMA((2, n)),
@@ -675,7 +674,7 @@
 
 def first_kernel(
     plan, lines, span, tokens_ref, gain_ref, aug_ref, wq_hbm, wk_hbm, wv_hbm,
-    x_ref, q_ref, own_ref, all_hbm,
+    x_ref, tok_ref, q_ref, own_ref, all_hbm,
     weights, zeros, load_sem, y_sem, own_sem, zero_sem, z_sem, x_sem, c_sem,
 ):
     spot = Spot(lines)
@@ -717,14 +716,30 @@
     theirs = (1 - wa) * half
 
     def y_copy(i, base):
-        at = rows_at(base + i * chunk, chunk)
-        return send(x_ref.at[at], x_ref.at[at], y_sem.at[0, i], y_sem.at[1, i], spot.y_mate())
+        return send(
+            tokens_ref.at[rows_at(i * chunk, chunk)],
+            tok_ref.at[rows_at(base + i * chunk, chunk)],
+            y_sem.at[0, i],
+            y_sem.at[1, i],
+            spot.y_mate(),
+        )
+
+    def y_start(i, unused):
+        y_copy(i, ours).start()
+        return unused
+
+    lax.fori_loop(0, 4, y_start, 0)
+
+    def scaled(rows_in):
+        rows_in = rows_in.astype(f32)
+        inv = lax.rsqrt(jnp.mean(rows_in * rows_in, axis=-1, keepdims=True) + eps)
+        return (rows_in * inv * gain_ref[...]).astype(bf16)
 
     def normal(i, unused):
-        rows_in = tokens_ref[rows_at(i * chunk, chunk), :].astype(f32)
-        inv = lax.rsqrt(jnp.mean(rows_in * rows_in, axis=-1, keepdims=True) + eps)
-        x_ref[rows_at(ours + i * chunk, chunk), :] = (rows_in * inv * gain_ref[...]).astype(bf16)
-        y_copy(i, ours).start()
+        at = rows_at(ours + i * chunk, chunk)
+        rows_in = tokens_ref[rows_at(i * chunk, chunk), :]
+        tok_ref[at, :] = rows_in
+        x_ref[at, :] = scaled(rows_in)
         return unused
 
     lax.fori_loop(0, 4, normal, 0)
@@ -844,6 +859,8 @@
 
     def y_wait(i, unused):
         y_copy(i, theirs).wait_recv()
+        at = rows_at(theirs + i * chunk, chunk)
+        x_ref[at, :] = scaled(tok_ref[at, :])
         return unused
 
     lax.fori_loop(0, 2, y_wait, 0)
@@ -916,12 +933,13 @@
         functools.partial(first_kernel, plan, lines, span),
         out_shape=[
             jax.ShapeDtypeStruct((pair, model), bf16),
+            jax.ShapeDtypeStruct((pair, model), bf16),
             jax.ShapeDtypeStruct((pair, WIDE), bf16),
             jax.ShapeDtypeStruct((pair, 2 * plan.cols), bf16),
             jax.ShapeDtypeStruct((lines, 2, 2, pair, 2 * plan.cols), bf16),
         ],
         in_specs=[vmem] * 3 + [hbm] * 3,
-        out_specs=[vmem] * 3 + [hbm],
+        out_specs=[vmem] * 4 + [hbm],
         scratch_shapes=[
             pltpu.VMEM((3 * plan.cols, model), bf16),
             pltpu.VMEM((pair, 2 * plan.cols), bf16),
@@ -973,7 +991,7 @@
 
 
 def finish_kernel(
-    plan, lines, dq_ref, dk_ref, dv_ref, mask_ref, w3_ref, normed_ref, att_ref, branch_ref,
+    plan, lines, dq_ref, dk_ref, dv_ref, mask_ref, w3_ref, normed_ref, att_ref, branch_ref, far_ref,
     tokens_ref, gain_ref, hidden_ref, gh_ref, ffn_ref, small_ref,
     out_ref, gt_ref, gm_ref, weights_ref, total_ref,
     mine, core_in, x_in, up_in, down_in, all_w, y_out, y_in, own_part, ffn_in, mask_in,
@@ -1018,12 +1036,16 @@
     fill(tn(dq_ref[...], normed_ref[...])[: plan.cols], 0)
     fill(tn(dk_ref[...], normed_ref[...])[: plan.cols], 1)
     fill(tn(dv_ref[...], normed_ref[...])[64:], 2)
-    fill(tn(att_ref[...], branch_ref[...])[64:], 3)
+    our_rows = pl.ds(pl.multiple_of(wa * half, half), half)
+    their_rows = pl.ds(pl.multiple_of((1 - wa) * half, half), half)
+    fill(
+        (tn(att_ref[our_rows, :], branch_ref[...]) + tn(att_ref[their_rows, :], far_ref[...]))[64:],
+        3,
+    )
     core_copy = send(
         mine.at[:, :, 1 - core], core_in, core_sem.at[0, 0], core_sem.at[1, 0], spot.core_mate()
     )
     core_copy.start()
-    their_rows = pl.ds(pl.multiple_of((1 - wa) * half, half), half)
     ffn_copy = send(
         ffn_ref.at[their_rows], ffn_in, y_sem.at[0, 3], y_sem.at[1, 3], spot.y_mate()
     )
@@ -1250,7 +1272,7 @@
 
 def finish(plan, cycle_size, *operands):
     lines = cycle_size // 4
-    half, model = operands[8].shape
+    half, model = operands[9].shape
     rows = 4 * plan.cols // cycle_size
     dma = pltpu.SemaphoreType.DMA
     return pl.pallas_call(
@@ -1303,20 +1325,33 @@
 
 
 def middle_kernel(
-    plan, cycle_size, att_ref, mixed_ref, wout_ref, tokens_ref, cot_ref, gain_ref,
-    wg_hbm, wu_hbm, wd_hbm,
-    hidden_ref, gh_ref, branch_ref, ffn_ref, do_ref, gain_part_ref, stack_hbm,
-    wg, wu, wd, inner, gg, gu, x_ref, a_out, a_in, d_out, d_in, acc_f, acc_g, own_g, rows_buf,
-    load_sem, y_sem, out_sem,
+    plan, cycle_size, att_ref, mixed_ref, tokens_ref, cot_ref, gain_ref,
+    wo_hbm, wo_far_hbm, wg_hbm, wu_hbm, wd_hbm,
+    hidden_ref, gh_ref, branch_ref, ffn_ref, do_ref, gain_part_ref, *refs,
 ):
+    stacks, refs = (refs[:3], refs[3:])
+    (
+        wg, wu, wd, wo, inner, gg, gu, x_ref, att_in, d_out, d_in, e_out, e_in,
+        acc_f, acc_g, rows_buf, load_sem, y_sem, out_sem,
+    ) = refs
     spot = Spot(cycle_size // 4)
     wa = spot.wa
-    half, model = tokens_ref.shape
+    pair, model = tokens_ref.shape
+    half = pair // 2
     units = wd.shape[1]
     chunk = half // 4
+    block = pair // 4
     loads = [
         pltpu.make_async_copy(src, dst, load_sem.at[i])
-        for i, (src, dst) in enumerate(((wg_hbm, wg), (wu_hbm, wu), (wd_hbm, wd)))
+        for i, (src, dst) in enumerate(
+            (
+                (wo_hbm, wo.at[0, 64:]),
+                (wo_far_hbm, wo.at[1, 64:]),
+                (wg_hbm, wg),
+                (wu_hbm, wu),
+                (wd_hbm, wd),
+            )
+        )
     ]
     for load in loads:
         load.start()
@@ -1324,6 +1359,7 @@
     pl.semaphore_signal(
         barrier, inc=1, device_id=spot.y_mate(), device_id_type=pl.DeviceIdType.MESH
     )
+    wo[:, :64, :] = jnp.zeros((2, 64, model), bf16)
     pl.semaphore_wait(barrier, 1)
     ours = wa * half
     theirs = (1 - wa) * half
@@ -1331,55 +1367,32 @@
     def rows_at(start, size):
         return pl.ds(pl.multiple_of(start, size), size)
 
-    def a_copy(i):
-        return send(a_out.at[i], a_in.at[i], y_sem.at[0, i], y_sem.at[1, i], spot.y_mate())
-
-    def d_copy(i):
-        return send(
-            d_out.at[i], d_in.at[i], y_sem.at[0, 4 + i], y_sem.at[1, 4 + i], spot.y_mate()
-        )
-
-    def b_copy(i, base):
-        at = rows_at(base + i * chunk, chunk)
-        return send(
-            x_ref.at[at], x_ref.at[at], y_sem.at[0, 8 + i], y_sem.at[1, 8 + i], spot.y_mate()
-        )
-
-    def e_copy(i, base):
-        at = rows_at(base + i * chunk, chunk)
-        return send(
-            branch_ref.at[at], branch_ref.at[at], y_sem.at[0, 12 + i], y_sem.at[1, 12 + i],
-            spot.y_mate(),
-        )
-
-    def send_branch(i, unused):
-        a_out[i] = nn(att_ref[rows_at(theirs + i * chunk, chunk), :], wout_ref[...]).astype(bf16)
-        a_copy(i).start()
-        return unused
-
-    lax.fori_loop(0, 4, send_branch, 0)
-
-    def own_branch(i, unused):
-        at = rows_at(i * chunk, chunk)
-        hidden_ref[at, :] = tokens_ref[at, :].astype(f32) + nn(
-            att_ref[rows_at(ours + i * chunk, chunk), :], wout_ref[...]
-        )
-        return unused
-
-    lax.fori_loop(0, 4, own_branch, 0)
-
-    def normal(i, unused):
-        a_copy(i).wait()
-        at = rows_at(i * chunk, chunk)
-        hidden = hidden_ref[at, :] + a_in[i].astype(f32)
-        hidden_ref[at, :] = hidden
+    def a_start(i):
+        return (theirs + i * block) if i < 2 else (ours + (i - 2) * block)
+
+    def a_copy(i, base):
+        at = rows_at(base + (i % 2) * block, block)
+        return send(att_ref.at[at], att_in.at[at], y_sem.at[0, i], y_sem.at[1, i], spot.y_mate())
+
+    order = (0, 1, 2, 3)
+    for i in order:
+        a_copy(i, ours if i < 2 else theirs).start()
+    loads[0].wait()
+    loads[1].wait()
+
+    def normal(i, base, keep):
+        a_copy(i, base).wait_recv()
+        at = rows_at(base + (i % 2) * block, block)
+        branch = nn(att_ref[at, :], wo[0]) + nn(att_in[at, :], wo[1])
+        hidden = tokens_ref[at, :].astype(f32) + branch
+        if keep:
+            hidden_ref[(i % 2) * block : (i % 2 + 1) * block, :] = hidden
         inv = lax.rsqrt(jnp.mean(hidden * hidden, axis=-1, keepdims=True) + eps)
-        x_ref[rows_at(ours + i * chunk, chunk), :] = (hidden * inv * gain_ref[...]).astype(bf16)
-        b_copy(i, ours).start()
-        return unused
-
-    lax.fori_loop(0, 4, normal, 0)
-    for load in loads:
+        x_ref[at, :] = (hidden * inv * gain_ref[...]).astype(bf16)
+
+    normal(0, theirs, False)
+    normal(1, theirs, False)
+    for load in loads[2:]:
         load.wait()
     wide = 256
 
@@ -1413,22 +1426,29 @@
         lax.fori_loop(0, units // wide, tile, 0)
         ffn_ref[rows, :] = acc_f[...].astype(bf16)
 
-    feed(ours)
-    own_g[...] = acc_g[...]
-
-    def b_wait(i, unused):
-        b_copy(i, theirs).wait_recv()
-        return unused
-
-    lax.fori_loop(0, 4, b_wait, 0)
-    feed(theirs)
+    def d_copy(i):
+        return send(
+            d_out.at[i], d_in.at[i], y_sem.at[0, 4 + i], y_sem.at[1, 4 + i], spot.y_mate()
+        )
 
     def send_grad(i, unused):
         d_out[i] = acc_g[rows_at(i * chunk, chunk), :].astype(bf16)
         d_copy(i).start()
         return unused
 
-    lax.fori_loop(0, 4, send_grad, 0)
+    def half_pass(k, unused):
+        base = theirs + k * (ours - theirs)
+        feed(base)
+
+        @pl.when(k == 0)
+        def _():
+            lax.fori_loop(0, 4, send_grad, 0)
+            normal(2, ours, True)
+            normal(3, ours, True)
+
+        return unused
+
+    lax.fori_loop(0, 2, half_pass, 0)
     parts = 2
     span = units // parts
     slices = cycle_size // parts
@@ -1437,9 +1457,7 @@
     def out_copy(n):
         m, p = (n // parts, n % parts)
         return pltpu.make_async_copy(
-            rows_buf.at[n % 2],
-            stack_hbm.at[pl.ds(p * slices, slices), m],
-            out_sem.at[n],
+            rows_buf.at[n % 2], stacks[m].at[pl.ds(p * slices, slices)], out_sem.at[n]
         )
 
     for n in range(3 * parts):
@@ -1456,30 +1474,37 @@
                 rows_buf[n % 2, s, :, c:end] = product[s * size : (s + 1) * size]
         out_copy(n).start()
 
+    def e_copy(i):
+        return send(
+            e_out.at[i], e_in.at[i], y_sem.at[0, 8 + i], y_sem.at[1, 8 + i], spot.y_mate()
+        )
+
     def normal_back(i, total):
         d_copy(i).wait()
         at = rows_at(i * chunk, chunk)
-        grad = own_g[at, :] + d_in[i].astype(f32)
+        grad = acc_g[at, :] + d_in[i].astype(f32)
         hidden = hidden_ref[at, :]
         inv = lax.rsqrt(jnp.mean(hidden * hidden, axis=-1, keepdims=True) + eps)
         scaled = gain_ref[...] * grad
         mean = jnp.mean(hidden * scaled, axis=-1, keepdims=True)
-        pair_at = rows_at(ours + i * chunk, chunk)
         grad_hidden = (
-            cot_ref[pair_at, :].astype(f32) + inv * scaled - hidden * (inv * inv * inv * mean)
+            cot_ref[rows_at(ours + i * chunk, chunk), :].astype(f32)
+            + inv * scaled
+            - hidden * (inv * inv * inv * mean)
         )
         gh_ref[at, :] = grad_hidden
-        branch_ref[pair_at, :] = grad_hidden.astype(bf16)
-        e_copy(i, ours).start()
+        low = grad_hidden.astype(bf16)
+        branch_ref[at, :] = low
+        e_out[i] = nt(low, wo[1]).astype(bf16)
+        e_copy(i).start()
+        do_ref[rows_at(ours + i * chunk, chunk), :] = nt(low, wo[0]).astype(bf16)
         return total + jnp.sum(grad * hidden * inv, axis=0, keepdims=True)
 
     gain_part_ref[...] = lax.fori_loop(0, 4, normal_back, jnp.zeros((1, model), f32))
 
-    def attended_grads(base):
-        rows = rows_at(base, half)
-        lane = lanes_of(half)
-        grad = nt(branch_ref[rows, :], wout_ref[...]).astype(bf16)
-        terms = grad.astype(f32) * mixed_ref[rows, :]
+    def row_terms(at, grad):
+        lane = lanes_of(chunk)
+        terms = grad.astype(f32) * mixed_ref[at, :]
         out = grad
         for h in range(plan.heads):
             row_term = jnp.sum(
@@ -1487,30 +1512,32 @@
             )
             for i, part in enumerate(split3(-row_term)):
                 out = jnp.where(lane == 3 * h + i, part, out)
-        do_ref[rows, :] = out
-
-    attended_grads(ours)
-
-    def e_wait(i, unused):
-        e_copy(i, theirs).wait_recv()
-        return unused
-
-    lax.fori_loop(0, 4, e_wait, 0)
-    attended_grads(theirs)
+        do_ref[at, :] = out
+
+    def own_terms(i, unused):
+        at = rows_at(ours + i * chunk, chunk)
+        row_terms(at, do_ref[at, :])
+        return unused
+
+    lax.fori_loop(0, 4, own_terms, 0)
+
+    def far_terms(i, unused):
+        e_copy(i).wait()
+        row_terms(rows_at(theirs + i * chunk, chunk), e_in[i])
+        return unused
+
+    lax.fori_loop(0, 4, far_terms, 0)
     for n in (3 * parts - 2, 3 * parts - 1):
         out_copy(n).wait()
-
-    def drain(i, unused):
-        b_copy(i, ours).wait_send()
-        e_copy(i, ours).wait_send()
-        return unused
-
-    lax.fori_loop(0, 4, drain, 0)
-
-
-def middle(plan, cycle_size, attended, mixed, w_out, tokens, cot, gain, w_gate, w_up, w_down):
-    half, model = tokens.shape
-    pair = attended.shape[0]
+    for i in order:
+        a_copy(i, ours if i < 2 else theirs).wait_send()
+
+
+def middle(
+    plan, cycle_size, attended, mixed, tokens, cot, gain, w_out, w_out_far, w_gate, w_up, w_down
+):
+    pair, model = tokens.shape
+    half = pair // 2
     units = w_down.shape[0]
     size = units // cycle_size
     chunk = half // 4
@@ -1521,39 +1548,40 @@
         out_shape=[
             jax.ShapeDtypeStruct((half, model), f32),
             jax.ShapeDtypeStruct((half, model), f32),
-            jax.ShapeDtypeStruct((pair, model), bf16),
+            jax.ShapeDtypeStruct((half, model), bf16),
             jax.ShapeDtypeStruct((pair, model), bf16),
             jax.ShapeDtypeStruct((pair, WIDE), bf16),
             jax.ShapeDtypeStruct((1, model), f32),
-            jax.ShapeDtypeStruct((cycle_size, 3, size, model), bf16),
-        ],
-        in_specs=[vmem] * 6 + [hbm] * 3,
-        out_specs=[vmem] * 6 + [hbm],
+        ]
+        + [jax.ShapeDtypeStruct((cycle_size, size, model), bf16)] * 3,
+        in_specs=[vmem] * 5 + [hbm] * 5,
+        out_specs=[vmem] * 6 + [hbm] * 3,
         scratch_shapes=[
             pltpu.VMEM((model, units), bf16),
             pltpu.VMEM((model, units), bf16),
             pltpu.VMEM((model, units), bf16),
+            pltpu.VMEM((2, WIDE, model), bf16),
             pltpu.VMEM((pair, units), bf16),
             pltpu.VMEM((pair, units), bf16),
             pltpu.VMEM((pair, units), bf16),
             pltpu.VMEM((pair, model), bf16),
+            pltpu.VMEM((pair, WIDE), bf16),
             pltpu.VMEM((4, chunk, model), bf16),
             pltpu.VMEM((4, chunk, model), bf16),
-            pltpu.VMEM((4, chunk, model), bf16),
-            pltpu.VMEM((4, chunk, model), bf16),
-            pltpu.VMEM((half, model), f32),
+            pltpu.VMEM((4, chunk, WIDE), bf16),
+            pltpu.VMEM((4, chunk, WIDE), bf16),
             pltpu.VMEM((half, model), f32),
             pltpu.VMEM((half, model), f32),
             pltpu.VMEM((2, cycle_size // 2, size, model), bf16),
-            dma((3,)),
-            dma((2, 16)),
+            dma((5,)),
+            dma((2, 12)),
             dma((6,)),
         ],
         compiler_params=pltpu.CompilerParams(
             vmem_limit_bytes=60 * 2**20, collective_id=3, has_side_effects=True
         ),
         name="feed_forward",
-    )(attended, mixed, w_out, tokens, cot, gain, w_gate, w_up, w_down.T)
+    )(attended, mixed, tokens, cot, gain, w_out, w_out_far, w_gate, w_up, w_down.T)
 
 
 def shards(
@@ -1632,7 +1660,7 @@
         lane == plan.mask_lane, 1.0, ((lane < plan.stat_lane) & ~own_differs).astype(f32)
     ).astype(bf16)
     q_aug = jnp.concatenate([jnp.zeros((pair, 128), bf16), q_aug], axis=1)
-    pair_normed, q_wide, own_kv, kv_all = first(
+    pair_normed, pair_tokens, q_wide, own_kv, kv_all = first(
         plan, cycle_size, reach, tokens, gain_attn[None], q_aug, w_query, w_key, w_value
     )
     kv_all = window(kv_all.reshape(total_rows, 2 * plan.cols))
@@ -1666,27 +1694,28 @@
         name="attention_forward",
     )(bounds, bias_table, kv_all, k_aug, q_wide, near_bias)
     q_all = window(gather(q_back))
-    w_out_pad = jnp.concatenate([jnp.zeros((64, model), bf16), w_out], axis=0)
-    hidden, grad_hidden, pair_branch, ffn_part, do_wide, gain_ffn_part, stacked = middle(
+    swap = functools.partial(lax.ppermute, axis_name="wa", perm=((0, 1), (1, 0)))
+    hidden, grad_hidden, branch, ffn_part, do_wide, gain_ffn_part, *stacks = middle(
         plan,
         cycle_size,
         attended,
         mixed,
-        w_out_pad,
-        tokens,
+        pair_tokens,
         pair_cot,
         gain_ffn[None],
+        w_out,
+        swap(w_out),
         w_gate,
         w_up,
         w_down,
     )
-    units = stacked.shape[2]
-    stacked = lax.psum_scatter(
-        stacked.reshape(-1, model), "ctx", scatter_dimension=0, tiled=True
+    far_branch = swap(branch)
+    do_all = window(gather(do_wide))
+    grad_w_down, grad_w_gate = reduce_scatter(stacks[:2], cycle_size)
+    grad_w_up = lax.psum_scatter(
+        stacks[2].reshape(-1, model), "ctx", scatter_dimension=0, tiled=True
     ).astype(f32)
-    grad_w_down = stacked[:units]
-    grad_w_gate, grad_w_up = (stacked[units : 2 * units].T, stacked[2 * units :].T)
-    do_all = window(gather(do_wide))
+    grad_w_gate, grad_w_up = (grad_w_gate.T, grad_w_up.T)
 
     grad_queries, table_part = pl.pallas_call(
         functools.partial(dq_kernel, plan, rows, pair),
@@ -1748,7 +1777,8 @@
         w_wide,
         pair_normed,
         attended,
-        pair_branch,
+        branch,
+        far_branch,
         tokens,
         gain_attn[None],
         hidden,

time: 480 us -> 490 us (1.021)
  Pallas kernels: 317 us -> 388 us
  waiting for transfers between devices: 77.8 us -> 13.6 us
    pallas_call x0 -> x1, Pallas kernels: none -> 145 us  [reduce_scatter(): pl.pallas_call(functools.partial(scatter_kernel, lines, units, z_first, c...]
    all_gather x1, waiting for transfers between devices: 38.9 us -> 0.01 us  [shards(): do_all = window(gather(do_wide))]
    reduce_scatter x1, waiting for transfers between devices: 38.5 us -> 0.01 us  [shards(): lax.psum_scatter(stacks[2].reshape(-1, model), 'ctx', scatter_dimension=0...]
    pallas_call x1, Pallas kernels: 134 us -> 98.4 us  [finish(): pl.pallas_call(functools.partial(finish_kernel, plan, lines), out_shape=[...]
    pallas_call x1, Pallas kernels: 91.5 us -> 55.8 us  [middle(): pl.pallas_call(functools.partial(middle_kernel, plan, cycle_size), out_sh...]
    ppermute x0 -> x2, waiting for transfers between devices: none -> 13.2 us  [the longest x1 13.2 us: shards(): swap(w_out)]
    unnamed x35 -> x43, local copies, waits for them, and re-layouts: 11.8 us -> 13.8 us
  transfers between devices with their start and end apart: 4 -> 6, of which waited for: 2 -> 1; matrix products, arithmetic and copies ran while one was open for 7% -> 7% of each run, Pallas kernels for 67% -> 80%
where the time goes in v6:
time: 490 us; the launch traced here: 484 us
  Pallas kernels  388 us (79%)
  local copies, waits for them, and re-layouts  31.9 us (7%)
  blocking collectives  23.1 us (5%)
  between operations  14.5 us (3%)
  waiting for transfers between devices  13.6 us (3%)
  other arithmetic  10 us (2%)
    pallas_call x1, Pallas kernels, reduce_scatter(): pl.pallas_call(functools.partial(scatter_kernel, lines, units, z_first, c...  145 us
    pallas_call x1, Pallas kernels, finish(): pl.pallas_call(functools.partial(finish_kernel, plan, lines), out_shape=[...  98.4 us
    pallas_call x1, Pallas kernels, middle(): pl.pallas_call(functools.partial(middle_kernel, plan, cycle_size), out_sh...  55.8 us
    pallas_call x1, Pallas kernels, first(): pl.pallas_call(functools.partial(first_kernel, plan, lines, span), out_sh...  44.2 us
    all_gather x1, blocking collectives, shards(): mask_all = lax.all_gather(key_mask, 'ctx', axis=0, tiled=True)  23.1 us
    pallas_call x1, Pallas kernels, shards(): pl.pallas_call(functools.partial(dq_kernel, plan, rows, pair), out_shape=...  14.2 us
    unnamed x43, local copies, waits for them, and re-layouts  13.8 us
    pallas_call x1, Pallas kernels, shards(): pl.pallas_call(functools.partial(fwd_kernel, plan, rows, pair), out_shape...  13.5 us
  transfers between devices with their start and end apart: 6, of which 1 were waited for; matrix products, arithmetic and copies ran while one was open for 7% of the time, Pallas kernels for 80%

profile of v6, /device:TPU:0, one launch (start us, length us, event | category | flops | bytes accessed | tf_op | source)
XLA Modules:
  0.0 484.0 jit_solution(15436839723464572151)
XLA Ops:
  7.3 2.3 copy.59
  11.5 1.2 copy.56.tokens_ref
  13.5 23.1 %all-gather = bf16[16,1,512]{2,1,0:T(2,128)(2,1)S(1)} all-gather(bf16[1,1,512]{2,1,0:T(2,128)(2,1)S(1)} %reshape.272), channel_id=1, replica_groups=mesh['ctx'=16,'wa'=2] {'ctx'}, dimensions={0}, use_global_device_ids=true | all-gather | bytes 17408 | tf_op jit(solution)/shard_map/all_gather | solution.py:1634
  36.7 5.0 %near_bias.1.near_ref = f32[2,3,256,512]{3,2,1,0:T(8,128)} custom-call(f32[32,3]{1,0:T(8,128)} %copy.60.table_ref), custom_call_target="tpu_custom_call" | custom-call | tf_op jit(solution)/shard_map/near_bias/pallas_call | solution.py:1667
  42.5 0.7 concatenate.16.aug_ref
  43.2 44.2 %project_gather.1 = (bf16[512,1472]{1,0:T(8,128)(2,1)}, bf16[512,1472]{1,0:T(8,128)(2,1)}, bf16[512,256]{1,0:T(8,128)(2,1)}, bf16[512,384]{1,0:T(8,128)(2,1)}, bf16[4,2,2,512,384]{4,3,2,1,0:T(8,128)(2,1)}) custom-call(bf16[256,1472]{1,0:T(8,128)(2,1)} %copy.56.tokens_ref, f32[1,1472]{1,0:T(1,128)} %broadcast_in_dim.109.gain_ref, ...), custom_call_target="tpu_custom_call" | custom-call | tf_op jit(solution)/shard_map/project_gather/pallas_call | solution.py:932
  87.4 4.6 select_convert_fusion.kaug_ref
  92.0 13.5 %attention_forward.1 = (bf16[512,256]{1,0:T(8,128)(2,1)}, f32[512,256]{1,0:T(8,128)}, bf16[512,256]{1,0:T(8,128)(2,1)}) custom-call(s32[5]{0:T(128)} %pad_add_fusion.1.bounds, f32[32,3]{1,0:T(8,128)} %copy.60.table_ref, bf16[8192,384]{1,0:T(8,128)(2,1)} %bitcast.45, bf16[8192,128]{1,0:T(8,128)(2,1)} %select_convert_fusion.kaug_ref, ...), custom_call_target="tpu_custom_call" | custom-call | tf_op jit(solution)/shard_map/attention_forward/pallas_call | solution.py:1677
  106.9 13.2 %collective-permute-done.wo_far_hbm = bf16[192,1472]{1,0:T(8,128)(2,1)S(1)} collective-permute-done((bf16[192,1472]{1,0:T(8,128)(2,1)S(1)}, bf16[192,1472]{1,0:T(8,128)(2,1)S(1)}, u32[]{:S(2)}, u32[]{:S(2)}) %collective-permute-start) | collective-permute-done | bytes 565280 | tf_op jit(solution)/shard_map/ppermute | solution.py:1707
  120.1 0.8 copy-done.9
  120.9 55.8 %feed_forward.1 = (f32[256,1472]{1,0:T(8,128)}, f32[256,1472]{1,0:T(8,128)}, bf16[256,1472]{1,0:T(8,128)(2,1)}, bf16[512,1472]{1,0:T(8,128)(2,1)}, bf16[512,256]...) custom-call(bf16[512,256]{1,0:T(8,128)(2,1)} %get-tuple-element.45.a, ...), custom_call_target="tpu_custom_call" | custom-call | tf_op jit(solution)/shard_map/feed_forward/pallas_call | solution.py:1546
  177.4 0.8 copy-done.1
  178.2 1.1 copy.65
  179.3 1.7 collective-permute-start.1
  182.1 4.3 concatenate.18.w3_ref
  186.4 1.6 constant_dynamic-slice_fusion.kaug_ref
  187.9 14.2 %attention_grad_queries.1 = (bf16[512,256]{1,0:T(8,128)(2,1)}, f32[3,32,128]{2,1,0:T(8,128)}) custom-call(s32[5]{0:T(128)} %pad_add_fusion.1.bounds, f32[32,3]{1,0:T(8,128)} %copy.60.table_ref, bf16[8192,384]{1,0:T(8,128)(2,1)} %bitcast.46, bf16[8192,128]{1,0:T(8,128)(2,1)} %select_convert_fusion.kaug_ref, bf16[512,256]{1,0:T(8,128)(2,1)} %get-tuple-element.44.qb_ref, ...), custom_call_target="tpu_custom_call" | custom-call | tf_op jit(solution)/shard_map/attention_grad_queries/pallas_call | solution.py:1720
  202.2 0.9 reduce_sum.75
  203.1 145.3 %weight_scatter.1 = (f32[112,1472]{1,0:T(8,128)}, f32[112,1472]{1,0:T(8,128)}) custom-call(bf16[4,2,2,112,1472]{4,3,2,1,0:T(8,128)(2,1)} %bitcast.47, bf16[4,2,2,112,1472]{4,3,2,1,0:T(8,128)(2,1)} %bitcast.48), custom_call_target="tpu_custom_call" | custom-call | tf_op jit(solution)/shard_map/weight_scatter/pallas_call | solution.py:652
  348.4 0.7 fusion.3.small_ref
  349.1 2.3 copy.66.far_ref
  351.4 11.6 %attention_grad_keys.1 = (bf16[512,256]{1,0:T(8,128)(2,1)}, bf16[512,256]{1,0:T(8,128)(2,1)}, f32[2,8,256]{2,1,0:T(8,128)}) custom-call(s32[5]{0:T(128)} %pad_add_fusion.1.bounds, f32[32,3]{1,0:T(8,128)} %copy.60.table_ref, bf16[8192,256]{1,0:T(8,128)(2,1)} %all-gather.7.cloned.1.call-done.qall_ref, ...), custom_call_target="tpu_custom_call" | custom-call | tf_op jit(solution)/shard_map/attention_grad_keys/pallas_call | solution.py:1741
  363.0 98.4 %finish.1 = (bf16[256,1472]{1,0:T(8,128)(2,1)}, f32[256,1472]{1,0:T(8,128)}, f32[8,256]{1,0:T(8,128)}, bf16[4,2,2,48,1472]{4,3,2,1,0:T(8,128)(2,1)}, f32[8,1472]{1,0:T(8,128)}) custom-call(bf16[512,256]{1,0:T(8,128)(2,1)} %get-tuple-element.49.dq_ref, bf16[512,256]{1,0:T(8,128)(2,1)} %get-tuple-element.51.dk_ref, bf16[512,256]{1,0:T(8,128)(2,1)} %get-tuple-element.52.dv_ref, ...), custom_call_target="tpu_custom_call" | custom-call | tf_op jit(solution)/shard_map/finish/pallas_call | solution.py:1278
  461.4 2.4 copy.68
  463.9 3.0 copy.69
  466.8 1.3 slice.28
  468.1 0.7 slice_reduce_fusion.2
  469.5 1.5 slice_reduce_fusion
  471.0 2.4 fusion.18
  473.4 2.0 convert_bitcast_fusion
  475.3 0.8 copy.72
  476.2 0.8 copy.73
  (83 shorter events, 7.2 us)
Async XLA Ops:
  7.2 2.6 copy-start.15
  7.2 3.6 copy-start.13
  7.2 4.3 copy-start.5
  7.2 5.5 %copy-start.10 = (f32[1472]{0:T(1024)S(1)}, f32[1472]{0:T(1024)}, u32[]{:S(2)}) copy-start(f32[1472]{0:T(1024)} %param.17) | copy-start | bytes 17668
  7.2 6.3 %copy-start.14 = (bf16[512]{0:T(512)(128)(2,1)S(1)}, bf16[512]{0:T(512)(128)(2,1)}, u32[]{:S(2)}) copy-start(bf16[512]{0:T(512)(128)(2,1)} %param.16) | copy-start | bytes 3076
  7.2 112.9 %all-gather.5.cloned.1.call-start = ((), (), s32[]{:S(2)}) async-start(), calls=%async_computation.1 | async-start | bytes 2359296 | tf_op jit(solution)/shard_map/all_gather | solution.py:1635
  9.6 341.8 %all-gather.7.cloned.1.call-start = ((), (), s32[]{:S(2)}) async-start(), calls=%async_computation.2 | async-start | bytes 4456448 | tf_op jit(solution)/shard_map/all_gather | solution.py:1696
  92.0 13.7 %copy-start.8 = (bf16[192,1472]{1,0:T(8,128)(2,1)S(1)}, bf16[192,1472]{1,0:T(8,128)(2,1)}, u32[]{:S(2)}) copy-start(bf16[192,1472]{1,0:T(8,128)(2,1)} %wo_hbm.1) | copy-start | bytes 1695748
  92.0 14.3 %copy-start.11 = (f32[1472]{0:T(1024)S(1)}, f32[1472]{0:T(1024)}, u32[]{:S(2)}) copy-start(f32[1472]{0:T(1024)} %param.23) | copy-start | bytes 17668
  105.5 245.9 %all-gather.9.cloned.1.call-start = ((), (), s32[]{:S(2)}) async-start(), calls=%async_computation.3 | async-start | bytes 4456448 | tf_op jit(solution)/shard_map/all_gather | solution.py:1713
  105.7 14.4 %collective-permute-start = (bf16[192,1472]{1,0:T(8,128)(2,1)S(1)}, bf16[192,1472]{1,0:T(8,128)(2,1)S(1)}, u32[]{:S(2)}, u32[]{:S(2)}) collective-permute-start(bf16[192,1472]{1,0:T(8,128)(2,1)S(1)} %copy-done.8), channel_id=1, source_target_pairs={{0,1},{1,0},{2,3},{3,2},{4,5},{5,4},{6,7},{7,6},{8,9},{9,8},{10,11... | collective-permute-start | bytes 1695752 | tf_op jit(solution)/shard_map/ppermute | solution.py:1707
  120.1 0.8 copy-start.9
  176.8 296.6 %reduce-scatter.2.cloned.1.call-start = ((), (), s32[]{:S(2)}) async-start(), calls=%async_computation.4 | async-start | bytes 5849088 | tf_op jit(solution)/shard_map/reduce_scatter | solution.py:1715
  177.0 1.1 copy-start.1
  177.0 4.0 copy-start.2
  177.3 4.0 copy-start.3
  177.3 4.2 copy-start.4
  179.3 169.8 %collective-permute-start.1 = (bf16[256,1472]{0,1:T(8,128)(2,1)}, bf16[256,1472]{0,1:T(8,128)(2,1)}, u32[]{:S(2)}, u32[]{:S(2)}) collective-permute-start(bf16[256,1472]{0,1:T(8,128)(2,1)} %copy.65), channel_id=1, source_target_pairs={{0,1},{1,0},{2,3},{3,2},{4,5},{5,4},{6,7},{7,6},{8,9},{9,8},{10,11... | collective-permute-start | bytes 2261000 | tf_op jit(solution)/shard_map/ppermute | solution.py:1712
  203.1 145.3 %copy-start.12 = (f32[1,1472]{1,0:T(1,128)S(1)}, f32[1,1472]{1,0:T(1,128)}, u32[]{:S(2)}) copy-start(f32[1,1472]{1,0:T(1,128)} %get-tuple-element.59) | copy-start | bytes 17668
  461.4 9.5 %copy-start = (bf16[4,2,2,48,1472]{4,3,2,1,0:T(8,128)(2,1)S(1)}, bf16[4,2,2,48,1472]{4,3,2,1,0:T(8,128)(2,1)}, u32[]{:S(2)}) copy-start(bf16[4,2,2,48,1472]{4,3,2,1,0:T(8,128)(2,1)} %get-tuple-element.65) | copy-start | bytes 6782980
  471.0 4.4 copy-start.7
  473.4 2.8 copy-start.6
Sparse Core Ops, SparseCore 0:
  10.2 29.9 all-gather.4
  105.6 64.4 all-gather.6
  176.9 67.6 all-gather.8
  248.3 98.8 reduce-scatter.1

commit v7 on v6

--- a/solution.py
+++ b/solution.py
@@ -91,7 +91,7 @@
     return lax.broadcasted_iota(jnp.int32, (rows, width), 1)
 
 
-def near_kernel(heads, table_ref, near_ref):
+def near_lanes(heads, table_ref, near_ref):
     row = lax.broadcasted_iota(jnp.int32, (EDGE, 3 * EDGE), 0)
     col = lax.broadcasted_iota(jnp.int32, (EDGE, 3 * EDGE), 1)
     relative = col - EDGE - row
@@ -112,7 +112,11 @@
             near_ref[flip, h, EDGE:, :EDGE] = far_l
 
 
-def build_keys(plan, g_ref, kaug_ref, km, vm, rows):
+def build_keys(plan, g_ref, kaug_ref, masks_ref, km, vm, mask_row, rows):
+    mask_row[...] = jnp.zeros_like(mask_row)
+    size = masks_ref.shape[2]
+    for n in range(masks_ref.shape[0]):
+        mask_row[:, PAD + n * size : PAD + (n + 1) * size] = masks_ref[n]
     km[:PAD, :] = jnp.broadcast_to(
         jnp.where(pad_lanes(plan), neg_big, 0.0).astype(bf16), (PAD, WIDE)
     )
@@ -142,10 +146,10 @@
 
 
 def fwd_kernel(
-    plan, rows, pair, bounds, table_ref, g_ref, kaug_ref, q_ref, near_ref,
-    low_ref, wide_ref, qb_ref, km, vm, acc, row_max, qh_ref,
+    plan, rows, pair, bounds, table_ref, g_ref, kaug_ref, masks_ref, q_ref, near_ref,
+    low_ref, wide_ref, qb_ref, km, vm, mask_row, acc, row_max, qh_ref,
 ):
-    build_keys(plan, g_ref, kaug_ref, km, vm, rows)
+    build_keys(plan, g_ref, kaug_ref, masks_ref, km, vm, mask_row, rows)
     lane = lanes_of(TQ)
 
     def tile(t, unused):
@@ -157,7 +161,7 @@
         for h in range(plan.heads):
             qh = jnp.where(plan.key_lanes(lane, h), q, jnp.zeros_like(q))
             qh_ref[h] = qh
-            s = nt(qh, km[near, :]) + near_ref[0, h]
+            s = nt(qh, km[near, :]) + near_ref[0, h] + mask_row[0:1, near]
             top = jnp.max(s, axis=1, keepdims=True)
             p = jnp.exp(s - top).astype(bf16)
             acc[h] = nn(p, vm[near, :])
@@ -167,7 +171,7 @@
             def step(first, n):
                 span = pl.ds(pl.multiple_of(first + n, 128), TK)
                 for h in range(plan.heads):
-                    s = nt(qh_ref[h], km[span, :])
+                    s = nt(qh_ref[h], km[span, :]) + mask_row[0:1, span]
                     offset = table_ref[bucket, h]
                     old = row_max[h][:, :1]
                     top = jnp.maximum(old, jnp.max(s, axis=1, keepdims=True) + offset)
@@ -203,10 +207,10 @@
 
 
 def dq_kernel(
-    plan, rows, pair, bounds, table_ref, g_ref, kaug_ref, qb_ref, do_ref, near_ref,
-    dq_ref, tab_ref, km, vm, acc, qh_ref, doh_ref, near_acc, far_acc,
+    plan, rows, pair, bounds, table_ref, g_ref, kaug_ref, masks_ref, qb_ref, do_ref, near_ref,
+    dq_ref, tab_ref, km, vm, mask_row, acc, qh_ref, doh_ref, near_acc, far_acc,
 ):
-    build_keys(plan, g_ref, kaug_ref, km, vm, rows)
+    build_keys(plan, g_ref, kaug_ref, masks_ref, km, vm, mask_row, rows)
     lane = lanes_of(TQ)
     near_acc[...] = jnp.zeros_like(near_acc)
     far_acc[...] = jnp.zeros_like(far_acc)
@@ -226,7 +230,9 @@
         for h in range(plan.heads):
             qh_ref[h] = jnp.where(plan.key_lanes(lane, h), q, jnp.zeros_like(q))
             doh_ref[h] = jnp.where(plan.value_lanes(lane, h), do, jnp.zeros_like(do))
-            ds = grads(h, nt(qh_ref[h], km[near, :]) + near_ref[0, h], near)
+            ds = grads(
+                h, nt(qh_ref[h], km[near, :]) + near_ref[0, h] + mask_row[0:1, near], near
+            )
             near_acc[h] += ds
             acc[h] = nn(ds.astype(bf16), km[near, :])
 
@@ -234,7 +240,8 @@
             def step(first, n):
                 span = pl.ds(pl.multiple_of(first + n, 128), TK)
                 for h in range(plan.heads):
-                    ds = grads(h, nt(qh_ref[h], km[span, :]) + table_ref[bucket, h], span)
+                    offset = mask_row[0:1, span] + table_ref[bucket, h]
+                    ds = grads(h, nt(qh_ref[h], km[span, :]) + offset, span)
                     acc[h] += nn(ds.astype(bf16), km[span, :])
                     far_acc[slot, h] += (
                         ds[:, 0:128] + ds[:, 128:256] + ds[:, 256:384] + ds[:, 384:512]
@@ -437,7 +444,7 @@
 
 
 def added(a, b):
-    return (a.astype(f32) + b.astype(f32)).astype(bf16)
+    return a + b
 
 
 def scatter_kernel(lines, units, z_first, count, *refs):
@@ -529,25 +536,28 @@
                     for copy in slot_copies(-1, d):
                         copy.start()
 
-        def relay():
-            def body(k, unused):
-                high = lines - 1 - k
-
-                @pl.when((z < high) & (z > 0))
-                def _():
-                    receive(1, high)
-                    for copy in slot_copies(1, high):
+        def relay(lag):
+            top = lines - 2 if lag == 2 else lag
+
+            @pl.when((z >= lag) & (z <= top))
+            def _():
+                def up(k, unused):
+                    receive(1, lines - 1 - k)
+                    for copy in slot_copies(1, lines - 1 - k):
                         copy.start()
-
-                @pl.when((z > k) & (z + 1 < lines))
-                def _():
+                    return unused
+
+                lax.fori_loop(0, lines - 1 - z, up, 0)
+
+            @pl.when((lines - 1 - z >= lag) & (lines - 1 - z <= top))
+            def _():
+                def down(k, unused):
                     receive(-1, k)
                     for copy in slot_copies(-1, k):
                         copy.start()
-
-                return unused
-
-            lax.fori_loop(0, lines - 1, body, 0)
+                    return unused
+
+                lax.fori_loop(0, z, down, 0)
 
         def arrive():
             @pl.when(z > 0)
@@ -618,16 +628,17 @@
         else:
             store(u)
 
-    for t in range(len(order) + 2):
+    for t in range(len(order) + 3):
         if t < len(order):
             u = order[t]
             if u not in z_first:
                 x_stage(u)
             flows[u][0]()
-        if 0 <= t - 1 < len(order):
-            flows[order[t - 1]][1]()
-        if 0 <= t - 2 < len(order):
-            settle(order[t - 2])
+        for lag in (1, 2):
+            if 0 <= t - lag < len(order):
+                flows[order[t - lag]][1](lag)
+        if 0 <= t - 3 < len(order):
+            settle(order[t - 3])
     for u, copy in last.items():
         m = units[u][0]
         copy.wait()
@@ -673,8 +684,9 @@
     )(*shaped)
 
 def first_kernel(
-    plan, lines, span, tokens_ref, gain_ref, aug_ref, wq_hbm, wk_hbm, wv_hbm,
-    x_ref, tok_ref, q_ref, own_ref, all_hbm,
+    plan, lines, span, reach, rows, starts, table_ref, tokens_ref, gain_ref, mask_ref,
+    wq_hbm, wk_hbm, wv_hbm, wo_hbm,
+    x_ref, tok_ref, q_ref, own_ref, aug_ref, own_aug_ref, near_ref, masks_ref, wo_far_hbm, all_hbm,
     weights, zeros, load_sem, y_sem, own_sem, zero_sem, z_sem, x_sem, c_sem,
 ):
     spot = Spot(lines)
@@ -704,6 +716,7 @@
     def zero_start(d, unused):
         @pl.when(outside(d))
         def _():
+            masks_ref[d] = jnp.zeros((2, 2) + mask_ref.shape, f32)
             for copy in zero_copies(d):
                 copy.start()
 
@@ -729,6 +742,8 @@
         return unused
 
     lax.fori_loop(0, 4, y_start, 0)
+    far_copy = send(wo_hbm, wo_far_hbm, y_sem.at[0, 4], y_sem.at[1, 4], spot.y_mate())
+    far_copy.start()
 
     def scaled(rows_in):
         rows_in = rows_in.astype(f32)
@@ -750,26 +765,35 @@
         rows = rows_at(base, half)
         qkv = nt(x_ref[rows, :], weights[...]).astype(bf16)
         own_ref[rows, :] = qkv[:, : 2 * cols]
-        q_ref[rows, :] = aug_ref[rows, :]
         q_ref[rows, :cols] = qkv[:, 2 * cols :]
 
     pieces = [
         (ours, half, True),
         (theirs, half // 2, True),
         (theirs + half // 2, half // 2, False),
+        None,
     ]
+    mask_piece = 3
+
+    def line_first(p):
+        return p == mask_piece or pieces[p][2]
 
     def piece_rows(p):
         return rows_at(pieces[p][0], pieces[p][1])
 
     def source(p, d, a):
+        if p == mask_piece:
+            return masks_ref.at[d, a, core]
         return all_hbm.at[d, a, core, piece_rows(p)]
+
+    def own_source(p):
+        return mask_ref if p == mask_piece else own_ref.at[piece_rows(p)]
 
     def pass_copy(p, step, d, own):
         i = 0 if step > 0 else 1
-        if pieces[p][2]:
+        if line_first(p):
             dst = source(p, d, x)
-            src = own_ref.at[piece_rows(p)] if own else dst
+            src = own_source(p) if own else dst
         else:
             dst = all_hbm.at[d, :, core, piece_rows(p)]
             src = dst
@@ -777,16 +801,19 @@
 
     def across(p, d, own):
         dst = source(p, d, x)
-        src = own_ref.at[piece_rows(p)] if own else dst
+        src = own_source(p) if own else dst
         return send(src, dst, x_sem.at[p, 0, d], x_sem.at[p, 1, d], spot.x_mate())
 
     def beside(p, d):
-        part = all_hbm.at[d, :, core, piece_rows(p)]
+        if p == mask_piece:
+            part = masks_ref.at[d, :, core]
+        else:
+            part = all_hbm.at[d, :, core, piece_rows(p)]
         return send(part, part, c_sem.at[p, 0, d], c_sem.at[p, 1, d], spot.core_mate())
 
     def own_copy(p):
         return pltpu.make_async_copy(
-            own_ref.at[piece_rows(p)], source(p, z, x), own_sem.at[p]
+            own_source(p), source(p, z, x), own_sem.at[p]
         )
 
     def both_ways(p, own):
@@ -801,7 +828,7 @@
     def begin(p):
         own_copy(p).start()
         across(p, z, True).start()
-        if pieces[p][2]:
+        if line_first(p):
             both_ways(p, True)
 
     def level(p, k):
@@ -815,7 +842,7 @@
                 def _():
                     pass_copy(p, 1, d, False).start()
 
-            if pieces[p][2]:
+            if line_first(p):
                 across(p, d, False).start()
             else:
                 beside(p, d).start()
@@ -830,7 +857,7 @@
                 def _():
                     pass_copy(p, -1, d, False).start()
 
-            if pieces[p][2]:
+            if line_first(p):
                 across(p, d, False).start()
             else:
                 beside(p, d).start()
@@ -853,9 +880,58 @@
                     own_copy(p).wait()
                 beside(p, d).start()
 
+    def doc_of(start, size):
+        position = start + lax.broadcasted_iota(jnp.int32, (size, 128), 0)
+
+        def count(e, total):
+            return total + (position >= starts[e]).astype(jnp.int32)
+
+        return lax.fori_loop(1, starts.shape[0], count, jnp.zeros((size, 128), jnp.int32))
+
+    def code_lanes(start, size):
+        lane = lanes_of(size, 128) + 128
+        code = jnp.maximum(lane - plan.doc_lane, 0)
+        bit = jnp.bitwise_and(jnp.right_shift(doc_of(start, size), code // 2), 1)
+        coded = (lane >= plan.doc_lane) & (lane < plan.stat_lane)
+        ones = (lane >= plan.stat_lane) & (lane < plan.stat_lane + 3 * plan.heads)
+        return lane, coded, bit != code % 2, ones
+
+    pair = 2 * half
+    base = spot.index * pair
+    origin = jnp.clip(base - reach * pair, 0, 4 * lines * pair - rows)
+
+    def key_lanes(n, unused):
+        at = rows_at(n * half, half)
+        lane, coded, differs, ones = code_lanes(origin + n * half, half)
+        aug_ref[at, :] = jnp.where(
+            coded & differs, neg_big, jnp.where(ones, 1.0, 0.0)
+        ).astype(bf16)
+        return unused
+
+    def own_lanes(n, unused):
+        at = rows_at(n * half, half)
+        lane, coded, differs, ones = code_lanes(base + n * half, half)
+        column = jnp.transpose(
+            jnp.broadcast_to(mask_ref[0:1, at], (128, half))
+        )
+        own_aug_ref[at, :] = jnp.where(
+            lane == plan.mask_lane,
+            column,
+            jnp.where(coded & differs, neg_big, jnp.where(ones, 1.0, 0.0)),
+        ).astype(bf16)
+        tail = jnp.where(
+            (lane == plan.mask_lane) | (coded & ~differs), 1.0, 0.0
+        ).astype(bf16)
+        q_ref[at, 128:] = tail
+        return unused
+
+    begin(mask_piece)
+    lax.fori_loop(0, 2, own_lanes, 0)
     project(ours)
     begin(0)
     lax.fori_loop(0, lines, zero_start, 0)
+    near_lanes(plan.heads, table_ref, near_ref)
+    lax.fori_loop(0, rows // half, key_lanes, 0)
 
     def y_wait(i, unused):
         y_copy(i, theirs).wait_recv()
@@ -865,35 +941,40 @@
 
     lax.fori_loop(0, 2, y_wait, 0)
     level(0, 1)
+    level(mask_piece, 1)
     lax.fori_loop(2, 4, y_wait, 0)
     project(theirs)
     begin(2)
     begin(1)
     if span > 1:
         level(0, 2)
+        level(mask_piece, 2)
     settle(0, 0)
+    settle(mask_piece, 0)
     turn(2)
     level(1, 1)
     settle(0, 1)
+    settle(mask_piece, 1)
     level(2, 1)
     if span > 1:
         level(1, 2)
         settle(0, 2)
+        settle(mask_piece, 2)
     settle(1, 0)
     settle(1, 1)
     if span > 1:
         level(2, 2)
         settle(1, 2)
     for k in range(3, span + 1):
-        for p in range(3):
+        for p in range(4):
             level(p, k)
-        for p in range(2):
+        for p in (0, 1, mask_piece):
             settle(p, k)
 
     def finish_line(d, unused):
         @pl.when(~outside(d))
         def _():
-            for p in range(3):
+            for p in range(4):
                 beside(p, d).wait()
 
         @pl.when(outside(d))
@@ -901,7 +982,7 @@
             for copy in zero_copies(d):
                 copy.wait()
 
-        for p in range(3):
+        for p in range(4):
 
             @pl.when((z + 1 < lines) & (d <= z) & (d > z - span))
             def _(p=p):
@@ -920,9 +1001,12 @@
         return unused
 
     lax.fori_loop(0, 4, y_drain, 0)
-
-
-def first(plan, cycle_size, reach, tokens, gain, aug, w_query, w_key, w_value):
+    far_copy.wait()
+
+
+def first(
+    plan, cycle_size, reach, rows, starts, table, tokens, gain, mask, w_query, w_key, w_value, w_out
+):
     lines = cycle_size // 4
     span = min(lines - 1, (reach + 3) // 4)
     half, model = tokens.shape
@@ -930,32 +1014,37 @@
     hbm = pl.BlockSpec(memory_space=pl.ANY)
     dma = pltpu.SemaphoreType.DMA
     return pl.pallas_call(
-        functools.partial(first_kernel, plan, lines, span),
+        functools.partial(first_kernel, plan, lines, span, reach, rows),
         out_shape=[
             jax.ShapeDtypeStruct((pair, model), bf16),
             jax.ShapeDtypeStruct((pair, model), bf16),
             jax.ShapeDtypeStruct((pair, WIDE), bf16),
             jax.ShapeDtypeStruct((pair, 2 * plan.cols), bf16),
+            jax.ShapeDtypeStruct((rows, 128), bf16),
+            jax.ShapeDtypeStruct((pair, 128), bf16),
+            jax.ShapeDtypeStruct((2, plan.heads, TQ, TK), f32),
+            jax.ShapeDtypeStruct((lines, 2, 2, 8, pair), f32),
+            jax.ShapeDtypeStruct(w_out.shape, bf16),
             jax.ShapeDtypeStruct((lines, 2, 2, pair, 2 * plan.cols), bf16),
         ],
-        in_specs=[vmem] * 3 + [hbm] * 3,
-        out_specs=[vmem] * 4 + [hbm],
+        in_specs=[smem] * 2 + [vmem] * 3 + [hbm] * 4,
+        out_specs=[vmem] * 8 + [hbm] * 2,
         scratch_shapes=[
             pltpu.VMEM((3 * plan.cols, model), bf16),
             pltpu.VMEM((pair, 2 * plan.cols), bf16),
             dma((3,)),
-            dma((2, 4)),
-            dma((3,)),
+            dma((2, 5)),
+            dma((4,)),
             dma((lines, 2, 2)),
-            dma((3, 4, lines)),
-            dma((3, 2, lines)),
-            dma((3, 2, lines)),
+            dma((4, 4, lines)),
+            dma((4, 2, lines)),
+            dma((4, 2, lines)),
         ],
         compiler_params=pltpu.CompilerParams(
             vmem_limit_bytes=56 * 2**20, collective_id=4, has_side_effects=True
         ),
         name="project_gather",
-    )(tokens, gain, aug, w_query.T, w_key.T, w_value.T)
+    )(starts, table, tokens, gain, mask, w_query.T, w_key.T, w_value.T, w_out)
 
 
 def tn(a, b):
@@ -1631,7 +1720,6 @@
         [(base - origin)[None], jnp.stack([n_left, n_right], axis=1).reshape(-1)]
     ).astype(jnp.int32)
 
-    mask_all = lax.all_gather(key_mask, "ctx", axis=0, tiled=True)
     pair_cot = lax.all_gather(cotangent, "wa", axis=0, tiled=True)
 
     def window(gathered):
@@ -1640,39 +1728,27 @@
         return lax.dynamic_slice_in_dim(gathered, origin, rows, 0)
 
     gather = functools.partial(lax.all_gather, axis_name="ctx", axis=0, tiled=True)
-    positions = origin + jnp.arange(rows, dtype=jnp.int32)
-    doc_of = doc_at(positions)
-    lane = jnp.arange(128, dtype=jnp.int32)[None, :] + 128
-    code = lane - plan.doc_lane
-    bit_differs = ((doc_of[:, None] >> (code >> 1)) & 1) != (code & 1)
-    k_aug = jnp.where(
-        lane == plan.mask_lane,
-        window(mask_all).astype(f32)[:, None],
-        jnp.where(
-            lane < plan.stat_lane,
-            jnp.where(bit_differs & (code >= 0), neg_big, 0.0),
-            (lane < plan.stat_lane + 3 * heads).astype(f32),
-        ),
-    ).astype(bf16)
-    own_docs = doc_at(base + jnp.arange(pair, dtype=jnp.int32))
-    own_differs = ((own_docs[:, None] >> (code >> 1)) & 1) != (code & 1)
-    q_aug = jnp.where(
-        lane == plan.mask_lane, 1.0, ((lane < plan.stat_lane) & ~own_differs).astype(f32)
-    ).astype(bf16)
-    q_aug = jnp.concatenate([jnp.zeros((pair, 128), bf16), q_aug], axis=1)
-    pair_normed, pair_tokens, q_wide, own_kv, kv_all = first(
-        plan, cycle_size, reach, tokens, gain_attn[None], q_aug, w_query, w_key, w_value
+    (
+        pair_normed, pair_tokens, q_wide, own_kv, k_aug, own_aug, near_bias, masks, far_out, kv_all,
+    ) = first(
+        plan,
+        cycle_size,
+        reach,
+        rows,
+        starts,
+        bias_table,
+        tokens,
+        gain_attn[None],
+        jnp.broadcast_to(key_mask.astype(f32)[None], (8, pair)),
+        w_query,
+        w_key,
+        w_value,
+        w_out,
     )
+    masks = masks.reshape(cycle_size, 8, pair)
+    if rows < total_rows:
+        masks = lax.dynamic_slice_in_dim(masks, origin // pair, rows // pair, 0)
     kv_all = window(kv_all.reshape(total_rows, 2 * plan.cols))
-    near_bias = pl.pallas_call(
-        functools.partial(near_kernel, heads),
-        out_shape=jax.ShapeDtypeStruct((2, heads, TQ, TK), f32),
-        in_specs=[smem],
-        out_specs=vmem,
-        compiler_params=params(),
-        name="near_bias",
-    )(bias_table)
-
     padded = rows + 2 * PAD
     attended, mixed, q_back = pl.pallas_call(
         functools.partial(fwd_kernel, plan, rows, pair),
@@ -1681,18 +1757,19 @@
             jax.ShapeDtypeStruct((pair, WIDE), f32),
             jax.ShapeDtypeStruct((pair, WIDE), bf16),
         ),
-        in_specs=[smem, smem, vmem, vmem, vmem, vmem],
+        in_specs=[smem, smem] + [vmem] * 5,
         out_specs=(vmem, vmem, vmem),
         scratch_shapes=[
             pltpu.VMEM((padded, WIDE), bf16),
             pltpu.VMEM((padded, WIDE), bf16),
+            pltpu.VMEM((8, padded), f32),
             pltpu.VMEM((heads, TQ, WIDE), f32),
             pltpu.VMEM((heads, TQ, 128), f32),
             pltpu.VMEM((heads, TQ, WIDE), bf16),
         ],
         compiler_params=params(),
         name="attention_forward",
-    )(bounds, bias_table, kv_all, k_aug, q_wide, near_bias)
+    )(bounds, bias_table, kv_all, k_aug, masks, q_wide, near_bias)
     q_all = window(gather(q_back))
     swap = functools.partial(lax.ppermute, axis_name="wa", perm=((0, 1), (1, 0)))
     hidden, grad_hidden, branch, ffn_part, do_wide, gain_ffn_part, *stacks = middle(
@@ -1704,17 +1781,14 @@
         pair_cot,
         gain_ffn[None],
         w_out,
-        swap(w_out),
+        far_out,
         w_gate,
         w_up,
         w_down,
     )
     far_branch = swap(branch)
     do_all = window(gather(do_wide))
-    grad_w_down, grad_w_gate = reduce_scatter(stacks[:2], cycle_size)
-    grad_w_up = lax.psum_scatter(
-        stacks[2].reshape(-1, model), "ctx", scatter_dimension=0, tiled=True
-    ).astype(f32)
+    grad_w_down, grad_w_gate, grad_w_up = reduce_scatter(stacks, cycle_size)
     grad_w_gate, grad_w_up = (grad_w_gate.T, grad_w_up.T)
 
     grad_queries, table_part = pl.pallas_call(
@@ -1723,11 +1797,12 @@
             jax.ShapeDtypeStruct((pair, WIDE), bf16),
             jax.ShapeDtypeStruct((heads, 32, 128), f32),
         ),
-        in_specs=[smem, smem, vmem, vmem, vmem, vmem, vmem],
+        in_specs=[smem, smem] + [vmem] * 6,
         out_specs=(vmem, vmem),
         scratch_shapes=[
             pltpu.VMEM((padded, WIDE), bf16),
             pltpu.VMEM((padded, WIDE), bf16),
+            pltpu.VMEM((8, padded), f32),
             pltpu.VMEM((heads, TQ, WIDE), f32),
             pltpu.VMEM((heads, TQ, WIDE), bf16),
             pltpu.VMEM((heads, TQ, WIDE), bf16),
@@ -1736,8 +1811,7 @@
         ],
         compiler_params=params(),
         name="attention_grad_queries",
-    )(bounds, bias_table, kv_all, k_aug, q_back, do_wide, near_bias)
-    own_aug = lax.dynamic_slice_in_dim(k_aug, base - origin, pair, 0)
+    )(bounds, bias_table, kv_all, k_aug, masks, q_back, do_wide, near_bias)
     grad_keys, grad_values, mask_part = pl.pallas_call(
         functools.partial(dkv_kernel, plan, rows, pair),
         out_shape=(

time: 490 us -> 448 us (0.914)
  blocking collectives: 23.1 us -> 0 us
  waiting for transfers between devices: 13.6 us -> 0.06 us
  other arithmetic: 10 us -> 3.01 us
    all_gather x1 -> x0, blocking collectives: 23.1 us -> none  [shards(): mask_all = lax.all_gather(key_mask, 'ctx', axis=0, tiled=True)]
    pallas_call x2 -> x1, Pallas kernels: 49.2 us -> 64.2 us  [first(): pl.pallas_call(functools.partial(first_kernel, plan, lines, span, reach,...]
    ppermute x1 -> x0, waiting for transfers between devices: 13.2 us -> none  [shards(): swap(w_out)]
    pallas_call x1, Pallas kernels: 145 us -> 136 us  [reduce_scatter(): pl.pallas_call(functools.partial(scatter_kernel, lines, units, z_first, c...]
    pallas_call x1, Pallas kernels: 98.4 us -> 93.5 us  [finish(): pl.pallas_call(functools.partial(finish_kernel, plan, lines), out_shape=[...]
    unnamed x43 -> x41, local copies, waits for them, and re-layouts: 13.8 us -> 13 us
  transfers between devices with their start and end apart: 6 -> 4, of which waited for: 1 -> 0; matrix products, arithmetic and copies ran while one was open for 7% -> 4% of each run, Pallas kernels for 80% -> 65%
where the time goes in v7:
time: 448 us; the launch traced here: 439 us
  Pallas kernels  390 us (87%)
  local copies, waits for them, and re-layouts  30.7 us (7%)
  between operations  14.4 us (3%)
    pallas_call x1, Pallas kernels, reduce_scatter(): pl.pallas_call(functools.partial(scatter_kernel, lines, units, z_first, c...  136 us
    pallas_call x1, Pallas kernels, finish(): pl.pallas_call(functools.partial(finish_kernel, plan, lines), out_shape=[...  93.5 us
    pallas_call x1, Pallas kernels, first(): pl.pallas_call(functools.partial(first_kernel, plan, lines, span, reach,...  64.2 us
    pallas_call x1, Pallas kernels, middle(): pl.pallas_call(functools.partial(middle_kernel, plan, cycle_size), out_sh...  56.7 us
    pallas_call x1, Pallas kernels, shards(): pl.pallas_call(functools.partial(dq_kernel, plan, rows, pair), out_shape=...  14.6 us
    pallas_call x1, Pallas kernels, shards(): pl.pallas_call(functools.partial(fwd_kernel, plan, rows, pair), out_shape...  13.5 us
    unnamed x41, local copies, waits for them, and re-layouts  13 us
    pallas_call x1, Pallas kernels, shards(): pl.pallas_call(functools.partial(dkv_kernel, plan, rows, pair), out_shape...  11.6 us
  transfers between devices with their start and end apart: 4, of which 0 were waited for; matrix products, arithmetic and copies ran while one was open for 4% of the time, Pallas kernels for 65%

profile of v7, /device:TPU:0, one launch (start us, length us, event | category | flops | bytes accessed | tf_op | source)
XLA Modules:
  0.0 439.3 jit_solution(5936010272652524608)
XLA Ops:
  7.3 2.3 copy.59
  10.7 0.7 copy.60.table_ref
  11.4 1.2 copy.57.tokens_ref
  12.6 0.6 broadcast_in_dim.54.gain_ref
  13.2 0.6 broadcast_in_dim.55.mask_ref
  13.8 64.2 %project_gather.1 = (bf16[512,1472]{1,0:T(8,128)(2,1)}, bf16[512,1472]{1,0:T(8,128)(2,1)}, bf16[512,256]{1,0:T(8,128)(2,1)}, bf16[512,384]{1,0:T(8,128)(2,1)}, b...) custom-call(s32[8]{0:T(128)} %copy-done.11, ...), custom_call_target="tpu_custom_call" | custom-call | tf_op jit(solution)/shard_map/project_gather/pallas_call | solution.py:1016
  78.0 0.6 pad_add_fusion.1.bounds
  78.6 13.5 %attention_forward.1 = (bf16[512,256]{1,0:T(8,128)(2,1)}, f32[512,256]{1,0:T(8,128)}, bf16[512,256]{1,0:T(8,128)(2,1)}) custom-call(s32[5]{0:T(128)} %pad_add_fusion.1.bounds, f32[32,3]{1,0:T(8,128)} %copy.60.table_ref, bf16[8192,384]{1,0:T(8,128)(2,1)} %bitcast.44, bf16[8192,128]{1,0:T(8,128)(2,1)} %get-tuple-element.49.kaug_ref, f32[16,8,512]{2,1,0:T(8,128)} %bitcast.57, ...), custom_call_target="tpu_custom_call" | custom-call | tf_op jit(solution)/shard_map/attention_forward/pallas_call | solution.py:1753
  92.3 0.6 broadcast_in_dim.56.gain_ref
  92.9 56.7 %feed_forward.1 = (f32[256,1472]{1,0:T(8,128)}, f32[256,1472]{1,0:T(8,128)}, bf16[256,1472]{1,0:T(8,128)(2,1)}, bf16[512,1472]{1,0:T(8,128)(2,1)}, bf16[512,256]...) custom-call(bf16[512,256]{1,0:T(8,128)(2,1)} %get-tuple-element.54.a, ...), custom_call_target="tpu_custom_call" | custom-call | tf_op jit(solution)/shard_map/feed_forward/pallas_call | solution.py:1635
  149.6 2.4 copy.65
  151.9 1.2 collective-permute-start
  153.4 0.3 copy.63
  153.7 0.3 copy.64
  154.2 4.3 concatenate.14.w3_ref
  158.5 14.6 %attention_grad_queries.1 = (bf16[512,256]{1,0:T(8,128)(2,1)}, f32[3,32,128]{2,1,0:T(8,128)}) custom-call(s32[5]{0:T(128)} %pad_add_fusion.1.bounds, f32[32,3]{1,0:T(8,128)} %copy.60.table_ref, bf16[8192,384]{1,0:T(8,128)(2,1)} %bitcast.45, bf16[8192,128]{1,0:T(8,128)(2,1)} %get-tuple-element.49.kaug_ref, f32[16,8,512]{2,1,0:T(8,128)} %bitcast.58, ...), custom_call_target="tpu_custom_call" | custom-call | tf_op jit(solution)/shard_map/attention_grad_queries/pallas_call | solution.py:1794
  173.1 0.9 reduce_sum.55
  174.0 135.7 %weight_scatter.1 = (f32[112,1472]{1,0:T(8,128)}, f32[112,1472]{1,0:T(8,128)}, f32[112,1472]{1,0:T(8,128)}) custom-call(bf16[4,2,2,112,1472]{4,3,2,1,0:T(8,128)(2,1)} %bitcast.46, bf16[4,2,2,112,1472]{4,3,2,1,0:T(8,128)(2,1)} %bitcast.47, bf16[4,2,2,112,1472]{4,3,2,1,0:T(8,128)(2,1)} %bitcast.48), custom_call_target="tpu_custom_call" | custom-call | tf_op jit(solution)/shard_map/weight_scatter/pallas_call | solution.py:663
  309.8 0.7 fusion.small_ref
  310.5 2.3 copy.66.far_ref
  312.7 11.6 %attention_grad_keys.1 = (bf16[512,256]{1,0:T(8,128)(2,1)}, bf16[512,256]{1,0:T(8,128)(2,1)}, f32[2,8,256]{2,1,0:T(8,128)}) custom-call(s32[5]{0:T(128)} %pad_add_fusion.1.bounds, f32[32,3]{1,0:T(8,128)} %copy.60.table_ref, bf16[8192,256]{1,0:T(8,128)(2,1)} %all-gather.6.cloned.1.call-done.qall_ref, ...), custom_call_target="tpu_custom_call" | custom-call | tf_op jit(solution)/shard_map/attention_grad_keys/pallas_call | solution.py:1815
  324.3 93.5 %finish.1 = (bf16[256,1472]{1,0:T(8,128)(2,1)}, f32[256,1472]{1,0:T(8,128)}, f32[8,256]{1,0:T(8,128)}, bf16[4,2,2,48,1472]{4,3,2,1,0:T(8,128)(2,1)}, f32[8,1472]{1,0:T(8,128)}) custom-call(bf16[512,256]{1,0:T(8,128)(2,1)} %get-tuple-element.59.dq_ref, bf16[512,256]{1,0:T(8,128)(2,1)} %get-tuple-element.62.dk_ref, bf16[512,256]{1,0:T(8,128)(2,1)} %get-tuple-element.63.dv_ref, ...), custom_call_target="tpu_custom_call" | custom-call | tf_op jit(solution)/shard_map/finish/pallas_call | solution.py:1367
  417.8 1.5 slice_reduce_fusion
  419.3 0.7 slice_reduce_fusion.2
  420.0 2.3 copy.68
  422.3 3.1 copy.69
  425.4 1.3 slice.28
  426.7 2.4 fusion.10
  429.1 0.7 reshape_squeeze.3
  429.7 0.8 copy.73
  430.6 0.8 copy.74
  431.4 0.8 copy.75
  (60 shorter events, 1.8 us)
Async XLA Ops:
  7.2 2.5 copy-start.14
  7.2 3.5 copy-start.12
  7.2 4.2 copy-start.4
  7.2 85.6 %all-gather.4.cloned.1.call-start = ((), (), s32[]{:S(2)}) async-start(), calls=%async_computation | async-start | bytes 2359296 | tf_op jit(solution)/shard_map/all_gather | solution.py:1723
  9.6 3.0 copy-start.8
  9.6 3.6 copy-start.13
  9.6 303.1 %all-gather.6.cloned.1.call-start = ((), (), s32[]{:S(2)}) async-start(), calls=%async_computation.1 | async-start | bytes 4456448 | tf_op jit(solution)/shard_map/all_gather | solution.py:1773
  9.9 3.9 copy-start.11
  78.6 13.6 %copy-start.9 = (f32[1472]{0:T(1024)S(1)}, f32[1472]{0:T(1024)}, u32[]{:S(2)}) copy-start(f32[1472]{0:T(1024)} %param.23) | copy-start | bytes 17668
  92.2 220.5 %all-gather.8.cloned.1.call-start = ((), (), s32[]{:S(2)}) async-start(), calls=%async_computation.2 | async-start | bytes 4456448 | tf_op jit(solution)/shard_map/all_gather | solution.py:1790
  149.5 3.6 copy-start.1
  149.5 3.9 copy-start.2
  151.9 1.8 copy-start.3
  151.9 158.5 %collective-permute-start = (bf16[256,1472]{0,1:T(8,128)(2,1)}, bf16[256,1472]{0,1:T(8,128)(2,1)}, u32[]{:S(2)}, u32[]{:S(2)}) collective-permute-start(bf16[256,1472]{0,1:T(8,128)(2,1)} %copy.65), channel_id=1, source_target_pairs={{0,1},{1,0},{2,3},{3,2},{4,5},{5,4},{6,7},{7,6},{8,9},{9,8},{10,11... | collective-permute-start | bytes 2261000 | tf_op jit(solution)/shard_map/ppermute | solution.py:1789
  174.0 135.7 %copy-start.10 = (f32[1,1472]{1,0:T(1,128)S(1)}, f32[1,1472]{1,0:T(1,128)}, u32[]{:S(2)}) copy-start(f32[1,1472]{1,0:T(1,128)} %get-tuple-element.70) | copy-start | bytes 17668
  422.3 4.4 %copy-start = (bf16[4,2,2,48,1472]{4,3,2,1,0:T(8,128)(2,1)S(1)}, bf16[4,2,2,48,1472]{4,3,2,1,0:T(8,128)(2,1)}, u32[]{:S(2)}) copy-start(bf16[4,2,2,48,1472]{4,3,2,1,0:T(8,128)(2,1)} %get-tuple-element.76) | copy-start | bytes 6782980
  426.7 3.1 copy-start.7
  429.1 1.5 copy-start.6
  429.1 2.4 copy-start.5
Sparse Core Ops, SparseCore 0:
  10.2 46.8 all-gather.3
  92.3 64.1 all-gather.5
  158.7 69.4 all-gather.7

commit v8 on v7

--- a/solution.py
+++ b/solution.py
@@ -140,6 +140,13 @@
     lax.fori_loop(0, rows // step, body, 0)
 
 
+def far_span(start, n, n_left, left_bucket, right_bucket):
+    on_left = n < n_left
+    at = start + PAD - EDGE + TK * jnp.where(on_left, -1 - n, 1 + n - n_left)
+    bucket = jnp.where(on_left, left_bucket, right_bucket)
+    return pl.ds(pl.multiple_of(at, 128), TK), bucket
+
+
 def pad_lanes(plan):
     lane = lanes_of(1)
     return (lane >= plan.doc_lane) & (lane < plan.stat_lane)
@@ -167,9 +174,9 @@
             acc[h] = nn(p, vm[near, :])
             row_max[h] = jnp.broadcast_to(top, (TQ, 128))
 
-        def far(bucket):
-            def step(first, n):
-                span = pl.ds(pl.multiple_of(first + n, 128), TK)
+        def far(n, unused):
+            span, bucket = far_span(start, n, n_left, far_left_bucket, far_right_bucket)
+            if True:
                 for h in range(plan.heads):
                     s = nt(qh_ref[h], km[span, :]) + mask_row[0:1, span]
                     offset = table_ref[bucket, h]
@@ -178,17 +185,9 @@
                     p = jnp.exp(s - (top - offset)).astype(bf16)
                     acc[h] = acc[h] * jnp.exp(old - top) + nn(p, vm[span, :])
                     row_max[h] = jnp.broadcast_to(top, (TQ, 128))
-            return step
-
-        left, right = (far(far_left_bucket), far(far_right_bucket))
-
-        @pl.loop(0, n_left)
-        def _(n):
-            left(start + PAD - EDGE - TK, -n * TK)
-
-        @pl.loop(0, n_right)
-        def _(n):
-            right(start + PAD - EDGE + TK, n * TK)
+            return unused
+
+        lax.fori_loop(0, n_left + n_right, far, 0)
 
         wide = jnp.zeros((TQ, WIDE), f32)
         qb = jnp.where(lane < plan.stat_lane, q, jnp.zeros_like(q))
@@ -236,9 +235,10 @@
             near_acc[h] += ds
             acc[h] = nn(ds.astype(bf16), km[near, :])
 
-        def far(bucket, slot):
-            def step(first, n):
-                span = pl.ds(pl.multiple_of(first + n, 128), TK)
+        def far(n, unused):
+            span, bucket = far_span(start, n, n_left, far_left_bucket, far_right_bucket)
+            slot = (n >= n_left).astype(jnp.int32)
+            if True:
                 for h in range(plan.heads):
                     offset = mask_row[0:1, span] + table_ref[bucket, h]
                     ds = grads(h, nt(qh_ref[h], km[span, :]) + offset, span)
@@ -246,17 +246,9 @@
                     far_acc[slot, h] += (
                         ds[:, 0:128] + ds[:, 128:256] + ds[:, 256:384] + ds[:, 384:512]
                     )
-            return step
-
-        left, right = (far(far_left_bucket, 0), far(far_right_bucket, 1))
-
-        @pl.loop(0, n_left)
-        def _(n):
-            left(start + PAD - EDGE - TK, -n * TK)
-
-        @pl.loop(0, n_right)
-        def _(n):
-            right(start + PAD - EDGE + TK, n * TK)
+            return unused
+
+        lax.fori_loop(0, n_left + n_right, far, 0)
 
         total = jnp.zeros((TQ, WIDE), f32)
         for h in range(plan.heads):
@@ -327,26 +319,18 @@
             vh_ref[h] = jnp.where(plan.value_lanes(lane, h), v, jnp.zeros_like(v))
             acc_v[h], acc_k[h] = grads(h, nt(kh_ref[h], qp[near, :]) + near_ref[1, h], near)
 
-        def far(bucket):
-            def step(first, n):
-                span = pl.ds(pl.multiple_of(first + n, 128), TK)
+        def far(n, unused):
+            span, bucket = far_span(start, n, n_left, far_right_bucket, far_left_bucket)
+            if True:
                 for h in range(plan.heads):
                     add_v, add_k = grads(
                         h, nt(kh_ref[h], qp[span, :]) + table_ref[bucket, h], span
                     )
                     acc_v[h] += add_v
                     acc_k[h] += add_k
-            return step
-
-        left, right = (far(far_right_bucket), far(far_left_bucket))
-
-        @pl.loop(0, n_left)
-        def _(n):
-            left(start + PAD - EDGE - TK, -n * TK)
-
-        @pl.loop(0, n_right)
-        def _(n):
-            right(start + PAD - EDGE + TK, n * TK)
+            return unused
+
+        lax.fori_loop(0, n_left + n_right, far, 0)
 
         dk = jnp.zeros((TQ, WIDE), f32)
         dv = jnp.zeros((TQ, WIDE), f32)
@@ -652,7 +636,8 @@
 def reduce_scatter(parts, cycle_size):
     lines = cycle_size // 4
     count = len(parts)
-    rows, model = parts[0].shape[1:]
+    units_here, model = parts[0].shape
+    rows = units_here // cycle_size
     cut = (rows // 2 + 15) // 16 * 16
     pieces = [(0, cut), (cut, rows - cut)] if cut < rows else [(0, rows)]
     units = [(m, at, size) for m in range(count) for at, size in pieces]
@@ -743,7 +728,6 @@
 
     lax.fori_loop(0, 4, y_start, 0)
     far_copy = send(wo_hbm, wo_far_hbm, y_sem.at[0, 4], y_sem.at[1, 4], spot.y_mate())
-    far_copy.start()
 
     def scaled(rows_in):
         rows_in = rows_in.astype(f32)
@@ -943,6 +927,7 @@
     level(0, 1)
     level(mask_piece, 1)
     lax.fori_loop(2, 4, y_wait, 0)
+    far_copy.start()
     project(theirs)
     begin(2)
     begin(1)
@@ -1080,16 +1065,29 @@
 
 
 def finish_kernel(
-    plan, lines, dq_ref, dk_ref, dv_ref, mask_ref, w3_ref, normed_ref, att_ref, branch_ref, far_ref,
+    plan, lines, dq_ref, dk_ref, dv_ref, mask_ref, wq_hbm, wk_hbm, wv_hbm, normed_ref, att_ref, branch_ref, far_ref,
     tokens_ref, gain_ref, hidden_ref, gh_ref, ffn_ref, small_ref,
     out_ref, gt_ref, gm_ref, weights_ref, total_ref,
-    mine, core_in, x_in, up_in, down_in, all_w, y_out, y_in, own_part, ffn_in, mask_in,
+    w3_ref, load_sem, lefts, rights, product, mine, core_in, x_in, up_in, down_in, all_w, y_out, y_in, own_part, ffn_in, mask_in,
     small_own, small_y, small_core, small_x, small_all,
     y_sem, core_sem, x_sem, up_sem, down_sem, gz_sem, gx_sem, gc_sem, sz_sem,
 ):
     spot = Spot(lines)
     z, x, core, wa = (spot.z, spot.x, spot.core, spot.wa)
+    cols = plan.cols
+    loads = [
+        pltpu.make_async_copy(src, w3_ref.at[pl.ds(at, cols)], load_sem.at[i])
+        for i, (src, at) in enumerate(((wq_hbm, 0), (wk_hbm, WIDE), (wv_hbm, 3 * WIDE - cols)))
+    ]
+    for load in loads:
+        load.start()
+    gap = jnp.zeros((WIDE - cols, tokens_ref.shape[1]), bf16)
+    w3_ref[cols:WIDE] = gap
+    w3_ref[WIDE + cols : 2 * WIDE] = gap
+    w3_ref[2 * WIDE : 3 * WIDE - cols] = gap
     greet(spot, True)
+    for load in loads:
+        load.wait()
     half = tokens_ref.shape[0]
     quarter = half // 2
     model = tokens_ref.shape[1]
@@ -1098,9 +1096,9 @@
     def grad_rows(at):
         at = pl.ds(pl.multiple_of(at, quarter), quarter)
         return (
-            nt(dq_ref[at, :], w3_ref[:, 0:256])
-            + nt(dk_ref[at, :], w3_ref[:, 256:512])
-            + nt(dv_ref[at, :], w3_ref[:, 512:768])
+            nn(dq_ref[at, :], w3_ref[0:256])
+            + nn(dk_ref[at, :], w3_ref[256:512])
+            + nn(dv_ref[at, :], w3_ref[512:768])
         )
 
     def y_copy(i):
@@ -1117,55 +1115,82 @@
     )
     mask_copy.start()
 
-    def fill(product, matrix):
-        for j in range(plan.cols // rows):
-            s = matrix * (plan.cols // rows) + j
-            mine[s // 4, (s // 2) % 2, s % 2] = product[j * rows : (j + 1) * rows].astype(bf16)
-
-    fill(tn(dq_ref[...], normed_ref[...])[: plan.cols], 0)
-    fill(tn(dk_ref[...], normed_ref[...])[: plan.cols], 1)
-    fill(tn(dv_ref[...], normed_ref[...])[64:], 2)
     our_rows = pl.ds(pl.multiple_of(wa * half, half), half)
     their_rows = pl.ds(pl.multiple_of((1 - wa) * half, half), half)
-    fill(
-        (tn(att_ref[our_rows, :], branch_ref[...]) + tn(att_ref[their_rows, :], far_ref[...]))[64:],
-        3,
-    )
-    core_copy = send(
-        mine.at[:, :, 1 - core], core_in, core_sem.at[0, 0], core_sem.at[1, 0], spot.core_mate()
-    )
-    core_copy.start()
+    lefts[0] = dq_ref[...]
+    lefts[1] = dk_ref[...]
+    lefts[2] = dv_ref[...]
+    lefts[3] = att_ref[...]
+    rights[0] = normed_ref[...]
+    rights[1, our_rows, :] = branch_ref[...]
+    rights[1, their_rows, :] = far_ref[...]
+    per = plan.cols // rows
+
+    def core_copy(m):
+        part = pl.ds(m * per // 4, per // 4)
+        return send(
+            mine.at[part, :, 1 - core],
+            core_in.at[part],
+            core_sem.at[0, m],
+            core_sem.at[1, m],
+            spot.core_mate(),
+        )
+
+    def fill(m, unused):
+        product[...] = tn(lefts[m], rights[m // 3]).astype(bf16)
+
+        def place(offset):
+            for j in range(per):
+                mine[m * per // 4 + j // 4, (j // 2) % 2, j % 2] = product[
+                    offset + j * rows : offset + (j + 1) * rows, :
+                ]
+
+        @pl.when(m < 2)
+        def _():
+            place(0)
+
+        @pl.when(m >= 2)
+        def _():
+            place(WIDE - plan.cols)
+
+        core_copy(m).start()
+        return unused
+
+    lax.fori_loop(0, 4, fill, 0)
     ffn_copy = send(
         ffn_ref.at[their_rows], ffn_in, y_sem.at[0, 3], y_sem.at[1, 3], spot.y_mate()
     )
     ffn_copy.start()
 
+    def x_copy(d):
+        return send(
+            mine.at[d, 1 - x, core], x_in.at[d], x_sem.at[0, d], x_sem.at[1, d], spot.x_mate()
+        )
+
+    def core_add(d, unused):
+        mine[d, 1 - x, core] = added(mine[d, 1 - x, core], core_in[d, 1 - x])
+        x_copy(d).start()
+        return unused
+
     def ours(i, unused):
         own_part[pl.ds(pl.multiple_of(i * quarter, quarter), quarter), :] = grad_rows(
             wa * half + i * quarter
         )
         return unused
 
-    lax.fori_loop(0, 2, ours, 0)
-    core_copy.wait()
-
-    def x_copy(d):
-        return send(
-            mine.at[d, 1 - x, core], x_in.at[d], x_sem.at[0, d], x_sem.at[1, d], spot.x_mate()
-        )
-
-    def core_add(d, unused):
-        mine[d, 1 - x, core] = added(mine[d, 1 - x, core], core_in[d, 1 - x])
-        x_copy(d).start()
-        return unused
-
-    lax.fori_loop(0, lines, core_add, 0)
+    def core_stage(m, unused):
+        core_copy(m).wait()
+        lax.fori_loop(m * per // 4, (m + 1) * per // 4, core_add, 0)
+        return unused
+
+    lax.fori_loop(0, 4, core_stage, 0)
 
     def core_add_own(d, unused):
         mine[d, x, core] = added(mine[d, x, core], core_in[d, x])
         return unused
 
     lax.fori_loop(0, lines, core_add_own, 0)
+    lax.fori_loop(0, 2, ours, 0)
 
     gain_sum = jnp.zeros((1, model), f32)
     step = 32
@@ -1223,7 +1248,7 @@
     row = lax.broadcasted_iota(jnp.int32, small_own.shape, 0)
     small_x[0] = small_own[...] + jnp.where(row < 2, small_y[...], 0.0)
     small_core_copy = send(
-        small_x.at[0], small_core, core_sem.at[0, 1], core_sem.at[1, 1], spot.core_mate()
+        small_x.at[0], small_core, core_sem.at[0, 4], core_sem.at[1, 4], spot.core_mate()
     )
     small_core_copy.start()
 
@@ -1361,7 +1386,7 @@
 
 def finish(plan, cycle_size, *operands):
     lines = cycle_size // 4
-    half, model = operands[9].shape
+    half, model = operands[11].shape
     rows = 4 * plan.cols // cycle_size
     dma = pltpu.SemaphoreType.DMA
     return pl.pallas_call(
@@ -1373,9 +1398,16 @@
             jax.ShapeDtypeStruct((lines, 2, 2, rows, model), bf16),
             jax.ShapeDtypeStruct((8, model), f32),
         ],
-        in_specs=[vmem] * len(operands),
+        in_specs=[vmem] * 4
+        + [pl.BlockSpec(memory_space=pl.ANY)] * 3
+        + [vmem] * (len(operands) - 7),
         out_specs=[vmem] * 5,
         scratch_shapes=[
+            pltpu.VMEM((3 * WIDE, model), bf16),
+            dma((3,)),
+            pltpu.VMEM((4, 2 * half, WIDE), bf16),
+            pltpu.VMEM((2, 2 * half, model), bf16),
+            pltpu.VMEM((WIDE, model), bf16),
             pltpu.VMEM((lines, 2, 2, rows, model), bf16),
             pltpu.VMEM((lines, 2, rows, model), bf16),
             pltpu.VMEM((lines, rows, model), bf16),
@@ -1393,7 +1425,7 @@
             pltpu.VMEM((3, 8, model), f32),
             pltpu.VMEM((lines, 8, model), f32),
             dma((2, 5)),
-            dma((2, 2)),
+            dma((2, 5)),
             dma((2, lines + 1)),
             dma((2, lines)),
             dma((2, lines)),
@@ -1538,30 +1570,30 @@
         return unused
 
     lax.fori_loop(0, 2, half_pass, 0)
-    parts = 2
-    span = units // parts
-    slices = cycle_size // parts
-    size = units // cycle_size
-
-    def out_copy(n):
-        m, p = (n // parts, n % parts)
+    count = units // wide
+
+    def out_copy(m, u):
         return pltpu.make_async_copy(
-            rows_buf.at[n % 2], stacks[m].at[pl.ds(p * slices, slices)], out_sem.at[n]
-        )
-
-    for n in range(3 * parts):
-        m, p = (n // parts, n % parts)
+            rows_buf.at[m, u % 2],
+            stacks[m].at[rows_at(u * wide, wide)],
+            out_sem.at[m, u % 2],
+        )
+
+    for m in range(3):
         left = (inner, gg, gu)[m]
         right = (cot_ref, x_ref, x_ref)[m]
-        if n >= 2:
-            out_copy(n - 2).wait()
-        turned = jnp.transpose(left[:, p * span : (p + 1) * span])
-        for c in range(0, model, wide):
-            end = min(model, c + wide)
-            product = nn(turned, right[:, c:end]).astype(bf16)
-            for s in range(slices):
-                rows_buf[n % 2, s, :, c:end] = product[s * size : (s + 1) * size]
-        out_copy(n).start()
+
+        def weight_rows(u, unused, m=m, left=left, right=right):
+            @pl.when(u >= 2)
+            def _():
+                out_copy(m, u - 2).wait()
+
+            turned = jnp.transpose(left[:, rows_at(u * wide, wide)])
+            rows_buf[m, u % 2] = nn(turned, right[...]).astype(bf16)
+            out_copy(m, u).start()
+            return unused
+
+        lax.fori_loop(0, count, weight_rows, 0)
 
     def e_copy(i):
         return send(
@@ -1616,8 +1648,9 @@
         return unused
 
     lax.fori_loop(0, 4, far_terms, 0)
-    for n in (3 * parts - 2, 3 * parts - 1):
-        out_copy(n).wait()
+    for m in range(3):
+        for u in range(max(0, count - 2), count):
+            out_copy(m, u).wait()
     for i in order:
         a_copy(i, ours if i < 2 else theirs).wait_send()
 
@@ -1628,7 +1661,6 @@
     pair, model = tokens.shape
     half = pair // 2
     units = w_down.shape[0]
-    size = units // cycle_size
     chunk = half // 4
     hbm = pl.BlockSpec(memory_space=pl.ANY)
     dma = pltpu.SemaphoreType.DMA
@@ -1642,7 +1674,7 @@
             jax.ShapeDtypeStruct((pair, WIDE), bf16),
             jax.ShapeDtypeStruct((1, model), f32),
         ]
-        + [jax.ShapeDtypeStruct((cycle_size, size, model), bf16)] * 3,
+        + [jax.ShapeDtypeStruct((units, model), bf16)] * 3,
         in_specs=[vmem] * 5 + [hbm] * 5,
         out_specs=[vmem] * 6 + [hbm] * 3,
         scratch_shapes=[
@@ -1661,10 +1693,10 @@
             pltpu.VMEM((4, chunk, WIDE), bf16),
             pltpu.VMEM((half, model), f32),
             pltpu.VMEM((half, model), f32),
-            pltpu.VMEM((2, cycle_size // 2, size, model), bf16),
+            pltpu.VMEM((3, 2, WIDE, model), bf16),
             dma((5,)),
             dma((2, 12)),
-            dma((6,)),
+            dma((3, 2)),
         ],
         compiler_params=pltpu.CompilerParams(
             vmem_limit_bytes=60 * 2**20, collective_id=3, has_side_effects=True
@@ -1720,8 +1752,6 @@
         [(base - origin)[None], jnp.stack([n_left, n_right], axis=1).reshape(-1)]
     ).astype(jnp.int32)
 
-    pair_cot = lax.all_gather(cotangent, "wa", axis=0, tiled=True)
-
     def window(gathered):
         if rows == total_rows:
             return gathered
@@ -1746,6 +1776,8 @@
         w_out,
     )
     masks = masks.reshape(cycle_size, 8, pair)
+    cot_late, near_bias = lax.optimization_barrier((cotangent, near_bias))
+    pair_cot = lax.all_gather(cot_late, "wa", axis=0, tiled=True)
     if rows < total_rows:
         masks = lax.dynamic_slice_in_dim(masks, origin // pair, rows // pair, 0)
     kv_all = window(kv_all.reshape(total_rows, 2 * plan.cols))
@@ -1833,8 +1865,6 @@
         name="attention_grad_keys",
     )(bounds, bias_table, q_all, do_all, own_kv, own_aug, near_bias)
     cols = plan.cols
-    gap = jnp.zeros((model, WIDE - cols), bf16)
-    w_wide = jnp.concatenate([w_query, gap, w_key, gap, gap, w_value], axis=1)
     table_row = jnp.sum(table_part, axis=2).reshape(1, -1)
     table_row = jnp.pad(table_row, ((0, 0), (0, model - table_row.shape[1])))
     small = jnp.concatenate(
@@ -1848,7 +1878,9 @@
         grad_keys,
         grad_values,
         mask_part.reshape(group, 8, own_rows),
-        w_wide,
+        w_query.T,
+        w_key.T,
+        w_value.T,
         pair_normed,
         attended,
         branch,

time: 448 us -> 429 us (0.958); the launches traced: 439 us -> 428 us
  Pallas kernels: 390 us -> 372 us
  waiting for transfers between devices: 0.06 us -> 10.9 us
  local copies, waits for them, and re-layouts: 30.7 us -> 24.7 us
    pallas_call x1, Pallas kernels: 64.2 us -> 50.6 us  [first(): pl.pallas_call(functools.partial(first_kernel, plan, lines, span, reach,...]
    all_gather x1, waiting for transfers between devices: 0.01 us -> 10.8 us  [shards(): pair_cot = lax.all_gather(cot_late, 'wa', axis=0, tiled=True)]
    pallas_call x1, Pallas kernels: 136 us -> 125 us  [reduce_scatter(): pl.pallas_call(functools.partial(scatter_kernel, lines, units, z_first, c...]
    pallas_call x1, Pallas kernels: 56.7 us -> 62.1 us  [middle(): pl.pallas_call(functools.partial(middle_kernel, plan, cycle_size), out_sh...]
    unnamed x41 -> x25, local copies, waits for them, and re-layouts: 13 us -> 11.6 us
  transfers between devices with their start and end apart: 4 -> 4, of which waited for: 0 -> 1; matrix products, arithmetic and copies ran while one was open for 4% -> 1% of each run, Pallas kernels for 65% -> 50%
where the time goes in v8:
time: 429 us; the launch traced here: 428 us
  Pallas kernels  372 us (87%)
  local copies, waits for them, and re-layouts  24.7 us (6%)
  between operations  13.9 us (3%)
  waiting for transfers between devices  10.9 us (3%)
  other arithmetic  4.81 us (1%)
    pallas_call x1, Pallas kernels, reduce_scatter(): pl.pallas_call(functools.partial(scatter_kernel, lines, units, z_first, c...  125 us
    pallas_call x1, Pallas kernels, finish(): pl.pallas_call(functools.partial(finish_kernel, plan, lines), out_shape=[...  94.7 us
    pallas_call x1, Pallas kernels, middle(): pl.pallas_call(functools.partial(middle_kernel, plan, cycle_size), out_sh...  62.1 us
    pallas_call x1, Pallas kernels, first(): pl.pallas_call(functools.partial(first_kernel, plan, lines, span, reach,...  50.6 us
    pallas_call x1, Pallas kernels, shards(): pl.pallas_call(functools.partial(dq_kernel, plan, rows, pair), out_shape=...  14.4 us
    pallas_call x1, Pallas kernels, shards(): pl.pallas_call(functools.partial(fwd_kernel, plan, rows, pair), out_shape...  13.7 us
    unnamed x25, local copies, waits for them, and re-layouts  11.6 us
    pallas_call x1, Pallas kernels, shards(): pl.pallas_call(functools.partial(dkv_kernel, plan, rows, pair), out_shape...  11.6 us
  transfers between devices with their start and end apart: 4, of which 1 were waited for; matrix products, arithmetic and copies ran while one was open for 1% of the time, Pallas kernels for 50%

profile of v8, /device:TPU:0, one launch (start us, length us, event | category | flops | bytes accessed | tf_op | source)
XLA Modules:
  0.0 428.4 jit_solution(4289571718076719363)
XLA Ops:
  7.2 0.8 reduce-window.8
  8.1 1.2 bitcast_subtract_fusion.2.starts
  9.2 1.4 copy.54.table_ref
  10.6 2.3 copy.51.tokens_ref
  12.9 1.3 broadcast_in_dim.51.gain_ref
  14.2 0.6 broadcast_in_dim.52.mask_ref
  14.8 50.6 %project_gather.1 = (bf16[512,1472]{1,0:T(8,128)(2,1)}, bf16[512,1472]{1,0:T(8,128)(2,1)}, bf16[512,256]{1,0:T(8,128)(2,1)}, bf16[512,384]{1,0:T(8,128)(2,1)}, b...) custom-call(s32[8]{0:T(128)} %bitcast_subtract_fusion.2.starts, ...), custom_call_target="tpu_custom_call" | custom-call | tf_op jit(solution)/shard_map/project_gather/pallas_call | solution.py:1001
  65.4 1.2 copy.53
  67.5 0.6 pad_add_fusion.1.bounds
  68.1 13.7 %attention_forward.1 = (bf16[512,256]{1,0:T(8,128)(2,1)}, f32[512,256]{1,0:T(8,128)}, bf16[512,256]{1,0:T(8,128)(2,1)}) custom-call(s32[5]{0:T(128)} %pad_add_fusion.1.bounds, f32[32,3]{1,0:T(8,128)} %copy.54.table_ref, bf16[8192,384]{1,0:T(8,128)(2,1)} %bitcast.44, bf16[8192,128]{1,0:T(8,128)(2,1)} %get-tuple-element.51.kaug_ref, f32[16,8,512]{2,1,0:T(8,128)} %bitcast.60, ...), custom_call_target="tpu_custom_call" | custom-call | tf_op jit(solution)/shard_map/attention_forward/pallas_call | solution.py:1785
  82.0 0.6 broadcast_in_dim.53.gain_ref
  82.6 10.8 %all-gather.4.cloned.1.call-done.cot_ref = bf16[512,1472]{1,0:T(8,128)(2,1)} async-done(((bf16[256,1472]{1,0:T(8,128)(2,1)}), bf16[512,1472]{1,0:T(8,128)(2,1)}) %all-gather.4.cloned.1.call-update) | async-done | bytes 1507344 | tf_op jit(solution)/shard_map/all_gather | solution.py:1780
  93.4 62.1 %feed_forward.1 = (f32[256,1472]{1,0:T(8,128)}, f32[256,1472]{1,0:T(8,128)}, bf16[256,1472]{1,0:T(8,128)(2,1)}, bf16[512,1472]{1,0:T(8,128)(2,1)}, bf16[512,256]...) custom-call(bf16[512,256]{1,0:T(8,128)(2,1)} %get-tuple-element.57.a, ...), custom_call_target="tpu_custom_call" | custom-call | tf_op jit(solution)/shard_map/feed_forward/pallas_call | solution.py:1667
  155.6 1.4 copy.56
  157.0 1.8 collective-permute-start
  158.9 14.4 %attention_grad_queries.1 = (bf16[512,256]{1,0:T(8,128)(2,1)}, f32[3,32,128]{2,1,0:T(8,128)}) custom-call(s32[5]{0:T(128)} %pad_add_fusion.1.bounds, f32[32,3]{1,0:T(8,128)} %copy.54.table_ref, bf16[8192,384]{1,0:T(8,128)(2,1)} %bitcast.45, bf16[8192,128]{1,0:T(8,128)(2,1)} %get-tuple-element.51.kaug_ref, f32[16,8,512]{2,1,0:T(8,128)} %bitcast.61, ...), custom_call_target="tpu_custom_call" | custom-call | tf_op jit(solution)/shard_map/attention_grad_queries/pallas_call | solution.py:1826
  173.3 0.9 reduce_sum.55
  174.3 124.9 %weight_scatter.1 = (f32[112,1472]{1,0:T(8,128)}, f32[112,1472]{1,0:T(8,128)}, f32[112,1472]{1,0:T(8,128)}) custom-call(bf16[4,2,2,112,1472]{4,3,2,1,0:T(8,128)(2,1)} %bitcast.46, bf16[4,2,2,112,1472]{4,3,2,1,0:T(8,128)(2,1)} %bitcast.47, bf16[4,2,2,112,1472]{4,3,2,1,0:T(8,128)(2,1)} %bitcast.48), custom_call_target="tpu_custom_call" | custom-call | tf_op jit(solution)/shard_map/weight_scatter/pallas_call | solution.py:648
  299.2 0.7 fusion.small_ref
  299.9 1.2 copy.57.far_ref
  301.1 11.6 %attention_grad_keys.1 = (bf16[512,256]{1,0:T(8,128)(2,1)}, bf16[512,256]{1,0:T(8,128)(2,1)}, f32[2,8,256]{2,1,0:T(8,128)}) custom-call(s32[5]{0:T(128)} %pad_add_fusion.1.bounds, f32[32,3]{1,0:T(8,128)} %copy.54.table_ref, bf16[8192,256]{1,0:T(8,128)(2,1)} %all-gather.6.cloned.1.call-done.qall_ref, ...), custom_call_target="tpu_custom_call" | custom-call | tf_op jit(solution)/shard_map/attention_grad_keys/pallas_call | solution.py:1847
  312.7 94.7 %finish.1 = (bf16[256,1472]{1,0:T(8,128)(2,1)}, f32[256,1472]{1,0:T(8,128)}, f32[8,256]{1,0:T(8,128)}, bf16[4,2,2,48,1472]{4,3,2,1,0:T(8,128)(2,1)}, f32[8,1472]{1,0:T(8,128)}) custom-call(bf16[512,256]{1,0:T(8,128)(2,1)} %get-tuple-element.63.dq_ref, bf16[512,256]{1,0:T(8,128)(2,1)} %get-tuple-element.66.dk_ref, bf16[512,256]{1,0:T(8,128)(2,1)} %get-tuple-element.67.dv_ref, ...), custom_call_target="tpu_custom_call" | custom-call | tf_op jit(solution)/shard_map/finish/pallas_call | solution.py:1392
  407.4 1.5 slice_reduce_fusion
  408.9 0.7 slice_reduce_fusion.2
  409.6 2.3 copy.59
  411.9 3.1 copy.60
  415.0 1.3 slice.28
  416.3 2.4 fusion.10
  418.7 0.7 reshape_squeeze.3
  419.3 0.8 copy.64
  420.2 0.8 copy.65
  421.0 0.8 copy.66
  (42 shorter events, 1.4 us)
Async XLA Ops:
  7.2 7.0 %copy-start.8 = (bf16[512]{0:T(512)(128)(2,1)S(1)}, bf16[512]{0:T(512)(128)(2,1)}, u32[]{:S(2)}) copy-start(bf16[512]{0:T(512)(128)(2,1)} %param.16) | copy-start | bytes 3076
  7.2 86.3 %all-gather.4.cloned.1.call-start = ((), (), s32[]{:S(2)}) async-start(), calls=%async_computation | async-start | bytes 2359296 | tf_op jit(solution)/shard_map/all_gather | solution.py:1780
  14.8 50.6 %copy-start.1 = (bf16[256,1472]{0,1:T(8,128)(2,1)S(1)}, bf16[256,1472]{0,1:T(8,128)(2,1)}, u32[]{:S(2)}) copy-start(bf16[256,1472]{0,1:T(8,128)(2,1)} %param.27) | copy-start | bytes 2260996
  65.4 1.3 copy-start.7
  66.6 234.5 %all-gather.6.cloned.1.call-start = ((), (), s32[]{:S(2)}) async-start(), calls=%async_computation.1 | async-start | bytes 4456448 | tf_op jit(solution)/shard_map/all_gather | solution.py:1805
  68.1 13.9 %copy-start.5 = (f32[1472]{0:T(1024)S(1)}, f32[1472]{0:T(1024)}, u32[]{:S(2)}) copy-start(f32[1472]{0:T(1024)} %param.23) | copy-start | bytes 17668
  81.8 219.3 %all-gather.8.cloned.1.call-start = ((), (), s32[]{:S(2)}) async-start(), calls=%async_computation.2 | async-start | bytes 4456448 | tf_op jit(solution)/shard_map/all_gather | solution.py:1822
  157.0 142.9 %collective-permute-start = (bf16[256,1472]{0,1:T(8,128)(2,1)S(1)}, bf16[256,1472]{0,1:T(8,128)(2,1)S(1)}, u32[]{:S(2)}, u32[]{:S(2)}) collective-permute-start(bf16[256,1472]{0,1:T(8,128)(2,1)S(1)} %copy.56), channel_id=1, source_target_pairs={{0,1},{1,0},{2,3},{3,2},{4,5},{5,4},{6,7},{7,6},{8,9},{9,8},{10,11... | collective-permute-start | bytes 2261000 | tf_op jit(solution)/shard_map/ppermute | solution.py:1821
  174.3 124.9 %copy-start.6 = (f32[1,1472]{1,0:T(1,128)S(1)}, f32[1,1472]{1,0:T(1,128)}, u32[]{:S(2)}) copy-start(f32[1,1472]{1,0:T(1,128)} %get-tuple-element.74) | copy-start | bytes 17668
  411.9 4.4 %copy-start = (bf16[4,2,2,48,1472]{4,3,2,1,0:T(8,128)(2,1)S(1)}, bf16[4,2,2,48,1472]{4,3,2,1,0:T(8,128)(2,1)}, u32[]{:S(2)}) copy-start(bf16[4,2,2,48,1472]{4,3,2,1,0:T(8,128)(2,1)} %get-tuple-element.80) | copy-start | bytes 6782980
  416.3 3.1 copy-start.4
  418.7 1.5 copy-start.3
  418.7 2.4 copy-start.2
Sparse Core Ops, SparseCore 0:
  66.7 26.6 all-gather.3
  96.2 52.1 all-gather.5
  155.7 68.8 all-gather.7

commit v9 on v8

--- a/solution.py
+++ b/solution.py
@@ -205,163 +205,6 @@
     lax.fori_loop(0, pair // TQ, tile, 0)
 
 
-def dq_kernel(
-    plan, rows, pair, bounds, table_ref, g_ref, kaug_ref, masks_ref, qb_ref, do_ref, near_ref,
-    dq_ref, tab_ref, km, vm, mask_row, acc, qh_ref, doh_ref, near_acc, far_acc,
-):
-    build_keys(plan, g_ref, kaug_ref, masks_ref, km, vm, mask_row, rows)
-    lane = lanes_of(TQ)
-    near_acc[...] = jnp.zeros_like(near_acc)
-    far_acc[...] = jnp.zeros_like(far_acc)
-
-    def tile(t, unused):
-        start = pl.multiple_of(bounds[0] + t * TQ, 128)
-        n_left, n_right = (bounds[1 + 2 * t], bounds[2 + 2 * t])
-        out = pl.ds(pl.multiple_of(t * TQ, TQ), TQ)
-        q = qb_ref[out, :]
-        do = do_ref[out, :]
-        near = pl.ds(pl.multiple_of(start + PAD - EDGE, 128), TK)
-
-        def grads(h, s, span):
-            p = jnp.exp(s)
-            return p * nt(doh_ref[h], vm[span, :])
-
-        for h in range(plan.heads):
-            qh_ref[h] = jnp.where(plan.key_lanes(lane, h), q, jnp.zeros_like(q))
-            doh_ref[h] = jnp.where(plan.value_lanes(lane, h), do, jnp.zeros_like(do))
-            ds = grads(
-                h, nt(qh_ref[h], km[near, :]) + near_ref[0, h] + mask_row[0:1, near], near
-            )
-            near_acc[h] += ds
-            acc[h] = nn(ds.astype(bf16), km[near, :])
-
-        def far(n, unused):
-            span, bucket = far_span(start, n, n_left, far_left_bucket, far_right_bucket)
-            slot = (n >= n_left).astype(jnp.int32)
-            if True:
-                for h in range(plan.heads):
-                    offset = mask_row[0:1, span] + table_ref[bucket, h]
-                    ds = grads(h, nt(qh_ref[h], km[span, :]) + offset, span)
-                    acc[h] += nn(ds.astype(bf16), km[span, :])
-                    far_acc[slot, h] += (
-                        ds[:, 0:128] + ds[:, 128:256] + ds[:, 256:384] + ds[:, 384:512]
-                    )
-            return unused
-
-        lax.fori_loop(0, n_left + n_right, far, 0)
-
-        total = jnp.zeros((TQ, WIDE), f32)
-        for h in range(plan.heads):
-            total = jnp.where(lane // 64 == h, acc[h], total)
-        dq_ref[out, :] = total.astype(bf16)
-        return unused
-
-    lax.fori_loop(0, pair // TQ, tile, 0)
-    row = lax.broadcasted_iota(jnp.int32, (EDGE, 3 * EDGE), 0)
-    col = lax.broadcasted_iota(jnp.int32, (EDGE, 3 * EDGE), 1)
-    bucket = bucket_of(col - EDGE - row)
-    for h in range(plan.heads):
-        band = near_acc[h, :EDGE, : 3 * EDGE] + near_acc[h, EDGE:, EDGE:]
-        extra_right = near_acc[h, :EDGE, 3 * EDGE :]
-        extra_left = near_acc[h, EDGE:, :EDGE]
-        for b in range(32):
-            part = jnp.sum(jnp.where(bucket == b, band, 0.0), axis=0, keepdims=True)
-            part = part[:, :128] + part[:, 128:256] + part[:, 256:]
-            if b == far_left_bucket:
-                part = part + jnp.sum(far_acc[0, h], axis=0, keepdims=True)
-                part = part + jnp.sum(extra_left, axis=0, keepdims=True)
-            if b == far_right_bucket:
-                part = part + jnp.sum(far_acc[1, h], axis=0, keepdims=True)
-                part = part + jnp.sum(extra_right, axis=0, keepdims=True)
-            tab_ref[h, b : b + 1, :] = part
-
-
-def dkv_kernel(
-    plan, rows, pair, bounds, table_ref, qall_ref, doall_ref, g_ref, kaug_ref, near_ref,
-    dk_ref, dv_ref, mask_ref, qp, dop, kh_ref, vh_ref, acc_k, acc_v,
-):
-    lane = lanes_of(TQ)
-    first = lanes_of(1)
-    stat = (first >= plan.stat_lane) & (first < plan.stat_lane + 3 * plan.heads)
-    qp[:PAD, :] = jnp.broadcast_to(jnp.where(stat, neg_big, 0.0).astype(bf16), (PAD, WIDE))
-    qp[pl.ds(PAD + rows, PAD), :] = qp[:PAD, :]
-    dop[:PAD, :] = jnp.zeros((PAD, WIDE), bf16)
-    dop[pl.ds(PAD + rows, PAD), :] = jnp.zeros((PAD, WIDE), bf16)
-    step = 512
-
-    def fill(n, unused):
-        at = pl.multiple_of(n * step, step)
-        to = pl.multiple_of(PAD + n * step, 128)
-        qp[pl.ds(to, step), :] = qall_ref[pl.ds(at, step), :]
-        dop[pl.ds(to, step), :] = doall_ref[pl.ds(at, step), :]
-        return unused
-
-    lax.fori_loop(0, rows // step, fill, 0)
-    low = lanes_of(TQ, 128) < 64
-    ones = (lanes_of(TQ, 128) < 3 * plan.heads).astype(bf16)
-
-    def tile(t, unused):
-        start = pl.multiple_of(bounds[0] + t * TQ, 128)
-        n_left, n_right = (bounds[1 + 2 * t], bounds[2 + 2 * t])
-        out = pl.ds(pl.multiple_of(t * TQ, TQ), TQ)
-        middle = g_ref[out, 128:256]
-        k = jnp.concatenate([g_ref[out, 0:128], jnp.where(low, middle, kaug_ref[out, :])], axis=1)
-        v = jnp.concatenate([jnp.where(low, ones, middle), g_ref[out, 256:384]], axis=1)
-        near = pl.ds(pl.multiple_of(start + PAD - EDGE, 128), TK)
-
-        def grads(h, s, span):
-            p = jnp.exp(s)
-            ds = p * nt(vh_ref[h], dop[span, :])
-            return nn(p.astype(bf16), dop[span, :]), nn(ds.astype(bf16), qp[span, :])
-
-        for h in range(plan.heads):
-            kh_ref[h] = jnp.where(plan.key_lanes(lane, h), k, jnp.zeros_like(k))
-            vh_ref[h] = jnp.where(plan.value_lanes(lane, h), v, jnp.zeros_like(v))
-            acc_v[h], acc_k[h] = grads(h, nt(kh_ref[h], qp[near, :]) + near_ref[1, h], near)
-
-        def far(n, unused):
-            span, bucket = far_span(start, n, n_left, far_right_bucket, far_left_bucket)
-            if True:
-                for h in range(plan.heads):
-                    add_v, add_k = grads(
-                        h, nt(kh_ref[h], qp[span, :]) + table_ref[bucket, h], span
-                    )
-                    acc_v[h] += add_v
-                    acc_k[h] += add_k
-            return unused
-
-        lax.fori_loop(0, n_left + n_right, far, 0)
-
-        dk = jnp.zeros((TQ, WIDE), f32)
-        dv = jnp.zeros((TQ, WIDE), f32)
-        mask_grad = jnp.zeros((TQ, 1), f32)
-        for h in range(plan.heads):
-            dk = jnp.where(lane // 64 == h, acc_k[h], dk)
-            dv = jnp.where(lane // 64 == h + 1, acc_v[h], dv)
-            mask_grad = mask_grad + acc_k[h][:, plan.mask_lane : plan.mask_lane + 1]
-        mask_ref[t] = jnp.transpose(jnp.broadcast_to(mask_grad, (TQ, 128)))[:8, :]
-        dk_ref[out, :] = dk.astype(bf16)
-        dv_ref[out, :] = dv.astype(bf16)
-        return unused
-
-    lax.fori_loop(0, pair // TQ, tile, 0)
-
-
-def grad_attended_kernel(plan, branch_ref, w_ref, wide_ref, do_ref):
-    rows = branch_ref.shape[0]
-    lane = lanes_of(rows)
-    grad = nt(branch_ref[...], w_ref[...]).astype(bf16)
-    terms = grad.astype(f32) * wide_ref[...]
-    out = grad
-    for h in range(plan.heads):
-        row_term = jnp.sum(
-            jnp.where(lane // 64 == h + 1, terms, 0.0), axis=1, keepdims=True
-        )
-        for i, part in enumerate(split3(-row_term)):
-            out = jnp.where(lane == 3 * h + i, part, out)
-    do_ref[...] = out
-
-
 vmem = pl.BlockSpec(memory_space=pltpu.VMEM)
 smem = pl.BlockSpec(memory_space=pltpu.SMEM)
 
@@ -430,243 +273,6 @@
 def added(a, b):
     return a + b
 
-
-def scatter_kernel(lines, units, z_first, count, *refs):
-    parts, outs = (refs[:count], refs[count : 2 * count])
-    mine, core_in, x_in, up_in, down_in, load_sem, core_sem, x_sem, up_sem, down_sem = refs[
-        2 * count :
-    ]
-    spot = Spot(lines)
-    z, x, core = (spot.z, spot.x, spot.core)
-    greet(spot, False)
-    loads = []
-    cores = []
-    order = z_first + [u for u in range(len(units)) if u not in z_first]
-
-    def rows_of(u):
-        return pl.ds(units[u][1], units[u][2])
-
-    for u in order:
-        m = units[u][0]
-        load = pltpu.make_async_copy(
-            parts[m].at[:, :, core, rows_of(u)], mine.at[m, :, :, rows_of(u)], load_sem.at[u]
-        )
-        load.start()
-        loads.append(load)
-        copy = send(
-            parts[m].at[:, :, 1 - core, rows_of(u)],
-            core_in.at[m, :, :, rows_of(u)],
-            core_sem.at[0, u],
-            core_sem.at[1, u],
-            spot.core_mate(),
-        )
-        copy.start()
-        cores.append(copy)
-
-    def add_slices(into, source, u, x_slot):
-        m = units[u][0]
-
-        def body(line, unused):
-            at = (m, line, x_slot, rows_of(u))
-            into[at] = added(into[at], source[at])
-            return unused
-
-        lax.fori_loop(0, lines, body, 0)
-
-    def x_copy(u, both):
-        m = units[u][0]
-        if both:
-            src = mine.at[m, :, 1 - x, rows_of(u)]
-            dst = x_in.at[m, :, rows_of(u)]
-        else:
-            src = mine.at[m, z, 1 - x, rows_of(u)]
-            dst = x_in.at[m, z, rows_of(u)]
-        return send(src, dst, x_sem.at[0, u], x_sem.at[1, u], spot.x_mate())
-
-    def line_flow(u, slots):
-        m = units[u][0]
-        n = len(slots)
-
-        def slot_copies(step, d):
-            ring, sem = (up_in, up_sem) if step > 0 else (down_in, down_sem)
-            return [
-                send(
-                    mine.at[m, d, s, rows_of(u)],
-                    ring.at[m, d, s, rows_of(u)],
-                    sem.at[0, u, d, i],
-                    sem.at[1, u, d, i],
-                    spot.z_mate(step),
-                )
-                for i, s in enumerate(slots)
-            ]
-
-        def receive(step, d):
-            ring = up_in if step > 0 else down_in
-            for copy, s in zip(slot_copies(step, d), slots):
-                copy.wait_recv()
-                at = (m, d, s, rows_of(u))
-                mine[at] = added(mine[at], ring[at])
-
-        def ends_first():
-            @pl.when(z == 0)
-            def _():
-                for d in range(lines - 1, 0, -1):
-                    for copy in slot_copies(1, d):
-                        copy.start()
-
-            @pl.when(z == lines - 1)
-            def _():
-                for d in range(lines - 1):
-                    for copy in slot_copies(-1, d):
-                        copy.start()
-
-        def relay(lag):
-            top = lines - 2 if lag == 2 else lag
-
-            @pl.when((z >= lag) & (z <= top))
-            def _():
-                def up(k, unused):
-                    receive(1, lines - 1 - k)
-                    for copy in slot_copies(1, lines - 1 - k):
-                        copy.start()
-                    return unused
-
-                lax.fori_loop(0, lines - 1 - z, up, 0)
-
-            @pl.when((lines - 1 - z >= lag) & (lines - 1 - z <= top))
-            def _():
-                def down(k, unused):
-                    receive(-1, k)
-                    for copy in slot_copies(-1, k):
-                        copy.start()
-                    return unused
-
-                lax.fori_loop(0, z, down, 0)
-
-        def arrive():
-            @pl.when(z > 0)
-            def _():
-                receive(1, z)
-
-            @pl.when(z + 1 < lines)
-            def _():
-                receive(-1, z)
-
-        def finish(k, unused):
-            @pl.when(z < lines - 1 - k)
-            def _():
-                for copy in slot_copies(1, lines - 1 - k):
-                    copy.wait_send()
-
-            @pl.when(z > k)
-            def _():
-                for copy in slot_copies(-1, k):
-                    copy.wait_send()
-
-            return unused
-
-        return (
-            ends_first,
-            relay,
-            arrive,
-            lambda: lax.fori_loop(0, lines - 1, finish, 0),
-        )
-
-    def store(u):
-        m = units[u][0]
-        outs[m][rows_of(u), :] = mine[m, z, x, rows_of(u)].astype(f32)
-
-    pending = {}
-    for i, u in enumerate(order):
-        loads[i].wait()
-        cores[i].wait()
-        if u in z_first:
-            add_slices(mine, core_in, u, 0)
-            add_slices(mine, core_in, u, 1)
-        else:
-            add_slices(mine, core_in, u, 1 - x)
-            copy = x_copy(u, True)
-            copy.start()
-            pending[u] = copy
-            add_slices(mine, core_in, u, x)
-    x_first = [u for u in order if u not in z_first]
-    flows = {u: line_flow(u, [0, 1] if u in z_first else [x]) for u in order}
-    last = {}
-
-    def x_stage(u):
-        m = units[u][0]
-        pending[u].wait()
-
-        def body(line, unused):
-            at = (m, line, x, rows_of(u))
-            mine[at] = added(mine[at], x_in[m, line, rows_of(u)])
-            return unused
-
-        lax.fori_loop(0, lines, body, 0)
-
-    def settle(u):
-        flows[u][2]()
-        if u in z_first:
-            last[u] = x_copy(u, False)
-            last[u].start()
-        else:
-            store(u)
-
-    for t in range(len(order) + 3):
-        if t < len(order):
-            u = order[t]
-            if u not in z_first:
-                x_stage(u)
-            flows[u][0]()
-        for lag in (1, 2):
-            if 0 <= t - lag < len(order):
-                flows[order[t - lag]][1](lag)
-        if 0 <= t - 3 < len(order):
-            settle(order[t - 3])
-    for u, copy in last.items():
-        m = units[u][0]
-        copy.wait()
-        at = (m, z, x, rows_of(u))
-        mine[at] = added(mine[at], x_in[m, z, rows_of(u)])
-        store(u)
-    for u in order:
-        flows[u][3]()
-
-
-def reduce_scatter(parts, cycle_size):
-    lines = cycle_size // 4
-    count = len(parts)
-    units_here, model = parts[0].shape
-    rows = units_here // cycle_size
-    cut = (rows // 2 + 15) // 16 * 16
-    pieces = [(0, cut), (cut, rows - cut)] if cut < rows else [(0, rows)]
-    units = [(m, at, size) for m in range(count) for at, size in pieces]
-    z_first = [len(units) - 1]
-    shaped = [part.reshape(lines, 2, 2, rows, model) for part in parts]
-    hbm = pl.BlockSpec(memory_space=pl.ANY)
-    n = len(units)
-    return pl.pallas_call(
-        functools.partial(scatter_kernel, lines, units, z_first, count),
-        out_shape=[jax.ShapeDtypeStruct((rows, model), f32)] * count,
-        in_specs=[hbm] * count,
-        out_specs=[vmem] * count,
-        scratch_shapes=[
-            pltpu.VMEM((count, lines, 2, rows, model), bf16),
-            pltpu.VMEM((count, lines, 2, rows, model), bf16),
-            pltpu.VMEM((count, lines, rows, model), bf16),
-            pltpu.VMEM((count, lines, 2, rows, model), bf16),
-            pltpu.VMEM((count, lines, 2, rows, model), bf16),
-            pltpu.SemaphoreType.DMA((n,)),
-            pltpu.SemaphoreType.DMA((2, n)),
-            pltpu.SemaphoreType.DMA((2, n)),
-            pltpu.SemaphoreType.DMA((2, n, lines, 2)),
-            pltpu.SemaphoreType.DMA((2, n, lines, 2)),
-        ],
-        compiler_params=pltpu.CompilerParams(
-            vmem_limit_bytes=58 * 2**20, collective_id=1, has_side_effects=True
-        ),
-        name="weight_scatter",
-    )(*shaped)
 
 def first_kernel(
     plan, lines, span, reach, rows, starts, table_ref, tokens_ref, gain_ref, mask_ref,
@@ -1705,6 +1311,674 @@
     )(attended, mixed, tokens, cot, gain, w_out, w_out_far, w_gate, w_up, w_down.T)
 
 
+class Scatter:
+    def __init__(self, spot, units, parts, outs, buffers, sems):
+        self.spot = spot
+        self.units = units
+        self.parts = parts
+        self.outs = outs
+        self.mine, self.core_in, self.x_in, self.up_in, self.down_in = buffers
+        self.load_sem, self.core_sem, self.x_sem, self.up_sem, self.down_sem = sems
+
+    def rows_of(self, u):
+        return pl.ds(self.units[u][1], self.units[u][2])
+
+    def load(self, u):
+        m = self.units[u][0]
+        return pltpu.make_async_copy(
+            self.parts[m].at[:, :, self.spot.core, self.rows_of(u)],
+            self.mine.at[m, :, :, self.rows_of(u)],
+            self.load_sem.at[u],
+        )
+
+    def core_copy(self, u):
+        m = self.units[u][0]
+        return send(
+            self.parts[m].at[:, :, 1 - self.spot.core, self.rows_of(u)],
+            self.core_in.at[m, :, :, self.rows_of(u)],
+            self.core_sem.at[0, u],
+            self.core_sem.at[1, u],
+            self.spot.core_mate(),
+        )
+
+    def x_copy(self, u):
+        m = self.units[u][0]
+        x = self.spot.x
+        src = self.mine.at[m, :, 1 - x, self.rows_of(u)]
+        dst = self.x_in.at[m, :, self.rows_of(u)]
+        return send(src, dst, self.x_sem.at[0, u], self.x_sem.at[1, u], self.spot.x_mate())
+
+    def begin(self, u):
+        self.load(u).start()
+        self.core_copy(u).start()
+
+    def core_stage(self, u):
+        m = self.units[u][0]
+        x = self.spot.x
+        self.load(u).wait()
+        self.core_copy(u).wait()
+
+        def add(slot):
+            def body(line, unused):
+                at = (m, line, slot, self.rows_of(u))
+                self.mine[at] = added(self.mine[at], self.core_in[at])
+                return unused
+
+            lax.fori_loop(0, self.spot.lines, body, 0)
+
+        add(1 - x)
+        self.x_copy(u).start()
+        add(x)
+
+    def x_stage(self, u):
+        m = self.units[u][0]
+        x = self.spot.x
+        self.x_copy(u).wait()
+
+        def body(line, unused):
+            at = (m, line, x, self.rows_of(u))
+            self.mine[at] = added(self.mine[at], self.x_in[m, line, self.rows_of(u)])
+            return unused
+
+        lax.fori_loop(0, self.spot.lines, body, 0)
+        self.ends(u)
+
+    def copy(self, u, step, d):
+        m = self.units[u][0]
+        sem = self.up_sem if step > 0 else self.down_sem
+        ring = self.up_in if step > 0 else self.down_in
+        return send(
+            self.mine.at[m, d, self.spot.x, self.rows_of(u)],
+            ring.at[m, d, self.rows_of(u)],
+            sem.at[0, u, d],
+            sem.at[1, u, d],
+            self.spot.z_mate(step),
+        )
+
+    def receive(self, u, step, d):
+        m = self.units[u][0]
+        self.copy(u, step, d).wait_recv()
+        ring = self.up_in if step > 0 else self.down_in
+        at = (m, d, self.spot.x, self.rows_of(u))
+        self.mine[at] = added(self.mine[at], ring[m, d, self.rows_of(u)])
+
+    def start(self, u, step, d):
+        self.copy(u, step, d).start()
+
+    def ends(self, u):
+        z, lines = (self.spot.z, self.spot.lines)
+
+        @pl.when(z == 0)
+        def _():
+            def up(k, unused):
+                self.start(u, 1, lines - 1 - k)
+                return unused
+
+            lax.fori_loop(0, lines - 1, up, 0)
+
+        @pl.when(z == lines - 1)
+        def _():
+            def down(k, unused):
+                self.start(u, -1, k)
+                return unused
+
+            lax.fori_loop(0, lines - 1, down, 0)
+
+    def relay(self, u, lag):
+        z, lines = (self.spot.z, self.spot.lines)
+        top = lines - 2 if lag == 2 else lag
+
+        @pl.when((z >= lag) & (z <= top))
+        def _():
+            def up(k, unused):
+                self.receive(u, 1, lines - 1 - k)
+                self.start(u, 1, lines - 1 - k)
+                return unused
+
+            lax.fori_loop(0, lines - 1 - z, up, 0)
+
+        @pl.when((lines - 1 - z >= lag) & (lines - 1 - z <= top))
+        def _():
+            def down(k, unused):
+                self.receive(u, -1, k)
+                self.start(u, -1, k)
+                return unused
+
+            lax.fori_loop(0, z, down, 0)
+
+    def settle(self, u):
+        z, lines = (self.spot.z, self.spot.lines)
+
+        @pl.when(z > 0)
+        def _():
+            self.receive(u, 1, z)
+
+        @pl.when(z + 1 < lines)
+        def _():
+            self.receive(u, -1, z)
+
+        self.store(u)
+
+    def store(self, u):
+        m = self.units[u][0]
+        self.outs[m][self.rows_of(u), :] = self.mine[
+            m, self.spot.z, self.spot.x, self.rows_of(u)
+        ].astype(f32)
+
+    def drain(self, u):
+        z, lines = (self.spot.z, self.spot.lines)
+
+        def body(k, unused):
+            @pl.when(z < lines - 1 - k)
+            def _():
+                self.copy(u, 1, lines - 1 - k).wait_send()
+
+            @pl.when(z > k)
+            def _():
+                self.copy(u, -1, k).wait_send()
+
+            return unused
+
+        lax.fori_loop(0, lines - 1, body, 0)
+
+
+def scatter_units(rows):
+    if rows % 16 or rows < 112:
+        return [(m, 0, rows) for m in range(3)]
+    tail = rows - 64
+    return [
+        (0, 0, 64), (1, 0, 64), (2, 0, 64), (0, 64, tail), (1, 64, tail), (2, 64, tail - 16),
+        (2, rows - 16, 16),
+    ]
+
+
+def backward_kernel(
+    plan, lines, span, reach, doc_most, rows, pair, table_ref, qb_ref, do_ref,
+    own_kv, own_aug, near_hbm, aug_hbm, masks_hbm, g_hbm, qall_hbm, branch_hbm, p0, p1, p2,
+    dq_ref, tab_ref, dk_ref, dv_ref, mask_ref, o0, o1, o2, far_hbm, all_do,
+    mine, core_in, x_in, up_in, down_in,
+    km, vm, mask_row, g_buf, aug_buf, qh_ref, doh_ref, acc, near_ref, near_acc, far_acc,
+    load_sem, core_sem, rx_sem, up_sem, down_sem, own_sem, zero_sem, z_sem, x_sem, c_sem, g_sem,
+    q_sem,
+):
+    spot = Spot(lines)
+    z, x, core = (spot.z, spot.x, spot.core)
+    units = scatter_units(o0.shape[0])
+    scatter = Scatter(
+        spot,
+        units,
+        (p0, p1, p2),
+        (o0, o1, o2),
+        (mine, core_in, x_in, up_in, down_in),
+        (load_sem, core_sem, rx_sem, up_sem, down_sem),
+    )
+    order = range(len(units))
+    greet(spot, True)
+    far_copy = send(branch_hbm, far_hbm, own_sem.at[2], own_sem.at[3], spot.y_mate())
+    far_copy.start()
+
+    def outside(d):
+        return (d < z - span) | (d > z + span)
+
+    def pass_copy(step, d):
+        i = 0 if step > 0 else 1
+        part = all_do.at[d, :, core]
+        return send(part, part, z_sem.at[i, d], z_sem.at[2 + i, d], spot.z_mate(step))
+
+    across = send(do_ref, all_do.at[z, x, core], x_sem.at[0], x_sem.at[1], spot.x_mate())
+
+    def beside(d):
+        part = all_do.at[d, :, core]
+        return send(part, part, c_sem.at[0, d], c_sem.at[1, d], spot.core_mate())
+
+    own_copy = pltpu.make_async_copy(do_ref, all_do.at[z, x, core], own_sem.at[0])
+
+    def zero_copies(d):
+        return [
+            pltpu.make_async_copy(vm.at[pl.ds(0, pair)], all_do.at[d, a, b], zero_sem.at[d, a, b])
+            for a in range(2)
+            for b in range(2)
+        ]
+
+    def zero_start(d, unused):
+        @pl.when(outside(d))
+        def _():
+            for copy in zero_copies(d):
+                copy.start()
+
+        return unused
+
+    def turn():
+        across.wait()
+        own_copy.wait()
+
+        @pl.when(z + 1 < lines)
+        def _():
+            pass_copy(1, z).start()
+
+        @pl.when(z > 0)
+        def _():
+            pass_copy(-1, z).start()
+
+        beside(z).start()
+
+    def level(k):
+        @pl.when(z - k >= 0)
+        def _():
+            d = jnp.maximum(z - k, 0)
+            pass_copy(1, d).wait_recv()
+            if k < span:
+
+                @pl.when(z + 1 < lines)
+                def _():
+                    pass_copy(1, d).start()
+
+            beside(d).start()
+
+        @pl.when(z + k < lines)
+        def _():
+            d = jnp.minimum(z + k, lines - 1)
+            pass_copy(-1, d).wait_recv()
+            if k < span:
+
+                @pl.when(z > 0)
+                def _():
+                    pass_copy(-1, d).start()
+
+            beside(d).start()
+
+    def gathered(d, unused):
+        @pl.when(~outside(d))
+        def _():
+            beside(d).wait()
+
+        @pl.when(outside(d))
+        def _():
+            for copy in zero_copies(d):
+                copy.wait()
+
+        @pl.when((z + 1 < lines) & (d <= z) & (d > z - span))
+        def _():
+            pass_copy(1, d).wait_send()
+
+        @pl.when((z > 0) & (d >= z) & (d < z + span))
+        def _():
+            pass_copy(-1, d).wait_send()
+
+        return unused
+
+    own_copy.start()
+    across.start()
+    for u in order:
+        scatter.begin(u)
+    vm[:PAD, :] = jnp.zeros((PAD, WIDE), bf16)
+    lax.fori_loop(0, lines, zero_start, 0)
+
+    base = spot.index * pair
+    total = 4 * lines * pair
+    origin = jnp.clip(base - reach * pair, 0, total - rows)
+    local = base - origin
+    blocks = rows // pair
+
+    def mask_copy(n):
+        to = pl.ds(pl.multiple_of(PAD + n * pair, 128), pair)
+        return pltpu.make_async_copy(masks_hbm.at[n], mask_row.at[:, to], q_sem.at[1 + n])
+
+    def mask_start(n, unused):
+        mask_copy(n).start()
+        return unused
+
+    lax.fori_loop(0, blocks, mask_start, 0)
+    mask_row[:, :PAD] = jnp.zeros((8, PAD), f32)
+    mask_row[:, PAD + rows :] = jnp.zeros((8, PAD), f32)
+    km[:PAD, :] = jnp.broadcast_to(
+        jnp.where(pad_lanes(plan), neg_big, 0.0).astype(bf16), (PAD, WIDE)
+    )
+    km[PAD + rows :, :] = km[:PAD, :]
+    vm[PAD + rows :, :] = jnp.zeros((PAD, WIDE), bf16)
+    low_block = lanes_of(pair, 128) < 64
+    ones_block = (lanes_of(pair, 128) < 3 * plan.heads).astype(bf16)
+
+    def g_copy(n):
+        at = pl.ds(pl.multiple_of(n * pair, pair), pair)
+        return pltpu.make_async_copy(g_hbm.at[at], g_buf.at[n % 2], g_sem.at[0, n % 2])
+
+    def aug_copy(n):
+        at = pl.ds(pl.multiple_of(n * pair, pair), pair)
+        return pltpu.make_async_copy(aug_hbm.at[at], aug_buf.at[n % 2], g_sem.at[1, n % 2])
+
+    def near_copy(flip):
+        return pltpu.make_async_copy(near_hbm.at[flip], near_ref, own_sem.at[1])
+
+    g_copy(0).start()
+    aug_copy(0).start()
+    near_copy(0).start()
+
+    def build(n, unused):
+        g_copy(n).wait()
+        aug_copy(n).wait()
+
+        @pl.when(n + 1 < blocks)
+        def _():
+            g_copy(n + 1).start()
+            aug_copy(n + 1).start()
+
+        mask_copy(n).wait()
+        to = pl.ds(pl.multiple_of(PAD + n * pair, 128), pair)
+        middle = g_buf[n % 2, :, 128:256]
+        km[to, 0:128] = g_buf[n % 2, :, 0:128]
+        km[to, 128:256] = jnp.where(low_block, middle, aug_buf[n % 2])
+        vm[to, 0:128] = jnp.where(low_block, ones_block, middle)
+        vm[to, 128:256] = g_buf[n % 2, :, 256:384]
+        return unused
+
+    lax.fori_loop(0, blocks, build, 0)
+    near_copy(0).wait()
+    near_acc[...] = jnp.zeros_like(near_acc)
+    far_acc[...] = jnp.zeros_like(far_acc)
+    lane = lanes_of(TQ)
+    low = lanes_of(TQ, 128) < 64
+    ones = (lanes_of(TQ, 128) < 3 * plan.heads).astype(bf16)
+
+    def chunks(t):
+        start = local + t * TQ
+        least = jnp.maximum(start - doc_most + 1, 0)
+        most = jnp.minimum(start + TQ + doc_most - 1, rows)
+        n_left = jnp.maximum(start - EDGE - least + TK - 1, 0) // TK
+        n_right = jnp.maximum(most - (start + TK - EDGE) + TK - 1, 0) // TK
+        return start, n_left, n_right
+
+    def rows_of_tile(t):
+        return pl.ds(pl.multiple_of(t * TQ, TQ), TQ)
+
+    def near_of(start):
+        return pl.ds(pl.multiple_of(start + PAD - EDGE, 128), TK)
+
+    def query_grads(h, s, part):
+        return jnp.exp(s) * nt(doh_ref[h], vm[part, :])
+
+    def dq_near(t, start):
+        out = rows_of_tile(t)
+        near = near_of(start)
+        q = qb_ref[out, :]
+        do = do_ref[out, :]
+        for h in range(plan.heads):
+            qh_ref[h] = jnp.where(plan.key_lanes(lane, h), q, jnp.zeros_like(q))
+            doh_ref[h] = jnp.where(plan.value_lanes(lane, h), do, jnp.zeros_like(do))
+            ds = query_grads(
+                h, nt(qh_ref[h], km[near, :]) + near_ref[h] + mask_row[0:1, near], near
+            )
+            near_acc[h] += ds
+            acc[h] = nn(ds.astype(bf16), km[near, :])
+
+    def dq_far(start, n, n_left):
+        part, bucket = far_span(start, n, n_left, far_left_bucket, far_right_bucket)
+        slot = (n >= n_left).astype(jnp.int32)
+        for h in range(plan.heads):
+            offset = mask_row[0:1, part] + table_ref[bucket, h]
+            ds = query_grads(h, nt(qh_ref[h], km[part, :]) + offset, part)
+            acc[h] += nn(ds.astype(bf16), km[part, :])
+            far_acc[slot, h] += ds[:, 0:128] + ds[:, 128:256] + ds[:, 256:384] + ds[:, 384:512]
+
+    def dq_end(t):
+        result = jnp.zeros((TQ, WIDE), f32)
+        for h in range(plan.heads):
+            result = jnp.where(lane // 64 == h, acc[h], result)
+        dq_ref[rows_of_tile(t), :] = result.astype(bf16)
+
+    def table_end():
+        row = lax.broadcasted_iota(jnp.int32, (EDGE, 3 * EDGE), 0)
+        col = lax.broadcasted_iota(jnp.int32, (EDGE, 3 * EDGE), 1)
+        bucket = bucket_of(col - EDGE - row)
+        for h in range(plan.heads):
+            band = near_acc[h, :EDGE, : 3 * EDGE] + near_acc[h, EDGE:, EDGE:]
+
+            def one(b, unused, band=band, h=h):
+                part = jnp.sum(jnp.where(bucket == b, band, 0.0), axis=0, keepdims=True)
+                tab_ref[h, pl.ds(b, 1), :] = part[:, :128] + part[:, 128:256] + part[:, 256:]
+                return unused
+
+            lax.fori_loop(0, 32, one, 0)
+            for b, slot, extra in (
+                (far_left_bucket, 0, near_acc[h, EDGE:, :EDGE]),
+                (far_right_bucket, 1, near_acc[h, :EDGE, 3 * EDGE :]),
+            ):
+                tab_ref[h, b : b + 1, :] += jnp.sum(
+                    far_acc[slot, h], axis=0, keepdims=True
+                ) + jnp.sum(extra, axis=0, keepdims=True)
+
+    def swap_operands():
+        near_copy(1).start()
+        lax.fori_loop(0, lines, gathered, 0)
+        q_copy = pltpu.make_async_copy(qall_hbm, km.at[pl.ds(PAD, rows)], q_sem.at[0])
+        q_copy.start()
+
+        def block_copy(n):
+            b = origin // pair + n
+            return pltpu.make_async_copy(
+                all_do.at[b // 4, (b // 2) % 2, b % 2],
+                vm.at[pl.ds(pl.multiple_of(PAD + n * pair, 128), pair)],
+                q_sem.at[1 + n],
+            )
+
+        def block_start(n, unused):
+            block_copy(n).start()
+            return unused
+
+        lax.fori_loop(0, blocks, block_start, 0)
+        first = lanes_of(1)
+        stat = (first >= plan.stat_lane) & (first < plan.stat_lane + 3 * plan.heads)
+        km[:PAD, :] = jnp.broadcast_to(jnp.where(stat, neg_big, 0.0).astype(bf16), (PAD, WIDE))
+        km[PAD + rows :, :] = km[:PAD, :]
+
+        def block_wait(n, unused):
+            block_copy(n).wait()
+            return unused
+
+        lax.fori_loop(0, blocks, block_wait, 0)
+        q_copy.wait()
+        near_copy(1).wait()
+
+    def key_grads(h, s, part):
+        p = jnp.exp(s)
+        ds = p * nt(doh_ref[h], vm[part, :])
+        return nn(p.astype(bf16), vm[part, :]), nn(ds.astype(bf16), km[part, :])
+
+    def dkv_near(t, start):
+        out = rows_of_tile(t)
+        near = near_of(start)
+        middle = own_kv[out, 128:256]
+        k = jnp.concatenate([own_kv[out, 0:128], jnp.where(low, middle, own_aug[out, :])], axis=1)
+        v = jnp.concatenate([jnp.where(low, ones, middle), own_kv[out, 256:384]], axis=1)
+        for h in range(plan.heads):
+            qh_ref[h] = jnp.where(plan.key_lanes(lane, h), k, jnp.zeros_like(k))
+            doh_ref[h] = jnp.where(plan.value_lanes(lane, h), v, jnp.zeros_like(v))
+            near_acc[h, :, :WIDE], acc[h] = key_grads(
+                h, nt(qh_ref[h], km[near, :]) + near_ref[h], near
+            )
+
+    def dkv_far(start, n, n_left):
+        part, bucket = far_span(start, n, n_left, far_right_bucket, far_left_bucket)
+        for h in range(plan.heads):
+            add_v, add_k = key_grads(h, nt(qh_ref[h], km[part, :]) + table_ref[bucket, h], part)
+            near_acc[h, :, :WIDE] += add_v
+            acc[h] += add_k
+
+    def dkv_end(t):
+        out = rows_of_tile(t)
+        dk = jnp.zeros((TQ, WIDE), f32)
+        dv = jnp.zeros((TQ, WIDE), f32)
+        mask_grad = jnp.zeros((TQ, 1), f32)
+        for h in range(plan.heads):
+            dk = jnp.where(lane // 64 == h, acc[h], dk)
+            dv = jnp.where(lane // 64 == h + 1, near_acc[h, :, :WIDE], dv)
+            mask_grad = mask_grad + acc[h][:, plan.mask_lane : plan.mask_lane + 1]
+        mask_ref[t] = jnp.transpose(jnp.broadcast_to(mask_grad, (TQ, 128)))[:8, :]
+        dk_ref[out, :] = dk.astype(bf16)
+        dv_ref[out, :] = dv.astype(bf16)
+
+    tiles = pair // TQ
+    steps = 1 + 2 * (-(-doc_most // TK)) + 1
+    half_slots = tiles * steps
+    last_step = steps - 1
+
+    def attention(w):
+        backward = w >= half_slots
+        t = (w % half_slots) // steps
+        n = w % steps
+        start, n_left, n_right = chunks(t)
+        live = (n > 0) & (n - 1 < n_left + n_right)
+
+        @pl.when(~backward)
+        def _():
+            @pl.when(n == 0)
+            def _():
+                dq_near(t, start)
+
+            @pl.when(live)
+            def _():
+                dq_far(start, n - 1, n_left)
+
+            @pl.when(n == last_step)
+            def _():
+                dq_end(t)
+
+        @pl.when(backward & (w < 2 * half_slots))
+        def _():
+            @pl.when(w == half_slots)
+            def _():
+                table_end()
+                swap_operands()
+
+            @pl.when(n == 0)
+            def _():
+                dkv_near(t, start)
+
+            @pl.when(live)
+            def _():
+                dkv_far(start, n - 1, n_left)
+
+            @pl.when(n == last_step)
+            def _():
+                dkv_end(t)
+
+    work = 2 * half_slots
+    events = []
+
+    def due(time, run, *args):
+        events.append((max(0, int((time - start_us) / slot_us)), functools.partial(run, *args)))
+
+    start_us, slot_us = (6.0, 1.05)
+    due(6.0, turn)
+    for k in range(1, span + 1):
+        due((22.0, 36.0)[min(k, 2) - 1], level, k)
+    times = (
+        (7.0, 26.0, 51.0, 61.0, 68.0),
+        (10.5, 43.0, 64.0, 74.0, 81.0),
+        (14.0, 60.0, 77.0, 87.0, 94.0),
+        (17.0, 73.0, 87.0, 95.0, 101.0),
+        (20.0, 86.0, 97.5, 106.0, 111.0),
+        (22.0, 95.0, 104.0, 110.0, 114.0),
+        (23.0, 99.0, 107.0, 111.0, 114.5),
+    )
+    for u in order:
+        core_at, x_at, one_at, two_at, end_at = times[u]
+        due(core_at, scatter.core_stage, u)
+        due(x_at, scatter.x_stage, u)
+        due(one_at, scatter.relay, u, 1)
+        due(two_at, scatter.relay, u, 2)
+        due(end_at, scatter.settle, u)
+    events.sort(key=lambda event: event[0])
+    end = max(work, events[-1][0] + 1)
+
+    def slot(w, unused):
+        for at, run in events:
+
+            @pl.when(w == at)
+            def _(run=run):
+                run()
+
+        attention(w)
+        return unused
+
+    lax.fori_loop(0, end, slot, 0)
+    for u in order:
+        scatter.drain(u)
+    far_copy.wait()
+
+
+def backward(
+    plan, cycle_size, reach, doc_most, rows, table, aug, masks, q_back, do_wide, own_kv, own_aug,
+    near_bias, kv_all, q_all, branch, parts,
+):
+    lines = cycle_size // 4
+    span = min(lines - 1, (reach + 3) // 4)
+    pair = q_back.shape[0]
+    units_here, model = parts[0].shape
+    size = units_here // cycle_size
+    units = scatter_units(size)
+    shaped = [part.reshape(lines, 2, 2, size, model) for part in parts]
+    n = len(units)
+    heads = plan.heads
+    padded = rows + 2 * PAD
+    hbm = pl.BlockSpec(memory_space=pl.ANY)
+    dma = pltpu.SemaphoreType.DMA
+    return pl.pallas_call(
+        functools.partial(backward_kernel, plan, lines, span, reach, doc_most, rows, pair),
+        out_shape=[
+            jax.ShapeDtypeStruct((pair, WIDE), bf16),
+            jax.ShapeDtypeStruct((heads, 32, 128), f32),
+            jax.ShapeDtypeStruct((pair, WIDE), bf16),
+            jax.ShapeDtypeStruct((pair, WIDE), bf16),
+            jax.ShapeDtypeStruct((pair // TQ, 8, TQ), f32),
+        ]
+        + [jax.ShapeDtypeStruct((size, model), f32)] * 3
+        + [
+            jax.ShapeDtypeStruct(branch.shape, bf16),
+            jax.ShapeDtypeStruct((lines, 2, 2, pair, WIDE), bf16),
+        ],
+        in_specs=[smem] + [vmem] * 4 + [hbm] * 9,
+        out_specs=[vmem] * 8 + [hbm] * 2,
+        scratch_shapes=[
+            pltpu.VMEM((3, lines, 2, size, model), bf16),
+            pltpu.VMEM((3, lines, 2, size, model), bf16),
+            pltpu.VMEM((3, lines, size, model), bf16),
+            pltpu.VMEM((3, lines, size, model), bf16),
+            pltpu.VMEM((3, lines, size, model), bf16),
+            pltpu.VMEM((padded, WIDE), bf16),
+            pltpu.VMEM((padded, WIDE), bf16),
+            pltpu.VMEM((8, padded), f32),
+            pltpu.VMEM((2, pair, 2 * plan.cols), bf16),
+            pltpu.VMEM((2, pair, 128), bf16),
+            pltpu.VMEM((heads, TQ, WIDE), bf16),
+            pltpu.VMEM((heads, TQ, WIDE), bf16),
+            pltpu.VMEM((heads, TQ, WIDE), f32),
+            pltpu.VMEM((heads, TQ, TK), f32),
+            pltpu.VMEM((heads, TQ, TK), f32),
+            pltpu.VMEM((2, heads, TQ, 128), f32),
+            dma((n,)),
+            dma((2, n)),
+            dma((2, n)),
+            dma((2, n, lines)),
+            dma((2, n, lines)),
+            dma((4,)),
+            dma((lines, 2, 2)),
+            dma((4, lines)),
+            dma((2,)),
+            dma((2, lines)),
+            dma((2, 2)),
+            dma((1 + rows // pair,)),
+        ],
+        compiler_params=pltpu.CompilerParams(
+            vmem_limit_bytes=62 * 2**20, collective_id=1, has_side_effects=True
+        ),
+        name="backward",
+    )(
+        table, q_back, do_wide, own_kv, own_aug, near_bias, aug, masks, kv_all, q_all,
+        branch, *shaped
+    )
+
+
 def shards(
     tokens,
     doc_lengths,
@@ -1803,7 +2077,6 @@
         name="attention_forward",
     )(bounds, bias_table, kv_all, k_aug, masks, q_wide, near_bias)
     q_all = window(gather(q_back))
-    swap = functools.partial(lax.ppermute, axis_name="wa", perm=((0, 1), (1, 0)))
     hidden, grad_hidden, branch, ffn_part, do_wide, gain_ffn_part, *stacks = middle(
         plan,
         cycle_size,
@@ -1818,52 +2091,29 @@
         w_up,
         w_down,
     )
-    far_branch = swap(branch)
-    do_all = window(gather(do_wide))
-    grad_w_down, grad_w_gate, grad_w_up = reduce_scatter(stacks, cycle_size)
+    (
+        grad_queries, table_part, grad_keys, grad_values, mask_part,
+        grad_w_down, grad_w_gate, grad_w_up, far_branch, unused_gathered,
+    ) = backward(
+        plan,
+        cycle_size,
+        reach,
+        doc_most,
+        rows,
+        bias_table,
+        k_aug,
+        masks,
+        q_back,
+        do_wide,
+        own_kv,
+        own_aug,
+        near_bias,
+        kv_all,
+        q_all,
+        branch,
+        stacks,
+    )
     grad_w_gate, grad_w_up = (grad_w_gate.T, grad_w_up.T)
-
-    grad_queries, table_part = pl.pallas_call(
-        functools.partial(dq_kernel, plan, rows, pair),
-        out_shape=(
-            jax.ShapeDtypeStruct((pair, WIDE), bf16),
-            jax.ShapeDtypeStruct((heads, 32, 128), f32),
-        ),
-        in_specs=[smem, smem] + [vmem] * 6,
-        out_specs=(vmem, vmem),
-        scratch_shapes=[
-            pltpu.VMEM((padded, WIDE), bf16),
-            pltpu.VMEM((padded, WIDE), bf16),
-            pltpu.VMEM((8, padded), f32),
-            pltpu.VMEM((heads, TQ, WIDE), f32),
-            pltpu.VMEM((heads, TQ, WIDE), bf16),
-            pltpu.VMEM((heads, TQ, WIDE), bf16),
-            pltpu.VMEM((heads, TQ, TK), f32),
-            pltpu.VMEM((2, heads, TQ, 128), f32),
-        ],
-        compiler_params=params(),
-        name="attention_grad_queries",
-    )(bounds, bias_table, kv_all, k_aug, masks, q_back, do_wide, near_bias)
-    grad_keys, grad_values, mask_part = pl.pallas_call(
-        functools.partial(dkv_kernel, plan, rows, pair),
-        out_shape=(
-            jax.ShapeDtypeStruct((pair, WIDE), bf16),
-            jax.ShapeDtypeStruct((pair, WIDE), bf16),
-            jax.ShapeDtypeStruct((tiles, 8, TQ), f32),
-        ),
-        in_specs=[smem, smem, vmem, vmem, vmem, vmem, vmem],
-        out_specs=(vmem, vmem, vmem),
-        scratch_shapes=[
-            pltpu.VMEM((padded, WIDE), bf16),
-            pltpu.VMEM((padded, WIDE), bf16),
-            pltpu.VMEM((heads, TQ, WIDE), bf16),
-            pltpu.VMEM((heads, TQ, WIDE), bf16),
-            pltpu.VMEM((heads, TQ, WIDE), f32),
-            pltpu.VMEM((heads, TQ, WIDE), f32),
-        ],
-        compiler_params=params(),
-        name="attention_grad_keys",
-    )(bounds, bias_table, q_all, do_all, own_kv, own_aug, near_bias)
     cols = plan.cols
     table_row = jnp.sum(table_part, axis=2).reshape(1, -1)
     table_row = jnp.pad(table_row, ((0, 0), (0, model - table_row.shape[1])))

time: 429 us -> 412 us (0.960)
  waiting for transfers between devices: 10.9 us -> 1.97 us
    pallas_call x1, Pallas kernels: 94.7 us -> 80.5 us  [finish(): pl.pallas_call(functools.partial(finish_kernel, plan, lines), out_shape=[...]
    all_gather x1, waiting for transfers between devices: 10.8 us -> 1.92 us  [shards(): pair_cot = lax.all_gather(cot_late, 'wa', axis=0, tiled=True)]
    pallas_call x1, Pallas kernels: 13.7 us -> 22.5 us  [shards(): pl.pallas_call(functools.partial(fwd_kernel, plan, rows, pair), out_shape...]
    pallas_call x3 -> x1, Pallas kernels: 151 us -> 155 us  [backward(): pl.pallas_call(functools.partial(backward_kernel, plan, lines, span, reac...]
    unnamed x25 -> x27, local copies, waits for them, and re-layouts: 11.6 us -> 8.94 us
  transfers between devices with their start and end apart: 4 -> 2, of which waited for: 1 -> 1; matrix products, arithmetic and copies ran while one was open for 1% -> 1% of each run, Pallas kernels for 50% -> 20%
where the time goes in v9:
time: 412 us
  Pallas kernels  370 us (90%)
  local copies, waits for them, and re-layouts  21.2 us (5%)
  between operations  14.2 us (3%)
  other arithmetic  4.82 us (1%)
    pallas_call x1, Pallas kernels, backward(): pl.pallas_call(functools.partial(backward_kernel, plan, lines, span, reac...  155 us
    pallas_call x1, Pallas kernels, finish(): pl.pallas_call(functools.partial(finish_kernel, plan, lines), out_shape=[...  80.5 us
    pallas_call x1, Pallas kernels, middle(): pl.pallas_call(functools.partial(middle_kernel, plan, cycle_size), out_sh...  61.1 us
    pallas_call x1, Pallas kernels, first(): pl.pallas_call(functools.partial(first_kernel, plan, lines, span, reach,...  50.5 us
    pallas_call x1, Pallas kernels, shards(): pl.pallas_call(functools.partial(fwd_kernel, plan, rows, pair), out_shape...  22.5 us
    unnamed x27, local copies, waits for them, and re-layouts  8.94 us
  transfers between devices with their start and end apart: 2, of which 1 were waited for; matrix products, arithmetic and copies ran while one was open for 1% of the time, Pallas kernels for 20%

profile of v9, /device:TPU:0, one launch (start us, length us, event | category | flops | bytes accessed | tf_op | source)
XLA Modules:
  0.0 412.3 jit_solution(13880831268847862495)
XLA Ops:
  7.2 0.8 reduce-window.8
  8.1 1.2 bitcast_subtract_fusion.2.starts
  9.2 1.4 copy.41.table_ref
  10.6 2.3 copy.38.tokens_ref
  12.9 1.3 broadcast_in_dim.51.gain_ref
  14.2 0.6 broadcast_in_dim.52.mask_ref
  14.8 50.5 %project_gather.1 = (bf16[512,1472]{1,0:T(8,128)(2,1)}, bf16[512,1472]{1,0:T(8,128)(2,1)}, bf16[512,256]{1,0:T(8,128)(2,1)}, bf16[512,384]{1,0:T(8,128)(2,1)}, b...) custom-call(s32[8]{0:T(128)} %bitcast_subtract_fusion.2.starts, ...), custom_call_target="tpu_custom_call" | custom-call | tf_op jit(solution)/shard_map/project_gather/pallas_call | solution.py:607
  65.3 1.2 copy.40
  66.5 0.2 all-gather.5.cloned.1.call-start
  66.8 0.2 fusion.2
  66.9 0.2 fusion.3
  67.2 0.2 fusion.5
  67.4 0.1 copy.36
  67.6 0.6 pad_add_fusion.1.bounds
  68.2 22.5 %attention_forward.1 = (bf16[512,256]{1,0:T(8,128)(2,1)}, f32[512,256]{1,0:T(8,128)}, bf16[512,256]{1,0:T(8,128)(2,1)}) custom-call(s32[5]{0:T(128)} %pad_add_fusion.1.bounds, f32[32,3]{1,0:T(8,128)} %copy.41.table_ref, bf16[8192,384]{1,0:T(8,128)(2,1)} %bitcast.44, bf16[8192,128]{1,0:T(8,128)(2,1)} %get-tuple-element.52.kaug_ref.aug_hbm, ...), custom_call_target="tpu_custom_call" | custom-call | tf_op jit(solution)/shard_map/attention_forward/pallas_call | solution.py:2059
  90.7 0.6 broadcast_in_dim.53.gain_ref
  91.4 1.9 all-gather.3.cloned.1.call-done.cot_ref
  93.3 61.1 %feed_forward.1 = (f32[256,1472]{1,0:T(8,128)}, f32[256,1472]{1,0:T(8,128)}, bf16[256,1472]{1,0:T(8,128)(2,1)}, bf16[512,1472]{1,0:T(8,128)(2,1)}, bf16[512,256]...) custom-call(bf16[512,256]{1,0:T(8,128)(2,1)} %get-tuple-element.58.a, ...), custom_call_target="tpu_custom_call" | custom-call | tf_op jit(solution)/shard_map/feed_forward/pallas_call | solution.py:1273
  154.5 155.2 %backward.1 = (bf16[512,256]{1,0:T(8,128)(2,1)}, f32[3,32,128]{2,1,0:T(8,128)}, bf16[512,256]{1,0:T(8,128)(2,1)}, bf16[512,256]{1,0:T(8,128)(2,1)}, f32[2,8,256]...) custom-call(f32[32,3]{1,0:T(8,128)} %copy.41.table_ref, ...), custom_call_target="tpu_custom_call" | custom-call | tf_op jit(solution)/shard_map/backward/pallas_call | solution.py:1926
  309.7 0.9 reduce_sum.55
  310.7 0.7 fusion.small_ref
  311.4 80.5 %finish.1 = (bf16[256,1472]{1,0:T(8,128)(2,1)}, f32[256,1472]{1,0:T(8,128)}, f32[8,256]{1,0:T(8,128)}, bf16[4,2,2,48,1472]{4,3,2,1,0:T(8,128)(2,1)}, f32[8,1472]{1,0:T(8,128)}) custom-call(bf16[512,256]{1,0:T(8,128)(2,1)} %get-tuple-element.70.dq_ref, bf16[512,256]{1,0:T(8,128)(2,1)} %get-tuple-element.71.dk_ref, bf16[512,256]{1,0:T(8,128)(2,1)} %get-tuple-element.72.dv_ref, ...), custom_call_target="tpu_custom_call" | custom-call | tf_op jit(solution)/shard_map/finish/pallas_call | solution.py:998
  391.9 1.5 slice_reduce_fusion
  393.4 0.7 slice_reduce_fusion.2
  394.1 4.1 fusion.10
  398.3 1.6 copy.44
  399.8 1.1 copy.43
  401.0 0.7 reshape_squeeze.3
  401.6 1.3 slice.28
  402.9 0.8 copy.48
  403.8 0.8 copy.49
  404.6 0.8 copy.50
  (35 shorter events, 0.4 us)
Async XLA Ops:
  7.2 7.0 %copy-start.9 = (bf16[512]{0:T(512)(128)(2,1)S(1)}, bf16[512]{0:T(512)(128)(2,1)}, u32[]{:S(2)}) copy-start(bf16[512]{0:T(512)(128)(2,1)} %param.16) | copy-start | bytes 3076
  7.2 86.2 %all-gather.3.cloned.1.call-start = ((), (), s32[]{:S(2)}) async-start(), calls=%async_computation | async-start | bytes 2359296 | tf_op jit(solution)/shard_map/all_gather | solution.py:2054
  14.8 50.5 %copy-start.2 = (bf16[256,1472]{0,1:T(8,128)(2,1)S(1)}, bf16[256,1472]{0,1:T(8,128)(2,1)}, u32[]{:S(2)}) copy-start(bf16[256,1472]{0,1:T(8,128)(2,1)} %param.27) | copy-start | bytes 2260996
  65.3 1.5 copy-start.8
  66.5 88.0 %all-gather.5.cloned.1.call-start = ((), (), s32[]{:S(2)}) async-start(), calls=%async_computation.1 | async-start | bytes 4456448 | tf_op jit(solution)/shard_map/all_gather | solution.py:2079
  68.2 22.6 %copy-start.6 = (f32[1472]{0:T(1024)S(1)}, f32[1472]{0:T(1024)}, u32[]{:S(2)}) copy-start(f32[1472]{0:T(1024)} %param.23) | copy-start | bytes 17668
  154.5 156.2 %copy-start.7 = (f32[1,1472]{1,0:T(1,128)S(1)}, f32[1,1472]{1,0:T(1,128)}, u32[]{:S(2)}) copy-start(f32[1,1472]{1,0:T(1,128)} %get-tuple-element.79) | copy-start | bytes 17668
  394.1 4.1 %copy-start = (f32[256,1472]{1,0:T(8,128)S(1)}, f32[256,1472]{1,0:T(8,128)}, u32[]{:S(2)}) copy-start(f32[256,1472]{1,0:T(8,128)} %get-tuple-element.103) | copy-start | bytes 4521988
  398.2 1.6 copy-start.1
  398.2 4.7 %copy-start.5 = (f32[112,1472]{1,0:T(8,128)S(1)}, f32[112,1472]{1,0:T(8,128)}, u32[]{:S(2)}) copy-start(f32[112,1472]{1,0:T(8,128)} %get-tuple-element.86) | copy-start | bytes 1978372
  399.8 3.9 copy-start.4
  401.0 3.6 copy-start.3
Sparse Core Ops, SparseCore 0:
  66.6 26.6 all-gather.2
  96.1 54.5 all-gather.4

commit v10 on v9

--- a/solution.py
+++ b/solution.py
@@ -672,9 +672,9 @@
 
 def finish_kernel(
     plan, lines, dq_ref, dk_ref, dv_ref, mask_ref, wq_hbm, wk_hbm, wv_hbm, normed_ref, att_ref, branch_ref, far_ref,
-    tokens_ref, gain_ref, hidden_ref, gh_ref, ffn_ref, small_ref,
-    out_ref, gt_ref, gm_ref, weights_ref, total_ref,
-    w3_ref, load_sem, lefts, rights, product, mine, core_in, x_in, up_in, down_in, all_w, y_out, y_in, own_part, ffn_in, mask_in,
+    tokens_ref, gain_ref, gh_ref, small_ref,
+    gt_ref, gm_ref, weights_ref, total_ref,
+    w3_ref, load_sem, lefts, rights, product, mine, core_in, x_in, up_in, down_in, all_w, y_out, y_in, own_part, mask_in,
     small_own, small_y, small_core, small_x, small_all,
     y_sem, core_sem, x_sem, up_sem, down_sem, gz_sem, gx_sem, gc_sem, sz_sem,
 ):
@@ -742,7 +742,8 @@
             spot.core_mate(),
         )
 
-    def fill(m, unused):
+    def fill(i, unused):
+        m = (3 * i) % 4
         product[...] = tn(lefts[m], rights[m // 3]).astype(bf16)
 
         def place(offset):
@@ -763,11 +764,6 @@
         return unused
 
     lax.fori_loop(0, 4, fill, 0)
-    ffn_copy = send(
-        ffn_ref.at[their_rows], ffn_in, y_sem.at[0, 3], y_sem.at[1, 3], spot.y_mate()
-    )
-    ffn_copy.start()
-
     def x_copy(d):
         return send(
             mine.at[d, 1 - x, core], x_in.at[d], x_sem.at[0, d], x_sem.at[1, d], spot.x_mate()
@@ -784,7 +780,8 @@
         )
         return unused
 
-    def core_stage(m, unused):
+    def core_stage(i, unused):
+        m = (3 * i) % 4
         core_copy(m).wait()
         lax.fori_loop(m * per // 4, (m + 1) * per // 4, core_add, 0)
         return unused
@@ -835,7 +832,8 @@
         ring = up_in if step > 0 else down_in
         mine[d, x, core] = added(mine[d, x, core], ring[d])
 
-    def x_add(d, unused):
+    def x_add(i, unused):
+        d = (i * (lines - 1)) % lines
         x_copy(d).wait()
         mine[d, x, core] = added(mine[d, x, core], x_in[d])
 
@@ -941,17 +939,6 @@
         return total + small_all[d]
 
     total_ref[...] = lax.fori_loop(1, lines, add_small, small_all[0])
-    ffn_copy.wait()
-
-    def last(j, unused):
-        at = pl.ds(pl.multiple_of(j * step, step), step)
-        here = pl.ds(pl.multiple_of(wa * half + j * step, step), step)
-        total = hidden_ref[at, :] + ffn_ref[here, :].astype(f32) + ffn_in[at, :].astype(f32)
-        out_ref[at, :] = total.astype(bf16)
-        return unused
-
-    lax.fori_loop(0, half // step, last, 0)
-
     def spread(d, unused):
         across(d).wait()
         beside(d).start()
@@ -998,7 +985,6 @@
     return pl.pallas_call(
         functools.partial(finish_kernel, plan, lines),
         out_shape=[
-            jax.ShapeDtypeStruct((half, model), bf16),
             jax.ShapeDtypeStruct((half, model), f32),
             jax.ShapeDtypeStruct((8, half), f32),
             jax.ShapeDtypeStruct((lines, 2, 2, rows, model), bf16),
@@ -1007,7 +993,7 @@
         in_specs=[vmem] * 4
         + [pl.BlockSpec(memory_space=pl.ANY)] * 3
         + [vmem] * (len(operands) - 7),
-        out_specs=[vmem] * 5,
+        out_specs=[vmem] * 4,
         scratch_shapes=[
             pltpu.VMEM((3 * WIDE, model), bf16),
             dma((3,)),
@@ -1023,7 +1009,6 @@
             pltpu.VMEM((2, half // 2, model), bf16),
             pltpu.VMEM((2, half // 2, model), bf16),
             pltpu.VMEM((half, model), f32),
-            pltpu.VMEM((half, model), bf16),
             pltpu.VMEM((8, half), f32),
             pltpu.VMEM((8, model), f32),
             pltpu.VMEM((8, model), f32),
@@ -1054,7 +1039,7 @@
 def middle_kernel(
     plan, cycle_size, att_ref, mixed_ref, tokens_ref, cot_ref, gain_ref,
     wo_hbm, wo_far_hbm, wg_hbm, wu_hbm, wd_hbm,
-    hidden_ref, gh_ref, branch_ref, ffn_ref, do_ref, gain_part_ref, *refs,
+    hidden_ref, gh_ref, branch_ref, ffn_ref, ffn_far_ref, do_ref, gain_part_ref, *refs,
 ):
     stacks, refs = (refs[:3], refs[3:])
     (
@@ -1151,7 +1136,6 @@
             return unused
 
         lax.fori_loop(0, units // wide, tile, 0)
-        ffn_ref[rows, :] = acc_f[...].astype(bf16)
 
     def d_copy(i):
         return send(
@@ -1172,6 +1156,11 @@
             lax.fori_loop(0, 4, send_grad, 0)
             normal(2, ours, True)
             normal(3, ours, True)
+            ffn_far_ref[...] = acc_f[...].astype(bf16)
+
+        @pl.when(k == 1)
+        def _():
+            ffn_ref[...] = acc_f[...].astype(bf16)
 
         return unused
 
@@ -1276,13 +1265,14 @@
             jax.ShapeDtypeStruct((half, model), f32),
             jax.ShapeDtypeStruct((half, model), f32),
             jax.ShapeDtypeStruct((half, model), bf16),
-            jax.ShapeDtypeStruct((pair, model), bf16),
+            jax.ShapeDtypeStruct((half, model), bf16),
+            jax.ShapeDtypeStruct((half, model), bf16),
             jax.ShapeDtypeStruct((pair, WIDE), bf16),
             jax.ShapeDtypeStruct((1, model), f32),
         ]
         + [jax.ShapeDtypeStruct((units, model), bf16)] * 3,
         in_specs=[vmem] * 5 + [hbm] * 5,
-        out_specs=[vmem] * 6 + [hbm] * 3,
+        out_specs=[vmem] * 7 + [hbm] * 3,
         scratch_shapes=[
             pltpu.VMEM((model, units), bf16),
             pltpu.VMEM((model, units), bf16),
@@ -1494,8 +1484,8 @@
 
 def backward_kernel(
     plan, lines, span, reach, doc_most, rows, pair, table_ref, qb_ref, do_ref,
-    own_kv, own_aug, near_hbm, aug_hbm, masks_hbm, g_hbm, qall_hbm, branch_hbm, p0, p1, p2,
-    dq_ref, tab_ref, dk_ref, dv_ref, mask_ref, o0, o1, o2, far_hbm, all_do,
+    own_kv, own_aug, near_hbm, aug_hbm, masks_hbm, g_hbm, qall_hbm, branch_hbm, ffn_hbm, p0, p1, p2,
+    dq_ref, tab_ref, dk_ref, dv_ref, mask_ref, o0, o1, o2, far_hbm, ffn_in_hbm, all_do,
     mine, core_in, x_in, up_in, down_in,
     km, vm, mask_row, g_buf, aug_buf, qh_ref, doh_ref, acc, near_ref, near_acc, far_acc,
     load_sem, core_sem, rx_sem, up_sem, down_sem, own_sem, zero_sem, z_sem, x_sem, c_sem, g_sem,
@@ -1516,6 +1506,8 @@
     greet(spot, True)
     far_copy = send(branch_hbm, far_hbm, own_sem.at[2], own_sem.at[3], spot.y_mate())
     far_copy.start()
+    ffn_copy = send(ffn_hbm, ffn_in_hbm, own_sem.at[4], own_sem.at[5], spot.y_mate())
+    ffn_copy.start()
 
     def outside(d):
         return (d < z - span) | (d > z + span)
@@ -1672,7 +1664,10 @@
         vm[to, 128:256] = g_buf[n % 2, :, 256:384]
         return unused
 
-    lax.fori_loop(0, blocks, build, 0)
+    early = min(6, blocks)
+    lax.fori_loop(0, early, build, 0)
+    scatter.core_stage(0)
+    lax.fori_loop(early, blocks, build, 0)
     near_copy(0).wait()
     near_acc[...] = jnp.zeros_like(near_acc)
     far_acc[...] = jnp.zeros_like(far_acc)
@@ -1711,14 +1706,27 @@
             near_acc[h] += ds
             acc[h] = nn(ds.astype(bf16), km[near, :])
 
-    def dq_far(start, n, n_left):
-        part, bucket = far_span(start, n, n_left, far_left_bucket, far_right_bucket)
-        slot = (n >= n_left).astype(jnp.int32)
+    def far_pair(start, n, n_left, count, left, right):
+        pair_of = []
+        for i in range(2):
+            part, bucket = far_span(start, 2 * n + i, n_left, left, right)
+            at = jnp.where(2 * n + i < count, part.start, 0)
+            pair_of.append((pl.ds(pl.multiple_of(at, 128), TK), bucket))
+        return pair_of
+
+    def dq_far(start, n, n_left, count):
+        parts = far_pair(start, n, n_left, count, far_left_bucket, far_right_bucket)
         for h in range(plan.heads):
-            offset = mask_row[0:1, part] + table_ref[bucket, h]
-            ds = query_grads(h, nt(qh_ref[h], km[part, :]) + offset, part)
-            acc[h] += nn(ds.astype(bf16), km[part, :])
-            far_acc[slot, h] += ds[:, 0:128] + ds[:, 128:256] + ds[:, 256:384] + ds[:, 384:512]
+            grads = []
+            for i, (part, bucket) in enumerate(parts):
+                slot = (2 * n + i >= n_left).astype(jnp.int32)
+                offset = mask_row[0:1, part] + table_ref[bucket, h]
+                ds = query_grads(h, nt(qh_ref[h], km[part, :]) + offset, part)
+                grads.append(nn(ds.astype(bf16), km[part, :]))
+                far_acc[slot, h] += (
+                    ds[:, 0:128] + ds[:, 128:256] + ds[:, 256:384] + ds[:, 384:512]
+                )
+            acc[h] += grads[0] + grads[1]
 
     def dq_end(t):
         result = jnp.zeros((TQ, WIDE), f32)
@@ -1797,12 +1805,15 @@
                 h, nt(qh_ref[h], km[near, :]) + near_ref[h], near
             )
 
-    def dkv_far(start, n, n_left):
-        part, bucket = far_span(start, n, n_left, far_right_bucket, far_left_bucket)
+    def dkv_far(start, n, n_left, count):
+        parts = far_pair(start, n, n_left, count, far_right_bucket, far_left_bucket)
         for h in range(plan.heads):
-            add_v, add_k = key_grads(h, nt(qh_ref[h], km[part, :]) + table_ref[bucket, h], part)
-            near_acc[h, :, :WIDE] += add_v
-            acc[h] += add_k
+            (v_one, k_one), (v_two, k_two) = [
+                key_grads(h, nt(qh_ref[h], km[part, :]) + table_ref[bucket, h], part)
+                for part, bucket in parts
+            ]
+            near_acc[h, :, :WIDE] += v_one + v_two
+            acc[h] += k_one + k_two
 
     def dkv_end(t):
         out = rows_of_tile(t)
@@ -1818,7 +1829,7 @@
         dv_ref[out, :] = dv.astype(bf16)
 
     tiles = pair // TQ
-    steps = 1 + 2 * (-(-doc_most // TK)) + 1
+    steps = 1 + -(-(2 * (-(-doc_most // TK)) + 1) // 2)
     half_slots = tiles * steps
     last_step = steps - 1
 
@@ -1827,7 +1838,8 @@
         t = (w % half_slots) // steps
         n = w % steps
         start, n_left, n_right = chunks(t)
-        live = (n > 0) & (n - 1 < n_left + n_right)
+        count = n_left + n_right
+        live = (n > 0) & (2 * (n - 1) < count)
 
         @pl.when(~backward)
         def _():
@@ -1837,7 +1849,7 @@
 
             @pl.when(live)
             def _():
-                dq_far(start, n - 1, n_left)
+                dq_far(start, n - 1, n_left, count)
 
             @pl.when(n == last_step)
             def _():
@@ -1856,7 +1868,7 @@
 
             @pl.when(live)
             def _():
-                dkv_far(start, n - 1, n_left)
+                dkv_far(start, n - 1, n_left, count)
 
             @pl.when(n == last_step)
             def _():
@@ -1868,7 +1880,7 @@
     def due(time, run, *args):
         events.append((max(0, int((time - start_us) / slot_us)), functools.partial(run, *args)))
 
-    start_us, slot_us = (6.0, 1.05)
+    start_us, slot_us = (6.0, 2.0)
     due(6.0, turn)
     for k in range(1, span + 1):
         due((22.0, 36.0)[min(k, 2) - 1], level, k)
@@ -1883,7 +1895,8 @@
     )
     for u in order:
         core_at, x_at, one_at, two_at, end_at = times[u]
-        due(core_at, scatter.core_stage, u)
+        if u > 0:
+            due(core_at, scatter.core_stage, u)
         due(x_at, scatter.x_stage, u)
         due(one_at, scatter.relay, u, 1)
         due(two_at, scatter.relay, u, 2)
@@ -1905,11 +1918,12 @@
     for u in order:
         scatter.drain(u)
     far_copy.wait()
+    ffn_copy.wait()
 
 
 def backward(
     plan, cycle_size, reach, doc_most, rows, table, aug, masks, q_back, do_wide, own_kv, own_aug,
-    near_bias, kv_all, q_all, branch, parts,
+    near_bias, kv_all, q_all, branch, ffn_far, parts,
 ):
     lines = cycle_size // 4
     span = min(lines - 1, (reach + 3) // 4)
@@ -1935,10 +1949,11 @@
         + [jax.ShapeDtypeStruct((size, model), f32)] * 3
         + [
             jax.ShapeDtypeStruct(branch.shape, bf16),
+            jax.ShapeDtypeStruct(branch.shape, bf16),
             jax.ShapeDtypeStruct((lines, 2, 2, pair, WIDE), bf16),
         ],
-        in_specs=[smem] + [vmem] * 4 + [hbm] * 9,
-        out_specs=[vmem] * 8 + [hbm] * 2,
+        in_specs=[smem] + [vmem] * 4 + [hbm] * 10,
+        out_specs=[vmem] * 8 + [hbm] * 3,
         scratch_shapes=[
             pltpu.VMEM((3, lines, 2, size, model), bf16),
             pltpu.VMEM((3, lines, 2, size, model), bf16),
@@ -1961,7 +1976,7 @@
             dma((2, n)),
             dma((2, n, lines)),
             dma((2, n, lines)),
-            dma((4,)),
+            dma((6,)),
             dma((lines, 2, 2)),
             dma((4, lines)),
             dma((2,)),
@@ -1975,7 +1990,7 @@
         name="backward",
     )(
         table, q_back, do_wide, own_kv, own_aug, near_bias, aug, masks, kv_all, q_all,
-        branch, *shaped
+        branch, ffn_far, *shaped
     )
 
 
@@ -2077,7 +2092,7 @@
         name="attention_forward",
     )(bounds, bias_table, kv_all, k_aug, masks, q_wide, near_bias)
     q_all = window(gather(q_back))
-    hidden, grad_hidden, branch, ffn_part, do_wide, gain_ffn_part, *stacks = middle(
+    hidden, grad_hidden, branch, ffn_own, ffn_far, do_wide, gain_ffn_part, *stacks = middle(
         plan,
         cycle_size,
         attended,
@@ -2093,7 +2108,7 @@
     )
     (
         grad_queries, table_part, grad_keys, grad_values, mask_part,
-        grad_w_down, grad_w_gate, grad_w_up, far_branch, unused_gathered,
+        grad_w_down, grad_w_gate, grad_w_up, far_branch, ffn_in, unused_gathered,
     ) = backward(
         plan,
         cycle_size,
@@ -2111,6 +2126,7 @@
         kv_all,
         q_all,
         branch,
+        ffn_far,
         stacks,
     )
     grad_w_gate, grad_w_up = (grad_w_gate.T, grad_w_up.T)
@@ -2121,7 +2137,8 @@
         [jnp.zeros((1, model), f32), gain_ffn_part, table_row, jnp.zeros((5, model), f32)],
         axis=0,
     )
-    layer_out, grad_tokens, grad_mask, weights, totals = finish(
+    layer_out = (hidden + ffn_own.astype(f32) + ffn_in.astype(f32)).astype(bf16)
+    grad_tokens, grad_mask, weights, totals = finish(
         plan,
         cycle_size,
         grad_queries,
@@ -2137,9 +2154,7 @@
         far_branch,
         tokens,
         gain_attn[None],
-        hidden,
         grad_hidden,
-        ffn_part,
         small,
     )
     weights = weights.reshape(4, cols, model).astype(f32)

time: 412 us -> 386 us (0.937)
  Pallas kernels: 370 us -> 331 us
  waiting for transfers between devices: 1.97 us -> 12 us
    pallas_call x1, Pallas kernels: 155 us -> 135 us  [backward(): pl.pallas_call(functools.partial(backward_kernel, plan, lines, span, reac...]
    all_gather x1, waiting for transfers between devices: 1.92 us -> 12 us  [shards(): pair_cot = lax.all_gather(cot_late, 'wa', axis=0, tiled=True)]
    pallas_call x1, Pallas kernels: 22.5 us -> 12.5 us  [shards(): pl.pallas_call(functools.partial(fwd_kernel, plan, rows, pair), out_shape...]
    pallas_call x1, Pallas kernels: 80.5 us -> 70.7 us  [finish(): pl.pallas_call(functools.partial(finish_kernel, plan, lines), out_shape=[...]
  transfers between devices with their start and end apart: 2 -> 2, of which waited for: 1 -> 1; matrix products, arithmetic and copies ran while one was open for 1% -> 1% of each run, Pallas kernels for 20% -> 19%
where the time goes in v10:
time: 386 us; the launch traced here: 385 us
  Pallas kernels  331 us (86%)
  local copies, waits for them, and re-layouts  21.2 us (5%)
  between operations  14.2 us (4%)
  waiting for transfers between devices  12 us (3%)
  other arithmetic  6.48 us (2%)
    pallas_call x1, Pallas kernels, backward(): pl.pallas_call(functools.partial(backward_kernel, plan, lines, span, reac...  135 us
    pallas_call x1, Pallas kernels, finish(): pl.pallas_call(functools.partial(finish_kernel, plan, lines), out_shape=[...  70.7 us
    pallas_call x1, Pallas kernels, middle(): pl.pallas_call(functools.partial(middle_kernel, plan, cycle_size), out_sh...  62.1 us
    pallas_call x1, Pallas kernels, first(): pl.pallas_call(functools.partial(first_kernel, plan, lines, span, reach,...  50.5 us
    pallas_call x1, Pallas kernels, shards(): pl.pallas_call(functools.partial(fwd_kernel, plan, rows, pair), out_shape...  12.5 us
    all_gather x1, waiting for transfers between devices, shards(): pair_cot = lax.all_gather(cot_late, 'wa', axis=0, tiled=True)  12 us
    unnamed x27, local copies, waits for them, and re-layouts  8.94 us
  transfers between devices with their start and end apart: 2, of which 1 were waited for; matrix products, arithmetic and copies ran while one was open for 1% of the time, Pallas kernels for 19%

profile of v10, /device:TPU:0, one launch (start us, length us, event | category | flops | bytes accessed | tf_op | source)
XLA Modules:
  0.0 385.0 jit_solution(18142628775812886942)
XLA Ops:
  7.2 0.8 reduce-window.8
  8.1 1.2 bitcast_subtract_fusion.2.starts
  9.2 1.4 copy.39.table_ref
  10.6 2.3 copy.38.tokens_ref
  12.9 1.3 broadcast_in_dim.51.gain_ref
  14.2 0.6 broadcast_in_dim.52.mask_ref
  14.8 50.5 %project_gather.1 = (bf16[512,1472]{1,0:T(8,128)(2,1)}, bf16[512,1472]{1,0:T(8,128)(2,1)}, bf16[512,256]{1,0:T(8,128)(2,1)}, bf16[512,384]{1,0:T(8,128)(2,1)}, b...) custom-call(s32[8]{0:T(128)} %bitcast_subtract_fusion.2.starts, ...), custom_call_target="tpu_custom_call" | custom-call | tf_op jit(solution)/shard_map/project_gather/pallas_call | solution.py:607
  65.4 1.2 copy.40
  66.5 0.2 all-gather.5.cloned.1.call-start
  66.8 0.2 fusion.2
  67.0 0.2 fusion.3
  67.2 0.2 fusion.5
  67.6 0.6 pad_add_fusion.1.bounds
  68.2 12.5 %attention_forward.1 = (bf16[512,256]{1,0:T(8,128)(2,1)}, f32[512,256]{1,0:T(8,128)}, bf16[512,256]{1,0:T(8,128)(2,1)}) custom-call(s32[5]{0:T(128)} %pad_add_fusion.1.bounds, f32[32,3]{1,0:T(8,128)} %copy.39.table_ref, bf16[8192,384]{1,0:T(8,128)(2,1)} %bitcast.44, bf16[8192,128]{1,0:T(8,128)(2,1)} %get-tuple-element.53.kaug_ref.aug_hbm, ...), custom_call_target="tpu_custom_call" | custom-call | tf_op jit(solution)/shard_map/attention_forward/pallas_call | solution.py:2074
  80.7 0.6 broadcast_in_dim.53.gain_ref
  81.4 12.0 %all-gather.3.cloned.1.call-done.cot_ref = bf16[512,1472]{1,0:T(8,128)(2,1)} async-done(((bf16[256,1472]{1,0:T(8,128)(2,1)}), bf16[512,1472]{1,0:T(8,128)(2,1)}) %all-gather.3.cloned.1.call-update) | async-done | bytes 1507344 | tf_op jit(solution)/shard_map/all_gather | solution.py:2069
  93.4 62.1 %feed_forward.1 = (f32[256,1472]{1,0:T(8,128)}, f32[256,1472]{1,0:T(8,128)}, bf16[256,1472]{1,0:T(8,128)(2,1)}, bf16[256,1472]{1,0:T(8,128)(2,1)}, bf16[256,1472...) custom-call(bf16[512,256]{1,0:T(8,128)(2,1)} %get-tuple-element.58.a, ...), custom_call_target="tpu_custom_call" | custom-call | tf_op jit(solution)/shard_map/feed_forward/pallas_call | solution.py:1262
  155.5 135.0 %backward.1 = (bf16[512,256]{1,0:T(8,128)(2,1)}, f32[3,32,128]{2,1,0:T(8,128)}, bf16[512,256]{1,0:T(8,128)(2,1)}, bf16[512,256]{1,0:T(8,128)(2,1)}, f32[2,8,256]...) custom-call(f32[32,3]{1,0:T(8,128)} %copy.39.table_ref, ...), custom_call_target="tpu_custom_call" | custom-call | tf_op jit(solution)/shard_map/backward/pallas_call | solution.py:1940
  290.6 0.9 reduce_sum.55
  291.6 0.7 fusion.small_ref
  292.3 70.7 %finish.1 = (f32[256,1472]{1,0:T(8,128)}, f32[8,256]{1,0:T(8,128)}, bf16[4,2,2,48,1472]{4,3,2,1,0:T(8,128)(2,1)}, f32[8,1472]{1,0:T(8,128)}) custom-call(bf16[512,256]{1,0:T(8,128)(2,1)} %get-tuple-element.75.dq_ref, bf16[512,256]{1,0:T(8,128)(2,1)} %get-tuple-element.76.dk_ref, bf16[512,256]{1,0:T(8,128)(2,1)} %get-tuple-element.77.dv_ref, ...), custom_call_target="tpu_custom_call" | custom-call | tf_op jit(solution)/shard_map/finish/pallas_call | solution.py:985
  363.0 1.5 slice_reduce_fusion
  364.5 0.7 slice_reduce_fusion.2
  365.2 4.1 %fusion.10 = (f32[1,2,2,48,1472]{4,3,2,1,0:T(8,128)}, f32[1,2,2,48,1472]{4,3,2,1,0:T(8,128)}, f32[1,2,2,48,1472]{4,3,2,1,0:T(8,128)}, f32[1,2,2,48,1472]{4,3,2,1,0:T(8,128)}) fusion(bf16[4,2,2,48,1472]{4,3,2,1,0:T(8,128)(2,1)} %get-tuple-element.87), kind=kLoop, calls=%fused_computation.39 | loop fusion | bytes 9043968 | tf_op jit(solution)/shard_map/slice | solution.py:2169
  369.3 1.6 copy.44
  370.9 0.7 reshape_squeeze.3
  371.5 1.3 slice.28
  372.8 1.7 add_convert_fusion
  374.5 1.1 copy.43
  375.6 0.8 copy.48
  376.5 0.8 copy.49
  377.3 0.8 copy.50
  (36 shorter events, 0.5 us)
Async XLA Ops:
  7.2 7.0 %copy-start.9 = (bf16[512]{0:T(512)(128)(2,1)S(1)}, bf16[512]{0:T(512)(128)(2,1)}, u32[]{:S(2)}) copy-start(bf16[512]{0:T(512)(128)(2,1)} %param.16) | copy-start | bytes 3076
  7.2 86.2 %all-gather.3.cloned.1.call-start = ((), (), s32[]{:S(2)}) async-start(), calls=%async_computation | async-start | bytes 2359296 | tf_op jit(solution)/shard_map/all_gather | solution.py:2069
  14.8 50.6 %copy-start.2 = (bf16[256,1472]{0,1:T(8,128)(2,1)S(1)}, bf16[256,1472]{0,1:T(8,128)(2,1)}, u32[]{:S(2)}) copy-start(bf16[256,1472]{0,1:T(8,128)(2,1)} %param.27) | copy-start | bytes 2260996
  65.3 1.5 copy-start.8
  66.5 89.0 %all-gather.5.cloned.1.call-start = ((), (), s32[]{:S(2)}) async-start(), calls=%async_computation.1 | async-start | bytes 4456448 | tf_op jit(solution)/shard_map/all_gather | solution.py:2094
  68.2 12.5 %copy-start.6 = (f32[1472]{0:T(1024)S(1)}, f32[1472]{0:T(1024)}, u32[]{:S(2)}) copy-start(f32[1472]{0:T(1024)} %param.23) | copy-start | bytes 17668
  155.5 136.0 %copy-start.7 = (f32[1,1472]{1,0:T(1,128)S(1)}, f32[1,1472]{1,0:T(1,128)}, u32[]{:S(2)}) copy-start(f32[1,1472]{1,0:T(1,128)} %get-tuple-element.82) | copy-start | bytes 17668
  365.2 4.1 %copy-start = (f32[256,1472]{1,0:T(8,128)S(1)}, f32[256,1472]{1,0:T(8,128)}, u32[]{:S(2)}) copy-start(f32[256,1472]{1,0:T(8,128)} %get-tuple-element.105) | copy-start | bytes 4521988
  369.3 3.5 copy-start.1
  374.4 1.2 copy-start.5
  374.4 2.0 copy-start.4
  375.6 1.7 copy-start.3
Sparse Core Ops, SparseCore 0:
  66.7 26.6 all-gather.2
  96.1 53.8 all-gather.4

commit v11 on v10

--- a/solution.py
+++ b/solution.py
@@ -101,43 +101,15 @@
         if flip:
             left, right = (right, left)
         for h in range(heads):
-            base = jnp.full((EDGE, 3 * EDGE), table_ref[0, h], f32)
+            base = jnp.full((EDGE, 3 * EDGE), table_ref[h, 0], f32)
             for b in range(1, 32):
-                base = jnp.where(bucket == b, table_ref[b, h], base)
-            far_l = jnp.full((EDGE, EDGE), table_ref[left, h], f32)
-            far_r = jnp.full((EDGE, EDGE), table_ref[right, h], f32)
+                base = jnp.where(bucket == b, table_ref[h, b], base)
+            far_l = jnp.full((EDGE, EDGE), table_ref[h, left], f32)
+            far_r = jnp.full((EDGE, EDGE), table_ref[h, right], f32)
             near_ref[flip, h, :EDGE, : 3 * EDGE] = base
             near_ref[flip, h, :EDGE, 3 * EDGE :] = far_r
             near_ref[flip, h, EDGE:, EDGE:] = base
             near_ref[flip, h, EDGE:, :EDGE] = far_l
-
-
-def build_keys(plan, g_ref, kaug_ref, masks_ref, km, vm, mask_row, rows):
-    mask_row[...] = jnp.zeros_like(mask_row)
-    size = masks_ref.shape[2]
-    for n in range(masks_ref.shape[0]):
-        mask_row[:, PAD + n * size : PAD + (n + 1) * size] = masks_ref[n]
-    km[:PAD, :] = jnp.broadcast_to(
-        jnp.where(pad_lanes(plan), neg_big, 0.0).astype(bf16), (PAD, WIDE)
-    )
-    km[pl.ds(PAD + rows, PAD), :] = km[:PAD, :]
-    vm[:PAD, :] = jnp.zeros((PAD, WIDE), bf16)
-    vm[pl.ds(PAD + rows, PAD), :] = jnp.zeros((PAD, WIDE), bf16)
-    step = 512
-    low = lanes_of(step, 128) < 64
-    ones = (lanes_of(step, 128) < 3 * plan.heads).astype(bf16)
-
-    def body(n, unused):
-        at = pl.multiple_of(n * step, step)
-        to = pl.multiple_of(PAD + n * step, 128)
-        middle = g_ref[pl.ds(at, step), 128:256]
-        km[pl.ds(to, step), 0:128] = g_ref[pl.ds(at, step), 0:128]
-        km[pl.ds(to, step), 128:256] = jnp.where(low, middle, kaug_ref[pl.ds(at, step), :])
-        vm[pl.ds(to, step), 0:128] = jnp.where(low, ones, middle)
-        vm[pl.ds(to, step), 128:256] = g_ref[pl.ds(at, step), 256:384]
-        return unused
-
-    lax.fori_loop(0, rows // step, body, 0)
 
 
 def far_span(start, n, n_left, left_bucket, right_bucket):
@@ -152,43 +124,130 @@
     return (lane >= plan.doc_lane) & (lane < plan.stat_lane)
 
 
+def far_pair(start, n, n_left, count, left, right):
+    pair_of = []
+    for i in range(2):
+        part, bucket = far_span(start, 2 * n + i, n_left, left, right)
+        at = jnp.where(2 * n + i < count, part.start, 0)
+        pair_of.append((pl.ds(pl.multiple_of(at, 128), TK), bucket))
+    return pair_of
+
+
 def fwd_kernel(
-    plan, rows, pair, bounds, table_ref, g_ref, kaug_ref, masks_ref, q_ref, near_ref,
-    low_ref, wide_ref, qb_ref, km, vm, mask_row, acc, row_max, qh_ref,
+    plan, lines, reach, rows, pair, lengths, table_ref, q_ref, near_hbm, g_hbm, aug_hbm, masks_hbm,
+    low_ref, wide_ref, qb_ref,
+    km, vm, mask_row, g_buf, aug_buf, near_ref, acc, row_max, qh_ref, g_sem, near_sem,
 ):
-    build_keys(plan, g_ref, kaug_ref, masks_ref, km, vm, mask_row, rows)
+    base = lax.axis_index("ctx") * pair
+    origin = jnp.clip(base - reach * pair, 0, 4 * lines * pair - rows)
+    blocks = rows // pair
+    tiles = pair // TQ
+    near_copy = pltpu.make_async_copy(near_hbm.at[0], near_ref, near_sem.at[0])
+    near_copy.start()
+
+    def document(position):
+        def look(e, carry):
+            begin, low, high = carry
+            end = begin + lengths[e]
+            inside = (begin <= position) & (position < end)
+            return (end, jnp.where(inside, begin, low), jnp.where(inside, end, high))
+
+        zero = jnp.int32(0)
+        return lax.fori_loop(0, lengths.shape[0], look, (zero, zero, zero))[1:]
+
+    def extent(t):
+        first = base + t * TQ
+        low = document(first)[0]
+        high = document(first + TQ - 1)[1]
+        n_left = jnp.maximum(0, first - EDGE - low + TK - 1) // TK
+        n_right = jnp.maximum(0, high - (first - EDGE + TK) + TK - 1) // TK
+        return low, high, n_left, n_right
+
+    low_end = extent(0)[0] - origin
+    high_end = extent(tiles - 1)[1] - origin
+    from_block = jnp.maximum(0, low_end - TK) // pair
+    to_block = jnp.minimum(blocks, (high_end + TK + pair - 1) // pair)
+
+    def loads(n):
+        at = pl.ds(pl.multiple_of(n * pair, pair), pair)
+        to = pl.ds(pl.multiple_of(PAD + n * pair, 128), pair)
+        slot = n % 2
+        return (
+            pltpu.make_async_copy(g_hbm.at[at], g_buf.at[slot], g_sem.at[0, slot]),
+            pltpu.make_async_copy(aug_hbm.at[at], aug_buf.at[slot], g_sem.at[1, slot]),
+            pltpu.make_async_copy(masks_hbm.at[n], mask_row.at[:, to], g_sem.at[2, slot]),
+        )
+
+    for copy in loads(from_block):
+        copy.start()
+    mask_row[:, :PAD] = jnp.zeros((8, PAD), f32)
+    mask_row[:, PAD + rows :] = jnp.zeros((8, PAD), f32)
+    km[:PAD, :] = jnp.broadcast_to(
+        jnp.where(pad_lanes(plan), neg_big, 0.0).astype(bf16), (PAD, WIDE)
+    )
+    km[PAD + rows :, :] = km[:PAD, :]
+    vm[:PAD, :] = jnp.zeros((PAD, WIDE), bf16)
+    vm[PAD + rows :, :] = jnp.zeros((PAD, WIDE), bf16)
+    low_lanes = lanes_of(pair, 128) < 64
+    ones = (lanes_of(pair, 128) < 3 * plan.heads).astype(bf16)
+
+    def build(n, unused):
+        for copy in loads(n):
+            copy.wait()
+
+        @pl.when(n + 1 < to_block)
+        def _():
+            for copy in loads(n + 1):
+                copy.start()
+
+        to = pl.ds(pl.multiple_of(PAD + n * pair, 128), pair)
+        middle = g_buf[n % 2, :, 128:256]
+        km[to, 0:128] = g_buf[n % 2, :, 0:128]
+        km[to, 128:256] = jnp.where(low_lanes, middle, aug_buf[n % 2])
+        vm[to, 0:128] = jnp.where(low_lanes, ones, middle)
+        vm[to, 128:256] = g_buf[n % 2, :, 256:384]
+        return unused
+
+    lax.fori_loop(from_block, to_block, build, 0)
+    near_copy.wait()
     lane = lanes_of(TQ)
 
     def tile(t, unused):
-        start = pl.multiple_of(bounds[0] + t * TQ, 128)
-        n_left, n_right = (bounds[1 + 2 * t], bounds[2 + 2 * t])
+        start = base - origin + t * TQ
+        low_doc, high_doc, n_left, n_right = extent(t)
+        count = n_left + n_right
         out = pl.ds(pl.multiple_of(t * TQ, TQ), TQ)
         q = q_ref[out, :]
         near = pl.ds(pl.multiple_of(start + PAD - EDGE, 128), TK)
         for h in range(plan.heads):
             qh = jnp.where(plan.key_lanes(lane, h), q, jnp.zeros_like(q))
             qh_ref[h] = qh
-            s = nt(qh, km[near, :]) + near_ref[0, h] + mask_row[0:1, near]
+            s = nt(qh, km[near, :]) + near_ref[h] + mask_row[0:1, near]
             top = jnp.max(s, axis=1, keepdims=True)
             p = jnp.exp(s - top).astype(bf16)
             acc[h] = nn(p, vm[near, :])
             row_max[h] = jnp.broadcast_to(top, (TQ, 128))
 
         def far(n, unused):
-            span, bucket = far_span(start, n, n_left, far_left_bucket, far_right_bucket)
-            if True:
-                for h in range(plan.heads):
-                    s = nt(qh_ref[h], km[span, :]) + mask_row[0:1, span]
-                    offset = table_ref[bucket, h]
-                    old = row_max[h][:, :1]
-                    top = jnp.maximum(old, jnp.max(s, axis=1, keepdims=True) + offset)
-                    p = jnp.exp(s - (top - offset)).astype(bf16)
-                    acc[h] = acc[h] * jnp.exp(old - top) + nn(p, vm[span, :])
-                    row_max[h] = jnp.broadcast_to(top, (TQ, 128))
+            parts = far_pair(start, n, n_left, count, far_left_bucket, far_right_bucket)
+            for h in range(plan.heads):
+                scores = [
+                    (nt(qh_ref[h], km[part, :]) + mask_row[0:1, part], table_ref[h, bucket])
+                    for part, bucket in parts
+                ]
+                old = row_max[h][:, :1]
+                top = old
+                for s, offset in scores:
+                    top = jnp.maximum(top, jnp.max(s, axis=1, keepdims=True) + offset)
+                more = [
+                    nn(jnp.exp(s - (top - offset)).astype(bf16), vm[part, :])
+                    for (s, offset), (part, bucket) in zip(scores, parts)
+                ]
+                acc[h] = acc[h] * jnp.exp(old - top) + (more[0] + more[1])
+                row_max[h] = jnp.broadcast_to(top, (TQ, 128))
             return unused
 
-        lax.fori_loop(0, n_left + n_right, far, 0)
-
+        lax.fori_loop(0, (count + 1) // 2, far, 0)
         wide = jnp.zeros((TQ, WIDE), f32)
         qb = jnp.where(lane < plan.stat_lane, q, jnp.zeros_like(q))
         for h in range(plan.heads):
@@ -202,7 +261,39 @@
         qb_ref[out, :] = qb
         return unused
 
-    lax.fori_loop(0, pair // TQ, tile, 0)
+    lax.fori_loop(0, tiles, tile, 0)
+
+
+def attend(plan, cycle_size, reach, rows, lengths, table, q_wide, near_bias, kv_all, aug, masks):
+    pair = q_wide.shape[0]
+    heads = plan.heads
+    padded = rows + 2 * PAD
+    hbm = pl.BlockSpec(memory_space=pl.ANY)
+    return pl.pallas_call(
+        functools.partial(fwd_kernel, plan, cycle_size // 4, reach, rows, pair),
+        out_shape=(
+            jax.ShapeDtypeStruct((pair, WIDE), bf16),
+            jax.ShapeDtypeStruct((pair, WIDE), f32),
+            jax.ShapeDtypeStruct((pair, WIDE), bf16),
+        ),
+        in_specs=[smem, smem, vmem] + [hbm] * 4,
+        out_specs=(vmem, vmem, vmem),
+        scratch_shapes=[
+            pltpu.VMEM((padded, WIDE), bf16),
+            pltpu.VMEM((padded, WIDE), bf16),
+            pltpu.VMEM((8, padded), f32),
+            pltpu.VMEM((2, pair, 2 * plan.cols), bf16),
+            pltpu.VMEM((2, pair, 128), bf16),
+            pltpu.VMEM((heads, TQ, TK), f32),
+            pltpu.VMEM((heads, TQ, WIDE), f32),
+            pltpu.VMEM((heads, TQ, 128), f32),
+            pltpu.VMEM((heads, TQ, WIDE), bf16),
+            pltpu.SemaphoreType.DMA((3, 2)),
+            pltpu.SemaphoreType.DMA((1,)),
+        ],
+        compiler_params=params(),
+        name="attention_forward",
+    )(lengths, table, q_wide, near_bias, kv_all, aug, masks)
 
 
 vmem = pl.BlockSpec(memory_space=pltpu.VMEM)
@@ -275,10 +366,10 @@
 
 
 def first_kernel(
-    plan, lines, span, reach, rows, starts, table_ref, tokens_ref, gain_ref, mask_ref,
+    plan, lines, span, reach, rows, lengths, table_ref, tokens_ref, gain_ref, key_mask_ref,
     wq_hbm, wk_hbm, wv_hbm, wo_hbm,
     x_ref, tok_ref, q_ref, own_ref, aug_ref, own_aug_ref, near_ref, masks_ref, wo_far_hbm, all_hbm,
-    weights, zeros, load_sem, y_sem, own_sem, zero_sem, z_sem, x_sem, c_sem,
+    weights, zeros, mask_ref, load_sem, y_sem, own_sem, zero_sem, z_sem, x_sem, c_sem,
 ):
     spot = Spot(lines)
     z, x, core, wa = (spot.z, spot.x, spot.core, spot.wa)
@@ -291,6 +382,7 @@
     ]
     for load in loads:
         load.start()
+    mask_ref[...] = jnp.broadcast_to(key_mask_ref[...].astype(f32)[None, :], mask_ref.shape)
     greet(spot, True)
     zeros[...] = jnp.zeros_like(zeros)
 
@@ -338,7 +430,7 @@
     def scaled(rows_in):
         rows_in = rows_in.astype(f32)
         inv = lax.rsqrt(jnp.mean(rows_in * rows_in, axis=-1, keepdims=True) + eps)
-        return (rows_in * inv * gain_ref[...]).astype(bf16)
+        return (rows_in * inv * gain_ref[...][None, :]).astype(bf16)
 
     def normal(i, unused):
         at = rows_at(ours + i * chunk, chunk)
@@ -473,10 +565,13 @@
     def doc_of(start, size):
         position = start + lax.broadcasted_iota(jnp.int32, (size, 128), 0)
 
-        def count(e, total):
-            return total + (position >= starts[e]).astype(jnp.int32)
-
-        return lax.fori_loop(1, starts.shape[0], count, jnp.zeros((size, 128), jnp.int32))
+        def count(e, carry):
+            begin, total = carry
+            begin = begin + lengths[e]
+            return (begin, total + (position >= begin).astype(jnp.int32))
+
+        zero = (jnp.int32(0), jnp.zeros((size, 128), jnp.int32))
+        return lax.fori_loop(0, lengths.shape[0] - 1, count, zero)[1]
 
     def code_lanes(start, size):
         lane = lanes_of(size, 128) + 128
@@ -596,7 +691,7 @@
 
 
 def first(
-    plan, cycle_size, reach, rows, starts, table, tokens, gain, mask, w_query, w_key, w_value, w_out
+    plan, cycle_size, reach, rows, lengths, table, tokens, gain, mask, w_query, w_key, w_value, w_out
 ):
     lines = cycle_size // 4
     span = min(lines - 1, (reach + 3) // 4)
@@ -623,6 +718,7 @@
         scratch_shapes=[
             pltpu.VMEM((3 * plan.cols, model), bf16),
             pltpu.VMEM((pair, 2 * plan.cols), bf16),
+            pltpu.VMEM((8, pair), f32),
             dma((3,)),
             dma((2, 5)),
             dma((4,)),
@@ -635,7 +731,7 @@
             vmem_limit_bytes=56 * 2**20, collective_id=4, has_side_effects=True
         ),
         name="project_gather",
-    )(starts, table, tokens, gain, mask, w_query.T, w_key.T, w_value.T, w_out)
+    )(lengths, table, tokens, gain, mask, w_query.T, w_key.T, w_value.T, w_out)
 
 
 def tn(a, b):
@@ -671,9 +767,9 @@
 
 
 def finish_kernel(
-    plan, lines, dq_ref, dk_ref, dv_ref, mask_ref, wq_hbm, wk_hbm, wv_hbm, normed_ref, att_ref, branch_ref, far_ref,
-    tokens_ref, gain_ref, gh_ref, small_ref,
-    gt_ref, gm_ref, weights_ref, total_ref,
+    plan, lines, dq_hbm, dk_hbm, dv_hbm, att_hbm, normed_hbm, branch_hbm, far_hbm,
+    wq_hbm, wk_hbm, wv_hbm, mask_ref, tokens_ref, gain_ref, gh_ref, table_ref, gain_part_ref,
+    gt_ref, gm_ref, weights_ref, gain_one_ref, gain_two_ref, table_out_ref,
     w3_ref, load_sem, lefts, rights, product, mine, core_in, x_in, up_in, down_in, all_w, y_out, y_in, own_part, mask_in,
     small_own, small_y, small_core, small_x, small_all,
     y_sem, core_sem, x_sem, up_sem, down_sem, gz_sem, gx_sem, gc_sem, sz_sem,
@@ -681,9 +777,23 @@
     spot = Spot(lines)
     z, x, core, wa = (spot.z, spot.x, spot.core, spot.wa)
     cols = plan.cols
+    half = tokens_ref.shape[0]
+    our_rows = pl.ds(pl.multiple_of(wa * half, half), half)
+    their_rows = pl.ds(pl.multiple_of((1 - wa) * half, half), half)
+    targets = (
+        (dq_hbm, lefts.at[0]),
+        (normed_hbm, rights.at[0]),
+        (att_hbm, lefts.at[3]),
+        (branch_hbm, rights.at[1, our_rows]),
+        (far_hbm, rights.at[1, their_rows]),
+        (dk_hbm, lefts.at[1]),
+        (dv_hbm, lefts.at[2]),
+        (wq_hbm, w3_ref.at[pl.ds(0, cols)]),
+        (wk_hbm, w3_ref.at[pl.ds(WIDE, cols)]),
+        (wv_hbm, w3_ref.at[pl.ds(3 * WIDE - cols, cols)]),
+    )
     loads = [
-        pltpu.make_async_copy(src, w3_ref.at[pl.ds(at, cols)], load_sem.at[i])
-        for i, (src, at) in enumerate(((wq_hbm, 0), (wk_hbm, WIDE), (wv_hbm, 3 * WIDE - cols)))
+        pltpu.make_async_copy(src, dst, load_sem.at[i]) for i, (src, dst) in enumerate(targets)
     ]
     for load in loads:
         load.start()
@@ -692,9 +802,6 @@
     w3_ref[WIDE + cols : 2 * WIDE] = gap
     w3_ref[2 * WIDE : 3 * WIDE - cols] = gap
     greet(spot, True)
-    for load in loads:
-        load.wait()
-    half = tokens_ref.shape[0]
     quarter = half // 2
     model = tokens_ref.shape[1]
     rows = mine.shape[3]
@@ -702,9 +809,9 @@
     def grad_rows(at):
         at = pl.ds(pl.multiple_of(at, quarter), quarter)
         return (
-            nn(dq_ref[at, :], w3_ref[0:256])
-            + nn(dk_ref[at, :], w3_ref[256:512])
-            + nn(dv_ref[at, :], w3_ref[512:768])
+            nn(lefts[0, at, :], w3_ref[0:256])
+            + nn(lefts[1, at, :], w3_ref[256:512])
+            + nn(lefts[2, at, :], w3_ref[512:768])
         )
 
     def y_copy(i):
@@ -715,21 +822,15 @@
         y_copy(i).start()
         return unused
 
+    for i in (0, 5, 6, 7, 8, 9):
+        loads[i].wait()
     lax.fori_loop(0, 2, theirs, 0)
     mask_copy = send(
         mask_ref.at[1 - wa], mask_in, y_sem.at[0, 2], y_sem.at[1, 2], spot.y_mate()
     )
     mask_copy.start()
-
-    our_rows = pl.ds(pl.multiple_of(wa * half, half), half)
-    their_rows = pl.ds(pl.multiple_of((1 - wa) * half, half), half)
-    lefts[0] = dq_ref[...]
-    lefts[1] = dk_ref[...]
-    lefts[2] = dv_ref[...]
-    lefts[3] = att_ref[...]
-    rights[0] = normed_ref[...]
-    rights[1, our_rows, :] = branch_ref[...]
-    rights[1, their_rows, :] = far_ref[...]
+    for i in (1, 2, 3, 4):
+        loads[i].wait()
     per = plan.cols // rows
 
     def core_copy(m):
@@ -795,6 +896,33 @@
     lax.fori_loop(0, lines, core_add_own, 0)
     lax.fori_loop(0, 2, ours, 0)
 
+    def flow(step, d):
+        ring, sem = (up_in, up_sem) if step > 0 else (down_in, down_sem)
+        return send(
+            mine.at[d, x, core], ring.at[d], sem.at[0, d], sem.at[1, d], spot.z_mate(step)
+        )
+
+    def merge(step, d):
+        flow(step, d).wait_recv()
+        ring = up_in if step > 0 else down_in
+        mine[d, x, core] = added(mine[d, x, core], ring[d])
+
+    def x_add(i, unused):
+        d = (i * (lines - 1)) % lines
+        x_copy(d).wait()
+        mine[d, x, core] = added(mine[d, x, core], x_in[d])
+
+        @pl.when((z == 0) & (d > 0))
+        def _():
+            flow(1, d).start()
+
+        @pl.when((z == lines - 1) & (d < lines - 1))
+        def _():
+            flow(-1, d).start()
+
+        return unused
+
+    lax.fori_loop(0, lines, x_add, 0)
     gain_sum = jnp.zeros((1, model), f32)
     step = 32
     for i in range(2):
@@ -806,48 +934,41 @@
             grad = own_part[at, :] + y_in[i, there, :].astype(f32)
             rows_in = tokens_ref[at, :].astype(f32)
             inv = lax.rsqrt(jnp.mean(rows_in * rows_in, axis=-1, keepdims=True) + eps)
-            scaled = gain_ref[...] * grad
+            scaled = gain_ref[...][None, :] * grad
             mean = jnp.mean(rows_in * scaled, axis=-1, keepdims=True)
             gt_ref[at, :] = gh_ref[at, :] + inv * scaled - rows_in * (inv * inv * inv * mean)
             return total + jnp.sum(grad * rows_in * inv, axis=0, keepdims=True)
 
         gain_sum = lax.fori_loop(0, quarter // step, normal, gain_sum)
-    small_own[...] = small_ref[...]
+    small_own[...] = jnp.zeros_like(small_own)
     small_own[0:1, :] = gain_sum
+    small_own[1:2, :] = gain_part_ref[...]
+    for h in range(plan.heads):
+        small_own[2:3, 32 * h : 32 * h + 32] = jnp.sum(
+            jnp.transpose(table_ref[h]), axis=0, keepdims=True
+        )
     small_copy = send(
         small_own, small_y, y_sem.at[0, 4], y_sem.at[1, 4], spot.y_mate()
     )
     small_copy.start()
     mask_copy.wait()
-    gm_ref[...] = mask_ref[wa] + mask_in[...]
-
-    def flow(step, d):
-        ring, sem = (up_in, up_sem) if step > 0 else (down_in, down_sem)
-        return send(
-            mine.at[d, x, core], ring.at[d], sem.at[0, d], sem.at[1, d], spot.z_mate(step)
-        )
-
-    def merge(step, d):
-        flow(step, d).wait_recv()
-        ring = up_in if step > 0 else down_in
-        mine[d, x, core] = added(mine[d, x, core], ring[d])
-
-    def x_add(i, unused):
-        d = (i * (lines - 1)) % lines
-        x_copy(d).wait()
-        mine[d, x, core] = added(mine[d, x, core], x_in[d])
-
-        @pl.when((z == 0) & (d > 0))
-        def _():
-            flow(1, d).start()
-
-        @pl.when((z == lines - 1) & (d < lines - 1))
-        def _():
-            flow(-1, d).start()
-
-        return unused
-
-    lax.fori_loop(0, lines, x_add, 0)
+    gm_ref[...] = jnp.sum(mask_ref[wa, 0:1] + mask_in[0:1], axis=0)
+    def relay(k, unused):
+        high = lines - 1 - k
+
+        @pl.when((z < high) & (z > 0))
+        def _():
+            merge(1, high)
+            flow(1, high).start()
+
+        @pl.when((z > k) & (z + 1 < lines))
+        def _():
+            merge(-1, k)
+            flow(-1, k).start()
+
+        return unused
+
+    lax.fori_loop(0, 1, relay, 0)
     small_copy.wait()
     row = lax.broadcasted_iota(jnp.int32, small_own.shape, 0)
     small_x[0] = small_own[...] + jnp.where(row < 2, small_y[...], 0.0)
@@ -855,23 +976,7 @@
         small_x.at[0], small_core, core_sem.at[0, 4], core_sem.at[1, 4], spot.core_mate()
     )
     small_core_copy.start()
-
-    def relay(k, unused):
-        high = lines - 1 - k
-
-        @pl.when((z < high) & (z > 0))
-        def _():
-            merge(1, high)
-            flow(1, high).start()
-
-        @pl.when((z > k) & (z + 1 < lines))
-        def _():
-            merge(-1, k)
-            flow(-1, k).start()
-
-        return unused
-
-    lax.fori_loop(0, lines - 1, relay, 0)
+    lax.fori_loop(1, lines - 1, relay, 0)
     small_core_copy.wait()
     small_x[1] = small_x[0] + small_core[...]
     small_x_copy = send(
@@ -923,22 +1028,24 @@
         across(d).start()
 
     across(z).start()
-    lax.fori_loop(
-        0, lines, line_relay(spot, lambda s, d: pass_w(s, d).start(), receive), 0
-    )
-    lax.fori_loop(
-        0,
-        lines,
-        line_relay(
-            spot, lambda s, d: pass_s(s, d).start(), lambda s, d: pass_s(s, d).wait_recv()
-        ),
-        0,
-    )
+    def pass_both(step, d):
+        pass_s(step, d).start()
+        pass_w(step, d).start()
+
+    def receive_both(step, d):
+        pass_s(step, d).wait_recv()
+        receive(step, d)
+
+    lax.fori_loop(0, lines, line_relay(spot, pass_both, receive_both), 0)
 
     def add_small(d, total):
         return total + small_all[d]
 
-    total_ref[...] = lax.fori_loop(1, lines, add_small, small_all[0])
+    totals = lax.fori_loop(1, lines, add_small, small_all[0])
+    gain_one_ref[...] = jnp.sum(totals[0:1], axis=0)
+    gain_two_ref[...] = jnp.sum(totals[1:2], axis=0)
+    for h in range(plan.heads):
+        table_out_ref[h : h + 1, :] = totals[2:3, 32 * h : 32 * h + 32]
     def spread(d, unused):
         across(d).wait()
         beside(d).start()
@@ -986,17 +1093,17 @@
         functools.partial(finish_kernel, plan, lines),
         out_shape=[
             jax.ShapeDtypeStruct((half, model), f32),
-            jax.ShapeDtypeStruct((8, half), f32),
+            jax.ShapeDtypeStruct((half,), f32),
             jax.ShapeDtypeStruct((lines, 2, 2, rows, model), bf16),
-            jax.ShapeDtypeStruct((8, model), f32),
+            jax.ShapeDtypeStruct((model,), f32),
+            jax.ShapeDtypeStruct((model,), f32),
+            jax.ShapeDtypeStruct((plan.heads, 32), f32),
         ],
-        in_specs=[vmem] * 4
-        + [pl.BlockSpec(memory_space=pl.ANY)] * 3
-        + [vmem] * (len(operands) - 7),
-        out_specs=[vmem] * 4,
+        in_specs=[pl.BlockSpec(memory_space=pl.ANY)] * 10 + [vmem] * 6,
+        out_specs=[vmem] * 6,
         scratch_shapes=[
             pltpu.VMEM((3 * WIDE, model), bf16),
-            dma((3,)),
+            dma((10,)),
             pltpu.VMEM((4, 2 * half, WIDE), bf16),
             pltpu.VMEM((2, 2 * half, model), bf16),
             pltpu.VMEM((WIDE, model), bf16),
@@ -1100,7 +1207,7 @@
         if keep:
             hidden_ref[(i % 2) * block : (i % 2 + 1) * block, :] = hidden
         inv = lax.rsqrt(jnp.mean(hidden * hidden, axis=-1, keepdims=True) + eps)
-        x_ref[at, :] = (hidden * inv * gain_ref[...]).astype(bf16)
+        x_ref[at, :] = (hidden * inv * gain_ref[...][None, :]).astype(bf16)
 
     normal(0, theirs, False)
     normal(1, theirs, False)
@@ -1201,7 +1308,7 @@
         grad = acc_g[at, :] + d_in[i].astype(f32)
         hidden = hidden_ref[at, :]
         inv = lax.rsqrt(jnp.mean(hidden * hidden, axis=-1, keepdims=True) + eps)
-        scaled = gain_ref[...] * grad
+        scaled = gain_ref[...][None, :] * grad
         mean = jnp.mean(hidden * scaled, axis=-1, keepdims=True)
         grad_hidden = (
             cot_ref[rows_at(ours + i * chunk, chunk), :].astype(f32)
@@ -1706,21 +1813,13 @@
             near_acc[h] += ds
             acc[h] = nn(ds.astype(bf16), km[near, :])
 
-    def far_pair(start, n, n_left, count, left, right):
-        pair_of = []
-        for i in range(2):
-            part, bucket = far_span(start, 2 * n + i, n_left, left, right)
-            at = jnp.where(2 * n + i < count, part.start, 0)
-            pair_of.append((pl.ds(pl.multiple_of(at, 128), TK), bucket))
-        return pair_of
-
     def dq_far(start, n, n_left, count):
         parts = far_pair(start, n, n_left, count, far_left_bucket, far_right_bucket)
         for h in range(plan.heads):
             grads = []
             for i, (part, bucket) in enumerate(parts):
                 slot = (2 * n + i >= n_left).astype(jnp.int32)
-                offset = mask_row[0:1, part] + table_ref[bucket, h]
+                offset = mask_row[0:1, part] + table_ref[h, bucket]
                 ds = query_grads(h, nt(qh_ref[h], km[part, :]) + offset, part)
                 grads.append(nn(ds.astype(bf16), km[part, :]))
                 far_acc[slot, h] += (
@@ -1809,7 +1908,7 @@
         parts = far_pair(start, n, n_left, count, far_right_bucket, far_left_bucket)
         for h in range(plan.heads):
             (v_one, k_one), (v_two, k_two) = [
-                key_grads(h, nt(qh_ref[h], km[part, :]) + table_ref[bucket, h], part)
+                key_grads(h, nt(qh_ref[h], km[part, :]) + table_ref[h, bucket], part)
                 for part, bucket in parts
             ]
             near_acc[h, :, :WIDE] += v_one + v_two
@@ -2023,23 +2122,7 @@
     base = lax.axis_index("ctx") * pair
     rows = min(total_rows, (2 * reach + 1) * pair)
     origin = jnp.clip(base - reach * pair, 0, total_rows - rows).astype(jnp.int32)
-    ends = jnp.cumsum(doc_lengths).astype(jnp.int32)
-    starts = ends - doc_lengths
-
-    def doc_at(positions):
-        return jnp.sum((positions[:, None] >= starts[None, :]).astype(jnp.int32), axis=1) - 1
-
-    tiles = pair // TQ
-    tile_start = base + TQ * jnp.arange(tiles, dtype=jnp.int32)
-    first_doc = jnp.arange(docs, dtype=jnp.int32)[None, :] == doc_at(tile_start)[:, None]
-    last_doc = jnp.arange(docs, dtype=jnp.int32)[None, :] == doc_at(tile_start + TQ - 1)[:, None]
-    low_end = jnp.sum(jnp.where(first_doc, starts[None, :], 0), axis=1)
-    high_end = jnp.sum(jnp.where(last_doc, ends[None, :], 0), axis=1)
-    n_left = jnp.maximum(0, (tile_start - EDGE - low_end + TK - 1) // TK)
-    n_right = jnp.maximum(0, (high_end - (tile_start - EDGE + TK) + TK - 1) // TK)
-    bounds = jnp.concatenate(
-        [(base - origin)[None], jnp.stack([n_left, n_right], axis=1).reshape(-1)]
-    ).astype(jnp.int32)
+    table = bias_table.T
 
     def window(gathered):
         if rows == total_rows:
@@ -2054,11 +2137,11 @@
         cycle_size,
         reach,
         rows,
-        starts,
-        bias_table,
+        doc_lengths,
+        table,
         tokens,
-        gain_attn[None],
-        jnp.broadcast_to(key_mask.astype(f32)[None], (8, pair)),
+        gain_attn,
+        key_mask,
         w_query,
         w_key,
         w_value,
@@ -2070,27 +2153,9 @@
     if rows < total_rows:
         masks = lax.dynamic_slice_in_dim(masks, origin // pair, rows // pair, 0)
     kv_all = window(kv_all.reshape(total_rows, 2 * plan.cols))
-    padded = rows + 2 * PAD
-    attended, mixed, q_back = pl.pallas_call(
-        functools.partial(fwd_kernel, plan, rows, pair),
-        out_shape=(
-            jax.ShapeDtypeStruct((pair, WIDE), bf16),
-            jax.ShapeDtypeStruct((pair, WIDE), f32),
-            jax.ShapeDtypeStruct((pair, WIDE), bf16),
-        ),
-        in_specs=[smem, smem] + [vmem] * 5,
-        out_specs=(vmem, vmem, vmem),
-        scratch_shapes=[
-            pltpu.VMEM((padded, WIDE), bf16),
-            pltpu.VMEM((padded, WIDE), bf16),
-            pltpu.VMEM((8, padded), f32),
-            pltpu.VMEM((heads, TQ, WIDE), f32),
-            pltpu.VMEM((heads, TQ, 128), f32),
-            pltpu.VMEM((heads, TQ, WIDE), bf16),
-        ],
-        compiler_params=params(),
-        name="attention_forward",
-    )(bounds, bias_table, kv_all, k_aug, masks, q_wide, near_bias)
+    attended, mixed, q_back = attend(
+        plan, cycle_size, reach, rows, doc_lengths, table, q_wide, near_bias, kv_all, k_aug, masks
+    )
     q_all = window(gather(q_back))
     hidden, grad_hidden, branch, ffn_own, ffn_far, do_wide, gain_ffn_part, *stacks = middle(
         plan,
@@ -2099,7 +2164,7 @@
         mixed,
         pair_tokens,
         pair_cot,
-        gain_ffn[None],
+        gain_ffn,
         w_out,
         far_out,
         w_gate,
@@ -2115,7 +2180,7 @@
         reach,
         doc_most,
         rows,
-        bias_table,
+        table,
         k_aug,
         masks,
         q_back,
@@ -2130,45 +2195,39 @@
         stacks,
     )
     grad_w_gate, grad_w_up = (grad_w_gate.T, grad_w_up.T)
-    cols = plan.cols
-    table_row = jnp.sum(table_part, axis=2).reshape(1, -1)
-    table_row = jnp.pad(table_row, ((0, 0), (0, model - table_row.shape[1])))
-    small = jnp.concatenate(
-        [jnp.zeros((1, model), f32), gain_ffn_part, table_row, jnp.zeros((5, model), f32)],
-        axis=0,
-    )
     layer_out = (hidden + ffn_own.astype(f32) + ffn_in.astype(f32)).astype(bf16)
-    grad_tokens, grad_mask, weights, totals = finish(
+    grad_tokens, grad_mask, weights, grad_gain_attn, grad_gain_ffn, grad_table = finish(
         plan,
         cycle_size,
         grad_queries,
         grad_keys,
         grad_values,
-        mask_part.reshape(group, 8, own_rows),
+        attended,
+        pair_normed,
+        branch,
+        far_branch,
         w_query.T,
         w_key.T,
         w_value.T,
-        pair_normed,
-        attended,
-        branch,
-        far_branch,
+        mask_part.reshape(group, 8, own_rows),
         tokens,
-        gain_attn[None],
+        gain_attn,
         grad_hidden,
-        small,
+        table_part,
+        gain_ffn_part,
     )
-    weights = weights.reshape(4, cols, model).astype(f32)
+    weights = weights.reshape(4, plan.cols, model).astype(f32)
     return (
         layer_out,
         grad_tokens,
-        grad_mask[0],
-        totals[0],
+        grad_mask,
+        grad_gain_attn,
         weights[0].T,
         weights[1].T,
         weights[2].T,
         weights[3],
-        totals[2, : heads * 32].reshape(heads, 32).T,
-        totals[1],
+        grad_table.T,
+        grad_gain_ffn,
         grad_w_gate,
         grad_w_up,
         grad_w_down,

time: 386 us -> 365 us (0.946)
  Pallas kernels: 331 us -> 320 us
  local copies, waits for them, and re-layouts: 21.2 us -> 15 us
  other arithmetic: 6.48 us -> 1.66 us
    pallas_call x1, Pallas kernels: 70.7 us -> 60.9 us  [finish(): pl.pallas_call(functools.partial(finish_kernel, plan, lines), out_shape=[...]
    unnamed x27 -> x30, local copies, waits for them, and re-layouts: 8.94 us -> 11.5 us
  transfers between devices with their start and end apart: 2 -> 2, of which waited for: 1 -> 1; matrix products, arithmetic and copies ran while one was open for 1% -> 0% of each run, Pallas kernels for 19% -> 21%
where the time goes in v11:
time: 365 us
  Pallas kernels  320 us (88%)
  local copies, waits for them, and re-layouts  15 us (4%)
  between operations  14.2 us (4%)
  waiting for transfers between devices  13.6 us (4%)
    pallas_call x1, Pallas kernels, backward(): pl.pallas_call(functools.partial(backward_kernel, plan, lines, span, reac...  133 us
    pallas_call x1, Pallas kernels, middle(): pl.pallas_call(functools.partial(middle_kernel, plan, cycle_size), out_sh...  62.2 us
    pallas_call x1, Pallas kernels, finish(): pl.pallas_call(functools.partial(finish_kernel, plan, lines), out_shape=[...  60.9 us
    pallas_call x1, Pallas kernels, first(): pl.pallas_call(functools.partial(first_kernel, plan, lines, span, reach,...  50.7 us
    all_gather x1, waiting for transfers between devices, shards(): pair_cot = lax.all_gather(cot_late, 'wa', axis=0, tiled=True)  13.6 us
    pallas_call x1, Pallas kernels, attend(): pl.pallas_call(functools.partial(fwd_kernel, plan, cycle_size // 4, reach...  13.2 us
    unnamed x30, local copies, waits for them, and re-layouts  11.5 us
  transfers between devices with their start and end apart: 2, of which 1 were waited for; matrix products, arithmetic and copies ran while one was open for 0% of the time, Pallas kernels for 21%

profile of v11, /device:TPU:0, one launch (start us, length us, event | category | flops | bytes accessed | tf_op | source)
XLA Modules:
  0.0 364.9 jit_solution(13700627151705738771)
XLA Ops:
  7.2 0.0 all-gather.3.cloned.1.call-start
  7.2 2.3 copy.27.tokens_ref
  9.5 50.7 %project_gather.1 = (bf16[512,1472]{1,0:T(8,128)(2,1)}, bf16[512,1472]{1,0:T(8,128)(2,1)}, bf16[512,256]{1,0:T(8,128)(2,1)}, bf16[512,384]{1,0:T(8,128)(2,1)}, b...) custom-call(s32[8]{0:T(128)} %lengths.3, ...), custom_call_target="tpu_custom_call" | custom-call | tf_op jit(solution)/shard_map/project_gather/pallas_call | solution.py:702
  60.2 0.0 copy-done.2
  60.2 1.2 copy.28
  61.4 0.0 all-gather.3.cloned.1.call-update
  61.4 0.0 all-gather.5.cloned.1.call-start
  61.4 13.2 %attention_forward.1 = (bf16[512,256]{1,0:T(8,128)(2,1)}, f32[512,256]{1,0:T(8,128)}, bf16[512,256]{1,0:T(8,128)(2,1)}) custom-call(s32[8]{0:T(128)} %lengths.3, f32[3,32]{1,0:T(4,128)} %bitcast.44, bf16[512,256]{1,0:T(8,128)(2,1)} %get-tuple-element.54.q_ref, f32[2,3,256,512]{3,2,1,0:T(8,128)} %get-tuple-element.56.near_hbm, bf16[8192,384]{1,0:T(8,128)(2,1)} %bitcast.23, ...), custom_call_target="tpu_custom_call" | custom-call | tf_op jit(solution)/shard_map/attention_forward/pallas_call | solution.py:272
  74.6 0.0 all-gather.5.cloned.1.call-update
  74.7 13.6 %all-gather.3.cloned.1.call-done.cot_ref = bf16[512,1472]{1,0:T(8,128)(2,1)} async-done(((bf16[256,1472]{1,0:T(8,128)(2,1)}), bf16[512,1472]{1,0:T(8,128)(2,1)}) %all-gather.3.cloned.1.call-update) | async-done | bytes 1507344 | tf_op jit(solution)/shard_map/all_gather | solution.py:2152
  88.2 62.2 %feed_forward.1 = (f32[256,1472]{1,0:T(8,128)}, f32[256,1472]{1,0:T(8,128)}, bf16[256,1472]{1,0:T(8,128)(2,1)}, bf16[256,1472]{1,0:T(8,128)(2,1)}, bf16[256,1472...) custom-call(bf16[512,256]{1,0:T(8,128)(2,1)} %get-tuple-element.60.a, ...), custom_call_target="tpu_custom_call" | custom-call | tf_op jit(solution)/shard_map/feed_forward/pallas_call | solution.py:1369
  150.4 0.0 all-gather.5.cloned.1.call-done.qall_hbm
  150.4 0.0 copy-start.1
  150.4 133.4 %backward.1 = (bf16[512,256]{1,0:T(8,128)(2,1)}, f32[3,32,128]{2,1,0:T(8,128)}, bf16[512,256]{1,0:T(8,128)(2,1)}, bf16[512,256]{1,0:T(8,128)(2,1)}, f32[2,8,256]...) custom-call(f32[3,32]{1,0:T(4,128)} %bitcast.45, ...), custom_call_target="tpu_custom_call" | custom-call | tf_op jit(solution)/shard_map/backward/pallas_call | solution.py:2039
  283.8 0.0 copy-done.1
  283.8 1.7 add_convert_fusion
  285.5 1.1 copy.30
  286.6 60.9 %finish.1 = (f32[256,1472]{1,0:T(8,128)}, f32[256]{0:T(256)}, bf16[4,2,2,48,1472]{4,3,2,1,0:T(8,128)(2,1)}, f32[1472]{0:T(1024)}, f32[1472]{0:T(1024)}, /*index=5*/f32[3,32]{1,0:T(4,128)}) custom-call(bf16[512,256]{1,0:T(8,128)(2,1)} %get-tuple-element.77.dq_hbm, bf16[512,256]{1,0:T(8,128)(2,1)} %get-tuple-element.78.dk_hbm, ...), custom_call_target="tpu_custom_call" | custom-call | tf_op jit(solution)/shard_map/finish/pallas_call | solution.py:1092
  347.6 0.0 copy-start
  347.6 3.1 copy.31
  350.7 0.0 copy-done
  350.7 0.0 copy-start.6
  350.7 0.0 copy-start.5
  350.8 2.4 fusion
  353.2 0.6 copy.39
  353.7 0.6 copy.40
  354.3 0.6 copy.41
  354.9 0.6 copy.42
  355.5 0.0 copy-done.5
  355.5 0.8 copy.43
  356.4 0.8 copy.44
  357.2 0.8 copy.45
  (12 shorter events, 0.0 us)
Async XLA Ops:
  7.2 81.0 %all-gather.3.cloned.1.call-start = ((), (), s32[]{:S(2)}) async-start(), calls=%async_computation | async-start | bytes 2359296 | tf_op jit(solution)/shard_map/all_gather | solution.py:2152
  9.5 50.7 %copy-start.2 = (bf16[256,1472]{0,1:T(8,128)(2,1)S(1)}, bf16[256,1472]{0,1:T(8,128)(2,1)}, u32[]{:S(2)}) copy-start(bf16[256,1472]{0,1:T(8,128)(2,1)} %param.27) | copy-start | bytes 2260996
  61.4 89.0 %all-gather.5.cloned.1.call-start = ((), (), s32[]{:S(2)}) async-start(), calls=%async_computation.1 | async-start | bytes 4456448 | tf_op jit(solution)/shard_map/all_gather | solution.py:2159
  150.4 133.4 %copy-start.1 = (f32[256,1472]{1,0:T(8,128)S(1)}, f32[256,1472]{1,0:T(8,128)}, u32[]{:S(2)}) copy-start(f32[256,1472]{1,0:T(8,128)} %get-tuple-element.65) | copy-start | bytes 4521988
  347.6 3.1 copy-start
  350.7 2.4 copy-start.9
  350.7 3.0 copy-start.7
  350.7 3.6 copy-start.8
  350.7 4.2 %copy-start.6 = (f32[1472]{0:T(1024)S(1)}, f32[1472]{0:T(1024)}, u32[]{:S(2)}) copy-start(f32[1472]{0:T(1024)} %get-tuple-element.134) | copy-start | bytes 17668
  350.7 4.8 %copy-start.5 = (f32[112,1472]{1,0:T(8,128)S(1)}, f32[112,1472]{1,0:T(8,128)}, u32[]{:S(2)}) copy-start(f32[112,1472]{1,0:T(8,128)} %get-tuple-element.92) | copy-start | bytes 1978372
  353.2 3.2 copy-start.4
  353.2 4.1 %copy-start.3 = (f32[112,1472]{1,0:T(8,128)S(1)}, f32[112,1472]{1,0:T(8,128)}, u32[]{:S(2)}) copy-start(f32[112,1472]{1,0:T(8,128)} %get-tuple-element.137) | copy-start | bytes 1978372
Sparse Core Ops, SparseCore 0:
  61.5 26.6 all-gather.2
  90.9 53.4 all-gather.4

commit v12 on v11

--- a/solution.py
+++ b/solution.py
@@ -14,6 +14,7 @@
 eps = 1e-06
 far_left_bucket = 15
 far_right_bucket = 31
+slack = 20.0
 WIDE = 256
 TQ = 256
 TK = 512
@@ -136,7 +137,7 @@
 def fwd_kernel(
     plan, lines, reach, rows, pair, lengths, table_ref, q_ref, near_hbm, g_hbm, aug_hbm, masks_hbm,
     low_ref, wide_ref, qb_ref,
-    km, vm, mask_row, g_buf, aug_buf, near_ref, acc, row_max, qh_ref, g_sem, near_sem,
+    km, vm, mask_row, g_buf, aug_buf, near_ref, acc, extra, row_max, qh_ref, g_sem, near_sem,
 ):
     base = lax.axis_index("ctx") * pair
     origin = jnp.clip(base - reach * pair, 0, 4 * lines * pair - rows)
@@ -230,21 +231,44 @@
 
         def far(n, unused):
             parts = far_pair(start, n, n_left, count, far_left_bucket, far_right_bucket)
-            for h in range(plan.heads):
-                scores = [
-                    (nt(qh_ref[h], km[part, :]) + mask_row[0:1, part], table_ref[h, bucket])
+
+            def scores_of(h):
+                return [
+                    (nt(qh_ref[h], km[part, :]) + (mask_row[0:1, part] + table_ref[h, bucket]), part)
                     for part, bucket in parts
                 ]
-                old = row_max[h][:, :1]
-                top = old
-                for s, offset in scores:
-                    top = jnp.maximum(top, jnp.max(s, axis=1, keepdims=True) + offset)
-                more = [
-                    nn(jnp.exp(s - (top - offset)).astype(bf16), vm[part, :])
-                    for (s, offset), (part, bucket) in zip(scores, parts)
-                ]
-                acc[h] = acc[h] * jnp.exp(old - top) + (more[0] + more[1])
-                row_max[h] = jnp.broadcast_to(top, (TQ, 128))
+
+            worst = jnp.full((TQ, 128), -slack, f32)
+            for h in range(plan.heads):
+                top = row_max[h]
+                more = jnp.zeros((TQ, WIDE), f32)
+                for s, part in scores_of(h):
+                    tiles_of = []
+                    for c in range(0, TK, 128):
+                        over = s[:, c : c + 128] - top
+                        worst = jnp.maximum(worst, over)
+                        tiles_of.append(jnp.exp(over).astype(bf16))
+                    more = more + nn(jnp.concatenate(tiles_of, axis=1), vm[part, :])
+                extra[h] = more
+            passed = jnp.max(worst) > slack
+
+            @pl.when(jnp.logical_not(passed))
+            def _():
+                for h in range(plan.heads):
+                    acc[h] += extra[h]
+
+            @pl.when(passed)
+            def _():
+                for h in range(plan.heads):
+                    scores = scores_of(h)
+                    old = row_max[h][:, :1]
+                    top = old
+                    for s, part in scores:
+                        top = jnp.maximum(top, jnp.max(s, axis=1, keepdims=True))
+                    more = [nn(jnp.exp(s - top).astype(bf16), vm[part, :]) for s, part in scores]
+                    acc[h] = acc[h] * jnp.exp(old - top) + (more[0] + more[1])
+                    row_max[h] = jnp.broadcast_to(top, (TQ, 128))
+
             return unused
 
         lax.fori_loop(0, (count + 1) // 2, far, 0)
@@ -286,6 +310,7 @@
             pltpu.VMEM((2, pair, 128), bf16),
             pltpu.VMEM((heads, TQ, TK), f32),
             pltpu.VMEM((heads, TQ, WIDE), f32),
+            pltpu.VMEM((heads, TQ, WIDE), f32),
             pltpu.VMEM((heads, TQ, 128), f32),
             pltpu.VMEM((heads, TQ, WIDE), bf16),
             pltpu.SemaphoreType.DMA((3, 2)),
@@ -443,16 +468,16 @@
     for load in loads:
         load.wait()
 
-    def project(base):
-        rows = rows_at(base, half)
+    def project(base, size):
+        rows = rows_at(base, size)
         qkv = nt(x_ref[rows, :], weights[...]).astype(bf16)
         own_ref[rows, :] = qkv[:, : 2 * cols]
         q_ref[rows, :cols] = qkv[:, 2 * cols :]
 
     pieces = [
         (ours, half, True),
-        (theirs, half // 2, True),
-        (theirs + half // 2, half // 2, False),
+        (theirs + half // 2, half // 2, True),
+        (theirs, half // 2, False),
         None,
     ]
     mask_piece = 3
@@ -612,7 +637,7 @@
 
     begin(mask_piece)
     lax.fori_loop(0, 2, own_lanes, 0)
-    project(ours)
+    project(ours, half)
     begin(0)
     lax.fori_loop(0, lines, zero_start, 0)
     near_lanes(plan.heads, table_ref, near_ref)
@@ -625,12 +650,13 @@
         return unused
 
     lax.fori_loop(0, 2, y_wait, 0)
+    project(theirs, half // 2)
+    begin(2)
     level(0, 1)
     level(mask_piece, 1)
     lax.fori_loop(2, 4, y_wait, 0)
     far_copy.start()
-    project(theirs)
-    begin(2)
+    project(theirs + half // 2, half // 2)
     begin(1)
     if span > 1:
         level(0, 2)
@@ -1151,7 +1177,7 @@
     stacks, refs = (refs[:3], refs[3:])
     (
         wg, wu, wd, wo, inner, gg, gu, x_ref, att_in, d_out, d_in, e_out, e_in,
-        acc_f, acc_g, rows_buf, load_sem, y_sem, out_sem,
+        acc_g, rows_buf, load_sem, y_sem, out_sem,
     ) = refs
     spot = Spot(cycle_size // 4)
     wa = spot.wa
@@ -1217,9 +1243,6 @@
 
     def feed(base):
         rows = rows_at(base, half)
-        acc_f[...] = jnp.zeros_like(acc_f)
-        acc_g[...] = jnp.zeros_like(acc_g)
-
         def tile(u, unused):
             cols = rows_at(u * wide, wide)
             gate = nn(x_ref[rows, :], wg[:, cols])
@@ -1238,11 +1261,34 @@
             inner[rows, cols] = inner_low
             gg[rows, cols] = gate_low
             gu[rows, cols] = up_low
-            acc_g[...] += nt(gate_low, wg[:, cols]) + nt(up_low, wu[:, cols])
-            acc_f[...] += nt(inner_low, wd[:, cols])
             return unused
 
         lax.fori_loop(0, units // wide, tile, 0)
+
+    def columns(body):
+        def chunk_of(c, unused):
+            body(rows_at(c * wide, wide))
+            return unused
+
+        lax.fori_loop(0, model // wide, chunk_of, 0)
+        if model % wide:
+            body(pl.ds(model // wide * wide, model % wide))
+
+    def back_to_rows(base):
+        rows = rows_at(base, half)
+
+        def body(cols):
+            acc_g[:, cols] = nt(gg[rows, :], wg[cols, :]) + nt(gu[rows, :], wu[cols, :])
+
+        columns(body)
+
+    def forward_to_rows(base, out):
+        rows = rows_at(base, half)
+
+        def body(cols):
+            out[:, cols] = nt(inner[rows, :], wd[cols, :]).astype(bf16)
+
+        columns(body)
 
     def d_copy(i):
         return send(
@@ -1257,21 +1303,19 @@
     def half_pass(k, unused):
         base = theirs + k * (ours - theirs)
         feed(base)
+        back_to_rows(base)
 
         @pl.when(k == 0)
         def _():
             lax.fori_loop(0, 4, send_grad, 0)
             normal(2, ours, True)
             normal(3, ours, True)
-            ffn_far_ref[...] = acc_f[...].astype(bf16)
-
-        @pl.when(k == 1)
-        def _():
-            ffn_ref[...] = acc_f[...].astype(bf16)
 
         return unused
 
     lax.fori_loop(0, 2, half_pass, 0)
+    forward_to_rows(theirs, ffn_far_ref)
+    forward_to_rows(ours, ffn_ref)
     count = units // wide
 
     def out_copy(m, u):
@@ -1395,7 +1439,6 @@
             pltpu.VMEM((4, chunk, WIDE), bf16),
             pltpu.VMEM((4, chunk, WIDE), bf16),
             pltpu.VMEM((half, model), f32),
-            pltpu.VMEM((half, model), f32),
             pltpu.VMEM((3, 2, WIDE, model), bf16),
             dma((5,)),
             dma((2, 12)),
@@ -1979,7 +2022,7 @@
     def due(time, run, *args):
         events.append((max(0, int((time - start_us) / slot_us)), functools.partial(run, *args)))
 
-    start_us, slot_us = (6.0, 2.0)
+    start_us, slot_us = (6.0, 2.5)
     due(6.0, turn)
     for k in range(1, span + 1):
         due((22.0, 36.0)[min(k, 2) - 1], level, k)

time: 365 us -> 353 us (0.967); the launches traced: 365 us -> 348 us
  waiting for transfers between devices: 13.6 us -> 4.91 us
  Pallas kernels: 320 us -> 312 us
    pallas_call x1, Pallas kernels: 13.2 us -> 25.8 us  [attend(): pl.pallas_call(functools.partial(fwd_kernel, plan, cycle_size // 4, reach...]
    pallas_call x1, Pallas kernels: 133 us -> 121 us  [backward(): pl.pallas_call(functools.partial(backward_kernel, plan, lines, span, reac...]
    all_gather x1, waiting for transfers between devices: 13.6 us -> 4.85 us  [shards(): pair_cot = lax.all_gather(cot_late, 'wa', axis=0, tiled=True)]
    pallas_call x1, Pallas kernels: 50.7 us -> 46 us  [first(): pl.pallas_call(functools.partial(first_kernel, plan, lines, span, reach,...]
  transfers between devices with their start and end apart: 2 -> 2, of which waited for: 1 -> 1; matrix products, arithmetic and copies ran while one was open for 0% -> 0% of each run, Pallas kernels for 21% -> 24%
where the time goes in v12:
time: 353 us; the launch traced here: 348 us
  Pallas kernels  312 us (88%)
  local copies, waits for them, and re-layouts  15 us (4%)
  between operations  14.2 us (4%)
  waiting for transfers between devices  4.91 us (1%)
    pallas_call x1, Pallas kernels, backward(): pl.pallas_call(functools.partial(backward_kernel, plan, lines, span, reac...  121 us
    pallas_call x1, Pallas kernels, finish(): pl.pallas_call(functools.partial(finish_kernel, plan, lines), out_shape=[...  59.7 us
    pallas_call x1, Pallas kernels, middle(): pl.pallas_call(functools.partial(middle_kernel, plan, cycle_size), out_sh...  59 us
    pallas_call x1, Pallas kernels, first(): pl.pallas_call(functools.partial(first_kernel, plan, lines, span, reach,...  46 us
    pallas_call x1, Pallas kernels, attend(): pl.pallas_call(functools.partial(fwd_kernel, plan, cycle_size // 4, reach...  25.8 us
    unnamed x30, local copies, waits for them, and re-layouts  11.5 us
  transfers between devices with their start and end apart: 2, of which 1 were waited for; matrix products, arithmetic and copies ran while one was open for 0% of the time, Pallas kernels for 24%

profile of v12, /device:TPU:0, one launch (start us, length us, event | category | flops | bytes accessed | tf_op | source)
XLA Modules:
  0.0 347.7 jit_solution(2279023731319031937)
XLA Ops:
  7.2 0.0 all-gather.3.cloned.1.call-start
  7.2 2.3 copy.27.tokens_ref
  9.5 46.0 %project_gather.1 = (bf16[512,1472]{1,0:T(8,128)(2,1)}, bf16[512,1472]{1,0:T(8,128)(2,1)}, bf16[512,256]{1,0:T(8,128)(2,1)}, bf16[512,384]{1,0:T(8,128)(2,1)}, b...) custom-call(s32[8]{0:T(128)} %lengths.3, ...), custom_call_target="tpu_custom_call" | custom-call | tf_op jit(solution)/shard_map/project_gather/pallas_call | solution.py:728
  55.5 0.0 copy-done.2
  55.5 1.2 copy.28
  56.7 0.0 all-gather.3.cloned.1.call-update
  56.7 0.0 all-gather.5.cloned.1.call-start
  56.8 25.8 %attention_forward.1 = (bf16[512,256]{1,0:T(8,128)(2,1)}, f32[512,256]{1,0:T(8,128)}, bf16[512,256]{1,0:T(8,128)(2,1)}) custom-call(s32[8]{0:T(128)} %lengths.3, f32[3,32]{1,0:T(4,128)} %bitcast.44, bf16[512,256]{1,0:T(8,128)(2,1)} %get-tuple-element.54.q_ref, f32[2,3,256,512]{3,2,1,0:T(8,128)} %get-tuple-element.56.near_hbm, bf16[8192,384]{1,0:T(8,128)(2,1)} %bitcast.23, ...), custom_call_target="tpu_custom_call" | custom-call | tf_op jit(solution)/shard_map/attention_forward/pallas_call | solution.py:296
  82.6 0.0 all-gather.5.cloned.1.call-update
  82.6 4.9 %all-gather.3.cloned.1.call-done.cot_ref = bf16[512,1472]{1,0:T(8,128)(2,1)} async-done(((bf16[256,1472]{1,0:T(8,128)(2,1)}), bf16[512,1472]{1,0:T(8,128)(2,1)}) %all-gather.3.cloned.1.call-update) | async-done | bytes 1507344 | tf_op jit(solution)/shard_map/all_gather | solution.py:2195
  87.5 59.0 %feed_forward.1 = (f32[256,1472]{1,0:T(8,128)}, f32[256,1472]{1,0:T(8,128)}, bf16[256,1472]{1,0:T(8,128)(2,1)}, bf16[256,1472]{1,0:T(8,128)(2,1)}, bf16[256,1472...) custom-call(bf16[512,256]{1,0:T(8,128)(2,1)} %get-tuple-element.60.a, ...), custom_call_target="tpu_custom_call" | custom-call | tf_op jit(solution)/shard_map/feed_forward/pallas_call | solution.py:1413
  146.5 0.0 all-gather.5.cloned.1.call-done.qall_hbm
  146.5 0.0 copy-start.1
  146.5 121.3 %backward.1 = (bf16[512,256]{1,0:T(8,128)(2,1)}, f32[3,32,128]{2,1,0:T(8,128)}, bf16[512,256]{1,0:T(8,128)(2,1)}, bf16[512,256]{1,0:T(8,128)(2,1)}, f32[2,8,256]...) custom-call(f32[3,32]{1,0:T(4,128)} %bitcast.45, ...), custom_call_target="tpu_custom_call" | custom-call | tf_op jit(solution)/shard_map/backward/pallas_call | solution.py:2082
  267.8 0.0 copy-done.1
  267.8 1.7 add_convert_fusion
  269.5 1.1 copy.30
  270.6 59.7 %finish.1 = (f32[256,1472]{1,0:T(8,128)}, f32[256]{0:T(256)}, bf16[4,2,2,48,1472]{4,3,2,1,0:T(8,128)(2,1)}, f32[1472]{0:T(1024)}, f32[1472]{0:T(1024)}, /*index=5*/f32[3,32]{1,0:T(4,128)}) custom-call(bf16[512,256]{1,0:T(8,128)(2,1)} %get-tuple-element.77.dq_hbm, bf16[512,256]{1,0:T(8,128)(2,1)} %get-tuple-element.78.dk_hbm, ...), custom_call_target="tpu_custom_call" | custom-call | tf_op jit(solution)/shard_map/finish/pallas_call | solution.py:1118
  330.4 0.0 copy-start
  330.4 3.1 copy.31
  333.5 0.0 copy-done
  333.5 2.4 fusion
  336.0 0.0 copy-done.9
  336.0 0.6 copy.39
  336.5 0.6 copy.40
  337.1 0.6 copy.41
  337.7 0.0 copy-done.6
  337.7 0.6 copy.42
  338.3 0.8 copy.43
  339.2 0.0 copy-done.4
  339.2 0.8 copy.44
  340.0 0.8 copy.45
  (12 shorter events, 0.0 us)
Async XLA Ops:
  7.2 80.3 %all-gather.3.cloned.1.call-start = ((), (), s32[]{:S(2)}) async-start(), calls=%async_computation | async-start | bytes 2359296 | tf_op jit(solution)/shard_map/all_gather | solution.py:2195
  9.5 46.0 %copy-start.2 = (bf16[256,1472]{0,1:T(8,128)(2,1)S(1)}, bf16[256,1472]{0,1:T(8,128)(2,1)}, u32[]{:S(2)}) copy-start(bf16[256,1472]{0,1:T(8,128)(2,1)} %param.27) | copy-start | bytes 2260996
  56.7 89.8 %all-gather.5.cloned.1.call-start = ((), (), s32[]{:S(2)}) async-start(), calls=%async_computation.1 | async-start | bytes 4456448 | tf_op jit(solution)/shard_map/all_gather | solution.py:2202
  146.5 121.3 %copy-start.1 = (f32[256,1472]{1,0:T(8,128)S(1)}, f32[256,1472]{1,0:T(8,128)}, u32[]{:S(2)}) copy-start(f32[256,1472]{1,0:T(8,128)} %get-tuple-element.65) | copy-start | bytes 4521988
  330.4 3.1 copy-start
  333.5 2.4 copy-start.9
  333.5 3.0 copy-start.7
  333.5 3.6 %copy-start.8 = (f32[3,32]{1,0:T(4,128)S(1)}, f32[3,32]{1,0:T(4,128)}, u32[]{:S(2)}) copy-start(f32[3,32]{1,0:T(4,128)} %get-tuple-element.90) | copy-start | bytes 1156
  333.5 4.2 %copy-start.6 = (f32[1472]{0:T(1024)S(1)}, f32[1472]{0:T(1024)}, u32[]{:S(2)}) copy-start(f32[1472]{0:T(1024)} %get-tuple-element.134) | copy-start | bytes 17668
  333.5 4.8 %copy-start.5 = (f32[112,1472]{1,0:T(8,128)S(1)}, f32[112,1472]{1,0:T(8,128)}, u32[]{:S(2)}) copy-start(f32[112,1472]{1,0:T(8,128)} %get-tuple-element.92) | copy-start | bytes 1978372
  336.0 3.2 copy-start.4
  336.0 4.1 %copy-start.3 = (f32[112,1472]{1,0:T(8,128)S(1)}, f32[112,1472]{1,0:T(8,128)}, u32[]{:S(2)}) copy-start(f32[112,1472]{1,0:T(8,128)} %get-tuple-element.137) | copy-start | bytes 1978372
Sparse Core Ops, SparseCore 0:
  56.8 30.5 all-gather.2
  90.2 50.6 all-gather.4

commit v13 on v12

--- a/solution.py
+++ b/solution.py
@@ -392,8 +392,8 @@
 
 def first_kernel(
     plan, lines, span, reach, rows, lengths, table_ref, tokens_ref, gain_ref, key_mask_ref,
-    wq_hbm, wk_hbm, wv_hbm, wo_hbm,
-    x_ref, tok_ref, q_ref, own_ref, aug_ref, own_aug_ref, near_ref, masks_ref, wo_far_hbm, all_hbm,
+    wq_hbm, wk_hbm, wv_hbm, cot_hbm,
+    x_ref, tok_ref, q_ref, own_ref, aug_ref, own_aug_ref, near_ref, masks_ref, cot_pair_hbm, all_hbm,
     weights, zeros, mask_ref, load_sem, y_sem, own_sem, zero_sem, z_sem, x_sem, c_sem,
 ):
     spot = Spot(lines)
@@ -450,7 +450,17 @@
         return unused
 
     lax.fori_loop(0, 4, y_start, 0)
-    far_copy = send(wo_hbm, wo_far_hbm, y_sem.at[0, 4], y_sem.at[1, 4], spot.y_mate())
+    far_copy = send(
+        cot_hbm,
+        cot_pair_hbm.at[rows_at(ours, half)],
+        y_sem.at[0, 4],
+        y_sem.at[1, 4],
+        spot.y_mate(),
+    )
+    near_copy = pltpu.make_async_copy(
+        cot_hbm, cot_pair_hbm.at[rows_at(ours, half)], load_sem.at[3]
+    )
+    near_copy.start()
 
     def scaled(rows_in):
         rows_in = rows_in.astype(f32)
@@ -714,10 +724,11 @@
 
     lax.fori_loop(0, 4, y_drain, 0)
     far_copy.wait()
+    near_copy.wait()
 
 
 def first(
-    plan, cycle_size, reach, rows, lengths, table, tokens, gain, mask, w_query, w_key, w_value, w_out
+    plan, cycle_size, reach, rows, lengths, table, tokens, gain, mask, w_query, w_key, w_value, cot
 ):
     lines = cycle_size // 4
     span = min(lines - 1, (reach + 3) // 4)
@@ -736,7 +747,7 @@
             jax.ShapeDtypeStruct((pair, 128), bf16),
             jax.ShapeDtypeStruct((2, plan.heads, TQ, TK), f32),
             jax.ShapeDtypeStruct((lines, 2, 2, 8, pair), f32),
-            jax.ShapeDtypeStruct(w_out.shape, bf16),
+            jax.ShapeDtypeStruct((pair, model), bf16),
             jax.ShapeDtypeStruct((lines, 2, 2, pair, 2 * plan.cols), bf16),
         ],
         in_specs=[smem] * 2 + [vmem] * 3 + [hbm] * 4,
@@ -745,7 +756,7 @@
             pltpu.VMEM((3 * plan.cols, model), bf16),
             pltpu.VMEM((pair, 2 * plan.cols), bf16),
             pltpu.VMEM((8, pair), f32),
-            dma((3,)),
+            dma((4,)),
             dma((2, 5)),
             dma((4,)),
             dma((lines, 2, 2)),
@@ -757,7 +768,7 @@
             vmem_limit_bytes=56 * 2**20, collective_id=4, has_side_effects=True
         ),
         name="project_gather",
-    )(lengths, table, tokens, gain, mask, w_query.T, w_key.T, w_value.T, w_out)
+    )(lengths, table, tokens, gain, mask, w_query.T, w_key.T, w_value.T, cot)
 
 
 def tn(a, b):
@@ -794,9 +805,10 @@
 
 def finish_kernel(
     plan, lines, dq_hbm, dk_hbm, dv_hbm, att_hbm, normed_hbm, branch_hbm, far_hbm,
-    wq_hbm, wk_hbm, wv_hbm, mask_ref, tokens_ref, gain_ref, gh_ref, table_ref, gain_part_ref,
-    gt_ref, gm_ref, weights_ref, gain_one_ref, gain_two_ref, table_out_ref,
-    w3_ref, load_sem, lefts, rights, product, mine, core_in, x_in, up_in, down_in, all_w, y_out, y_in, own_part, mask_in,
+    wq_hbm, wk_hbm, wv_hbm, hidden_hbm, own_hbm, in_hbm,
+    mask_ref, tokens_ref, gain_ref, gh_ref, table_ref, gain_part_ref,
+    out_ref, turned_ref, gm_ref, weights_ref, gain_one_ref, gain_two_ref, table_out_ref,
+    gt_ref, hidden_ref, ffn_own, ffn_in, w3_ref, load_sem, lefts, rights, product, mine, core_in, x_in, up_in, down_in, all_w, y_out, y_in, own_part, mask_in,
     small_own, small_y, small_core, small_x, small_all,
     y_sem, core_sem, x_sem, up_sem, down_sem, gz_sem, gx_sem, gc_sem, sz_sem,
 ):
@@ -817,6 +829,9 @@
         (wq_hbm, w3_ref.at[pl.ds(0, cols)]),
         (wk_hbm, w3_ref.at[pl.ds(WIDE, cols)]),
         (wv_hbm, w3_ref.at[pl.ds(3 * WIDE - cols, cols)]),
+        (hidden_hbm, hidden_ref),
+        (own_hbm, ffn_own),
+        (in_hbm, ffn_in),
     )
     loads = [
         pltpu.make_async_copy(src, dst, load_sem.at[i]) for i, (src, dst) in enumerate(targets)
@@ -1072,6 +1087,14 @@
     gain_two_ref[...] = jnp.sum(totals[1:2], axis=0)
     for h in range(plan.heads):
         table_out_ref[h : h + 1, :] = totals[2:3, 32 * h : 32 * h + 32]
+    for i in (10, 11, 12):
+        loads[i].wait()
+    for c in range(0, model, 128):
+        end = min(model, c + 128)
+        turned_ref[c:end, :] = jnp.transpose(gt_ref[:, c:end])
+        total = hidden_ref[:, c:end] + ffn_own[:, c:end].astype(f32) + ffn_in[:, c:end].astype(f32)
+        out_ref[c:end, :] = jnp.transpose(total).astype(bf16)
+
     def spread(d, unused):
         across(d).wait()
         beside(d).start()
@@ -1112,24 +1135,29 @@
 
 def finish(plan, cycle_size, *operands):
     lines = cycle_size // 4
-    half, model = operands[11].shape
+    half, model = operands[14].shape
     rows = 4 * plan.cols // cycle_size
     dma = pltpu.SemaphoreType.DMA
     return pl.pallas_call(
         functools.partial(finish_kernel, plan, lines),
         out_shape=[
-            jax.ShapeDtypeStruct((half, model), f32),
+            jax.ShapeDtypeStruct((model, half), bf16),
+            jax.ShapeDtypeStruct((model, half), f32),
             jax.ShapeDtypeStruct((half,), f32),
             jax.ShapeDtypeStruct((lines, 2, 2, rows, model), bf16),
             jax.ShapeDtypeStruct((model,), f32),
             jax.ShapeDtypeStruct((model,), f32),
             jax.ShapeDtypeStruct((plan.heads, 32), f32),
         ],
-        in_specs=[pl.BlockSpec(memory_space=pl.ANY)] * 10 + [vmem] * 6,
-        out_specs=[vmem] * 6,
+        in_specs=[pl.BlockSpec(memory_space=pl.ANY)] * 13 + [vmem] * 6,
+        out_specs=[vmem] * 7,
         scratch_shapes=[
+            pltpu.VMEM((half, model), f32),
+            pltpu.VMEM((half, model), f32),
+            pltpu.VMEM((half, model), bf16),
+            pltpu.VMEM((half, model), bf16),
             pltpu.VMEM((3 * WIDE, model), bf16),
-            dma((10,)),
+            dma((13,)),
             pltpu.VMEM((4, 2 * half, WIDE), bf16),
             pltpu.VMEM((2, 2 * half, model), bf16),
             pltpu.VMEM((WIDE, model), bf16),
@@ -1171,7 +1199,7 @@
 
 def middle_kernel(
     plan, cycle_size, att_ref, mixed_ref, tokens_ref, cot_ref, gain_ref,
-    wo_hbm, wo_far_hbm, wg_hbm, wu_hbm, wd_hbm,
+    wo_hbm, wo_pair_hbm, wg_hbm, wu_hbm, wd_hbm,
     hidden_ref, gh_ref, branch_ref, ffn_ref, ffn_far_ref, do_ref, gain_part_ref, *refs,
 ):
     stacks, refs = (refs[:3], refs[3:])
@@ -1191,7 +1219,7 @@
         for i, (src, dst) in enumerate(
             (
                 (wo_hbm, wo.at[0, 64:]),
-                (wo_far_hbm, wo.at[1, 64:]),
+                (wo_pair_hbm.at[1 - wa], wo.at[1, 64:]),
                 (wg_hbm, wg),
                 (wu_hbm, wu),
                 (wd_hbm, wd),
@@ -1402,7 +1430,7 @@
 
 
 def middle(
-    plan, cycle_size, attended, mixed, tokens, cot, gain, w_out, w_out_far, w_gate, w_up, w_down
+    plan, cycle_size, attended, mixed, tokens, cot, gain, w_out, w_out_pair, w_gate, w_up, w_down
 ):
     pair, model = tokens.shape
     half = pair // 2
@@ -1448,7 +1476,7 @@
             vmem_limit_bytes=60 * 2**20, collective_id=3, has_side_effects=True
         ),
         name="feed_forward",
-    )(attended, mixed, tokens, cot, gain, w_out, w_out_far, w_gate, w_up, w_down.T)
+    )(attended, mixed, tokens, cot, gain, w_out, w_out_pair, w_gate, w_up, w_down.T)
 
 
 class Scatter:
@@ -1603,7 +1631,7 @@
         m = self.units[u][0]
         self.outs[m][self.rows_of(u), :] = self.mine[
             m, self.spot.z, self.spot.x, self.rows_of(u)
-        ].astype(f32)
+        ]
 
     def drain(self, u):
         z, lines = (self.spot.z, self.spot.lines)
@@ -2088,7 +2116,7 @@
             jax.ShapeDtypeStruct((pair, WIDE), bf16),
             jax.ShapeDtypeStruct((pair // TQ, 8, TQ), f32),
         ]
-        + [jax.ShapeDtypeStruct((size, model), f32)] * 3
+        + [jax.ShapeDtypeStruct((size, model), bf16)] * 3
         + [
             jax.ShapeDtypeStruct(branch.shape, bf16),
             jax.ShapeDtypeStruct(branch.shape, bf16),
@@ -2174,7 +2202,7 @@
 
     gather = functools.partial(lax.all_gather, axis_name="ctx", axis=0, tiled=True)
     (
-        pair_normed, pair_tokens, q_wide, own_kv, k_aug, own_aug, near_bias, masks, far_out, kv_all,
+        pair_normed, pair_tokens, q_wide, own_kv, k_aug, own_aug, near_bias, masks, pair_cot, kv_all,
     ) = first(
         plan,
         cycle_size,
@@ -2188,11 +2216,11 @@
         w_query,
         w_key,
         w_value,
-        w_out,
+        cotangent,
     )
     masks = masks.reshape(cycle_size, 8, pair)
-    cot_late, near_bias = lax.optimization_barrier((cotangent, near_bias))
-    pair_cot = lax.all_gather(cot_late, "wa", axis=0, tiled=True)
+    w_late, near_bias = lax.optimization_barrier((w_out, near_bias))
+    pair_w_out = lax.all_gather(w_late, "wa", axis=0)
     if rows < total_rows:
         masks = lax.dynamic_slice_in_dim(masks, origin // pair, rows // pair, 0)
     kv_all = window(kv_all.reshape(total_rows, 2 * plan.cols))
@@ -2209,7 +2237,7 @@
         pair_cot,
         gain_ffn,
         w_out,
-        far_out,
+        pair_w_out,
         w_gate,
         w_up,
         w_down,
@@ -2237,9 +2265,10 @@
         ffn_far,
         stacks,
     )
-    grad_w_gate, grad_w_up = (grad_w_gate.T, grad_w_up.T)
-    layer_out = (hidden + ffn_own.astype(f32) + ffn_in.astype(f32)).astype(bf16)
-    grad_tokens, grad_mask, weights, grad_gain_attn, grad_gain_ffn, grad_table = finish(
+    grad_w_down, grad_w_gate, grad_w_up = (
+        grad_w_down.astype(f32), grad_w_gate.astype(f32).T, grad_w_up.astype(f32).T
+    )
+    layer_out, grad_tokens, grad_mask, weights, grad_gain_attn, grad_gain_ffn, grad_table = finish(
         plan,
         cycle_size,
         grad_queries,
@@ -2252,6 +2281,9 @@
         w_query.T,
         w_key.T,
         w_value.T,
+        hidden,
+        ffn_own,
+        ffn_in,
         mask_part.reshape(group, 8, own_rows),
         tokens,
         gain_attn,
@@ -2261,8 +2293,8 @@
     )
     weights = weights.reshape(4, plan.cols, model).astype(f32)
     return (
-        layer_out,
-        grad_tokens,
+        layer_out.T,
+        grad_tokens.T,
         grad_mask,
         grad_gain_attn,
         weights[0].T,

time: 353 us -> 348 us (0.986)
  Pallas kernels: 312 us -> 302 us
  waiting for transfers between devices: 4.91 us -> 14.9 us
    pallas_call x1, Pallas kernels: 25.8 us -> 11.4 us  [attend(): pl.pallas_call(functools.partial(fwd_kernel, plan, cycle_size // 4, reach...]
    all_gather x1, waiting for transfers between devices: 4.85 us -> 14.8 us  [shards(): pair_w_out = lax.all_gather(w_late, 'wa', axis=0)]
    unnamed x30 -> x28, local copies, waits for them, and re-layouts: 11.5 us -> 7.86 us
  transfers between devices with their start and end apart: 2 -> 2, of which waited for: 1 -> 1; matrix products, arithmetic and copies ran while one was open for 0% -> 0% of each run, Pallas kernels for 24% -> 20%
where the time goes in v13:
time: 348 us; the launch traced here: 345 us
  Pallas kernels  302 us (87%)
  waiting for transfers between devices  14.9 us (4%)
  between operations  14.2 us (4%)
  local copies, waits for them, and re-layouts  11.9 us (3%)
    pallas_call x1, Pallas kernels, backward(): pl.pallas_call(functools.partial(backward_kernel, plan, lines, span, reac...  125 us
    pallas_call x1, Pallas kernels, finish(): pl.pallas_call(functools.partial(finish_kernel, plan, lines), out_shape=[...  60.6 us
    pallas_call x1, Pallas kernels, middle(): pl.pallas_call(functools.partial(middle_kernel, plan, cycle_size), out_sh...  59 us
    pallas_call x1, Pallas kernels, first(): pl.pallas_call(functools.partial(first_kernel, plan, lines, span, reach,...  45.9 us
    all_gather x1, waiting for transfers between devices, shards(): pair_w_out = lax.all_gather(w_late, 'wa', axis=0)  14.8 us
    pallas_call x1, Pallas kernels, attend(): pl.pallas_call(functools.partial(fwd_kernel, plan, cycle_size // 4, reach...  11.4 us
    unnamed x28, local copies, waits for them, and re-layouts  7.86 us
  transfers between devices with their start and end apart: 2, of which 1 were waited for; matrix products, arithmetic and copies ran while one was open for 0% of the time, Pallas kernels for 20%

profile of v13, /device:TPU:0, one launch (start us, length us, event | category | flops | bytes accessed | tf_op | source)
XLA Modules:
  0.0 344.7 jit_solution(3976218796894862048)
XLA Ops:
  7.2 0.0 copy-start.1
  7.2 0.0 all-gather.6.cloned.1.call-start
  7.2 2.3 copy.27.tokens_ref
  9.6 0.0 copy-done.1
  9.6 1.2 copy.28.cot_hbm
  10.7 45.9 %project_gather.1 = (bf16[512,1472]{1,0:T(8,128)(2,1)}, bf16[512,1472]{1,0:T(8,128)(2,1)}, bf16[512,256]{1,0:T(8,128)(2,1)}, bf16[512,384]{1,0:T(8,128)(2,1)}, b...) custom-call(s32[8]{0:T(128)} %lengths.3, ...), custom_call_target="tpu_custom_call" | custom-call | tf_op jit(solution)/shard_map/project_gather/pallas_call | solution.py:739
  56.7 0.0 all-gather.6.cloned.1.call-update
  56.7 0.0 all-gather.4.cloned.1.call-start
  56.7 11.4 %attention_forward.1 = (bf16[512,256]{1,0:T(8,128)(2,1)}, f32[512,256]{1,0:T(8,128)}, bf16[512,256]{1,0:T(8,128)(2,1)}) custom-call(s32[8]{0:T(128)} %lengths.3, f32[3,32]{1,0:T(4,128)} %bitcast.50, bf16[512,256]{1,0:T(8,128)(2,1)} %get-tuple-element.55.q_ref, f32[2,3,256,512]{3,2,1,0:T(8,128)} %get-tuple-element.57.near_hbm, bf16[8192,384]{1,0:T(8,128)(2,1)} %bitcast.28, ...), custom_call_target="tpu_custom_call" | custom-call | tf_op jit(solution)/shard_map/attention_forward/pallas_call | solution.py:296
  68.2 0.0 all-gather.4.cloned.1.call-update
  68.2 14.8 %all-gather.6.cloned.1.call-done = bf16[384,1472]{1,0:T(8,128)(2,1)} async-done(((bf16[192,1472]{1,0:T(8,128)(2,1)}), bf16[384,1472]{1,0:T(8,128)(2,1)}) %all-gather.6.cloned.1.call-update) | async-done | bytes 1130512 | tf_op jit(solution)/shard_map/all_gather | solution.py:2223
  83.0 59.0 %feed_forward.1 = (f32[256,1472]{1,0:T(8,128)}, f32[256,1472]{1,0:T(8,128)}, bf16[256,1472]{1,0:T(8,128)(2,1)}, bf16[256,1472]{1,0:T(8,128)(2,1)}, bf16[256,1472...) custom-call(bf16[512,256]{1,0:T(8,128)(2,1)} %get-tuple-element.62.a, ...), custom_call_target="tpu_custom_call" | custom-call | tf_op jit(solution)/shard_map/feed_forward/pallas_call | solution.py:1441
  142.0 0.0 all-gather.4.cloned.1.call-done.qall_hbm
  142.0 124.6 %backward.1 = (bf16[512,256]{1,0:T(8,128)(2,1)}, f32[3,32,128]{2,1,0:T(8,128)}, bf16[512,256]{1,0:T(8,128)(2,1)}, bf16[512,256]{1,0:T(8,128)(2,1)}, f32[2,8,256]...) custom-call(f32[3,32]{1,0:T(4,128)} %bitcast.51, ...), custom_call_target="tpu_custom_call" | custom-call | tf_op jit(solution)/shard_map/backward/pallas_call | solution.py:2110
  266.6 0.0 copy-start.3
  266.6 60.6 %finish.1 = (bf16[1472,256]{1,0:T(8,128)(2,1)}, f32[1472,256]{1,0:T(8,128)}, f32[256]{0:T(256)}, bf16[4,2,2,48,1472]{4,3,2,1,0:T(8,128)(2,1)}, f32[1472]{0:T(1024)}, /*index=5*/f32[1472]{0:T(1024)}, f32[3,32]{1,0:T(4,128)}) custom-call(bf16[512,256]{1,0:T(8,128)(2,1)} %get-tuple-element.75.dq_hbm, bf16[512,256]{1,0:T(8,128)(2,1)} %get-tuple-element.76.dk_hbm, ...), custom_call_target="tpu_custom_call" | custom-call | tf_op jit(solution)/shard_map/finish/pallas_call | solution.py:1141
  327.2 0.0 copy-done.3
  327.2 0.9 convert_element_type.10
  328.1 4.1 %fusion = (f32[1,2,2,48,1472]{4,3,2,1,0:T(8,128)}, f32[1,2,2,48,1472]{4,3,2,1,0:T(8,128)}, f32[1,2,2,48,1472]{4,3,2,1,0:T(8,128)}, f32[1,2,2,48,1472]{4,3,2,1,0:T(8,128)}) fusion(bf16[4,2,2,48,1472]{4,3,2,1,0:T(8,128)(2,1)} %get-tuple-element.91), kind=kLoop, calls=%fused_computation.2 | loop fusion | bytes 9043968 | tf_op jit(solution)/shard_map/slice | solution.py:2303
  332.2 0.0 copy-done.4
  332.2 0.0 copy-done.5
  332.2 0.0 copy-start
  332.2 1.2 convert_bitcast_fusion
  333.5 0.0 copy-done.2
  333.5 0.9 copy.36
  334.3 0.0 copy-done
  334.4 0.0 copy-start.6
  334.4 1.1 copy.37
  335.5 0.6 copy.38
  336.1 0.6 copy.39
  336.7 0.6 copy.40
  337.2 0.6 copy.41
  (10 shorter events, 0.0 us)
Async XLA Ops:
  7.2 2.4 copy-start.1
  7.2 75.8 %all-gather.6.cloned.1.call-start = ((), (), s32[]{:S(2)}) async-start(), calls=%async_computation.1 | async-start | bytes 1769472 | tf_op jit(solution)/shard_map/all_gather | solution.py:2223
  56.7 85.3 %all-gather.4.cloned.1.call-start = ((), (), s32[]{:S(2)}) async-start(), calls=%async_computation | async-start | bytes 4456448 | tf_op jit(solution)/shard_map/all_gather | solution.py:2230
  266.6 60.6 %copy-start.3 = (bf16[112,1472]{1,0:T(8,128)(2,1)S(1)}, bf16[112,1472]{1,0:T(8,128)(2,1)}, u32[]{:S(2)}) copy-start(bf16[112,1472]{1,0:T(8,128)(2,1)} %get-tuple-element.96) | copy-start | bytes 989188
  328.1 4.1 %copy-start.4 = (bf16[112,1472]{1,0:T(8,128)(2,1)S(1)}, bf16[112,1472]{1,0:T(8,128)(2,1)}, u32[]{:S(2)}) copy-start(bf16[112,1472]{1,0:T(8,128)(2,1)} %get-tuple-element.94) | copy-start | bytes 989188
  328.1 4.1 %copy-start.5 = (bf16[112,1472]{1,0:T(8,128)(2,1)S(1)}, bf16[112,1472]{1,0:T(8,128)(2,1)}, u32[]{:S(2)}) copy-start(bf16[112,1472]{1,0:T(8,128)(2,1)} %get-tuple-element.95) | copy-start | bytes 989188
  332.2 1.3 copy-start.2
  332.2 2.1 copy-start
  334.3 1.1 copy-start.9
  334.3 1.7 copy-start.7
  334.3 2.3 copy-start.8
  334.4 2.9 copy-start.6
Sparse Core Ops, SparseCore 0:
  56.8 26.1 all-gather.5
  85.7 51.2 all-gather.3

commit v14 on v13

--- a/solution.py
+++ b/solution.py
@@ -2068,8 +2068,8 @@
         if u > 0:
             due(core_at, scatter.core_stage, u)
         due(x_at, scatter.x_stage, u)
-        due(one_at, scatter.relay, u, 1)
-        due(two_at, scatter.relay, u, 2)
+        due(one_at - 3.0, scatter.relay, u, 1)
+        due(two_at - 3.0, scatter.relay, u, 2)
         due(end_at, scatter.settle, u)
     events.sort(key=lambda event: event[0])
     end = max(work, events[-1][0] + 1)

time: 348 us -> 346 us (level)
  waiting for transfers between devices: 14.9 us -> 0.08 us
  Pallas kernels: 302 us -> 316 us
    pallas_call x1, Pallas kernels: 11.4 us -> 26.8 us  [attend(): pl.pallas_call(functools.partial(fwd_kernel, plan, cycle_size // 4, reach...]
    all_gather x1, waiting for transfers between devices: 14.8 us -> 0.02 us  [shards(): pair_w_out = lax.all_gather(w_late, 'wa', axis=0)]
  transfers between devices with their start and end apart: 2 -> 2, of which waited for: 1 -> 0; matrix products, arithmetic and copies ran while one was open for 0% -> 0% of each run, Pallas kernels for 20% -> 25%
where the time goes in v14:
time: 346 us; the launch traced here: 345 us
  Pallas kernels  316 us (91%)
  between operations  14.2 us (4%)
  local copies, waits for them, and re-layouts  11.9 us (3%)
    pallas_call x1, Pallas kernels, backward(): pl.pallas_call(functools.partial(backward_kernel, plan, lines, span, reac...  124 us
    pallas_call x1, Pallas kernels, middle(): pl.pallas_call(functools.partial(middle_kernel, plan, cycle_size), out_sh...  60.1 us
    pallas_call x1, Pallas kernels, finish(): pl.pallas_call(functools.partial(finish_kernel, plan, lines), out_shape=[...  60 us
    pallas_call x1, Pallas kernels, first(): pl.pallas_call(functools.partial(first_kernel, plan, lines, span, reach,...  45.9 us
    pallas_call x1, Pallas kernels, attend(): pl.pallas_call(functools.partial(fwd_kernel, plan, cycle_size // 4, reach...  26.8 us
    unnamed x28, local copies, waits for them, and re-layouts  7.86 us
  transfers between devices with their start and end apart: 2, of which 0 were waited for; matrix products, arithmetic and copies ran while one was open for 0% of the time, Pallas kernels for 25%

profile of v14, /device:TPU:0, one launch (start us, length us, event | category | flops | bytes accessed | tf_op | source)
XLA Modules:
  0.0 344.8 jit_solution(17754011059862045607)
XLA Ops:
  7.2 0.0 copy-start.1
  7.2 0.0 all-gather.6.cloned.1.call-start
  7.2 2.3 copy.27.tokens_ref
  9.6 0.0 copy-done.1
  9.6 1.2 copy.28.cot_hbm
  10.7 45.9 %project_gather.1 = (bf16[512,1472]{1,0:T(8,128)(2,1)}, bf16[512,1472]{1,0:T(8,128)(2,1)}, bf16[512,256]{1,0:T(8,128)(2,1)}, bf16[512,384]{1,0:T(8,128)(2,1)}, b...) custom-call(s32[8]{0:T(128)} %lengths.3, ...), custom_call_target="tpu_custom_call" | custom-call | tf_op jit(solution)/shard_map/project_gather/pallas_call | solution.py:739
  56.7 0.0 all-gather.6.cloned.1.call-update
  56.7 0.0 all-gather.4.cloned.1.call-start
  56.7 26.8 %attention_forward.1 = (bf16[512,256]{1,0:T(8,128)(2,1)}, f32[512,256]{1,0:T(8,128)}, bf16[512,256]{1,0:T(8,128)(2,1)}) custom-call(s32[8]{0:T(128)} %lengths.3, f32[3,32]{1,0:T(4,128)} %bitcast.50, bf16[512,256]{1,0:T(8,128)(2,1)} %get-tuple-element.55.q_ref, f32[2,3,256,512]{3,2,1,0:T(8,128)} %get-tuple-element.57.near_hbm, bf16[8192,384]{1,0:T(8,128)(2,1)} %bitcast.28, ...), custom_call_target="tpu_custom_call" | custom-call | tf_op jit(solution)/shard_map/attention_forward/pallas_call | solution.py:296
  83.6 0.0 all-gather.4.cloned.1.call-update
  83.6 0.0 all-gather.6.cloned.1.call-done
  83.6 60.1 %feed_forward.1 = (f32[256,1472]{1,0:T(8,128)}, f32[256,1472]{1,0:T(8,128)}, bf16[256,1472]{1,0:T(8,128)(2,1)}, bf16[256,1472]{1,0:T(8,128)(2,1)}, bf16[256,1472...) custom-call(bf16[512,256]{1,0:T(8,128)(2,1)} %get-tuple-element.62.a, ...), custom_call_target="tpu_custom_call" | custom-call | tf_op jit(solution)/shard_map/feed_forward/pallas_call | solution.py:1441
  143.7 0.0 all-gather.4.cloned.1.call-done.qall_hbm
  143.8 123.5 %backward.1 = (bf16[512,256]{1,0:T(8,128)(2,1)}, f32[3,32,128]{2,1,0:T(8,128)}, bf16[512,256]{1,0:T(8,128)(2,1)}, bf16[512,256]{1,0:T(8,128)(2,1)}, f32[2,8,256]...) custom-call(f32[3,32]{1,0:T(4,128)} %bitcast.51, ...), custom_call_target="tpu_custom_call" | custom-call | tf_op jit(solution)/shard_map/backward/pallas_call | solution.py:2110
  267.3 0.0 copy-start.3
  267.3 60.0 %finish.1 = (bf16[1472,256]{1,0:T(8,128)(2,1)}, f32[1472,256]{1,0:T(8,128)}, f32[256]{0:T(256)}, bf16[4,2,2,48,1472]{4,3,2,1,0:T(8,128)(2,1)}, f32[1472]{0:T(1024)}, /*index=5*/f32[1472]{0:T(1024)}, f32[3,32]{1,0:T(4,128)}) custom-call(bf16[512,256]{1,0:T(8,128)(2,1)} %get-tuple-element.75.dq_hbm, bf16[512,256]{1,0:T(8,128)(2,1)} %get-tuple-element.76.dk_hbm, ...), custom_call_target="tpu_custom_call" | custom-call | tf_op jit(solution)/shard_map/finish/pallas_call | solution.py:1141
  327.4 0.0 copy-done.3
  327.4 0.9 convert_element_type.10
  328.3 4.1 %fusion = (f32[1,2,2,48,1472]{4,3,2,1,0:T(8,128)}, f32[1,2,2,48,1472]{4,3,2,1,0:T(8,128)}, f32[1,2,2,48,1472]{4,3,2,1,0:T(8,128)}, f32[1,2,2,48,1472]{4,3,2,1,0:T(8,128)}) fusion(bf16[4,2,2,48,1472]{4,3,2,1,0:T(8,128)(2,1)} %get-tuple-element.91), kind=kLoop, calls=%fused_computation.2 | loop fusion | bytes 9043968 | tf_op jit(solution)/shard_map/slice | solution.py:2303
  332.4 0.0 copy-done.4
  332.4 0.0 copy-done.5
  332.4 0.0 copy-start
  332.4 1.2 convert_bitcast_fusion
  333.6 0.0 copy-done.2
  333.6 0.9 copy.36
  334.5 0.0 copy-done
  334.5 0.0 copy-start.6
  334.5 1.1 copy.37
  335.6 0.6 copy.38
  336.2 0.6 copy.39
  336.8 0.6 copy.40
  337.4 0.6 copy.41
  (10 shorter events, 0.0 us)
Async XLA Ops:
  7.2 2.4 copy-start.1
  7.2 76.4 %all-gather.6.cloned.1.call-start = ((), (), s32[]{:S(2)}) async-start(), calls=%async_computation.1 | async-start | bytes 1769472 | tf_op jit(solution)/shard_map/all_gather | solution.py:2223
  56.7 87.1 %all-gather.4.cloned.1.call-start = ((), (), s32[]{:S(2)}) async-start(), calls=%async_computation | async-start | bytes 4456448 | tf_op jit(solution)/shard_map/all_gather | solution.py:2230
  267.3 60.0 %copy-start.3 = (bf16[112,1472]{1,0:T(8,128)(2,1)S(1)}, bf16[112,1472]{1,0:T(8,128)(2,1)}, u32[]{:S(2)}) copy-start(bf16[112,1472]{1,0:T(8,128)(2,1)} %get-tuple-element.96) | copy-start | bytes 989188
  328.3 4.1 %copy-start.4 = (bf16[112,1472]{1,0:T(8,128)(2,1)S(1)}, bf16[112,1472]{1,0:T(8,128)(2,1)}, u32[]{:S(2)}) copy-start(bf16[112,1472]{1,0:T(8,128)(2,1)} %get-tuple-element.94) | copy-start | bytes 989188
  328.3 4.1 %copy-start.5 = (bf16[112,1472]{1,0:T(8,128)(2,1)S(1)}, bf16[112,1472]{1,0:T(8,128)(2,1)}, u32[]{:S(2)}) copy-start(bf16[112,1472]{1,0:T(8,128)(2,1)} %get-tuple-element.95) | copy-start | bytes 989188
  332.4 1.3 copy-start.2
  332.4 2.1 copy-start
  334.5 1.1 copy-start.9
  334.5 1.7 copy-start.7
  334.5 2.3 copy-start.8
  334.5 2.9 copy-start.6
Sparse Core Ops, SparseCore 0:
  56.8 26.1 all-gather.5
  85.7 55.0 all-gather.3
